TPU v7x, 32 devices: a whole 2x2x4 slice. The times are simulated.
32 devices in a mesh: seq: 8 (over z, x), mp: 4 (over y, core).
Axes of the slice: x: 2, y: 2, z: 4, core: 2. Of those that a mesh axis runs over, the one named last changes fastest.
Arguments:
- frames: bfloat16 [8, 1024, 1024], P('mp', 'seq'), may hold values from -6 to 6
- segments: int32 [8, 1024], P('mp', 'seq'), may hold values from 0 to 7, never falling along the last dimension, each value on 1 to 896 neighbouring positions
- padding: int32 [8, 1024], P('mp', 'seq'), may hold values from 0 to 1, as said below
- codec_tokens: int32 [2, 8, 1024], P(None, 'mp', 'seq'), may hold values from 0 to 1023
- codebooks: bfloat16 [2048, 1024], P('mp'), may hold values from -6 to 6
- frame_prenorm: bfloat16 [1024], P('mp'), may hold values from 0.099609375 to 1.8984375
- frame_project: bfloat16 [1024, 3072], P('mp'), may hold values from -0.1875 to 0.1875
- frame_output: bfloat16 [1024, 1024], P('mp'), may hold values from -1.5 to 1.5
- frame_postnorm: bfloat16 [1024], P('mp'), may hold values from 0.099609375 to 1.8984375
- frame_expand: bfloat16 [1024, 4096], P('mp'), may hold values from -0.1875 to 0.1875
- frame_contract: bfloat16 [4096, 1024], P('mp'), may hold values from -0.09375 to 0.09375
- codec_prenorm: bfloat16 [1024], P('mp'), may hold values from 0.099609375 to 1.8984375
- codec_project: bfloat16 [1024, 3072], P('mp'), may hold values from -0.9375 to 0.9375
- codec_output: bfloat16 [1024, 1024], P('mp'), may hold values from -0.0546875 to 0.0546875
- codec_postnorm: bfloat16 [1024], P('mp'), may hold values from 0.099609375 to 1.8984375
- codec_expand: bfloat16 [1024, 4096], P('mp'), may hold values from -0.1875 to 0.1875
- codec_contract: bfloat16 [4096, 1024], P('mp'), may hold values from -0.09375 to 0.09375
- cotangent: bfloat16 [8, 1024, 3, 1024], P('mp', 'seq'), may hold values from -6 to 6
Outputs:
- output: bfloat16 [8, 1024, 3, 1024], P('mp', 'seq')
- frames_grad: float32 [8, 1024, 1024], P('mp', 'seq')
- codebooks_grad: float32 [2048, 1024], P('mp', 'seq')
- frame_prenorm_grad: float32 [1024], replicated
- frame_project_grad: float32 [1024, 3072], P('mp', 'seq')
- frame_output_grad: float32 [1024, 1024], P('mp', 'seq')
- frame_postnorm_grad: float32 [1024], replicated
- frame_expand_grad: float32 [1024, 4096], P('mp', 'seq')
- frame_contract_grad: float32 [4096, 1024], P('mp', 'seq')
- codec_prenorm_grad: float32 [1024], replicated
- codec_project_grad: float32 [1024, 3072], P('mp', 'seq')
- codec_output_grad: float32 [1024, 1024], P('mp', 'seq')
- codec_postnorm_grad: float32 [1024], replicated
- codec_expand_grad: float32 [1024, 4096], P('mp', 'seq')
- codec_contract_grad: float32 [4096, 1024], P('mp', 'seq')
Inputs may be any that keep to these rules, and one draw needn't show every extreme that they name: `segments`: within a row segment numbers never fall; each segment covers at most 896 frames, and one exactly that many. In each row padding is 1 on the frames before the row's live length and 0 after it; live lengths lie between 512 and 1024, and the first row has no padding.
All inputs are finite; a program needn't handle non-finite values.
Results may differ from a plain program's by a relative error of at most 0.018.
Values may be sent and summed in bfloat16 or wider, within the bound.
No kernel may reach another device: no remote copies, remote signals or barrier semaphores. Data moves between devices by JAX's collectives and lax.ppermute only.
A program may use at most 384 MiB of HBM per device.

v0:
```python
import jax
import jax.numpy as jnp
from jax import lax
from jax.sharding import PartitionSpec as P

HEADS = 16
HEAD = 64
CODES = 1024


EPSILON = 1e-05
MASKED = -1e30


def rms_scale(values, gain_vec):
    return (
        values * lax.rsqrt(jnp.mean(values * values, axis=-1, keepdims=True) + EPSILON) * gain_vec
    )


def matmul(former, latter):
    return jnp.dot(former, latter, preferred_element_type=jnp.float32)


def inner_left(former, latter):
    return lax.dot_general(
        former, latter, (((0,), (0,)), ((), ())), preferred_element_type=jnp.float32
    )


def inner_right(former, latter):
    return lax.dot_general(
        former, latter, (((1,), (1,)), ((), ())), preferred_element_type=jnp.float32
    )


def split_heads(values):
    return values.reshape(values.shape[:-1] + (HEADS, HEAD))


def front_pass(hidden, weights):
    normed = rms_scale(hidden, weights[0].astype(jnp.float32)).astype(jnp.bfloat16)
    projected = matmul(normed, weights[1]).astype(jnp.bfloat16)
    return (normed, projected)


def rear_pass(hidden, attended, weights):
    mixed_sum = hidden + matmul(attended, weights[2])
    normed_two = rms_scale(mixed_sum, weights[3].astype(jnp.float32)).astype(jnp.bfloat16)
    expanded = matmul(normed_two, weights[4])
    activated = jax.nn.gelu(expanded).astype(jnp.bfloat16)
    result = mixed_sum + matmul(activated, weights[5])
    return (result, (mixed_sum, normed_two, expanded, activated))


def rear_grads(result_grad, attended, saved_state, weights):
    mixed_sum, normed_two, expanded, activated = saved_state
    contract_input = result_grad.astype(jnp.bfloat16)
    contract_grad = inner_left(activated, contract_input)
    active_grad = inner_right(contract_input, weights[5])
    expand_input = jax.vjp(jax.nn.gelu, expanded)[1](active_grad)[0].astype(jnp.bfloat16)
    expand_grad = inner_left(normed_two, expand_input)
    normed_grad = inner_right(expand_input, weights[4])
    mixed_part, postnorm_grad = jax.vjp(rms_scale, mixed_sum, weights[3].astype(jnp.float32))[1](
        normed_grad
    )
    mixed_grad = result_grad + mixed_part
    output_input = mixed_grad.astype(jnp.bfloat16)
    output_grad = inner_left(attended, output_input)
    attended_grad = inner_right(output_input, weights[2]).astype(jnp.bfloat16)
    return (mixed_grad, attended_grad, (postnorm_grad, expand_grad, contract_grad, output_grad))


def front_grads(hidden, normed, projected_grad, mixed_grad, weights):
    project_grad = inner_left(normed, projected_grad)
    normed_grad = inner_right(projected_grad, weights[1])
    hidden_part, prenorm_grad = jax.vjp(rms_scale, hidden, weights[0].astype(jnp.float32))[1](
        normed_grad
    )
    return (mixed_grad + hidden_part, prenorm_grad, project_grad)


def frame_portions(queries, keys, query_seg, key_seg, query_pos):
    factor = HEAD ** (-0.5)
    scores = (
        jnp.einsum(
            "ihd,jhd->hij",
            split_heads(queries),
            split_heads(keys),
            preferred_element_type=jnp.float32,
        )
        * factor
    )
    key_pos = jnp.arange(keys.shape[0])
    allowed = (query_seg[:, None] == key_seg[None, :]) & (key_pos[None, :] <= query_pos[:, None])
    return jax.nn.softmax(jnp.where(allowed[None], scores, MASKED), axis=-1)


def frame_attend(projected, gathered, query_seg, query_pos):
    model_width = projected.shape[-1] // 3

    def one_row(row_items):
        row_proj, row_keys, row_values, row_qseg, row_kseg = row_items
        portions = frame_portions(
            row_proj[:, :model_width], row_keys, row_qseg, row_kseg, query_pos
        )
        attended = jnp.einsum(
            "hij,jhd->ihd",
            portions.astype(jnp.bfloat16),
            split_heads(row_values),
            preferred_element_type=jnp.float32,
        )
        return attended.reshape(row_proj.shape[0], model_width).astype(jnp.bfloat16)

    return lax.map(one_row, (projected, gathered[0], gathered[1], query_seg, gathered[2]))


def frame_attend_grads(projected, gathered, query_seg, query_pos, attended_grad):
    model_width = projected.shape[-1] // 3
    factor = HEAD ** (-0.5)

    def one_row(row_items):
        row_proj, row_keys, row_values, row_qseg, row_kseg, row_grad = row_items
        portions = frame_portions(
            row_proj[:, :model_width], row_keys, row_qseg, row_kseg, query_pos
        )
        portion_grad = jnp.einsum(
            "ihd,jhd->hij",
            split_heads(row_grad),
            split_heads(row_values),
            preferred_element_type=jnp.float32,
        )
        score_grad = (
            portions * (portion_grad - jnp.sum(portions * portion_grad, axis=-1, keepdims=True))
        ).astype(jnp.bfloat16)
        query_grad = (
            jnp.einsum(
                "hij,jhd->ihd",
                score_grad,
                split_heads(row_keys),
                preferred_element_type=jnp.float32,
            )
            * factor
        )
        return (
            query_grad.reshape(row_proj.shape[0], model_width),
            score_grad,
            portions.astype(jnp.bfloat16),
        )

    return lax.map(
        one_row, (projected, gathered[0], gathered[1], query_seg, gathered[2], attended_grad)
    )


def codec_heads(projected):
    split_view = projected.reshape(projected.shape[:-1] + (3, HEADS, HEAD))
    return (split_view[:, :, 0], split_view[:, :, 1], split_view[:, :, 2])


def codec_portions(queries, keys):
    factor = HEAD ** (-0.5)
    scores = (
        jnp.einsum("mihd,mjhd->mhij", queries, keys, preferred_element_type=jnp.float32) * factor
    )
    position = jnp.arange(queries.shape[1])
    causal = position[:, None] >= position[None, :]
    return jax.nn.softmax(jnp.where(causal, scores, MASKED), axis=-1)


def spread(grad):
    seq_count = lax.axis_size("seq")
    model_count = lax.axis_size("mp")
    height, breadth = grad.shape
    blocks = grad.reshape(model_count, height // model_count, seq_count, breadth // seq_count)
    return jnp.transpose(blocks, (2, 0, 1, 3)).reshape(
        seq_count * model_count, height // model_count, breadth // seq_count
    )


def shards(
    frames,
    segments,
    padding,
    codec_tokens,
    codebooks,
    frame_prenorm,
    frame_project,
    frame_output,
    frame_postnorm,
    frame_expand,
    frame_contract,
    codec_prenorm,
    codec_project,
    codec_output,
    codec_postnorm,
    codec_expand,
    codec_contract,
    cotangent,
):
    row_count, frames_dev, width = frames.shape
    frame_total = row_count * frames_dev
    positions = cotangent.shape[2]
    factor = HEAD ** (-0.5)
    frame_weights = (
        lax.all_gather(frame_prenorm, "mp", axis=0, tiled=True),
        lax.all_gather(frame_project, "mp", axis=0, tiled=True),
        lax.all_gather(frame_output, "mp", axis=0, tiled=True),
        lax.all_gather(frame_postnorm, "mp", axis=0, tiled=True),
        lax.all_gather(frame_expand, "mp", axis=0, tiled=True),
        lax.all_gather(frame_contract, "mp", axis=0, tiled=True),
    )
    codec_all = (
        lax.all_gather(codec_prenorm, "mp", axis=0, tiled=True),
        lax.all_gather(codec_project, "mp", axis=0, tiled=True),
        lax.all_gather(codec_output, "mp", axis=0, tiled=True),
        lax.all_gather(codec_postnorm, "mp", axis=0, tiled=True),
        lax.all_gather(codec_expand, "mp", axis=0, tiled=True),
        lax.all_gather(codec_contract, "mp", axis=0, tiled=True),
        lax.all_gather(codebooks, "mp", axis=0, tiled=True),
    )
    codec_weights = codec_all[:6]
    table = codec_all[6]
    query_pos = lax.axis_index("seq") * frames_dev + jnp.arange(frames_dev)
    query_seg = segments.astype(jnp.bfloat16)
    hidden = frames.astype(jnp.float32).reshape(frame_total, width)
    normed, projected_flat = front_pass(hidden, frame_weights)
    projected = projected_flat.reshape(row_count, frames_dev, 3 * width)
    gathered_first = (
        lax.all_gather(projected[..., width : 2 * width], "seq", axis=1, tiled=True),
        lax.all_gather(projected[..., 2 * width :], "seq", axis=1, tiled=True),
        lax.all_gather(query_seg, "seq", axis=1, tiled=True),
    )
    attended_rows = frame_attend(projected, gathered_first, query_seg, query_pos).reshape(
        frame_total, width
    )
    global_out, frame_saved = rear_pass(hidden, attended_rows, frame_weights)
    global_low = global_out.astype(jnp.bfloat16)
    codes_flat = codec_tokens.reshape(codec_tokens.shape[0], frame_total)
    group_in = lax.all_to_all(global_low, "seq", split_axis=0, concat_axis=0, tiled=True)
    group_codes = lax.all_to_all(codes_flat, "seq", split_axis=1, concat_axis=1, tiled=True)
    group_count = group_in.shape[0]
    table_rows = group_codes + (jnp.arange(codec_tokens.shape[0], dtype=jnp.int32) * CODES)[:, None]
    embedded = jnp.transpose(table[table_rows], (1, 0, 2)).astype(jnp.float32)
    frame_base = group_in.astype(jnp.float32)[:, None, :]
    local_in = jnp.concatenate([frame_base, frame_base + embedded], axis=1)
    codec_hidden = local_in.reshape(group_count * positions, width)
    codec_normed, codec_projected = front_pass(codec_hidden, codec_weights)
    queries, keys, values = codec_heads(codec_projected.reshape(group_count, positions, 3 * width))
    codec_soft = codec_portions(queries, keys)
    codec_attended = jnp.einsum(
        "mhij,mjhd->mihd",
        codec_soft.astype(jnp.bfloat16),
        values,
        preferred_element_type=jnp.float32,
    )
    codec_attended = codec_attended.reshape(group_count * positions, width).astype(jnp.bfloat16)
    codec_result, codec_saved = rear_pass(codec_hidden, codec_attended, codec_weights)
    result_low = codec_result.astype(jnp.bfloat16).reshape(group_count, positions, width)
    home_mask = padding.reshape(frame_total)[:, None, None].astype(jnp.bfloat16)
    masked_grad = cotangent.reshape(frame_total, positions, width) * home_mask
    home_result = lax.all_to_all(result_low, "seq", split_axis=0, concat_axis=0, tiled=True)
    group_grad = lax.all_to_all(masked_grad, "seq", split_axis=0, concat_axis=0, tiled=True)
    output = (home_result * home_mask).reshape(row_count, frames_dev, positions, width)
    codec_grad = group_grad.astype(jnp.float32).reshape(group_count * positions, width)
    mixed_grad, attended_grad, codec_rear = rear_grads(
        codec_grad, codec_attended, codec_saved, codec_weights
    )
    grad_heads = attended_grad.reshape(group_count, positions, HEADS, HEAD)
    portion_grad = jnp.einsum(
        "mihd,mjhd->mhij", grad_heads, values, preferred_element_type=jnp.float32
    )
    score_grad = (
        codec_soft * (portion_grad - jnp.sum(codec_soft * portion_grad, axis=-1, keepdims=True))
    ).astype(jnp.bfloat16)
    query_grad = (
        jnp.einsum("mhij,mjhd->mihd", score_grad, keys, preferred_element_type=jnp.float32) * factor
    )
    key_grad = (
        jnp.einsum("mhij,mihd->mjhd", score_grad, queries, preferred_element_type=jnp.float32)
        * factor
    )
    value_grad = jnp.einsum(
        "mhij,mihd->mjhd",
        codec_soft.astype(jnp.bfloat16),
        grad_heads,
        preferred_element_type=jnp.float32,
    )
    codec_projected_grad = jnp.concatenate(
        [
            query_grad.reshape(group_count * positions, width),
            key_grad.reshape(group_count * positions, width),
            value_grad.reshape(group_count * positions, width),
        ],
        axis=-1,
    ).astype(jnp.bfloat16)
    input_grad, codec_prenorm_grad, codec_project_grad = front_grads(
        codec_hidden, codec_normed, codec_projected_grad, mixed_grad, codec_weights
    )
    input_grad = input_grad.reshape(group_count, positions, width)
    table_grad = jax.ops.segment_sum(
        jnp.transpose(input_grad[:, 1:], (1, 0, 2)).reshape(-1, width),
        table_rows.reshape(-1),
        num_segments=table.shape[0],
    )
    base_grad = jnp.sum(input_grad, axis=1).astype(jnp.bfloat16)
    codec_postnorm_grad, codec_expand_grad, codec_contract_grad, codec_output_grad = codec_rear
    codec_sums = (
        lax.psum_scatter(
            spread(codec_project_grad), ("seq", "mp"), scatter_dimension=0, tiled=True
        ),
        lax.psum_scatter(spread(codec_output_grad), ("seq", "mp"), scatter_dimension=0, tiled=True),
        lax.psum_scatter(spread(codec_expand_grad), ("seq", "mp"), scatter_dimension=0, tiled=True),
        lax.psum_scatter(
            spread(codec_contract_grad), ("seq", "mp"), scatter_dimension=0, tiled=True
        ),
        lax.psum_scatter(spread(table_grad), ("seq", "mp"), scatter_dimension=0, tiled=True),
    )
    home_grad = lax.all_to_all(base_grad, "seq", split_axis=0, concat_axis=0, tiled=True)
    key_sets = (
        lax.all_gather(projected[..., width : 2 * width], "seq", axis=1, tiled=True),
        lax.all_gather(projected[..., 2 * width :], "seq", axis=1, tiled=True),
        lax.all_gather(query_seg, "seq", axis=1, tiled=True),
    )
    attended_rows = frame_attend(projected, key_sets, query_seg, query_pos).reshape(
        frame_total, width
    )
    frame_saved = rear_pass(hidden, attended_rows, frame_weights)[1]
    frame_mixed_grad, frame_attended_grad, frame_rear = rear_grads(
        home_grad.astype(jnp.float32), attended_rows, frame_saved, frame_weights
    )
    attended_heads = frame_attended_grad.reshape(row_count, frames_dev, width)
    frame_query_grad, score_grads, portion_keep = frame_attend_grads(
        projected, key_sets, query_seg, query_pos, attended_heads
    )
    query_heads = split_heads(projected[..., :width])
    output_heads = split_heads(attended_heads)
    extent = frames_dev * lax.axis_size("seq")
    key_part = (
        jnp.einsum("rhij,rihd->jrhd", score_grads, query_heads, preferred_element_type=jnp.float32)
        * factor
    )
    value_part = jnp.einsum(
        "rhij,rihd->jrhd", portion_keep, output_heads, preferred_element_type=jnp.float32
    )
    key_value_grad = jnp.transpose(
        lax.psum_scatter(
            jnp.concatenate(
                [
                    key_part.reshape(extent, row_count, width),
                    value_part.reshape(extent, row_count, width),
                ],
                axis=-1,
            ),
            "seq",
            scatter_dimension=0,
            tiled=True,
        ),
        (1, 0, 2),
    )
    frame_projected_grad = (
        jnp.concatenate([frame_query_grad, key_value_grad], axis=-1)
        .astype(jnp.bfloat16)
        .reshape(frame_total, 3 * width)
    )
    frames_grad, frame_prenorm_grad, frame_project_grad = front_grads(
        hidden, normed, frame_projected_grad, frame_mixed_grad, frame_weights
    )
    frame_postnorm_grad, frame_expand_grad, frame_contract_grad, frame_output_grad = frame_rear
    frame_sums = (
        lax.psum_scatter(
            spread(frame_project_grad), ("seq", "mp"), scatter_dimension=0, tiled=True
        ),
        lax.psum_scatter(spread(frame_output_grad), ("seq", "mp"), scatter_dimension=0, tiled=True),
        lax.psum_scatter(spread(frame_expand_grad), ("seq", "mp"), scatter_dimension=0, tiled=True),
        lax.psum_scatter(
            spread(frame_contract_grad), ("seq", "mp"), scatter_dimension=0, tiled=True
        ),
    )
    gain_sums = lax.psum(
        (frame_prenorm_grad, frame_postnorm_grad, codec_prenorm_grad, codec_postnorm_grad),
        ("seq", "mp"),
    )
    return (
        output,
        frames_grad.reshape(row_count, frames_dev, width),
        codec_sums[4][0],
        gain_sums[0],
        frame_sums[0][0],
        frame_sums[1][0],
        gain_sums[1],
        frame_sums[2][0],
        frame_sums[3][0],
        gain_sums[2],
        codec_sums[0][0],
        codec_sums[1][0],
        gain_sums[3],
        codec_sums[2][0],
        codec_sums[3][0],
    )


def solution(mesh):
    placed = (
        P("mp", "seq", None),
        P("mp", "seq"),
        P("mp", "seq"),
        P(None, "mp", "seq"),
        P("mp", None),
        P("mp"),
        P("mp", None),
        P("mp", None),
        P("mp"),
        P("mp", None),
        P("mp", None),
        P("mp"),
        P("mp", None),
        P("mp", None),
        P("mp"),
        P("mp", None),
        P("mp", None),
        P("mp", "seq", None, None),
    )
    return jax.shard_map(
        shards,
        mesh=mesh,
        in_specs=placed,
        out_specs=(
            P("mp", "seq", None, None),
            P("mp", "seq", None),
            P("mp", "seq"),
            P(),
            P("mp", "seq"),
            P("mp", "seq"),
            P(),
            P("mp", "seq"),
            P("mp", "seq"),
            P(),
            P("mp", "seq"),
            P("mp", "seq"),
            P(),
            P("mp", "seq"),
            P("mp", "seq"),
        ),
        check_vma=False,
    )
```

profile of v0, /device:TPU:0, one launch (start us, length us, event | category | flops | bytes accessed | tf_op | source)
XLA Modules:
  0.0 2776.2 jit_solution(11864190268415142735)
XLA Ops:
  18.3 40.4 %all-gather.16.cloned.1.call-done = bf16[1024,3072]{1,0:T(8,128)(2,1)} async-done(((bf16[256,3072]{1,0:T(8,128)(2,1)}), bf16[1024,3072]{1,0:T(8,128)(2,1)}) %all-gather.16.cloned.1.call-update) | async-done | bytes 6291472 | tf_op jit(solution)/shard_map/all_gather | solution.py:207
  77.6 21.1 all_gather.54
  104.0 36.8 %all-gather.18.cloned.1.call-done = bf16[2,1024,1024]{1,2,0:T(8,128)(2,1)} async-done(((bf16[2,128,1024]{1,2,0:T(8,128)(2,1)}), bf16[2,1024,1024]{1,2,0:T(8,128)(2,1)}) %all-gather.18.cloned.1.call-update) | async-done | bytes 4194320 | tf_op jit(solution)/shard_map/all_gather | solution.py:231
  140.8 75.9 %all-gather.20.cloned.1.call-done = bf16[2,1024,1024]{1,2,0:T(8,128)(2,1)} async-done(((bf16[2,128,1024]{1,2,0:T(8,128)(2,1)}), bf16[2,1024,1024]{1,2,0:T(8,128)(2,1)}) %all-gather.20.cloned.1.call-update) | async-done | bytes 4194320 | tf_op jit(solution)/shard_map/all_gather | solution.py:230
  216.6 40.2 %while.30 = (s32[]{:T(128)}, bf16[2,128,1024]{2,1,0:T(8,128)(2,1)S(1)}, bf16[2,1024,1024]{1,2,0:T(8,128)(2,1)}, bf16[2,128]{1,0:T(2,128)(2,1)S(1)}, bf16[2,1024]...) while((s32[]{:T(128)}, ...), condition=%wide.region_4.5_spmd.clone, body=%wide.region_1.4_spmd.clone.sunk | while | flops 550241408 | bytes 33316732 | solution.py:115
  221.6 8.2 fusion.198
  240.8 8.9 fusion.198
  249.6 7.0 fusion.199
  260.9 37.7 %all-gather.24.cloned.1.call-done = bf16[1024,4096]{1,0:T(8,128)(2,1)} async-done(((bf16[256,4096]{1,0:T(8,128)(2,1)}), bf16[1024,4096]{1,0:T(8,128)(2,1)}) %all-gather.24.cloned.1.call-update) | async-done | bytes 8388624 | tf_op jit(solution)/shard_map/all_gather | solution.py:210
  298.6 9.5 fusion.60
  308.1 50.2 %all-gather.26.cloned.1.call-done = bf16[4096,1024]{1,0:T(8,128)(2,1)} async-done(((bf16[1024,1024]{1,0:T(8,128)(2,1)}), bf16[4096,1024]{1,0:T(8,128)(2,1)}) %all-gather.26.cloned.1.call-update) | async-done | bytes 8388624 | tf_op jit(solution)/shard_map/all_gather | solution.py:211
  358.3 8.2 fusion.85
  383.3 11.2 all-gather.28.cloned.1.call-done
  418.6 23.9 all-gather.30.cloned.1.call-done
  442.4 9.6 convolution_convert_fusion
  452.0 12.3 reshape_reshape.6
  464.4 6.7 fusion.118
  471.1 18.8 fusion.120
  489.9 8.3 fusion.66
  511.6 14.8 all-gather.34.cloned.1.call-done
  526.3 17.5 fusion.43
  543.8 42.4 %all-gather.36.cloned.1.call-done = bf16[4096,1024]{1,0:T(8,128)(2,1)} async-done(((bf16[1024,1024]{1,0:T(8,128)(2,1)}), bf16[4096,1024]{1,0:T(8,128)(2,1)}) %all-gather.36.cloned.1.call-update) | async-done | bytes 8388624 | tf_op jit(solution)/shard_map/all_gather | solution.py:219
  586.2 14.1 add_convert_fusion
  613.9 45.9 %all-to-all-done.2 = bf16[256,3,1024]{2,1,0:T(4,128)(2,1)S(1)} async-done(((bf16[256,3,1024]{2,1,0:T(4,128)(2,1)}), bf16[256,3,1024]{2,1,0:T(4,128)(2,1)S(1)}, u32[]{:S(2)}, u32[]{:S(2)}) %all-to-all-start.2) | async-done | bytes 1572896 | tf_op jit(solution)/shard_map/all_to_all | solution.py:262
  664.7 52.3 %all_to_all.43 = bf16[256,3,1024]{2,1,0:T(4,128)(2,1)} all-to-all(bf16[256,3,1024]{2,1,0:T(4,128)(2,1)S(1)} %copy.328), channel_id=1, replica_groups=mesh['seq'=8,'mp'=4] {'seq'}, dimensions={0} | all-to-all | bytes 3145728 | tf_op jit(solution)/shard_map/all_to_all | solution.py:263
  721.0 18.0 fusion.35
  739.1 12.6 multiply_reduce_fusion.3
  760.6 13.4 multiply_reduce_fusion.1
  774.0 7.4 multiply_convert_fusion.4
  794.1 8.7 fusion.67
  829.7 9.8 multiply_reduce_fusion.4
  856.4 12.0 all-to-all-done.4
  868.5 11.4 fusion.52
  892.3 50.4 %while.31 = (s32[]{:T(128)}, bf16[2,128,1024]{2,1,0:T(8,128)(2,1)}, bf16[2,16,128,1024]{3,2,1,0:T(8,128)(2,1)}, bf16[2,16,128,1024]{3,2,1,0:T(8,128)(2,1)}, bf16...) while((s32[]{:T(128)}, bf16[2,128,1024]{2,1,0:T(8,128)(2,1)}, ...), condition=%wide.region_19.20_spmd.clone, body=%wide.region_15.19_spmd.clone.sunk | while | flops 831388800 | bytes 122732592 | solution.py:151
  942.7 8.5 fusion.88
  951.2 8.8 copy.342
  960.0 8.0 broadcast_multiply_fusion
  968.0 8.7 copy.341
  976.7 11.8 pad_maximum_fusion
  1007.1 8.9 scatter_custom_fusion
  1029.0 6.7 copy.356
  1035.8 10.3 convolution_bitcast_fusion.2
  1046.1 10.7 copy.358
  1058.9 9.1 fusion.112
  1068.0 19.1 copy.413
  1087.0 7.1 bitcast_bitcast_fusion
  1094.1 19.3 copy.362
  1113.5 8.8 copy.385
  1123.0 9.1 convolution_bitcast_fusion
  1142.7 10.8 copy.412
  1155.5 19.1 copy.352
  1188.9 79.8 %reduce-scatter.11.cloned.1.call-done = f32[128,2,2048]{2,0,1:T(8,128)} async-done(((f32[1024,2,2048]{2,0,1:T(8,128)}), f32[128,2,2048]{2,0,1:T(8,128)}) %reduce-scatter.11.cloned.1.call-update) | async-done | bytes 2097168 | tf_op jit(solution)/shard_map/reduce_scatter | solution.py:347
  1272.5 7.4 convolution_bitcast_fusion.3
  1280.0 10.6 copy.348
  1298.8 39.5 %all-reduce = (f32[1024]{0:T(1024)}, f32[1024]{0:T(1024)}, f32[1024]{0:T(1024)}, f32[1024]{0:T(1024)}) all-reduce(f32[1024]{0:T(1024)S(1)} %get-tuple-element.409, f32[1024]{0:T(1024)S(1)} %copy-done.74, f32[1024]{0:T(1024)S(1)} %copy-done.73, f32[1024]{0:T(1024)S(1)} %copy-done.72), channel_id=1, replica_groups=mesh['seq'=8,'mp'=4] {'seq','mp'}, use_global_device_ids=true, to_apply=%region_25.26 | all-reduce | flops 4096 | bytes 32768 | tf_op jit(solution)/shard_map/psum | solution.py:380
  1339.6 72.3 %reduce-scatter.25.cloned.1.call-done = f32[1,256,128]{2,1,0:T(8,128)} async-done(((f32[32,256,128]{2,1,0:T(8,128)}), f32[1,256,128]{2,1,0:T(8,128)}) %reduce-scatter.25.cloned.1.call-update) | async-done | bytes 131088 | tf_op jit(solution)/shard_map/reduce_scatter | solution.py:312
  1411.9 139.8 %reduce-scatter.17.cloned.1.call-done = f32[1,256,128]{2,1,0:T(8,128)} async-done(((f32[32,256,128]{2,1,0:T(8,128)}), f32[1,256,128]{2,1,0:T(8,128)}) %reduce-scatter.17.cloned.1.call-update) | async-done | bytes 131088 | tf_op jit(solution)/shard_map/reduce_scatter | solution.py:374
  1551.8 147.4 %reduce-scatter.13.cloned.1.call-done = f32[1,512,128]{2,1,0:T(8,128)} async-done(((f32[32,512,128]{2,1,0:T(8,128)}), f32[1,512,128]{2,1,0:T(8,128)}) %reduce-scatter.13.cloned.1.call-update) | async-done | bytes 262160 | tf_op jit(solution)/shard_map/reduce_scatter | solution.py:317
  1699.2 159.1 %reduce-scatter.23.cloned.1.call-done = f32[1,256,384]{2,1,0:T(8,128)} async-done(((f32[32,256,384]{2,1,0:T(8,128)}), f32[1,256,384]{2,1,0:T(8,128)}) %reduce-scatter.23.cloned.1.call-update) | async-done | bytes 393232 | tf_op jit(solution)/shard_map/reduce_scatter | solution.py:309
  1858.3 184.9 %reduce-scatter.27.cloned.1.call-done = f32[1,256,512]{2,1,0:T(8,128)} async-done(((f32[32,256,512]{2,1,0:T(8,128)}), f32[1,256,512]{2,1,0:T(8,128)}) %reduce-scatter.27.cloned.1.call-update) | async-done | bytes 524304 | tf_op jit(solution)/shard_map/reduce_scatter | solution.py:313
  2043.2 187.3 %reduce-scatter.29.cloned.1.call-done = f32[1,1024,128]{2,1,0:T(8,128)} async-done(((f32[32,1024,128]{2,1,0:T(8,128)}), f32[1,1024,128]{2,1,0:T(8,128)}) %reduce-scatter.29.cloned.1.call-update) | async-done | bytes 524304 | tf_op jit(solution)/shard_map/reduce_scatter | solution.py:314
  2230.5 187.5 %reduce-scatter.19.cloned.1.call-done = f32[1,256,512]{2,1,0:T(8,128)} async-done(((f32[32,256,512]{2,1,0:T(8,128)}), f32[1,256,512]{2,1,0:T(8,128)}) %reduce-scatter.19.cloned.1.call-update) | async-done | bytes 524304 | tf_op jit(solution)/shard_map/reduce_scatter | solution.py:375
  2418.0 187.3 %reduce-scatter.21.cloned.1.call-done = f32[1,1024,128]{2,1,0:T(8,128)} async-done(((f32[32,1024,128]{2,1,0:T(8,128)}), f32[1,1024,128]{2,1,0:T(8,128)}) %reduce-scatter.21.cloned.1.call-update) | async-done | bytes 524304 | tf_op jit(solution)/shard_map/reduce_scatter | solution.py:376
  2605.3 163.6 %reduce-scatter.15.cloned.1.call-done = f32[1,256,384]{2,1,0:T(8,128)} async-done(((f32[32,256,384]{2,1,0:T(8,128)}), f32[1,256,384]{2,1,0:T(8,128)}) %reduce-scatter.15.cloned.1.call-update) | async-done | bytes 393232 | tf_op jit(solution)/shard_map/reduce_scatter | solution.py:371
  (403 shorter events, 333.6 us)
Async XLA Ops:
  7.2 51.5 %all-gather.16.cloned.1.call-start = ((), (), s32[]{:S(2)}) async-start(), calls=%async_computation.15 | async-start | bytes 7864320 | tf_op jit(solution)/shard_map/all_gather | solution.py:207
  7.9 132.8 %all-gather.18.cloned.1.call-start = ((), (), s32[]{:S(2)}) async-start(), calls=%async_computation.16 | async-start | bytes 4718592 | tf_op jit(solution)/shard_map/all_gather | solution.py:231
  18.3 45.0 %copy-start.39 = (bf16[256,1024]{1,0:T(8,128)(2,1)}, bf16[256,1024]{1,0:T(8,128)(2,1)S(1)}, u32[]{:S(2)}) copy-start(bf16[256,1024]{1,0:T(8,128)(2,1)S(1)} %multiply_convert_fusion.17) | copy-start | bytes 1572868
  65.3 151.3 %all-gather.20.cloned.1.call-start = ((), (), s32[]{:S(2)}) async-start(), calls=%async_computation.17 | async-start | bytes 4718592 | tf_op jit(solution)/shard_map/all_gather | solution.py:230
  66.0 190.9 %all-gather.22.cloned.1.call-start = ((), (), s32[]{:S(2)}) async-start(), calls=%async_computation.18 | async-start | bytes 2621440 | tf_op jit(solution)/shard_map/all_gather | solution.py:208
  66.6 232.0 %all-gather.24.cloned.1.call-start = ((), (), s32[]{:S(2)}) async-start(), calls=%async_computation.19 | async-start | bytes 10485760 | tf_op jit(solution)/shard_map/all_gather | solution.py:210
  67.2 291.1 %all-gather.26.cloned.1.call-start = ((), (), s32[]{:S(2)}) async-start(), calls=%async_computation.20 | async-start | bytes 10485760 | tf_op jit(solution)/shard_map/all_gather | solution.py:211
  67.8 9.8 copy-start.81
  67.8 30.9 %copy-start.83 = (bf16[256]{0:T(256)(128)(2,1)S(1)}, bf16[256]{0:T(256)(128)(2,1)}, u32[]{:S(2)}) copy-start(bf16[256]{0:T(256)(128)(2,1)} %param.30) | copy-start | bytes 1540
  67.8 326.6 %all-gather.28.cloned.1.call-start = ((), (), s32[]{:S(2)}) async-start(), calls=%async_computation.21 | async-start | bytes 5242880 | tf_op jit(solution)/shard_map/all_gather | solution.py:220
  68.6 373.9 %all-gather.30.cloned.1.call-start = ((), (), s32[]{:S(2)}) async-start(), calls=%async_computation.22 | async-start | bytes 7864320 | tf_op jit(solution)/shard_map/all_gather | solution.py:215
  69.3 436.7 %all-gather.32.cloned.1.call-start = ((), (), s32[]{:S(2)}) async-start(), calls=%async_computation.23 | async-start | bytes 2621440 | tf_op jit(solution)/shard_map/all_gather | solution.py:216
  70.0 456.3 %all-gather.34.cloned.1.call-start = ((), (), s32[]{:S(2)}) async-start(), calls=%async_computation.24 | async-start | bytes 10485760 | tf_op jit(solution)/shard_map/all_gather | solution.py:218
  71.3 295.2 %all-to-all-start.1 = ((s32[2,8,32]{2,0,1:T(2,128)}), s32[2,8,32]{2,0,1:T(2,128)S(1)}, u32[]{:S(2)}, u32[]{:S(2)}) async-start(s32[2,8,32]{2,0,1:T(2,128)} %copy.318), calls=%async_computation.1 | async-start | bytes 16384 | tf_op jit(solution)/shard_map/all_to_all | solution.py:241
  76.8 509.4 %all-gather.36.cloned.1.call-start = ((), (), s32[]{:S(2)}) async-start(), calls=%async_computation.25 | async-start | bytes 10485760 | tf_op jit(solution)/shard_map/all_gather | solution.py:219
  104.0 194.6 %copy-start.50 = (f32[4,1,256]{2,1,0:T(1,128)}, f32[4,1,256]{2,1,0:T(1,128)S(1)}, u32[]{:S(2)}) copy-start(f32[4,1,256]{2,1,0:T(1,128)S(1)} %convert_element_type.215) | copy-start | bytes 12292
  216.6 41.0 %copy-start.18 = (bf16[2,128,1024]{2,1,0:T(8,128)(2,1)S(1)}, bf16[2,128,1024]{2,1,0:T(8,128)(2,1)}, u32[]{:S(2)}) copy-start(bf16[2,128,1024]{2,1,0:T(8,128)(2,1)} %param.22) | copy-start | bytes 1572868
  256.8 51.3 %copy-start.1 = (bf16[2,128,3072]{1,2,0:T(8,128)(2,1)}, bf16[2,128,3072]{1,2,0:T(8,128)(2,1)S(1)}, u32[]{:S(2)}) copy-start(bf16[2,128,3072]{1,2,0:T(8,128)(2,1)S(1)} %get-tuple-element.727) | copy-start | bytes 4718596
  256.8 51.2 %copy-start.44 = (bf16[2,1024]{1,0:T(2,128)(2,1)}, bf16[2,1024]{1,0:T(2,128)(2,1)S(1)}, u32[]{:S(2)}) copy-start(bf16[2,1024]{1,0:T(2,128)(2,1)S(1)} %get-tuple-element.776) | copy-start | bytes 12292
  256.9 51.2 %copy-start.78 = (bf16[2,128]{1,0:T(2,128)(2,1)}, bf16[2,128]{1,0:T(2,128)(2,1)S(1)}, u32[]{:S(2)}) copy-start(bf16[2,128]{1,0:T(2,128)(2,1)S(1)} %get-tuple-element.778) | copy-start | bytes 1540
  260.3 98.0 %copy-start.12 = (f32[256,1024]{1,0:T(8,128)}, f32[256,1024]{1,0:T(8,128)S(1)}, u32[]{:S(2)}) copy-start(f32[256,1024]{1,0:T(8,128)S(1)} %get-tuple-element.482) | copy-start | bytes 3145732
  260.9 47.2 %copy-start.59 = (f32[256]{0:T(256)}, f32[256]{0:T(256)S(1)}, u32[]{:S(2)}) copy-start(f32[256]{0:T(256)S(1)} %fusion.97) | copy-start | bytes 3076
  358.3 13.7 copy-start.84
  358.3 18.8 copy-start.85
  366.5 35.6 %all-to-all-start = ((bf16[8,32,1024]{2,1,0:T(8,128)(2,1)}), bf16[8,32,1024]{2,1,0:T(8,128)(2,1)S(1)}, u32[]{:S(2)}, u32[]{:S(2)}) async-start(bf16[8,32,1024]{2,1,0:T(8,128)(2,1)} %bitcast.6), calls=%async_computation | async-start | bytes 1048576 | tf_op jit(solution)/shard_map/all_to_all | solution.py:240
  377.2 65.3 %copy-start.62 = (f32[4,1,256]{2,1,0:T(1,128)}, f32[4,1,256]{2,1,0:T(1,128)S(1)}, u32[]{:S(2)}) copy-start(f32[4,1,256]{2,1,0:T(1,128)S(1)} %convert_element_type.216) | copy-start | bytes 12292
  382.7 369.0 %copy-start.46 = (f32[4,1,256]{2,1,0:T(1,128)}, f32[4,1,256]{2,1,0:T(1,128)S(1)}, u32[]{:S(2)}) copy-start(f32[4,1,256]{2,1,0:T(1,128)S(1)} %convert_element_type.217) | copy-start | bytes 12292
  382.7 17.9 copy-start.53
  418.3 87.7 %copy-start.5 = (f32[768,1024]{1,0:T(8,128)}, f32[768,1024]{1,0:T(8,128)S(1)}, u32[]{:S(2)}) copy-start(f32[768,1024]{1,0:T(8,128)S(1)} %reshape.503) | copy-start | bytes 9437188
  418.5 33.5 %copy-start.55 = (f32[768]{0:T(1024)}, f32[768]{0:T(1024)S(1)}, u32[]{:S(2)}) copy-start(f32[768]{0:T(1024)S(1)} %add.220) | copy-start | bytes 9220
  418.6 33.5 %copy-start.64 = (f32[768]{0:T(1024)}, f32[768]{0:T(1024)S(1)}, u32[]{:S(2)}) copy-start(f32[768]{0:T(1024)S(1)} %rsqrt.47) | copy-start | bytes 9220
  511.6 240.1 %copy-start.48 = (f32[768]{0:T(1024)}, f32[768]{0:T(1024)S(1)}, u32[]{:S(2)}) copy-start(f32[768]{0:T(1024)S(1)} %fusion.95) | copy-start | bytes 9220
  526.3 59.9 %copy-start.7 = (f32[768,1024]{1,0:T(8,128)S(1)}, f32[768,1024]{1,0:T(8,128)}, u32[]{:S(2)}) copy-start(f32[768,1024]{1,0:T(8,128)} %get-tuple-element.486) | copy-start | bytes 9437188
  605.5 8.4 copy-start.82
  605.5 54.3 %all-to-all-start.2 = ((bf16[256,3,1024]{2,1,0:T(4,128)(2,1)}), bf16[256,3,1024]{2,1,0:T(4,128)(2,1)S(1)}, u32[]{:S(2)}, u32[]{:S(2)}) async-start(bf16[256,3,1024]{2,1,0:T(4,128)(2,1)} %reshape.504), calls=%async_computation.2 | async-start | bytes 4194304 | tf_op jit(solution)/shard_map/all_to_all | solution.py:262
  721.0 30.7 %copy-start.3 = (bf16[768,1024]{1,0:T(8,128)(2,1)}, bf16[768,1024]{1,0:T(8,128)(2,1)S(1)}, u32[]{:S(2)}) copy-start(bf16[768,1024]{1,0:T(8,128)(2,1)S(1)} %reshape.507) | copy-start | bytes 4718596
  721.0 18.1 copy-start.8
  739.1 12.6 copy-start.24
  774.0 7.4 copy-start.31
  781.5 6.7 copy-start.30
  829.7 9.8 copy-start.56
  829.7 9.8 copy-start.11
  850.6 17.8 all-to-all-start.4
  854.3 414.5 %reduce-scatter.11.cloned.1.call-start = ((), (), s32[]{:S(2)}) async-start(), calls=%async_computation.26 | async-start | bytes 18874368 | tf_op jit(solution)/shard_map/reduce_scatter | solution.py:347
  868.4 19.3 copy-start.25
  868.5 12.7 copy-start.13
  868.5 12.7 copy-start.51
  868.5 12.7 copy-start.60
  881.2 6.6 copy-start.69
  902.6 6.5 slice-start.1
  951.2 8.8 copy-start.29
  988.5 423.4 %reduce-scatter.25.cloned.1.call-start = ((), (), s32[]{:S(2)}) async-start(), calls=%async_computation.33 | async-start | bytes 4325376 | tf_op jit(solution)/shard_map/reduce_scatter | solution.py:312
  997.9 553.9 %reduce-scatter.17.cloned.1.call-start = ((), (), s32[]{:S(2)}) async-start(), calls=%async_computation.29 | async-start | bytes 4325376 | tf_op jit(solution)/shard_map/reduce_scatter | solution.py:374
  1002.4 696.8 %reduce-scatter.13.cloned.1.call-start = ((), (), s32[]{:S(2)}) async-start(), calls=%async_computation.27 | async-start | bytes 8650752 | tf_op jit(solution)/shard_map/reduce_scatter | solution.py:317
  1027.0 831.3 %reduce-scatter.23.cloned.1.call-start = ((), (), s32[]{:S(2)}) async-start(), calls=%async_computation.32 | async-start | bytes 12976128 | tf_op jit(solution)/shard_map/reduce_scatter | solution.py:309
  1056.8 986.4 %reduce-scatter.27.cloned.1.call-start = ((), (), s32[]{:S(2)}) async-start(), calls=%async_computation.34 | async-start | bytes 17301504 | tf_op jit(solution)/shard_map/reduce_scatter | solution.py:313
  1113.4 1117.0 %reduce-scatter.29.cloned.1.call-start = ((), (), s32[]{:S(2)}) async-start(), calls=%async_computation.35 | async-start | bytes 17301504 | tf_op jit(solution)/shard_map/reduce_scatter | solution.py:314
  1113.5 8.8 copy-start.4
  1138.3 1279.6 %reduce-scatter.19.cloned.1.call-start = ((), (), s32[]{:S(2)}) async-start(), calls=%async_computation.30 | async-start | bytes 17301504 | tf_op jit(solution)/shard_map/reduce_scatter | solution.py:375
  1174.7 1430.6 %reduce-scatter.21.cloned.1.call-start = ((), (), s32[]{:S(2)}) async-start(), calls=%async_computation.31 | async-start | bytes 17301504 | tf_op jit(solution)/shard_map/reduce_scatter | solution.py:376
  1186.9 84.5 %copy-start.43 = (bf16[2,128,1024]{2,1,0:T(8,128)(2,1)S(1)}, bf16[2,128,1024]{2,1,0:T(8,128)(2,1)}, u32[]{:S(2)}) copy-start(bf16[2,128,1024]{2,1,0:T(8,128)(2,1)} %get-tuple-element.133) | copy-start | bytes 1572868
  1186.9 1581.9 %reduce-scatter.15.cloned.1.call-start = ((), (), s32[]{:S(2)}) async-start(), calls=%async_computation.28 | async-start | bytes 12976128 | tf_op jit(solution)/shard_map/reduce_scatter | solution.py:371
  1293.3 45.0 %copy-start.67 = (f32[2,128]{1,0:T(2,128)S(1)}, f32[2,128]{1,0:T(2,128)}, u32[]{:S(2)}) copy-start(f32[2,128]{1,0:T(2,128)} %copy-done.66) | copy-start | bytes 3076
  1293.3 45.0 %copy-start.16 = (f32[256,1024]{1,0:T(8,128)S(1)}, f32[256,1024]{1,0:T(8,128)}, u32[]{:S(2)}) copy-start(f32[256,1024]{1,0:T(8,128)} %copy-done.15) | copy-start | bytes 3145732
  (55 other events, 160.2 us)
Sparse Core Ops, SparseCore 0:
  9.6 49.0 all-gather.15
  65.4 75.3 all-gather.17
  143.4 73.1 all-gather.19
  218.0 20.7 all-gather.21
  240.3 58.2 all-gather.23
  300.0 58.2 all-gather.25
  359.9 34.5 all-gather.27
  396.0 46.3 all-gather.29
  444.0 22.5 all-gather.31
  468.0 58.2 all-gather.33
  527.9 58.2 all-gather.35
  988.6 280.0 reduce-scatter.10
  1271.7 140.1 reduce-scatter.24
  1414.7 136.9 reduce-scatter.16
  1554.6 144.5 reduce-scatter.12
  1706.7 151.5 reduce-scatter.22
  1861.0 182.0 reduce-scatter.26
  2045.9 184.5 reduce-scatter.28
  2233.3 184.5 reduce-scatter.18
  2420.7 184.5 reduce-scatter.20
  2611.9 156.9 reduce-scatter.14
where the time goes:
time: 2780 us
  waiting for transfers between devices  1910 us (69%)
  matrix products  320 us (12%)
  local copies, waits for them, and re-layouts  309 us (11%)
  blocking collectives  135 us (5%)
  other arithmetic  68.3 us (2%)
    reduce_scatter x1, waiting for transfers between devices, shards(): lax.psum_scatter(spread(frame_expand_grad), ('seq', 'mp'), scatter_dimens...  187 us
    reduce_scatter x1, waiting for transfers between devices, shards(): lax.psum_scatter(spread(codec_contract_grad), ('seq', 'mp'), scatter_dime...  187 us
    reduce_scatter x1, waiting for transfers between devices, shards(): lax.psum_scatter(spread(frame_contract_grad), ('seq', 'mp'), scatter_dime...  187 us
    reduce_scatter x1, waiting for transfers between devices, shards(): lax.psum_scatter(spread(codec_expand_grad), ('seq', 'mp'), scatter_dimens...  185 us
    reduce_scatter x1, waiting for transfers between devices, shards(): lax.psum_scatter(spread(frame_project_grad), ('seq', 'mp'), scatter_dimen...  164 us
    reduce_scatter x1, waiting for transfers between devices, shards(): lax.psum_scatter(spread(codec_project_grad), ('seq', 'mp'), scatter_dimen...  159 us
    reduce_scatter x1, waiting for transfers between devices, shards(): lax.psum_scatter(spread(table_grad), ('seq', 'mp'), scatter_dimension=0,...  147 us
    reduce_scatter x1, waiting for transfers between devices, shards(): lax.psum_scatter(spread(frame_output_grad), ('seq', 'mp'), scatter_dimens...  140 us
  transfers between devices with their start and end apart: 25, of which 21 were waited for; matrix products, arithmetic and copies ran while one was open for 14% of the time, Pallas kernels for 0%

commit v1 on v0

v1 whole, which is shorter than its diff:
```python
import jax
import jax.numpy as jnp
from jax import lax
from jax.sharding import PartitionSpec as P

HEADS = 16
HEAD = 64
CODES = 1024


EPSILON = 1e-05
MASKED = -1e30
FACTOR = HEAD ** (-0.5)

BF = jnp.bfloat16
F32 = jnp.float32


def rms_scale(values, gain_vec):
    return (
        values * lax.rsqrt(jnp.mean(values * values, axis=-1, keepdims=True) + EPSILON) * gain_vec
    )


def matmul(former, latter):
    return jnp.dot(former, latter, preferred_element_type=F32)


def inner_left(former, latter):
    return lax.dot_general(former, latter, (((0,), (0,)), ((), ())), preferred_element_type=F32)


def inner_right(former, latter):
    return lax.dot_general(former, latter, (((1,), (1,)), ((), ())), preferred_element_type=F32)


def split_heads(values):
    return values.reshape(values.shape[:-1] + (-1, HEAD))


def swap(values, axis, bit):
    return lax.ppermute(values, axis, [(i, i ^ bit) for i in range(lax.axis_size(axis))])


def pick(values, index, axis):
    return lax.dynamic_index_in_dim(values, index, axis, keepdims=False)


class Place:
    def __init__(self):
        self.seq_count = lax.axis_size("seq")
        self.mp_count = lax.axis_size("mp")
        self.seq = lax.axis_index("seq")
        self.mp = lax.axis_index("mp")
        self.seq_low = self.seq % 2


def gather_weight(shard, place):
    height, breadth = shard.shape
    half = height // 2
    mine = lax.dynamic_slice(shard, (place.seq_low * half, 0), (half, breadth))
    first = swap(mine, "mp", 2)
    second = swap(first, "seq", 1)
    near_other = swap(shard, "mp", 1)
    far = jnp.zeros((height, breadth), shard.dtype)
    far = lax.dynamic_update_slice(far, first, (place.seq_low * half, 0))
    far = lax.dynamic_update_slice(far, second, ((1 - place.seq_low) * half, 0))
    far_other = swap(far, "mp", 1)
    whole = jnp.zeros((height * place.mp_count, breadth), shard.dtype)
    for flip, piece in ((0, shard), (1, near_other), (2, far), (3, far_other)):
        whole = lax.dynamic_update_slice(whole, piece, ((place.mp ^ flip) * height, 0))
    return whole


def line_scatter(blocks, place):
    count = place.seq_count // 2
    position = place.seq // 2
    size = 2 * count
    state = blocks
    up_in = down_in = None
    for step in range(1, count):
        up_index = jnp.clip(count - step + position, 0, count - 1)
        down_index = jnp.clip(step - 1 - (count - 1 - position), 0, count - 1)
        up_perm = [(i, i + 2) for i in range(size - 2) if i // 2 < step]
        down_perm = [(i, i - 2) for i in range(2, size) if (count - 1 - i // 2) < step]
        up_out = pick(blocks, up_index, 1)
        down_out = pick(blocks, down_index, 1)
        if up_in is not None:
            up_out = up_out + up_in
            down_out = down_out + down_in
        up_in = lax.ppermute(up_out, "seq", up_perm)
        down_in = lax.ppermute(down_out, "seq", down_perm)
    own = pick(blocks, position, 1).astype(F32)
    return own + up_in.astype(F32) + down_in.astype(F32)


def weight_grad(former, latter, place, seq_first):
    height = former.shape[1] // place.mp_count
    rows = former.shape[0]
    breadth = latter.shape[1] // place.seq_count
    low = place.seq_low
    view = latter.reshape(rows, place.seq_count // 2, 2, breadth)
    half = breadth * (place.seq_count // 2)
    give = pick(view, 1 - low, 2).reshape(rows, half)
    keep = pick(view, low, 2).reshape(rows, half)
    both = jnp.concatenate([give, keep], axis=1)

    def columns(flip):
        return lax.dynamic_slice(former, (0, (place.mp ^ flip) * height), (rows, height))

    own, other, far, far_other = (columns(flip) for flip in (0, 1, 2, 3))
    part = inner_left(jnp.concatenate([far_other, other], axis=1), both).astype(BF)
    part = swap(part, "mp", 1).astype(F32)
    if seq_first:
        send = inner_left(jnp.concatenate([far, own], axis=1), give) + part[:, :half]
        low_in = swap(send.astype(BF), "seq", 1).astype(F32)
        send = inner_left(far, keep) + part[:height, half:] + low_in[:height]
        far_in = swap(send.astype(BF), "mp", 2).astype(F32)
        total = inner_left(own, keep) + part[height:, half:] + low_in[height:] + far_in
    else:
        send = inner_left(far, both) + part[:height]
        far_in = swap(send.astype(BF), "mp", 2).astype(F32)
        send = inner_left(own, give) + part[height:, :half] + far_in[:, :half]
        low_in = swap(send.astype(BF), "seq", 1).astype(F32)
        total = inner_left(own, keep) + part[height:, half:] + far_in[:, half:] + low_in
    return total.astype(BF).reshape(height, place.seq_count // 2, breadth)


def finish_grads(partials, place):
    sizes = [part.shape[2] for part in partials]
    total = line_scatter(jnp.concatenate(partials, axis=2), place)
    pieces, start = [], 0
    for size in sizes:
        pieces.append(total[:, start : start + size])
        start += size
    return pieces


def sum_everywhere(values, place):
    for axis, count in (("mp", place.mp_count), ("seq", place.seq_count)):
        bit = 1
        while bit < count:
            values = values + swap(values, axis, bit)
            bit *= 2
    return values


def front_pass(hidden, weights):
    normed = rms_scale(hidden, weights[0].astype(F32)).astype(BF)
    projected = matmul(normed, weights[1]).astype(BF)
    return (normed, projected)


def rear_pass(hidden, attended, weights):
    mixed_sum = hidden + matmul(attended, weights[2])
    normed_two = rms_scale(mixed_sum, weights[3].astype(F32)).astype(BF)
    expanded = matmul(normed_two, weights[4])
    activated = jax.nn.gelu(expanded).astype(BF)
    result = mixed_sum + matmul(activated, weights[5])
    return (result, (mixed_sum, normed_two, expanded, activated))


def rear_grads(result_grad, saved_state, weights):
    mixed_sum, normed_two, expanded, activated = saved_state
    contract_input = result_grad.astype(BF)
    active_grad = inner_right(contract_input, weights[5])
    expand_input = jax.vjp(jax.nn.gelu, expanded)[1](active_grad)[0].astype(BF)
    normed_grad = inner_right(expand_input, weights[4])
    mixed_part, postnorm_grad = jax.vjp(rms_scale, mixed_sum, weights[3].astype(F32))[1](
        normed_grad
    )
    mixed_grad = result_grad + mixed_part
    output_input = mixed_grad.astype(BF)
    attended_grad = inner_right(output_input, weights[2]).astype(BF)
    return (mixed_grad, attended_grad, postnorm_grad, contract_input, expand_input, output_input)


def front_grads(hidden, projected_grad, mixed_grad, weights):
    normed_grad = inner_right(projected_grad, weights[1])
    hidden_part, prenorm_grad = jax.vjp(rms_scale, hidden, weights[0].astype(F32))[1](normed_grad)
    return (mixed_grad + hidden_part, prenorm_grad)


def portions_of(queries, keys, allowed):
    scores = jnp.einsum("ihd,jhd->hij", queries, keys, preferred_element_type=F32) * FACTOR
    return jax.nn.softmax(jnp.where(allowed[None], scores, MASKED), axis=-1)


def attend(queries, keys, values, allowed):
    portions = portions_of(queries, keys, allowed)
    return jnp.einsum(
        "hij,jhd->ihd", portions.astype(BF), values, preferred_element_type=F32
    ).astype(BF)


def attend_grads(queries, keys, values, allowed, out_grad):
    portions = portions_of(queries, keys, allowed)
    portion_grad = jnp.einsum("ihd,jhd->hij", out_grad, values, preferred_element_type=F32)
    score_grad = (
        portions * (portion_grad - jnp.sum(portions * portion_grad, axis=-1, keepdims=True))
    ).astype(BF)
    query_grad = (
        jnp.einsum("hij,jhd->ihd", score_grad, keys, preferred_element_type=F32) * FACTOR
    )
    key_grad = (
        jnp.einsum("hij,ihd->jhd", score_grad, queries, preferred_element_type=F32) * FACTOR
    )
    value_grad = jnp.einsum("hij,ihd->jhd", portions.astype(BF), out_grad, preferred_element_type=F32)
    return query_grad, key_grad, value_grad


def to_heads(values, place):
    rows, own, parts, width = values.shape
    count = place.seq_count
    view = values.reshape(rows, own, parts, count, width // count)
    moved = lax.all_to_all(
        jnp.transpose(view, (3, 0, 1, 2, 4)), "seq", split_axis=0, concat_axis=0, tiled=True
    )
    return jnp.transpose(moved, (1, 0, 2, 3, 4)).reshape(rows, count * own, parts, width // count)


def to_frames(values, place):
    rows, total, parts, width = values.shape
    count = place.seq_count
    view = values.reshape(rows, count, total // count, parts, width)
    moved = lax.all_to_all(
        jnp.transpose(view, (1, 0, 2, 3, 4)), "seq", split_axis=0, concat_axis=0, tiled=True
    )
    return jnp.transpose(moved, (1, 2, 3, 0, 4)).reshape(
        rows, total // count, parts, count * width
    )


def allowed_of(query_seg, key_seg, query_pos, key_pos):
    return (query_seg[:, None] == key_seg[None, :]) & (key_pos[None, :] <= query_pos[:, None])


def frame_attention(projected, segments, place):
    rows, own, triple = projected.shape
    width = triple // 3
    parts = projected.reshape(rows, own, 3, width)
    every_segment = lax.all_gather(segments, "seq", axis=1, tiled=True)
    every_pos = jnp.arange(own * place.seq_count)
    if HEADS % place.seq_count == 0:
        packed = to_heads(parts, place)
        sets = [split_heads(packed[:, :, part]) for part in range(3)]

        def one_row(items):
            queries, keys, values, segs = items
            return attend(queries, keys, values, allowed_of(segs, segs, every_pos, every_pos))

        attended = lax.map(one_row, (*sets, every_segment))
        attended = to_frames(attended.reshape(rows, own * place.seq_count, 1, -1), place)

        def backward(out_grad):
            grads = to_heads(out_grad.reshape(rows, own, 1, width), place)[:, :, 0]

            def one_row(items):
                queries, keys, values, segs, grad = items
                return attend_grads(
                    queries, keys, values, allowed_of(segs, segs, every_pos, every_pos), grad
                )

            found = lax.map(one_row, (*sets, every_segment, split_heads(grads)))
            packed_grad = jnp.stack(
                [grad.reshape(rows, own * place.seq_count, -1) for grad in found], axis=2
            ).astype(BF)
            return to_frames(packed_grad, place).reshape(rows, own, triple)

        return attended.reshape(rows, own, width), backward

    keys = lax.all_gather(parts[:, :, 1], "seq", axis=1, tiled=True)
    values = lax.all_gather(parts[:, :, 2], "seq", axis=1, tiled=True)
    sets = (split_heads(parts[:, :, 0]), split_heads(keys), split_heads(values))
    own_pos = place.seq * own + jnp.arange(own)

    def one_row(items):
        row_q, row_k, row_v, own_segs, segs = items
        return attend(row_q, row_k, row_v, allowed_of(own_segs, segs, own_pos, every_pos))

    attended = lax.map(one_row, (*sets, segments, every_segment)).reshape(rows, own, width)

    def backward(out_grad):
        def one_row(items):
            row_q, row_k, row_v, own_segs, segs, grad = items
            allowed = allowed_of(own_segs, segs, own_pos, every_pos)
            return attend_grads(row_q, row_k, row_v, allowed, grad)

        query_grad, key_grad, value_grad = lax.map(
            one_row, (*sets, segments, every_segment, split_heads(out_grad))
        )
        both = jnp.stack([key_grad.reshape(rows, -1, width), value_grad.reshape(rows, -1, width)], 2)
        both = lax.psum_scatter(both, "seq", scatter_dimension=1, tiled=True)
        parts_grad = [query_grad.reshape(rows, own, width), both[:, :, 0], both[:, :, 1]]
        return jnp.concatenate(parts_grad, axis=-1).astype(BF)

    return attended, backward


def head_sums(values, marks):
    return jnp.dot(values, marks, precision=lax.Precision.HIGHEST, preferred_element_type=F32)


def head_spread(values, marks):
    return lax.dot_general(
        values.astype(BF), marks.astype(BF), (((1,), (1,)), ((), ())), preferred_element_type=F32
    )


def codec_softmax(queries, keys, marks):
    result = []
    for later in range(len(queries)):
        scores = [
            head_sums(queries[later].astype(F32) * keys[earlier].astype(F32), marks) * FACTOR
            for earlier in range(later + 1)
        ]
        top = scores[0]
        for score in scores[1:]:
            top = jnp.maximum(top, score)
        powers = [jnp.exp(score - top) for score in scores]
        total = sum(powers)
        result.append([power / total for power in powers])
    return result


def codec_attend(soft, values, marks):
    result = []
    for row in soft:
        total = 0.0
        for earlier, portion in enumerate(row):
            total = total + head_spread(portion, marks) * values[earlier].astype(F32)
        result.append(total.astype(BF))
    return result


def codec_attend_grads(soft, queries, keys, values, grads, marks):
    count = len(queries)
    query_grad = []
    key_grad = [0.0] * count
    value_grad = [0.0] * count
    for later in range(count):
        grad = grads[later].astype(F32)
        portion_grads = [
            head_sums(grad * values[earlier].astype(F32), marks) for earlier in range(later + 1)
        ]
        mean = sum(soft[later][i] * portion_grads[i] for i in range(later + 1))
        total = 0.0
        for earlier in range(later + 1):
            score_grad = soft[later][earlier] * (portion_grads[earlier] - mean)
            wide = head_spread(score_grad, marks)
            total = total + wide * keys[earlier].astype(F32)
            key_grad[earlier] = key_grad[earlier] + wide * queries[later].astype(F32)
            value_grad[earlier] = value_grad[earlier] + head_spread(soft[later][earlier], marks) * grad
        query_grad.append(total * FACTOR)
    return jnp.concatenate(
        [
            jnp.concatenate(
                [query_grad[t], key_grad[t] * FACTOR, value_grad[t]], axis=-1
            ).astype(BF)
            for t in range(count)
        ],
        axis=0,
    )


def shards(
    frames,
    segments,
    padding,
    codec_tokens,
    codebooks,
    frame_prenorm,
    frame_project,
    frame_output,
    frame_postnorm,
    frame_expand,
    frame_contract,
    codec_prenorm,
    codec_project,
    codec_output,
    codec_postnorm,
    codec_expand,
    codec_contract,
    cotangent,
):
    place = Place()
    row_count, frames_dev, width = frames.shape
    frame_total = row_count * frames_dev
    positions = cotangent.shape[2]
    gains = lax.all_gather(
        jnp.stack([frame_prenorm, frame_postnorm, codec_prenorm, codec_postnorm]),
        "mp",
        axis=1,
        tiled=True,
    )
    frame_weights = (
        gains[0],
        gather_weight(frame_project, place),
        gather_weight(frame_output, place),
        gains[1],
        gather_weight(frame_expand, place),
        gather_weight(frame_contract, place),
    )
    codec_weights = (
        gains[2],
        gather_weight(codec_project, place),
        gather_weight(codec_output, place),
        gains[3],
        gather_weight(codec_expand, place),
        gather_weight(codec_contract, place),
    )
    table = gather_weight(codebooks, place)

    hidden = frames.astype(F32).reshape(frame_total, width)
    normed, projected = front_pass(hidden, frame_weights)
    attended, attention_back = frame_attention(
        projected.reshape(row_count, frames_dev, 3 * width), segments, place
    )
    attended = attended.reshape(frame_total, width)
    frame_result, frame_saved = rear_pass(hidden, attended, frame_weights)
    base = frame_result.astype(BF).astype(F32)

    table_rows = codec_tokens.reshape(positions - 1, frame_total) + (
        jnp.arange(positions - 1, dtype=jnp.int32) * CODES
    )[:, None]
    embedded = table[table_rows].astype(F32)
    codec_hidden = jnp.concatenate([base[None], base[None] + embedded], axis=0).reshape(
        positions * frame_total, width
    )
    codec_normed, codec_projected = front_pass(codec_hidden, codec_weights)
    marks = (
        jnp.arange(width)[:, None] // HEAD == jnp.arange(HEADS)[None, :]
    ).astype(F32)
    view = codec_projected.reshape(positions, frame_total, 3, width)
    queries, keys, values = ([view[t, :, part] for t in range(positions)] for part in range(3))
    soft = codec_softmax(queries, keys, marks)
    codec_attended = jnp.concatenate(codec_attend(soft, values, marks), axis=0)
    codec_result, codec_saved = rear_pass(codec_hidden, codec_attended, codec_weights)
    live = padding.reshape(frame_total).astype(F32)[None, :, None]
    output = jnp.transpose(
        (codec_result.reshape(positions, frame_total, width) * live).astype(BF), (1, 0, 2)
    ).reshape(row_count, frames_dev, positions, width)

    codec_grad = (
        jnp.transpose(cotangent.reshape(frame_total, positions, width), (1, 0, 2)).astype(F32) * live
    ).reshape(positions * frame_total, width)
    mixed_grad, attended_grad, codec_postnorm_grad, contract_in, expand_in, output_in = rear_grads(
        codec_grad, codec_saved, codec_weights
    )
    codec_contract_part = weight_grad(codec_saved[3], contract_in, place, True)
    codec_expand_part = weight_grad(codec_saved[1], expand_in, place, False)
    codec_output_part = weight_grad(codec_attended, output_in, place, True)
    grad_view = attended_grad.reshape(positions, frame_total, width)
    codec_projected_grad = codec_attend_grads(
        soft, queries, keys, values, [grad_view[t] for t in range(positions)], marks
    )
    codec_project_part = weight_grad(codec_normed, codec_projected_grad, place, True)
    input_grad, codec_prenorm_grad = front_grads(
        codec_hidden, codec_projected_grad, mixed_grad, codec_weights
    )
    input_grad = input_grad.reshape(positions, frame_total, width)
    chosen = (
        table_rows.reshape(-1)[:, None] == jnp.arange(table.shape[0], dtype=jnp.int32)[None, :]
    ).astype(BF)
    table_part = weight_grad(chosen, input_grad[1:].reshape(-1, width).astype(BF), place, False)
    base_grad = jnp.sum(input_grad, axis=0).astype(BF).astype(F32)

    (codec_contract_grad,) = finish_grads([codec_contract_part], place)
    codec_expand_grad, codec_output_grad, codec_project_grad = finish_grads(
        [codec_expand_part, codec_output_part, codec_project_part], place
    )
    (table_grad,) = finish_grads([table_part], place)

    frame_mixed_grad, frame_attended_grad, frame_postnorm_grad, contract_in, expand_in, output_in = (
        rear_grads(base_grad, frame_saved, frame_weights)
    )
    frame_projected_grad = attention_back(
        frame_attended_grad.reshape(row_count, frames_dev, width)
    ).reshape(frame_total, 3 * width)
    frame_contract_part = weight_grad(frame_saved[3], contract_in, place, True)
    frame_expand_part = weight_grad(frame_saved[1], expand_in, place, False)
    frame_output_part = weight_grad(attended, output_in, place, True)
    frame_project_part = weight_grad(normed, frame_projected_grad, place, True)
    frames_grad, frame_prenorm_grad = front_grads(
        hidden, frame_projected_grad, frame_mixed_grad, frame_weights
    )
    (frame_contract_grad,) = finish_grads([frame_contract_part], place)
    frame_expand_grad, frame_output_grad = finish_grads(
        [frame_expand_part, frame_output_part], place
    )
    (frame_project_grad,) = finish_grads([frame_project_part], place)
    gain_sums = sum_everywhere(
        jnp.stack(
            [frame_prenorm_grad, frame_postnorm_grad, codec_prenorm_grad, codec_postnorm_grad]
        ),
        place,
    )
    return (
        output,
        frames_grad.reshape(row_count, frames_dev, width),
        table_grad,
        gain_sums[0],
        frame_project_grad,
        frame_output_grad,
        gain_sums[1],
        frame_expand_grad,
        frame_contract_grad,
        gain_sums[2],
        codec_project_grad,
        codec_output_grad,
        gain_sums[3],
        codec_expand_grad,
        codec_contract_grad,
    )


def solution(mesh):
    placed = (
        P("mp", "seq", None),
        P("mp", "seq"),
        P("mp", "seq"),
        P(None, "mp", "seq"),
        P("mp", None),
        P("mp"),
        P("mp", None),
        P("mp", None),
        P("mp"),
        P("mp", None),
        P("mp", None),
        P("mp"),
        P("mp", None),
        P("mp", None),
        P("mp"),
        P("mp", None),
        P("mp", None),
        P("mp", "seq", None, None),
    )
    return jax.shard_map(
        shards,
        mesh=mesh,
        in_specs=placed,
        out_specs=(
            P("mp", "seq", None, None),
            P("mp", "seq", None),
            P("mp", "seq"),
            P(),
            P("mp", "seq"),
            P("mp", "seq"),
            P(),
            P("mp", "seq"),
            P("mp", "seq"),
            P(),
            P("mp", "seq"),
            P("mp", "seq"),
            P(),
            P("mp", "seq"),
            P("mp", "seq"),
        ),
        check_vma=False,
    )
```

time: 2780 us -> 1410 us (0.51)
  waiting for transfers between devices: 1910 us -> 315 us
  starting transfers between devices: 21.3 us -> 177 us
  local copies, waits for them, and re-layouts: 309 us -> 432 us
  blocking collectives: 135 us -> 38.5 us
  other arithmetic: 68.3 us -> 111 us
    reduce_scatter x10 -> x0, waiting for transfers between devices: 1510 us -> none  [the longest x1 187 us: shards(): lax.psum_scatter(spread(frame_expand_grad), ('seq', 'mp'), scatter_dimens...]
    all_gather x11 -> x0, waiting for transfers between devices: 333 us -> none  [the longest x1 75.9 us: shards(): lax.all_gather(projected[..., width:2 * width], 'seq', axis=1, tiled=True)]
    ppermute x0 -> x104, waiting for transfers between devices: none -> 295 us  [the longest x68 274 us: swap(): lax.ppermute(values, axis, [(i, i ^ bit) for i in range(lax.axis_size(axi...]
    ppermute x0 -> x104, starting transfers between devices: none -> 157 us  [the longest x18 80.2 us: line_scatter(): up_in = lax.ppermute(up_out, 'seq', up_perm)]
    transpose x15 -> x5, local copies, waits for them, and re-layouts: 97.9 us -> 8.16 us  [the longest x2 3.87 us: to_frames(): jnp.transpose(moved, (1, 2, 3, 0, 4))]
    dynamic_slice x12 -> x54, local copies, waits for them, and re-layouts: 18 us -> 104 us  [the longest x33 69.4 us: pick(): return lax.dynamic_index_in_dim(values, index, axis, keepdims=False)]
    dynamic_update_slice x8 -> x54, local copies, waits for them, and re-layouts: 0.7 us -> 80.9 us  [the longest x36 65 us: gather_weight(): lax.dynamic_update_slice(whole, piece, ((place.mp ^ flip) * height, 0))]
    convert_element_type x10 -> x41, other arithmetic: 11.3 us -> 76.9 us  [the longest x9 30.4 us: weight_grad(): part = swap(part, 'mp', 1).astype(F32)]
  transfers between devices with their start and end apart: 25 -> 108, of which waited for: 21 -> 33; matrix products, arithmetic and copies ran while one was open for 14% -> 44% of each run, Pallas kernels for 0% -> 0%
where the time goes in v1:
time: 1410 us; the launch traced here: 1390 us
  local copies, waits for them, and re-layouts  432 us (31%)
  waiting for transfers between devices  315 us (22%)
  matrix products  314 us (22%)
  starting transfers between devices  177 us (13%)
  other arithmetic  111 us (8%)
  blocking collectives  38.5 us (3%)
    ppermute x68, waiting for transfers between devices, swap(): lax.ppermute(values, axis, [(i, i ^ bit) for i in range(lax.axis_size(axi...  274 us
    dot_general x36, matrix products, inner_left(): lax.dot_general(former, latter, (((0,), (0,)), ((), ())), preferred_eleme...  108 us
    unnamed x499, local copies, waits for them, and re-layouts  91.4 us
    ppermute x18, starting transfers between devices, line_scatter(): up_in = lax.ppermute(up_out, 'seq', up_perm)  80.2 us
    dynamic_slice x33, local copies, waits for them, and re-layouts, pick(): return lax.dynamic_index_in_dim(values, index, axis, keepdims=False)  69.4 us
    dot_general x8, matrix products, matmul(): return jnp.dot(former, latter, preferred_element_type=F32)  67.1 us
    dynamic_update_slice x36, local copies, waits for them, and re-layouts, gather_weight(): lax.dynamic_update_slice(whole, piece, ((place.mp ^ flip) * height, 0))  65 us
    dot_general x8, matrix products, inner_right(): lax.dot_general(former, latter, (((1,), (1,)), ((), ())), preferred_eleme...  62.8 us
  transfers between devices with their start and end apart: 108, of which 33 were waited for; matrix products, arithmetic and copies ran while one was open for 44% of the time, Pallas kernels for 0%

profile of v1, /device:TPU:0, one launch (start us, length us, event | category | flops | bytes accessed | tf_op | source)
XLA Modules:
  0.0 1392.6 jit_solution(14339717348990320980)
XLA Ops:
  13.3 17.1 %all_gather.6 = bf16[4,1024]{1,0:T(4,128)(2,1)S(1)} all-gather(bf16[4,256]{1,0:T(4,128)(2,1)S(1)} %pad_maximum_fusion.17), channel_id=1, replica_groups=mesh['seq'=8,'mp'=4] {'mp'}, dimensions={1}, use_global_device_ids=true | all-gather | bytes 10240 | tf_op jit(solution)/shard_map/all_gather | solution.py:390
  107.3 21.4 %all_gather.7 = s32[2,1024]{1,0:T(2,128)S(1)} all-gather(s32[2,128]{1,0:T(2,128)S(1)} %copy-done.229), channel_id=1, replica_groups=mesh['seq'=8,'mp'=4] {'seq'}, dimensions={1}, use_global_device_ids=true | all-gather | bytes 9216 | tf_op jit(solution)/shard_map/all_gather | solution.py:242
  144.8 7.1 collective-permute-done.1
  153.8 15.0 %collective-permute-done.21 = bf16[128,3072]{1,0:T(8,128)(2,1)S(1)} collective-permute-done((bf16[128,3072]{1,0:T(8,128)(2,1)S(1)}, bf16[128,3072]{1,0:T(8,128)(2,1)S(1)}, u32[]{:S(2)}, u32[]{:S(2)}) %collective-permute-start.21) | collective-permute-done | bytes 786464 | tf_op jit(solution)/shard_map/ppermute | solution.py:42
  184.1 7.2 collective-permute-done.13
  193.9 42.4 %collective-permute-done.33 = bf16[512,1024]{1,0:T(8,128)(2,1)} collective-permute-done((bf16[512,1024]{1,0:T(8,128)(2,1)S(1)}, bf16[512,1024]{1,0:T(8,128)(2,1)}, u32[]{:S(2)}, u32[]{:S(2)}) %collective-permute-start.33) | collective-permute-done | bytes 1048608 | tf_op jit(solution)/shard_map/ppermute | solution.py:42
  244.7 9.6 collective-permute-done.29
  258.0 16.7 %collective-permute-done.2 = bf16[128,3072]{1,0:T(8,128)(2,1)S(1)} collective-permute-done((bf16[128,3072]{1,0:T(8,128)(2,1)S(1)}, bf16[128,3072]{1,0:T(8,128)(2,1)S(1)}, u32[]{:S(2)}, u32[]{:S(2)}) %collective-permute-start.2) | collective-permute-done | bytes 786464 | tf_op jit(solution)/shard_map/ppermute | solution.py:42
  279.2 12.4 collective-permute-done.22
  297.0 17.1 %collective-permute-done.14 = bf16[512,1024]{1,0:T(8,128)(2,1)S(1)} collective-permute-done((bf16[512,1024]{1,0:T(8,128)(2,1)S(1)}, bf16[512,1024]{1,0:T(8,128)(2,1)S(1)}, u32[]{:S(2)}, u32[]{:S(2)}) %collective-permute-start.14) | collective-permute-done | bytes 1048608 | tf_op jit(solution)/shard_map/ppermute | solution.py:42
  323.0 6.3 gather_fusion
  329.3 7.4 collective-permute-done.10
  340.7 18.4 %collective-permute-done.34 = bf16[512,1024]{1,0:T(8,128)(2,1)} collective-permute-done((bf16[512,1024]{1,0:T(8,128)(2,1)}, bf16[512,1024]{1,0:T(8,128)(2,1)}, u32[]{:S(2)}, u32[]{:S(2)}) %collective-permute-start.34) | collective-permute-done | bytes 1048608 | tf_op jit(solution)/shard_map/ppermute | solution.py:42
  365.0 11.2 collective-permute-done.30
  412.7 12.5 fusion.442
  425.1 11.6 all-to-all-done
  443.2 26.5 %while.26 = (s32[]{:T(128)}, bf16[2,1024,2,64]{1,3,2,0:T(8,128)(2,1)}, bf16[2,1024,2,64]{1,3,2,0:T(8,128)(2,1)}, s32[2,1024]{1,0:T(2,128)S(1)}, bf16[2,1024,2,64...) while((s32[]{:T(128)}, bf16[2,1024,2,64]{1,3,2,0:T(8,128)(2,1)}, ...), condition=%wide.region_4.5_spmd.clone, body=%wide.region_1.4_spmd.clone.sunk | while | flops 552731648 | bytes 19953752 | solution.py:252
  443.8 7.6 fusion.543
  457.0 7.6 fusion.543
  482.8 7.8 all-to-all-done.1
  493.0 9.0 multiply_convert_fusion.2
  502.0 6.5 fusion.185
  511.1 9.4 convolution_convert_fusion.2
  520.5 13.7 reshape.572
  534.1 14.1 %fusion.439 = (bf16[1,256,1,1024]{3,2,1,0:T(2,128)(2,1)S(1)}, bf16[1,256,1,1024]{3,2,1,0:T(2,128)(2,1)S(1)}, bf16[1,256,1,1024]{3,2,1,0:T(2,128)(2,1)S(1)}, bf16...) fusion(bf16[3,256,3,1024]{3,2,1,0:T(4,128)(2,1)} %reshape.572), kind=kLoop, calls=%fused_computation.767 | loop fusion | bytes 9437184 | tf_op jit(solution)/shard_map/slice | solution.py:435
  562.6 23.5 %fusion.110 = (bf16[768,4096]{1,0:T(8,128)(2,1)}, bf16[768,4096]{1,0:T(8,128)(2,1)}) fusion(f32[768,4096]{1,0:T(8,128)} %fusion.442, bf16[768,1024]{1,0:T(8,128)(2,1)S(1)} %multiply_convert_fusion.4, bf16[1024,4096]{1,0:T(8,128)(2,1)} %constant_dynamic-update-slice_fusion.6), kind=kOutput, calls=%fused_computation.95 | convolution fusion | flops 6511656960 | bytes 35127296 | tf_op jit(solution)/shard_map/dot_general | solution.py:26
  586.1 13.4 multiply_reduce_fusion.1
  616.9 9.3 multiply_reduce_fusion.2
  632.0 11.4 fusion.130
  644.7 7.4 multiply_reduce_fusion.6
  668.9 11.2 reshape.600
  701.3 11.4 convolution_add_fusion
  712.7 5.6 constant_dynamic-slice_fusion.9
  742.1 6.3 constant_dynamic-slice_fusion.50
  772.1 15.9 %constant_dynamic-slice_fusion.27 = (bf16[768,4,1,512]{3,2,1,0:T(2,128)(2,1)}, bf16[768,4,1,512]{3,2,1,0:T(2,128)(2,1)}) fusion(bf16[768,4,2,512]{3,2,1,0:T(2,128)(2,1)} %reshape.600, s32[]{:T(128)S(6)} %select_n.324, s32[]{:T(128)S(6)} %select_n.323), kind=kLoop, calls=%fused_computation.563 | loop fusion | bytes 12582920 | tf_op jit(solution)/shard_map/jit(dynamic_index_in_dim)/dynamic_slice | solution.py:46
  788.0 15.4 %copy.556 = bf16[768,4,1,512]{0,3,1,2:T(8,128)(2,1)} copy(bf16[768,4,1,512]{3,2,1,0:T(2,128)(2,1)} %get-tuple-element.291) | data formatting | bytes 6291456
  835.9 7.0 fusion.121
  853.5 13.3 copy.557
  869.8 7.6 convolution_convert_fusion
  878.9 43.1 %while.27 = (s32[]{:T(128)}, bf16[2,1024,2,64]{1,3,2,0:T(8,128)(2,1)}, bf16[2,1024,2,64]{1,3,2,0:T(8,128)(2,1)}, bf16[2,1024,2,64]{1,3,2,0:T(8,128)(2,1)}, bf16[...) while((s32[]{:T(128)}, ...), condition=%wide.region_16.17_spmd.clone, body=%wide.region_12.16_spmd.clone.sunk | while | flops 1372847104 | bytes 112526768 | solution.py:264
  879.8 7.7 fusion.554
  901.2 7.7 fusion.554
  927.5 6.5 all-to-all-start.3
  967.3 10.0 collective-permute-done.84
  994.5 5.5 multiply_reduce_fusion.7
  1007.3 11.4 collective-permute-done.38
  1028.9 5.4 collective-permute-start.49
  1051.9 10.4 collective-permute-start.40
  1083.6 6.6 convert_element_type.773
  1093.0 5.6 fusion.131
  1105.6 6.5 convert_element_type.743
  1112.8 7.3 fusion.132
  1120.1 25.0 %collective-permute-done.88 = bf16[256,1536]{1,0:T(8,128)(2,1)} collective-permute-done((bf16[256,1536]{1,0:T(8,128)(2,1)}, bf16[256,1536]{1,0:T(8,128)(2,1)}, u32[]{:S(2)}, u32[]{:S(2)}) %collective-permute-start.88) | collective-permute-done | bytes 786464 | tf_op jit(solution)/shard_map/ppermute | solution.py:42
  1160.4 29.1 %collective-permute-done.96 = bf16[2048,512]{0,1:T(8,128)(2,1)} collective-permute-done((bf16[2048,512]{0,1:T(8,128)(2,1)}, bf16[2048,512]{0,1:T(8,128)(2,1)}, u32[]{:S(2)}, u32[]{:S(2)}) %collective-permute-start.96) | collective-permute-done | bytes 2097184 | tf_op jit(solution)/shard_map/ppermute | solution.py:42
  1193.3 5.2 fusion.150
  1201.9 5.5 fusion.153
  1225.5 12.9 collective-permute-done.82
  1288.2 5.5 collective-permute-done.89
  1298.8 5.7 collective-permute-done.75
  1309.0 5.8 collective-permute-start.99
  1316.1 6.2 collective-permute-start.76
  1332.7 7.6 collective-permute-start.100
  1350.4 5.9 collective-permute-start.91
  1367.3 5.2 collective-permute-start.53
  (1079 shorter events, 709.1 us)
Async XLA Ops:
  0.7 133.2 %collective-permute-start.24 = (bf16[256,1024]{1,0:T(8,128)(2,1)}, bf16[256,1024]{1,0:T(8,128)(2,1)}, u32[]{:S(2)}, u32[]{:S(2)}) collective-permute-start(bf16[256,1024]{1,0:T(8,128)(2,1)} %param.35), channel_id=1, source_target_pairs={{0,1},{1,0},{2,3},{3,2},{4,5},{5,4},{6,7},{7,6},{8,9},{9,8},{10,11... | collective-permute-start | bytes 1572872 | tf_op jit(solution)/shard_map/ppermute | solution.py:42
  2.8 128.2 %collective-permute-start.25 = (bf16[128,1024]{1,0:T(8,128)(2,1)}, bf16[128,1024]{1,0:T(8,128)(2,1)S(1)}, u32[]{:S(2)}, u32[]{:S(2)}) collective-permute-start(bf16[128,1024]{1,0:T(8,128)(2,1)} %constant_dynamic-slice_fusion.80), channel_id=1, source_target_pairs={{0,2},{1,3},{2,0},{3,1},{4,6},{5,7},{6,4},{7,5},{8,10},{9,11},{10,... | collective-permute-start | bytes 786440 | tf_op jit(solution)/shard_map/ppermute | solution.py:42
  7.3 136.0 %collective-permute-start.17 = (bf16[256,1024]{1,0:T(8,128)(2,1)}, bf16[256,1024]{1,0:T(8,128)(2,1)}, u32[]{:S(2)}, u32[]{:S(2)}) collective-permute-start(bf16[256,1024]{1,0:T(8,128)(2,1)} %constant_dynamic-slice_fusion.82), channel_id=1, source_target_pairs={{0,2},{1,3},{2,0},{3,1},{4,6},{5,7},{6,4},{7,5},{8,10},{9,11},{10,... | collective-permute-start | bytes 1572872 | tf_op jit(solution)/shard_map/ppermute | solution.py:42
  7.3 134.3 %collective-permute-start.4 = (bf16[256,1024]{1,0:T(8,128)(2,1)}, bf16[256,1024]{1,0:T(8,128)(2,1)}, u32[]{:S(2)}, u32[]{:S(2)}) collective-permute-start(bf16[256,1024]{1,0:T(8,128)(2,1)} %param.29), channel_id=1, source_target_pairs={{0,1},{1,0},{2,3},{3,2},{4,5},{5,4},{6,7},{7,6},{8,9},{9,8},{10,11... | collective-permute-start | bytes 1572872 | tf_op jit(solution)/shard_map/ppermute | solution.py:42
  9.1 122.0 %collective-permute-start.5 = (bf16[128,1024]{1,0:T(8,128)(2,1)}, bf16[128,1024]{1,0:T(8,128)(2,1)}, u32[]{:S(2)}, u32[]{:S(2)}) collective-permute-start(bf16[128,1024]{1,0:T(8,128)(2,1)} %constant_dynamic-slice_fusion.85), channel_id=1, source_target_pairs={{0,2},{1,3},{2,0},{3,1},{4,6},{5,7},{6,4},{7,5},{8,10},{9,11},{10,... | collective-permute-start | bytes 786440 | tf_op jit(solution)/shard_map/ppermute | solution.py:42
  138.7 30.0 %collective-permute-start.21 = (bf16[128,3072]{1,0:T(8,128)(2,1)S(1)}, bf16[128,3072]{1,0:T(8,128)(2,1)S(1)}, u32[]{:S(2)}, u32[]{:S(2)}) collective-permute-start(bf16[128,3072]{1,0:T(8,128)(2,1)S(1)} %copy-done.187), channel_id=1, source_target_pairs={{0,2},{1,3},{2,0},{3,1},{4,6},{5,7},{6,4},{7,5},{8,10},{9,11},{10,... | collective-permute-start | bytes 2359304 | tf_op jit(solution)/shard_map/ppermute | solution.py:42
  141.5 28.8 %collective-permute-start.27 = (bf16[256,1024]{1,0:T(8,128)(2,1)S(1)}, bf16[256,1024]{1,0:T(8,128)(2,1)S(1)}, u32[]{:S(2)}, u32[]{:S(2)}) collective-permute-start(bf16[256,1024]{1,0:T(8,128)(2,1)S(1)} %constant_dynamic-update-slice_fusion.14), channel_id=1, source_target_pairs={{0,1},{1,0},{2,3},{3,2},{4,5},{5,4},{6,7},{7,6},{8,9},{9,8},{10,11... | collective-permute-start | bytes 1572872 | tf_op jit(solution)/shard_map/ppermute | solution.py:42
  141.6 29.2 %collective-permute-start.7 = (bf16[256,1024]{1,0:T(8,128)(2,1)S(1)}, bf16[256,1024]{1,0:T(8,128)(2,1)S(1)}, u32[]{:S(2)}, u32[]{:S(2)}) collective-permute-start(bf16[256,1024]{1,0:T(8,128)(2,1)S(1)} %constant_dynamic-update-slice_fusion.44), channel_id=1, source_target_pairs={{0,1},{1,0},{2,3},{3,2},{4,5},{5,4},{6,7},{7,6},{8,9},{9,8},{10,11... | collective-permute-start | bytes 1572872 | tf_op jit(solution)/shard_map/ppermute | solution.py:42
  143.3 31.9 %collective-permute-start.16 = (bf16[512,1024]{1,0:T(8,128)(2,1)S(1)}, bf16[512,1024]{1,0:T(8,128)(2,1)S(1)}, u32[]{:S(2)}, u32[]{:S(2)}) collective-permute-start(bf16[512,1024]{1,0:T(8,128)(2,1)S(1)} %copy-done.112), channel_id=1, source_target_pairs={{0,1},{1,0},{2,3},{3,2},{4,5},{5,4},{6,7},{7,6},{8,9},{9,8},{10,11... | collective-permute-start | bytes 3145736 | tf_op jit(solution)/shard_map/ppermute | solution.py:42
  151.9 39.3 %collective-permute-start.13 = (bf16[512,1024]{1,0:T(8,128)(2,1)S(1)}, bf16[512,1024]{1,0:T(8,128)(2,1)S(1)}, u32[]{:S(2)}, u32[]{:S(2)}) collective-permute-start(bf16[512,1024]{1,0:T(8,128)(2,1)S(1)} %copy-done.175), channel_id=1, source_target_pairs={{0,2},{1,3},{2,0},{3,1},{4,6},{5,7},{6,4},{7,5},{8,10},{9,11},{10,... | collective-permute-start | bytes 3145736 | tf_op jit(solution)/shard_map/ppermute | solution.py:42
  168.7 71.5 %collective-permute-start.9 = (bf16[128,4096]{1,0:T(8,128)(2,1)S(1)}, bf16[128,4096]{1,0:T(8,128)(2,1)}, u32[]{:S(2)}, u32[]{:S(2)}) collective-permute-start(bf16[128,4096]{1,0:T(8,128)(2,1)S(1)} %copy-done.172), channel_id=1, source_target_pairs={{0,2},{1,3},{2,0},{3,1},{4,6},{5,7},{6,4},{7,5},{8,10},{9,11},{10,... | collective-permute-start | bytes 3145736 | tf_op jit(solution)/shard_map/ppermute | solution.py:42
  170.4 65.9 %collective-permute-start.33 = (bf16[512,1024]{1,0:T(8,128)(2,1)S(1)}, bf16[512,1024]{1,0:T(8,128)(2,1)}, u32[]{:S(2)}, u32[]{:S(2)}) collective-permute-start(bf16[512,1024]{1,0:T(8,128)(2,1)S(1)} %copy-done.174), channel_id=1, source_target_pairs={{0,2},{1,3},{2,0},{3,1},{4,6},{5,7},{6,4},{7,5},{8,10},{9,11},{10,... | collective-permute-start | bytes 3145736 | tf_op jit(solution)/shard_map/ppermute | solution.py:42
  175.2 81.2 %collective-permute-start = (bf16[256,3072]{1,0:T(8,128)(2,1)S(1)}, bf16[256,3072]{1,0:T(8,128)(2,1)S(1)}, u32[]{:S(2)}, u32[]{:S(2)}) collective-permute-start(bf16[256,3072]{1,0:T(8,128)(2,1)S(1)} %copy-done.96), channel_id=1, source_target_pairs={{0,1},{1,0},{2,3},{3,2},{4,5},{5,4},{6,7},{7,6},{8,9},{9,8},{10,11... | collective-permute-start | bytes 4718600 | tf_op jit(solution)/shard_map/ppermute | solution.py:42
  180.2 74.1 %collective-permute-start.29 = (bf16[128,4096]{1,0:T(8,128)(2,1)S(1)}, bf16[128,4096]{1,0:T(8,128)(2,1)S(1)}, u32[]{:S(2)}, u32[]{:S(2)}) collective-permute-start(bf16[128,4096]{1,0:T(8,128)(2,1)S(1)} %copy-done.173), channel_id=1, source_target_pairs={{0,2},{1,3},{2,0},{3,1},{4,6},{5,7},{6,4},{7,5},{8,10},{9,11},{10,... | collective-permute-start | bytes 3145736 | tf_op jit(solution)/shard_map/ppermute | solution.py:42
  191.2 170.2 %collective-permute-start.8 = (bf16[256,4096]{1,0:T(8,128)(2,1)}, bf16[256,4096]{1,0:T(8,128)(2,1)}, u32[]{:S(2)}, u32[]{:S(2)}) collective-permute-start(bf16[256,4096]{1,0:T(8,128)(2,1)} %param.31), channel_id=1, source_target_pairs={{0,1},{1,0},{2,3},{3,2},{4,5},{5,4},{6,7},{7,6},{8,9},{9,8},{10,11... | collective-permute-start | bytes 6291464 | tf_op jit(solution)/shard_map/ppermute | solution.py:42
  236.3 80.6 %collective-permute-start.12 = (bf16[1024,1024]{1,0:T(8,128)(2,1)S(1)}, bf16[1024,1024]{1,0:T(8,128)(2,1)S(1)}, u32[]{:S(2)}, u32[]{:S(2)}) collective-permute-start(bf16[1024,1024]{1,0:T(8,128)(2,1)S(1)} %copy-done.72), channel_id=1, source_target_pairs={{0,1},{1,0},{2,3},{3,2},{4,5},{5,4},{6,7},{7,6},{8,9},{9,8},{10,11... | collective-permute-start | bytes 6291464 | tf_op jit(solution)/shard_map/ppermute | solution.py:42
  240.2 36.0 %collective-permute-start.20 = (bf16[256,3072]{1,0:T(8,128)(2,1)S(1)}, bf16[256,3072]{1,0:T(8,128)(2,1)S(1)}, u32[]{:S(2)}, u32[]{:S(2)}) collective-permute-start(bf16[256,3072]{1,0:T(8,128)(2,1)S(1)} %copy-done.98), channel_id=1, source_target_pairs={{0,1},{1,0},{2,3},{3,2},{4,5},{5,4},{6,7},{7,6},{8,9},{9,8},{10,11... | collective-permute-start | bytes 4718600 | tf_op jit(solution)/shard_map/ppermute | solution.py:42
  256.4 35.2 %collective-permute-start.22 = (bf16[128,3072]{1,0:T(8,128)(2,1)S(1)}, bf16[128,3072]{1,0:T(8,128)(2,1)S(1)}, u32[]{:S(2)}, u32[]{:S(2)}) collective-permute-start(bf16[128,3072]{1,0:T(8,128)(2,1)S(1)} %collective-permute-done.21), channel_id=1, source_target_pairs={{0,4},{4,0},{8,12},{12,8},{16,20},{20,16},{24,28},{28,24},{1,5},{5... | collective-permute-start | bytes 2359304 | tf_op jit(solution)/shard_map/ppermute | solution.py:42
  274.8 46.7 %collective-permute-start.19 = (bf16[512,1024]{1,0:T(8,128)(2,1)S(1)}, bf16[512,1024]{1,0:T(8,128)(2,1)S(1)}, u32[]{:S(2)}, u32[]{:S(2)}) collective-permute-start(bf16[512,1024]{1,0:T(8,128)(2,1)S(1)} %constant_dynamic-update-slice_fusion.26), channel_id=1, source_target_pairs={{0,1},{1,0},{2,3},{3,2},{4,5},{5,4},{6,7},{7,6},{8,9},{9,8},{10,11... | collective-permute-start | bytes 3145736 | tf_op jit(solution)/shard_map/ppermute | solution.py:42
  276.2 37.9 %collective-permute-start.14 = (bf16[512,1024]{1,0:T(8,128)(2,1)S(1)}, bf16[512,1024]{1,0:T(8,128)(2,1)S(1)}, u32[]{:S(2)}, u32[]{:S(2)}) collective-permute-start(bf16[512,1024]{1,0:T(8,128)(2,1)S(1)} %collective-permute-done.13), channel_id=1, source_target_pairs={{0,4},{4,0},{8,12},{12,8},{16,20},{20,16},{24,28},{28,24},{1,5},{5... | collective-permute-start | bytes 3145736 | tf_op jit(solution)/shard_map/ppermute | solution.py:42
  291.6 45.0 %collective-permute-start.10 = (bf16[128,4096]{1,0:T(8,128)(2,1)}, bf16[128,4096]{1,0:T(8,128)(2,1)}, u32[]{:S(2)}, u32[]{:S(2)}) collective-permute-start(bf16[128,4096]{1,0:T(8,128)(2,1)} %collective-permute-done.9), channel_id=1, source_target_pairs={{0,4},{4,0},{8,12},{12,8},{16,20},{20,16},{24,28},{28,24},{1,5},{5... | collective-permute-start | bytes 3145736 | tf_op jit(solution)/shard_map/ppermute | solution.py:42
  314.1 45.0 %collective-permute-start.34 = (bf16[512,1024]{1,0:T(8,128)(2,1)}, bf16[512,1024]{1,0:T(8,128)(2,1)}, u32[]{:S(2)}, u32[]{:S(2)}) collective-permute-start(bf16[512,1024]{1,0:T(8,128)(2,1)} %collective-permute-done.33), channel_id=1, source_target_pairs={{0,4},{4,0},{8,12},{12,8},{16,20},{20,16},{24,28},{28,24},{1,5},{5... | collective-permute-start | bytes 3145736 | tf_op jit(solution)/shard_map/ppermute | solution.py:42
  316.9 66.4 %collective-permute-start.32 = (bf16[1024,1024]{1,0:T(8,128)(2,1)}, bf16[1024,1024]{1,0:T(8,128)(2,1)}, u32[]{:S(2)}, u32[]{:S(2)}) collective-permute-start(bf16[1024,1024]{1,0:T(8,128)(2,1)} %param.38), channel_id=1, source_target_pairs={{0,1},{1,0},{2,3},{3,2},{4,5},{5,4},{6,7},{7,6},{8,9},{9,8},{10,11... | collective-permute-start | bytes 6291464 | tf_op jit(solution)/shard_map/ppermute | solution.py:42
  321.5 58.0 %collective-permute-start.28 = (bf16[256,4096]{1,0:T(8,128)(2,1)}, bf16[256,4096]{1,0:T(8,128)(2,1)}, u32[]{:S(2)}, u32[]{:S(2)}) collective-permute-start(bf16[256,4096]{1,0:T(8,128)(2,1)} %param.37), channel_id=1, source_target_pairs={{0,1},{1,0},{2,3},{3,2},{4,5},{5,4},{6,7},{7,6},{8,9},{9,8},{10,11... | collective-permute-start | bytes 6291464 | tf_op jit(solution)/shard_map/ppermute | solution.py:42
  336.7 39.6 %collective-permute-start.30 = (bf16[128,4096]{1,0:T(8,128)(2,1)S(1)}, bf16[128,4096]{1,0:T(8,128)(2,1)S(1)}, u32[]{:S(2)}, u32[]{:S(2)}) collective-permute-start(bf16[128,4096]{1,0:T(8,128)(2,1)S(1)} %copy-done.177), channel_id=1, source_target_pairs={{0,4},{4,0},{8,12},{12,8},{16,20},{20,16},{24,28},{28,24},{1,5},{5... | collective-permute-start | bytes 3145736 | tf_op jit(solution)/shard_map/ppermute | solution.py:42
  359.1 27.2 %collective-permute-start.3 = (bf16[256,3072]{1,0:T(8,128)(2,1)}, bf16[256,3072]{1,0:T(8,128)(2,1)S(1)}, u32[]{:S(2)}, u32[]{:S(2)}) collective-permute-start(bf16[256,3072]{1,0:T(8,128)(2,1)} %copy-done.66), channel_id=1, source_target_pairs={{0,1},{1,0},{2,3},{3,2},{4,5},{5,4},{6,7},{7,6},{8,9},{9,8},{10,11... | collective-permute-start | bytes 4718600 | tf_op jit(solution)/shard_map/ppermute | solution.py:42
  361.4 42.3 %collective-permute-start.23 = (bf16[256,3072]{1,0:T(8,128)(2,1)}, bf16[256,3072]{1,0:T(8,128)(2,1)}, u32[]{:S(2)}, u32[]{:S(2)}) collective-permute-start(bf16[256,3072]{1,0:T(8,128)(2,1)} %constant_dynamic-update-slice_fusion.20), channel_id=1, source_target_pairs={{0,1},{1,0},{2,3},{3,2},{4,5},{5,4},{6,7},{7,6},{8,9},{9,8},{10,11... | collective-permute-start | bytes 4718600 | tf_op jit(solution)/shard_map/ppermute | solution.py:42
  376.2 100.1 %collective-permute-start.11 = (bf16[256,4096]{1,0:T(8,128)(2,1)}, bf16[256,4096]{1,0:T(8,128)(2,1)}, u32[]{:S(2)}, u32[]{:S(2)}) collective-permute-start(bf16[256,4096]{1,0:T(8,128)(2,1)} %constant_dynamic-update-slice_fusion.38), channel_id=1, source_target_pairs={{0,1},{1,0},{2,3},{3,2},{4,5},{5,4},{6,7},{7,6},{8,9},{9,8},{10,11... | collective-permute-start | bytes 6291464 | tf_op jit(solution)/shard_map/ppermute | solution.py:42
  379.5 26.9 %collective-permute-start.15 = (bf16[1024,1024]{1,0:T(8,128)(2,1)}, bf16[1024,1024]{1,0:T(8,128)(2,1)}, u32[]{:S(2)}, u32[]{:S(2)}) collective-permute-start(bf16[1024,1024]{1,0:T(8,128)(2,1)} %constant_dynamic-update-slice_fusion.32), channel_id=1, source_target_pairs={{0,1},{1,0},{2,3},{3,2},{4,5},{5,4},{6,7},{7,6},{8,9},{9,8},{10,11... | collective-permute-start | bytes 6291464 | tf_op jit(solution)/shard_map/ppermute | solution.py:42
  383.2 26.2 %collective-permute-start.35 = (bf16[1024,1024]{1,0:T(8,128)(2,1)}, bf16[1024,1024]{1,0:T(8,128)(2,1)}, u32[]{:S(2)}, u32[]{:S(2)}) collective-permute-start(bf16[1024,1024]{1,0:T(8,128)(2,1)} %constant_dynamic-update-slice_fusion.2), channel_id=1, source_target_pairs={{0,1},{1,0},{2,3},{3,2},{4,5},{5,4},{6,7},{7,6},{8,9},{9,8},{10,11... | collective-permute-start | bytes 6291464 | tf_op jit(solution)/shard_map/ppermute | solution.py:42
  386.4 93.1 %collective-permute-start.31 = (bf16[256,4096]{1,0:T(8,128)(2,1)S(1)}, bf16[256,4096]{1,0:T(8,128)(2,1)}, u32[]{:S(2)}, u32[]{:S(2)}) collective-permute-start(bf16[256,4096]{1,0:T(8,128)(2,1)S(1)} %constant_dynamic-update-slice_fusion.8), channel_id=1, source_target_pairs={{0,1},{1,0},{2,3},{3,2},{4,5},{5,4},{6,7},{7,6},{8,9},{9,8},{10,11... | collective-permute-start | bytes 6291464 | tf_op jit(solution)/shard_map/ppermute | solution.py:42
  394.5 42.2 %all-to-all-start = ((bf16[8,2,128,3,128]{4,2,3,1,0:T(8,128)(2,1)}), bf16[8,2,128,3,128]{4,2,3,1,0:T(8,128)(2,1)}, u32[]{:S(2)}, u32[]{:S(2)}) async-start(bf16[8,2,128,3,128]{4,2,3,1,0:T(8,128)(2,1)} %bitcast.580), calls=%async_computation | async-start | bytes 3145728 | tf_op jit(solution)/shard_map/all_to_all | solution.py:216
  721.2 156.2 %all-to-all-start.2 = ((bf16[8,2,128,1,128]{4,2,1,3,0:T(8,128)(2,1)}), bf16[8,2,128,1,128]{4,2,1,3,0:T(8,128)(2,1)}, u32[]{:S(2)}, u32[]{:S(2)}) async-start(bf16[8,2,128,1,128]{4,2,1,3,0:T(8,128)(2,1)} %bitcast.493), calls=%async_computation.2 | async-start | bytes 1048576 | tf_op jit(solution)/shard_map/all_to_all | solution.py:216
  739.7 211.4 %collective-permute-start.36 = (bf16[1024,1024]{0,1:T(8,128)(2,1)}, bf16[1024,1024]{0,1:T(8,128)(2,1)}, u32[]{:S(2)}, u32[]{:S(2)}) collective-permute-start(bf16[1024,1024]{0,1:T(8,128)(2,1)} %convolution_convert_fusion.7), channel_id=1, source_target_pairs={{0,1},{1,0},{2,3},{3,2},{4,5},{5,4},{6,7},{7,6},{8,9},{9,8},{10,11... | collective-permute-start | bytes 6291464 | tf_op jit(solution)/shard_map/ppermute | solution.py:42
  764.0 302.6 %collective-permute-start.59 = (bf16[512,4096]{1,0:T(8,128)(2,1)}, bf16[512,4096]{1,0:T(8,128)(2,1)}, u32[]{:S(2)}, u32[]{:S(2)}) collective-permute-start(bf16[512,4096]{1,0:T(8,128)(2,1)} %convolution_convert_fusion.1), channel_id=1, source_target_pairs={{0,1},{1,0},{2,3},{3,2},{4,5},{5,4},{6,7},{7,6},{8,9},{9,8},{10,11... | collective-permute-start | bytes 12582920 | tf_op jit(solution)/shard_map/ppermute | solution.py:42
  769.0 171.3 %collective-permute-start.62 = (bf16[512,1024]{1,0:T(8,128)(2,1)}, bf16[512,1024]{1,0:T(8,128)(2,1)}, u32[]{:S(2)}, u32[]{:S(2)}) collective-permute-start(bf16[512,1024]{1,0:T(8,128)(2,1)} %convolution_convert_fusion.9), channel_id=1, source_target_pairs={{0,1},{1,0},{2,3},{3,2},{4,5},{5,4},{6,7},{7,6},{8,9},{9,8},{10,11... | collective-permute-start | bytes 3145736 | tf_op jit(solution)/shard_map/ppermute | solution.py:42
  820.6 124.4 %collective-permute-start.83 = (bf16[512,1024]{1,0:T(8,128)(2,1)}, bf16[512,1024]{1,0:T(8,128)(2,1)}, u32[]{:S(2)}, u32[]{:S(2)}) collective-permute-start(bf16[512,1024]{1,0:T(8,128)(2,1)} %fusion.179), channel_id=1, source_target_pairs={{0,1},{1,0},{2,3},{3,2},{4,5},{5,4},{6,7},{7,6},{8,9},{9,8},{10,11... | collective-permute-start | bytes 3145736 | tf_op jit(solution)/shard_map/ppermute | solution.py:42
  842.9 138.8 %collective-permute-start.86 = (bf16[512,3072]{1,0:T(8,128)(2,1)}, bf16[512,3072]{1,0:T(8,128)(2,1)}, u32[]{:S(2)}, u32[]{:S(2)}) collective-permute-start(bf16[512,3072]{1,0:T(8,128)(2,1)} %fusion.121), channel_id=1, source_target_pairs={{0,1},{1,0},{2,3},{3,2},{4,5},{5,4},{6,7},{7,6},{8,9},{9,8},{10,11... | collective-permute-start | bytes 9437192 | tf_op jit(solution)/shard_map/ppermute | solution.py:42
  927.5 62.5 %all-to-all-start.3 = ((bf16[8,2,128,3,128]{4,2,3,1,0:T(8,128)(2,1)}), bf16[8,2,128,3,128]{4,2,3,1,0:T(8,128)(2,1)}, u32[]{:S(2)}, u32[]{:S(2)}) async-start(bf16[8,2,128,3,128]{4,2,3,1,0:T(8,128)(2,1)} %copy.452), calls=%async_computation.3 | async-start | bytes 3145728 | tf_op jit(solution)/shard_map/all_to_all | solution.py:226
  949.3 28.0 %collective-permute-start.84 = (bf16[512,512]{1,0:T(8,128)(2,1)}, bf16[512,512]{1,0:T(8,128)(2,1)}, u32[]{:S(2)}, u32[]{:S(2)}) collective-permute-start(bf16[512,512]{1,0:T(8,128)(2,1)} %fusion.219), channel_id=1, source_target_pairs={{0,4},{4,0},{8,12},{12,8},{16,20},{20,16},{24,28},{28,24},{1,5},{5... | collective-permute-start | bytes 1572872 | tf_op jit(solution)/shard_map/ppermute | solution.py:42
  957.0 31.4 %collective-permute-start.37 = (bf16[512,1024]{0,1:T(8,128)(2,1)S(1)}, bf16[512,1024]{0,1:T(8,128)(2,1)S(1)}, u32[]{:S(2)}, u32[]{:S(2)}) collective-permute-start(bf16[512,1024]{0,1:T(8,128)(2,1)S(1)} %fusion.162), channel_id=1, source_target_pairs={{0,2},{1,3},{2,0},{3,1},{4,6},{5,7},{6,4},{7,5},{8,10},{9,11},{10,... | collective-permute-start | bytes 3145736 | tf_op jit(solution)/shard_map/ppermute | solution.py:42
  966.1 105.0 %collective-permute-start.71 = (bf16[2048,1024]{0,1:T(8,128)(2,1)}, bf16[2048,1024]{0,1:T(8,128)(2,1)}, u32[]{:S(2)}, u32[]{:S(2)}) collective-permute-start(bf16[2048,1024]{0,1:T(8,128)(2,1)} %convolution_convert_fusion.5), channel_id=1, source_target_pairs={{0,1},{1,0},{2,3},{3,2},{4,5},{5,4},{6,7},{7,6},{8,9},{9,8},{10,11... | collective-permute-start | bytes 12582920 | tf_op jit(solution)/shard_map/ppermute | solution.py:42
  977.3 126.8 %collective-permute-start.80 = (bf16[512,4096]{1,0:T(8,128)(2,1)}, bf16[512,4096]{1,0:T(8,128)(2,1)}, u32[]{:S(2)}, u32[]{:S(2)}) collective-permute-start(bf16[512,4096]{1,0:T(8,128)(2,1)} %convolution_convert_fusion), channel_id=1, source_target_pairs={{0,1},{1,0},{2,3},{3,2},{4,5},{5,4},{6,7},{7,6},{8,9},{9,8},{10,11... | collective-permute-start | bytes 12582920 | tf_op jit(solution)/shard_map/ppermute | solution.py:42
  981.7 100.6 %collective-permute-start.95 = (bf16[2048,1024]{0,1:T(8,128)(2,1)}, bf16[2048,1024]{0,1:T(8,128)(2,1)}, u32[]{:S(2)}, u32[]{:S(2)}) collective-permute-start(bf16[2048,1024]{0,1:T(8,128)(2,1)} %convolution_convert_fusion.6), channel_id=1, source_target_pairs={{0,1},{1,0},{2,3},{3,2},{4,5},{5,4},{6,7},{7,6},{8,9},{9,8},{10,11... | collective-permute-start | bytes 12582920 | tf_op jit(solution)/shard_map/ppermute | solution.py:42
  1066.0 32.7 %collective-permute-start.87 = (bf16[512,1536]{1,0:T(8,128)(2,1)S(1)}, bf16[512,1536]{1,0:T(8,128)(2,1)S(1)}, u32[]{:S(2)}, u32[]{:S(2)}) collective-permute-start(bf16[512,1536]{1,0:T(8,128)(2,1)S(1)} %copy-done.231), channel_id=1, source_target_pairs={{0,4},{4,0},{8,12},{12,8},{16,20},{20,16},{24,28},{28,24},{1,5},{5... | collective-permute-start | bytes 4718600 | tf_op jit(solution)/shard_map/ppermute | solution.py:42
  1066.5 36.3 %collective-permute-start.44 = (bf16[512,128]{1,0:T(8,128)(2,1)S(1)}, bf16[512,128]{1,0:T(8,128)(2,1)S(1)}, u32[]{:S(2)}, u32[]{:S(2)}) collective-permute-start(bf16[512,128]{1,0:T(8,128)(2,1)S(1)} %bitcast_add_fusion.18), channel_id=1, source_target_pairs={{8,0},{12,4},{16,8},{20,12},{24,16},{28,20},{9,1},{13,5},{17,9},{2... | collective-permute-start | bytes 393224 | tf_op jit(solution)/shard_map/ppermute | solution.py:92
  1071.2 40.9 %collective-permute-start.41 = (bf16[512,128]{1,0:T(8,128)(2,1)S(1)}, bf16[512,128]{1,0:T(8,128)(2,1)S(1)}, u32[]{:S(2)}, u32[]{:S(2)}) collective-permute-start(bf16[512,128]{1,0:T(8,128)(2,1)S(1)} %bitcast_add_fusion.20), channel_id=1, source_target_pairs={{0,8},{4,12},{8,16},{12,20},{16,24},{20,28},{1,9},{5,13},{9,17},{1... | collective-permute-start | bytes 393224 | tf_op jit(solution)/shard_map/ppermute | solution.py:91
  1082.4 69.3 %collective-permute-start.60 = (bf16[256,4096]{1,0:T(8,128)(2,1)}, bf16[256,4096]{1,0:T(8,128)(2,1)}, u32[]{:S(2)}, u32[]{:S(2)}) collective-permute-start(bf16[256,4096]{1,0:T(8,128)(2,1)} %fusion.134), channel_id=1, source_target_pairs={{0,2},{1,3},{2,0},{3,1},{4,6},{5,7},{6,4},{7,5},{8,10},{9,11},{10,... | collective-permute-start | bytes 6291464 | tf_op jit(solution)/shard_map/ppermute | solution.py:42
  1098.7 55.9 %collective-permute-start.72 = (bf16[2048,512]{0,1:T(8,128)(2,1)}, bf16[2048,512]{0,1:T(8,128)(2,1)}, u32[]{:S(2)}, u32[]{:S(2)}) collective-permute-start(bf16[2048,512]{0,1:T(8,128)(2,1)} %fusion.133), channel_id=1, source_target_pairs={{0,4},{4,0},{8,12},{12,8},{16,20},{20,16},{24,28},{28,24},{1,5},{5... | collective-permute-start | bytes 6291464 | tf_op jit(solution)/shard_map/ppermute | solution.py:42
  1102.8 86.7 %collective-permute-start.96 = (bf16[2048,512]{0,1:T(8,128)(2,1)}, bf16[2048,512]{0,1:T(8,128)(2,1)}, u32[]{:S(2)}, u32[]{:S(2)}) collective-permute-start(bf16[2048,512]{0,1:T(8,128)(2,1)} %fusion.131), channel_id=1, source_target_pairs={{0,4},{4,0},{8,12},{12,8},{16,20},{20,16},{24,28},{28,24},{1,5},{5... | collective-permute-start | bytes 6291464 | tf_op jit(solution)/shard_map/ppermute | solution.py:42
  1104.1 41.0 %collective-permute-start.88 = (bf16[256,1536]{1,0:T(8,128)(2,1)}, bf16[256,1536]{1,0:T(8,128)(2,1)}, u32[]{:S(2)}, u32[]{:S(2)}) collective-permute-start(bf16[256,1536]{1,0:T(8,128)(2,1)} %fusion.163), channel_id=1, source_target_pairs={{0,2},{1,3},{2,0},{3,1},{4,6},{5,7},{6,4},{7,5},{8,10},{9,11},{10,... | collective-permute-start | bytes 2359304 | tf_op jit(solution)/shard_map/ppermute | solution.py:42
  1112.8 94.6 %collective-permute-start.50 = (bf16[512,3072]{1,0:T(8,128)(2,1)}, bf16[512,3072]{1,0:T(8,128)(2,1)}, u32[]{:S(2)}, u32[]{:S(2)}) collective-permute-start(bf16[512,3072]{1,0:T(8,128)(2,1)} %convolution_convert_fusion.3), channel_id=1, source_target_pairs={{0,1},{1,0},{2,3},{3,2},{4,5},{5,4},{6,7},{7,6},{8,9},{9,8},{10,11... | collective-permute-start | bytes 9437192 | tf_op jit(solution)/shard_map/ppermute | solution.py:42
  1145.1 54.9 %collective-permute-start.81 = (bf16[256,4096]{1,0:T(8,128)(2,1)}, bf16[256,4096]{1,0:T(8,128)(2,1)S(1)}, u32[]{:S(2)}, u32[]{:S(2)}) collective-permute-start(bf16[256,4096]{1,0:T(8,128)(2,1)} %fusion.132), channel_id=1, source_target_pairs={{0,2},{1,3},{2,0},{3,1},{4,6},{5,7},{6,4},{7,5},{8,10},{9,11},{10,... | collective-permute-start | bytes 6291464 | tf_op jit(solution)/shard_map/ppermute | solution.py:42
  1151.7 69.7 %collective-permute-start.64 = (bf16[256,512]{1,0:T(8,128)(2,1)S(1)}, bf16[256,512]{1,0:T(8,128)(2,1)}, u32[]{:S(2)}, u32[]{:S(2)}) collective-permute-start(bf16[256,512]{1,0:T(8,128)(2,1)S(1)} %copy-done.204), channel_id=1, source_target_pairs={{0,2},{1,3},{2,0},{3,1},{4,6},{5,7},{6,4},{7,5},{8,10},{9,11},{10,... | collective-permute-start | bytes 786440 | tf_op jit(solution)/shard_map/ppermute | solution.py:42
  1154.6 99.1 %collective-permute-start.85 = (bf16[256,512]{1,0:T(8,128)(2,1)}, bf16[256,512]{1,0:T(8,128)(2,1)}, u32[]{:S(2)}, u32[]{:S(2)}) collective-permute-start(bf16[256,512]{1,0:T(8,128)(2,1)} %fusion.270), channel_id=1, source_target_pairs={{0,2},{1,3},{2,0},{3,1},{4,6},{5,7},{6,4},{7,5},{8,10},{9,11},{10,... | collective-permute-start | bytes 786440 | tf_op jit(solution)/shard_map/ppermute | solution.py:42
  1189.5 26.4 %collective-permute-start.61 = (bf16[256,2048]{1,0:T(8,128)(2,1)}, bf16[256,2048]{1,0:T(8,128)(2,1)}, u32[]{:S(2)}, u32[]{:S(2)}) collective-permute-start(bf16[256,2048]{1,0:T(8,128)(2,1)} %fusion.159), channel_id=1, source_target_pairs={{0,4},{4,0},{8,12},{12,8},{16,20},{20,16},{24,28},{28,24},{1,5},{5... | collective-permute-start | bytes 3145736 | tf_op jit(solution)/shard_map/ppermute | solution.py:42
  1200.0 45.9 %collective-permute-start.73 = (bf16[1024,512]{0,1:T(8,128)(2,1)}, bf16[1024,512]{0,1:T(8,128)(2,1)}, u32[]{:S(2)}, u32[]{:S(2)}) collective-permute-start(bf16[1024,512]{0,1:T(8,128)(2,1)} %fusion.156), channel_id=1, source_target_pairs={{0,2},{1,3},{2,0},{3,1},{4,6},{5,7},{6,4},{7,5},{8,10},{9,11},{10,... | collective-permute-start | bytes 3145736 | tf_op jit(solution)/shard_map/ppermute | solution.py:42
  1207.4 31.0 %collective-permute-start.82 = (bf16[256,2048]{1,0:T(8,128)(2,1)}, bf16[256,2048]{1,0:T(8,128)(2,1)}, u32[]{:S(2)}, u32[]{:S(2)}) collective-permute-start(bf16[256,2048]{1,0:T(8,128)(2,1)} %fusion.153), channel_id=1, source_target_pairs={{0,4},{4,0},{8,12},{12,8},{16,20},{20,16},{24,28},{28,24},{1,5},{5... | collective-permute-start | bytes 3145736 | tf_op jit(solution)/shard_map/ppermute | solution.py:42
  1215.9 41.0 %collective-permute-start.97 = (bf16[1024,512]{0,1:T(8,128)(2,1)}, bf16[1024,512]{0,1:T(8,128)(2,1)}, u32[]{:S(2)}, u32[]{:S(2)}) collective-permute-start(bf16[1024,512]{0,1:T(8,128)(2,1)} %fusion.150), channel_id=1, source_target_pairs={{0,2},{1,3},{2,0},{3,1},{4,6},{5,7},{6,4},{7,5},{8,10},{9,11},{10,... | collective-permute-start | bytes 3145736 | tf_op jit(solution)/shard_map/ppermute | solution.py:42
  1221.4 118.9 %collective-permute-start.51 = (bf16[512,1536]{1,0:T(8,128)(2,1)}, bf16[512,1536]{1,0:T(8,128)(2,1)}, u32[]{:S(2)}, u32[]{:S(2)}) collective-permute-start(bf16[512,1536]{1,0:T(8,128)(2,1)} %fusion.139), channel_id=1, source_target_pairs={{0,4},{4,0},{8,12},{12,8},{16,20},{20,16},{24,28},{28,24},{1,5},{5... | collective-permute-start | bytes 4718600 | tf_op jit(solution)/shard_map/ppermute | solution.py:42
  1238.4 47.8 %collective-permute-start.65 = (bf16[256,640]{1,0:T(8,128)(2,1)}, bf16[256,640]{1,0:T(8,128)(2,1)}, u32[]{:S(2)}, u32[]{:S(2)}) collective-permute-start(bf16[256,640]{1,0:T(8,128)(2,1)} %get-tuple-element.343), channel_id=1, source_target_pairs={{0,8},{4,12},{1,9},{5,13},{2,10},{6,14},{3,11},{7,15}} | collective-permute-start | bytes 983048 | tf_op jit(solution)/shard_map/ppermute | solution.py:91
  1245.9 68.9 %collective-permute-start.68 = (bf16[256,640]{1,0:T(8,128)(2,1)}, bf16[256,640]{1,0:T(8,128)(2,1)}, u32[]{:S(2)}, u32[]{:S(2)}) collective-permute-start(bf16[256,640]{1,0:T(8,128)(2,1)} %get-tuple-element.344), channel_id=1, source_target_pairs={{24,16},{28,20},{25,17},{29,21},{26,18},{30,22},{27,19},{31,23}} | collective-permute-start | bytes 983048 | tf_op jit(solution)/shard_map/ppermute | solution.py:92
  1284.5 63.8 %collective-permute-start.92 = (bf16[256,1024]{1,0:T(8,128)(2,1)}, bf16[256,1024]{1,0:T(8,128)(2,1)S(1)}, u32[]{:S(2)}, u32[]{:S(2)}) collective-permute-start(bf16[256,1024]{1,0:T(8,128)(2,1)} %get-tuple-element.308), channel_id=1, source_target_pairs={{24,16},{28,20},{25,17},{29,21},{26,18},{30,22},{27,19},{31,23}} | collective-permute-start | bytes 1572872 | tf_op jit(solution)/shard_map/ppermute | solution.py:92
  1350.4 37.3 %collective-permute-start.91 = (bf16[256,1024]{1,0:T(8,128)(2,1)}, bf16[256,1024]{1,0:T(8,128)(2,1)}, u32[]{:S(2)}, u32[]{:S(2)}) collective-permute-start(bf16[256,1024]{1,0:T(8,128)(2,1)} %get-tuple-element.305), channel_id=1, source_target_pairs={{0,8},{4,12},{8,16},{12,20},{16,24},{20,28},{1,9},{5,13},{9,17},{1... | collective-permute-start | bytes 1572872 | tf_op jit(solution)/shard_map/ppermute | solution.py:91
  (297 other events, 2791.0 us)

commit v2 on v1

--- a/solution.py
+++ b/solution.py
@@ -1,6 +1,10 @@
+import functools
+
 import jax
 import jax.numpy as jnp
 from jax import lax
+from jax.experimental import pallas as pl
+from jax.experimental.pallas import tpu as pltpu
 from jax.sharding import PartitionSpec as P
 
 HEADS = 16
@@ -363,7 +367,650 @@
     )
 
 
-def shards(
+LANES = 128
+TILE = 256
+VMEM_LIMIT = 48 * 1024 * 1024
+
+
+def whole_block(shape):
+    return pl.BlockSpec(shape, lambda *_: (0,) * len(shape))
+
+
+def causal_tiles(length):
+    tile = min(TILE, length)
+    return [(start, tile, start + tile) for start in range(0, length, tile)]
+
+
+def head_masks(dtype):
+    lane = lax.broadcasted_iota(jnp.int32, (1, LANES), 1)
+    return [((lane // HEAD) == head).astype(dtype) for head in range(LANES // HEAD)]
+
+
+def frame_attend_kernel(packed_ref, seg_col_ref, seg_row_ref, out_ref):
+    chunks, _, own, _ = packed_ref.shape
+    length = chunks * own
+    packed = packed_ref[...].reshape(length, 3 * LANES)
+    queries, keys, values = (packed[:, LANES * i : LANES * (i + 1)] for i in range(3))
+    masks = head_masks(BF)
+    lane = lax.broadcasted_iota(jnp.int32, (1, LANES), 1)
+    for start, tile, end in causal_tiles(length):
+        query_pos = start + lax.broadcasted_iota(jnp.int32, (tile, end), 0)
+        key_pos = lax.broadcasted_iota(jnp.int32, (tile, end), 1)
+        allowed = (seg_col_ref[0, start:end] == seg_row_ref[0, :, :end]) & (key_pos <= query_pos)
+        result = jnp.zeros((tile, LANES), F32)
+        for head, mask in enumerate(masks):
+            scores = inner_right(queries[start:end] * mask, keys[:end]) * FACTOR
+            scores = jnp.where(allowed, scores, MASKED)
+            powers = jnp.exp(scores - jnp.max(scores, axis=1, keepdims=True))
+            portions = powers / jnp.sum(powers, axis=1, keepdims=True)
+            found = matmul(portions.astype(BF), values[:end])
+            result = jnp.where(lane // HEAD == head, found, result)
+        out_ref[start // own : end // own, 0] = result.astype(BF).reshape(tile // own, own, LANES)
+
+
+def frame_attend_grads_kernel(packed_ref, grad_ref, seg_col_ref, seg_row_ref, out_ref, key_sum, value_sum):
+    chunks, _, own, _ = packed_ref.shape
+    length = chunks * own
+    packed = packed_ref[...].reshape(length, 3 * LANES)
+    queries, keys, values = (packed[:, LANES * i : LANES * (i + 1)] for i in range(3))
+    grads = grad_ref[...].reshape(length, LANES)
+    masks = head_masks(BF)
+    lane = lax.broadcasted_iota(jnp.int32, (1, LANES), 1)
+    key_sum[...] = jnp.zeros_like(key_sum)
+    value_sum[...] = jnp.zeros_like(value_sum)
+    for start, tile, end in causal_tiles(length):
+        key_pos = lax.broadcasted_iota(jnp.int32, (end, tile), 0)
+        query_pos = start + lax.broadcasted_iota(jnp.int32, (end, tile), 1)
+        allowed = (seg_col_ref[0, :end] == seg_row_ref[0, :, start:end]) & (key_pos <= query_pos)
+        query_grad = jnp.zeros((tile, LANES), F32)
+        for head, mask in enumerate(masks):
+            query = queries[start:end] * mask
+            grad = grads[start:end] * mask
+            scores = inner_right(keys[:end], query) * FACTOR
+            scores = jnp.where(allowed, scores, MASKED)
+            powers = jnp.exp(scores - jnp.max(scores, axis=0, keepdims=True))
+            portions = powers / jnp.sum(powers, axis=0, keepdims=True)
+            portion_grad = inner_right(values[:end], grad)
+            mean = jnp.sum(portions * portion_grad, axis=0, keepdims=True)
+            score_grad = (portions * (portion_grad - mean)).astype(BF)
+            key_sum[:end] += matmul(score_grad, query)
+            value_sum[:end] += matmul(portions.astype(BF), grad)
+            found = inner_left(score_grad, keys[:end])
+            query_grad = jnp.where(lane // HEAD == head, found, query_grad)
+        out_ref[start // own : end // own, 0, :, :LANES] = (
+            (query_grad * FACTOR).astype(BF).reshape(tile // own, own, LANES)
+        )
+    out_ref[:, 0, :, LANES : 2 * LANES] = (key_sum[...] * FACTOR).astype(BF).reshape(chunks, own, LANES)
+    out_ref[:, 0, :, 2 * LANES :] = value_sum[...].astype(BF).reshape(chunks, own, LANES)
+
+
+def row_spec(chunks, own, breadth):
+    return pl.BlockSpec((chunks, 1, own, breadth), lambda row: (0, row, 0, 0))
+
+
+def segment_specs(length):
+    return [
+        pl.BlockSpec((1, length, 1), lambda row: (row, 0, 0)),
+        pl.BlockSpec((1, 1, length), lambda row: (row, 0, 0)),
+    ]
+
+
+def frame_attend_call(packed, segments):
+    chunks, rows, own, _ = packed.shape
+    length = chunks * own
+    return pl.pallas_call(
+        frame_attend_kernel,
+        grid=(rows,),
+        in_specs=[row_spec(chunks, own, 3 * LANES), *segment_specs(length)],
+        out_specs=row_spec(chunks, own, LANES),
+        out_shape=jax.ShapeDtypeStruct((chunks, rows, own, LANES), BF),
+        compiler_params=pltpu.CompilerParams(vmem_limit_bytes=VMEM_LIMIT),
+        cost_estimate=pl.CostEstimate(
+            flops=rows * length * length * LANES * 5,
+            bytes_accessed=packed.size * 3,
+            transcendentals=rows * length * length,
+        ),
+        name="frame_attend",
+    )(packed, segments[:, :, None], segments[:, None, :])
+
+
+def frame_attend_grads_call(packed, grads, segments):
+    chunks, rows, own, _ = packed.shape
+    length = chunks * own
+    return pl.pallas_call(
+        frame_attend_grads_kernel,
+        grid=(rows,),
+        in_specs=[
+            row_spec(chunks, own, 3 * LANES),
+            row_spec(chunks, own, LANES),
+            *segment_specs(length),
+        ],
+        out_specs=row_spec(chunks, own, 3 * LANES),
+        out_shape=jax.ShapeDtypeStruct((chunks, rows, own, 3 * LANES), BF),
+        scratch_shapes=[pltpu.VMEM((length, LANES), F32), pltpu.VMEM((length, LANES), F32)],
+        compiler_params=pltpu.CompilerParams(vmem_limit_bytes=VMEM_LIMIT),
+        cost_estimate=pl.CostEstimate(
+            flops=rows * length * length * LANES * 12,
+            bytes_accessed=packed.size * 5,
+            transcendentals=rows * length * length,
+        ),
+        name="frame_attend_grads",
+    )(packed, grads, segments[:, :, None], segments[:, None, :])
+
+
+def position_pairs(positions):
+    return [(later, earlier) for later in range(1, positions) for earlier in range(later + 1)]
+
+
+def codec_sums(products, marks):
+    stacked = jnp.concatenate(products, axis=0)
+    high = stacked.astype(BF)
+    low = (stacked - high.astype(F32)).astype(BF)
+    total = matmul(high, marks) + matmul(low, marks)
+    size = products[0].shape[0]
+    return [total[size * i : size * (i + 1)] for i in range(len(products))]
+
+
+def codec_spread(portions, marks):
+    stacked = jnp.concatenate([portion.astype(BF) for portion in portions], axis=0)
+    total = inner_right(stacked, marks)
+    size = portions[0].shape[0]
+    return [total[size * i : size * (i + 1)] for i in range(len(portions))]
+
+
+def codec_portions(queries, keys, marks, pairs):
+    scores = codec_sums(
+        [queries[later].astype(F32) * keys[earlier].astype(F32) for later, earlier in pairs], marks
+    )
+    scores = dict(zip(pairs, [score * FACTOR for score in scores]))
+    portions = {}
+    for later in range(1, len(queries)):
+        row = [scores[later, earlier] for earlier in range(later + 1)]
+        top = functools.reduce(jnp.maximum, row)
+        powers = [jnp.exp(score - top) for score in row]
+        total = functools.reduce(jnp.add, powers)
+        for earlier in range(later + 1):
+            portions[later, earlier] = powers[earlier] / total
+    return portions
+
+
+def codec_parts(packed_ref, width):
+    positions = packed_ref.shape[0]
+    return [
+        [packed_ref[t, :, width * part : width * (part + 1)] for t in range(positions)]
+        for part in range(3)
+    ]
+
+
+def codec_attend_kernel(packed_ref, marks_ref, out_ref):
+    positions, _, width = out_ref.shape
+    queries, keys, values = codec_parts(packed_ref, width)
+    marks = marks_ref[...]
+    pairs = position_pairs(positions)
+    portions = codec_portions(queries, keys, marks, pairs)
+    wide = dict(zip(pairs, codec_spread([portions[pair] for pair in pairs], marks)))
+    out_ref[0] = values[0]
+    for later in range(1, positions):
+        terms = [wide[later, e] * values[e].astype(F32) for e in range(later + 1)]
+        out_ref[later] = functools.reduce(jnp.add, terms).astype(BF)
+
+
+def codec_attend_grads_kernel(packed_ref, grad_ref, marks_ref, out_ref):
+    positions, _, width = grad_ref.shape
+    queries, keys, values = codec_parts(packed_ref, width)
+    marks = marks_ref[...]
+    pairs = position_pairs(positions)
+    portions = codec_portions(queries, keys, marks, pairs)
+    grads = [grad_ref[t].astype(F32) for t in range(positions)]
+    portion_grads = dict(
+        zip(
+            pairs,
+            codec_sums([grads[later] * values[earlier].astype(F32) for later, earlier in pairs], marks),
+        )
+    )
+    score_grads = {}
+    for later in range(1, positions):
+        mean = functools.reduce(
+            jnp.add, [portions[later, e] * portion_grads[later, e] for e in range(later + 1)]
+        )
+        for e in range(later + 1):
+            score_grads[later, e] = portions[later, e] * (portion_grads[later, e] - mean)
+    wide = dict(zip(pairs, codec_spread([portions[pair] for pair in pairs], marks)))
+    wide_grads = dict(zip(pairs, codec_spread([score_grads[pair] for pair in pairs], marks)))
+    zero = jnp.zeros_like(grads[0])
+    for t in range(positions):
+        query_grad = key_grad = zero
+        value_grad = grads[0] if t == 0 else zero
+        for later, earlier in pairs:
+            if later == t:
+                query_grad = query_grad + wide_grads[later, earlier] * keys[earlier].astype(F32)
+            if earlier == t:
+                key_grad = key_grad + wide_grads[later, earlier] * queries[later].astype(F32)
+                value_grad = value_grad + wide[later, earlier] * grads[later]
+        out_ref[t, :, :width] = (query_grad * FACTOR).astype(BF)
+        out_ref[t, :, width : 2 * width] = (key_grad * FACTOR).astype(BF)
+        out_ref[t, :, 2 * width :] = value_grad.astype(BF)
+
+
+def codec_tile(frame_total):
+    return 64 if frame_total % 64 == 0 else frame_total
+
+
+def codec_spec(positions, tile, breadth):
+    return pl.BlockSpec((positions, tile, breadth), lambda i: (0, i, 0))
+
+
+def head_marks(width):
+    return (
+        jnp.arange(width)[:, None] // HEAD == jnp.arange(LANES)[None, :]
+    ).astype(BF)
+
+
+def codec_attend_call(packed):
+    positions, total, triple = packed.shape
+    width = triple // 3
+    tile = codec_tile(total)
+    return pl.pallas_call(
+        codec_attend_kernel,
+        grid=(total // tile,),
+        in_specs=[codec_spec(positions, tile, triple), whole_block((width, LANES))],
+        out_specs=codec_spec(positions, tile, width),
+        out_shape=jax.ShapeDtypeStruct((positions, total, width), BF),
+        compiler_params=pltpu.CompilerParams(vmem_limit_bytes=VMEM_LIMIT),
+        cost_estimate=pl.CostEstimate(
+            flops=total * width * LANES * 30, bytes_accessed=packed.size * 3, transcendentals=0
+        ),
+        name="codec_attend",
+    )(packed, head_marks(width))
+
+
+def codec_attend_grads_call(packed, grads):
+    positions, total, triple = packed.shape
+    width = triple // 3
+    tile = codec_tile(total)
+    return pl.pallas_call(
+        codec_attend_grads_kernel,
+        grid=(total // tile,),
+        in_specs=[
+            codec_spec(positions, tile, triple),
+            codec_spec(positions, tile, width),
+            whole_block((width, LANES)),
+        ],
+        out_specs=codec_spec(positions, tile, triple),
+        out_shape=jax.ShapeDtypeStruct((positions, total, triple), BF),
+        compiler_params=pltpu.CompilerParams(vmem_limit_bytes=VMEM_LIMIT),
+        cost_estimate=pl.CostEstimate(
+            flops=total * width * LANES * 70, bytes_accessed=packed.size * 5, transcendentals=0
+        ),
+        name="codec_attend_grads",
+    )(packed, grads, head_marks(width))
+
+
+def grad_order(place):
+    seqs = [place.seq ^ (2 * spot + 1 - side) for side in range(2) for spot in range(4)]
+    return jnp.stack([place.mp ^ 2, place.mp] + seqs + [place.seq]).astype(jnp.int32)
+
+
+def grad_rows_kernel(mp_first, wide, order_ref, far_own, far_rec, own_own, own_rec, latter_own, latter_rec, *refs):
+    send_ref, keep_ref, turned = refs[-3:]
+    rows = latter_own.shape[0]
+    height = far_own.shape[1]
+
+    @pl.when(pl.program_id(0) == 0)
+    def _():
+        for at, (own, rec) in enumerate(((far_own, far_rec), (own_own, own_rec))):
+            turned[height * at : height * (at + 1), :rows] = own[...].T
+            turned[height * at : height * (at + 1), rows:] = rec[...].T
+
+    total = matmul(turned[:, :rows], latter_own[...]) + matmul(turned[:, rows:], latter_rec[...])
+    grad_rows_store(mp_first, wide, order_ref, total.astype(BF), height, send_ref, keep_ref)
+
+
+def grad_rows_store(mp_first, wide, order_ref, total, height, send_ref, keep_ref):
+    units = height // TILE
+    if wide:
+        chunks = total.shape[1] // 8 // LANES
+        for seq in range(8):
+            change = order_ref[10] ^ seq
+            side = 1 - (change & 1)
+            spot = change >> 1
+            for chunk in range(chunks):
+                first = (seq * chunks + chunk) * LANES
+                value = total[:, first : first + LANES]
+                for unit in range(units):
+                    given = value[unit * TILE : (unit + 1) * TILE]
+                    kept = value[height + unit * TILE : height + (unit + 1) * TILE]
+                    at = chunk * units + unit
+                    if mp_first:
+                        send_ref[side, spot, at] = given
+                        keep_ref[side, spot, at] = kept
+                    else:
+
+                        @pl.when(side == 0)
+                        def _(given=given, kept=kept, at=at, spot=spot):
+                            send_ref[0, spot, at] = given
+                            send_ref[1, spot, at] = kept
+
+                        @pl.when(side == 1)
+                        def _(given=given, kept=kept, at=at, spot=spot):
+                            keep_ref[0, spot, at] = given
+                            keep_ref[1, spot, at] = kept
+
+        return
+    chunks = total.shape[1] // LANES
+    for chunk in range(chunks):
+        value = total[:, chunk * LANES : (chunk + 1) * LANES]
+        given, kept = value[:height], value[height:]
+        if mp_first:
+            send_ref[0, 0, chunk] = given
+            keep_ref[0, 0, chunk] = kept
+        else:
+
+            @pl.when(pl.program_id(0) < 4)
+            def _(given=given, kept=kept, chunk=chunk):
+                send_ref[0, 0, chunk] = given
+                send_ref[1, 0, chunk] = kept
+
+            @pl.when(pl.program_id(0) >= 4)
+            def _(given=given, kept=kept, chunk=chunk):
+                keep_ref[0, 0, chunk] = given
+                keep_ref[1, 0, chunk] = kept
+
+
+def grad_buffers(units):
+    return [jax.ShapeDtypeStruct((2, 4, units, TILE, LANES), BF)] * 2
+
+
+def grad_call(kernel, order, arrays, in_specs, out_specs, units, into, steps, scratch, flops, name):
+    aliases = {}
+    moved = 2 * sum(array.size for array in arrays)
+    if into is not None:
+        aliases = {len(arrays) + 1: 0, len(arrays) + 2: 1}
+        in_specs = in_specs + [pl.BlockSpec(memory_space=pl.ANY)] * 2
+        arrays = arrays + list(into)
+    return pl.pallas_call(
+        kernel,
+        grid_spec=pltpu.PrefetchScalarGridSpec(
+            num_scalar_prefetch=1,
+            grid=(steps,),
+            in_specs=in_specs,
+            out_specs=out_specs,
+            scratch_shapes=[scratch],
+        ),
+        out_shape=grad_buffers(units),
+        input_output_aliases=aliases,
+        compiler_params=pltpu.CompilerParams(vmem_limit_bytes=VMEM_LIMIT),
+        cost_estimate=pl.CostEstimate(flops=flops, bytes_accessed=moved, transcendentals=0),
+        name=name,
+    )(order, *arrays)
+
+
+def grad_rows(former, latter, order, mp_first, units, offset, into=None):
+    rows, breadth = latter[0].shape
+    height = former[0].shape[1] // 4
+    wide = breadth // 8 == LANES
+    chunks = breadth // 8 // LANES
+    steps = 1 if wide else 8
+    arrays = [former[0], former[1], former[0], former[1], latter[0], latter[1]]
+    former_specs = [
+        pl.BlockSpec((rows, height), lambda j, t, at=at: (0, t[at]), pipeline_mode=pl.Buffered(1))
+        for at in (0, 0, 1, 1)
+    ]
+    if wide:
+        latter_specs = [whole_block((rows, breadth))] * 2
+        block = (2, 4, 1, TILE, LANES)
+        out_specs = [pl.BlockSpec(block, lambda j, t: (0, 0, offset, 0, 0))] * 2
+    else:
+        latter_specs = [pl.BlockSpec((rows, breadth // 8), lambda j, t: (0, t[2 + j]))] * 2
+        base = offset // chunks
+        if mp_first:
+            block = (1, 1, chunks, TILE, LANES)
+            out_specs = [pl.BlockSpec(block, lambda j, t: (j // 4, j % 4, base, 0, 0))] * 2
+        else:
+            block = (2, 1, chunks, TILE, LANES)
+            out_specs = [
+                pl.BlockSpec(block, lambda j, t: (0, jnp.minimum(j, 3), base, 0, 0)),
+                pl.BlockSpec(block, lambda j, t: (0, jnp.maximum(j - 4, 0), base, 0, 0)),
+            ]
+    return grad_call(
+        functools.partial(grad_rows_kernel, mp_first, wide),
+        order,
+        arrays,
+        former_specs + latter_specs,
+        out_specs,
+        units,
+        into,
+        steps,
+        pltpu.VMEM((2 * height, 2 * rows), BF),
+        2 * 2 * rows * 2 * height * breadth,
+        "grad_rows",
+    )
+
+
+def grad_columns_kernel(order_ref, latter_own, latter_rec, former_own, former_rec, *refs):
+    send_ref, keep_ref, turned = refs[-3:]
+    rows = latter_own.shape[0]
+    step = pl.program_id(0)
+
+    @pl.when(step == 0)
+    def _():
+        turned[:, :rows] = latter_own[...].T
+        turned[:, rows:] = latter_rec[...].T
+
+    total = matmul(turned[:, :rows], former_own[...]) + matmul(turned[:, rows:], former_rec[...])
+    total = total.astype(BF)
+    chunks = total.shape[1] // LANES
+    for target, when in ((send_ref, step < pl.num_programs(0) // 2), (keep_ref, step >= pl.num_programs(0) // 2)):
+
+        @pl.when(when)
+        def _(target=target):
+            for seq in range(8):
+                change = order_ref[10] ^ seq
+                side = 1 - (change & 1)
+                spot = change >> 1
+                for chunk in range(chunks):
+                    target[side, spot, chunk // 2, (chunk % 2) * LANES : (chunk % 2 + 1) * LANES] = total[
+                        seq * LANES : (seq + 1) * LANES, chunk * LANES : (chunk + 1) * LANES
+                    ]
+
+
+def grad_columns(former, latter, order, units, offset, into=None):
+    rows, breadth = latter[0].shape
+    height = former[0].shape[1] // 4
+    step = min(512, height)
+    per = height // step
+    block = (2, 4, step // TILE, TILE, LANES)
+    base = offset // (step // TILE)
+    latter_specs = [
+        pl.BlockSpec((rows, breadth), lambda j, t: (0, 0), pipeline_mode=pl.Buffered(1))
+    ] * 2
+    former_specs = [pl.BlockSpec((rows, step), lambda j, t: (0, t[j // per] * per + j % per))] * 2
+    out_specs = [
+        pl.BlockSpec(block, lambda j, t: (0, 0, base + jnp.minimum(j, per - 1), 0, 0)),
+        pl.BlockSpec(block, lambda j, t: (0, 0, base + jnp.maximum(j - per, 0), 0, 0)),
+    ]
+    return grad_call(
+        grad_columns_kernel,
+        order,
+        [latter[0], latter[1], former[0], former[1]],
+        latter_specs + former_specs,
+        out_specs,
+        units,
+        into,
+        2 * per,
+        pltpu.VMEM((breadth, 2 * rows), BF),
+        2 * 2 * rows * 2 * height * breadth,
+        "grad_columns",
+    )
+
+
+def grad_table_kernel(height, order_ref, codes_ref, latter_own, latter_rec, *refs):
+    send_ref, keep_ref, _ = refs[-3:]
+    rows = latter_own.shape[0]
+    parts = []
+    for at in range(2):
+        entry = order_ref[at] * height + lax.broadcasted_iota(jnp.int32, (height, 2 * rows), 0)
+        parts.append((entry == codes_ref[...]).astype(F32).astype(BF))
+    chosen = jnp.concatenate(parts, axis=0)
+    total = matmul(chosen[:, :rows], latter_own[...]) + matmul(chosen[:, rows:], latter_rec[...])
+    grad_rows_store(False, True, order_ref, total.astype(BF), height, send_ref, keep_ref)
+
+
+def grad_table(codes, latter, order, height, units, offset, into=None):
+    rows, breadth = latter[0].shape
+    block = (2, 4, height // TILE, TILE, LANES)
+    base = offset // (height // TILE)
+    return grad_call(
+        functools.partial(grad_table_kernel, height),
+        order,
+        [codes, latter[0], latter[1]],
+        [whole_block(codes.shape), whole_block((rows, breadth)), whole_block((rows, breadth))],
+        [pl.BlockSpec(block, lambda j, t: (0, 0, base, 0, 0))] * 2,
+        units,
+        into,
+        1,
+        pltpu.VMEM((8, LANES), F32),
+        2 * 2 * rows * 2 * height * breadth,
+        "grad_table",
+    )
+
+
+def reduce_blocks(send, keep, mp_first):
+    stages = (("mp", 2), ("seq", 1)) if mp_first else (("seq", 1), ("mp", 2))
+    first = swap(send, *stages[0])
+    given = (keep[0].astype(F32) + first[0].astype(F32)).astype(BF)
+    second = swap(given, *stages[1])
+    total = (keep[1].astype(F32) + first[1].astype(F32) + second.astype(F32)).astype(BF)
+    far = swap(total[2:], "seq", 4)
+    total = total[:2].astype(F32) + far.astype(F32)
+    near = swap(total[1].astype(BF), "seq", 2)
+    return total[0] + near.astype(F32)
+
+
+def rows_from_units(units, height):
+    tiles = height // TILE
+    chunks = units.shape[0] // tiles
+    return jnp.transpose(
+        units.reshape(chunks, height, LANES), (1, 0, 2)
+    ).reshape(height, chunks * LANES)
+
+
+def columns_from_units(units):
+    count = units.shape[0]
+    return jnp.transpose(units.reshape(2 * count, LANES, LANES), (0, 2, 1)).reshape(count * TILE, LANES)
+
+
+def join_kernel(layout, place_ref, *refs):
+    count = len(layout)
+    own, other, first, second, first_other, second_other = refs[:6]
+    outs = refs[6 : 6 + count]
+    held = refs[6 + count : 6 + 2 * count]
+    sems, out_sems = refs[-2:]
+    half = first.shape[0]
+    width = own.shape[1]
+    me = place_ref[0]
+    low = place_ref[1]
+    copies = []
+    for at, (height, breadth, start) in enumerate(layout):
+        for column in range(breadth // width):
+            row = start + column * height
+            columns = pl.ds(column * width, width)
+            for flip, source in ((0, own), (1, other)):
+                target = held[at].at[pl.ds(pl.multiple_of((me ^ flip) * height, height), height), columns]
+                copies.append((at, None, source.at[pl.ds(row, height)], target))
+            for flip, sources in ((2, (first, second)), (3, (first_other, second_other))):
+                for side in range(2):
+                    begin, end = max(row, side * half), min(row + height, (side + 1) * half)
+                    if begin >= end:
+                        continue
+                    rows = pl.ds(begin - side * half, end - begin)
+                    target = held[at].at[
+                        pl.ds(pl.multiple_of((me ^ flip) * height + begin - row, 16), end - begin), columns
+                    ]
+                    copies.append((at, side, sources[0].at[rows], target))
+                    copies.append((at, 1 - side, sources[1].at[rows], target))
+
+    def act(action, number):
+        _, when, source, target = copies[number]
+        copy = pltpu.make_async_copy(source, target, sems.at[number])
+        if when is None:
+            getattr(copy, action)()
+        else:
+
+            @pl.when(low == when)
+            def _():
+                getattr(copy, action)()
+
+    for number in range(len(copies)):
+        act("start", number)
+    for at in range(count):
+        for number in range(len(copies)):
+            if copies[number][0] == at:
+                act("wait", number)
+        pltpu.make_async_copy(held[at], outs[at], out_sems.at[at]).start()
+    for at in range(count):
+        pltpu.make_async_copy(held[at], outs[at], out_sems.at[at]).wait()
+
+
+def join_count(layout, half, width):
+    count = 0
+    for height, breadth, start in layout:
+        for column in range(breadth // width):
+            row = start + column * height
+            count += 2
+            for side in range(2):
+                if max(row, side * half) < min(row + height, (side + 1) * half):
+                    count += 4
+    return count
+
+
+def pack_weights(shards):
+    width = 1024
+    pieces = []
+    for shard in shards:
+        for column in range(shard.shape[1] // width):
+            pieces.append(shard[:, column * width : (column + 1) * width])
+    return pieces[0] if len(pieces) == 1 else jnp.concatenate(pieces, axis=0)
+
+
+def pack_layout(shards):
+    layout, start = [], 0
+    for shard in shards:
+        height, breadth = shard.shape
+        layout.append((height, breadth, start))
+        start += height * (breadth // 1024)
+    return tuple(layout), start
+
+
+def join_weights(pack, other, first, second, first_other, second_other, layout, place):
+    half, width = first.shape
+    any_spec = pl.BlockSpec(memory_space=pl.ANY)
+    outs = [jax.ShapeDtypeStruct((4 * height, breadth), BF) for height, breadth, _ in layout]
+    return pl.pallas_call(
+        functools.partial(join_kernel, layout),
+        in_specs=[pl.BlockSpec(memory_space=pltpu.SMEM)] + [any_spec] * 6,
+        out_specs=[any_spec] * len(outs),
+        out_shape=outs,
+        scratch_shapes=[pltpu.VMEM(out.shape, BF) for out in outs]
+        + [
+            pltpu.SemaphoreType.DMA((join_count(layout, half, width),)),
+            pltpu.SemaphoreType.DMA((len(outs),)),
+        ],
+        compiler_params=pltpu.CompilerParams(vmem_limit_bytes=VMEM_LIMIT),
+        cost_estimate=pl.CostEstimate(flops=0, bytes_accessed=16 * pack.size, transcendentals=0),
+        name="join_weights",
+    )(
+        jnp.stack([place.mp, place.seq_low]).astype(jnp.int32),
+        pack,
+        other,
+        first,
+        second,
+        first_other,
+        second_other,
+    )
+
+
+def shards_general(
     frames,
     segments,
     padding,
@@ -514,6 +1161,207 @@
     )
 
 
+def tie(values, *after):
+    flat, tree = jax.tree.flatten(values)
+    held = lax.optimization_barrier(tuple(flat) + tuple(after))
+    return jax.tree.unflatten(tree, held[: len(flat)])
+
+
+def start_pack(pack, place, *after):
+    half = pack.shape[0] // 2
+    mine = lax.dynamic_slice(pack, (place.seq_low * half, 0), (half, pack.shape[1]))
+    if after:
+        pack, mine = tie((pack, mine), *after)
+    first = swap(mine, "mp", 2)
+    other = swap(pack, "mp", 1)
+    second = swap(first, "seq", 1)
+    return [pack, other, first, second, swap(first, "mp", 1), swap(second, "mp", 1)]
+
+
+def pair(values):
+    return (values, swap(values, "mp", 1))
+
+
+def shards(
+    frames,
+    segments,
+    padding,
+    codec_tokens,
+    codebooks,
+    frame_prenorm,
+    frame_project,
+    frame_output,
+    frame_postnorm,
+    frame_expand,
+    frame_contract,
+    codec_prenorm,
+    codec_project,
+    codec_output,
+    codec_postnorm,
+    codec_expand,
+    codec_contract,
+    cotangent,
+):
+    place = Place()
+    order = grad_order(place)
+    row_count, frames_dev, width = frames.shape
+    frame_total = row_count * frames_dev
+    positions = cotangent.shape[2]
+
+    packs = (
+        [frame_project],
+        [frame_expand, frame_contract, frame_output],
+        [codec_project, codebooks],
+        [codec_expand, codec_contract, codec_output],
+    )
+    pieces = []
+    for members in packs:
+        pack = pack_weights(members)
+        pieces.append(start_pack(pack, place, *([pieces[-1][2]] if pieces else [])))
+
+    def joined(at):
+        return join_weights(*pieces[at], pack_layout(packs[at])[0], place)
+
+    gains = lax.all_gather(
+        jnp.stack([frame_prenorm, frame_postnorm, codec_prenorm, codec_postnorm]),
+        "mp",
+        axis=1,
+        tiled=True,
+    )
+    every_segment = lax.all_gather(segments, "seq", axis=1, tiled=True)
+    codes = codec_tokens.reshape(1, (positions - 1) * frame_total) + jnp.repeat(
+        jnp.arange(positions - 1, dtype=jnp.int32) * CODES, frame_total
+    )
+    codes_both = jnp.concatenate(pair(codes), axis=1)
+    live = padding.reshape(frame_total).astype(F32)[None, :, None]
+    codec_grad = (
+        jnp.transpose(cotangent.reshape(frame_total, positions, width), (1, 0, 2)).astype(F32) * live
+    ).reshape(positions * frame_total, width)
+    contract_in = pair(codec_grad.astype(BF))
+
+    (weight_project,) = joined(0)
+    hidden = frames.astype(F32).reshape(frame_total, width)
+    normed, projected = front_pass(hidden, (gains[0], weight_project))
+    normed_both = pair(normed)
+    count = place.seq_count
+    packed = jnp.transpose(
+        projected.reshape(row_count, frames_dev, 3, count, LANES), (3, 0, 1, 2, 4)
+    ).reshape(count, row_count, frames_dev, 3 * LANES)
+    packed = lax.all_to_all(packed, "seq", split_axis=0, concat_axis=0, tiled=True)
+    attended = lax.all_to_all(
+        frame_attend_call(packed, every_segment), "seq", split_axis=0, concat_axis=0, tiled=True
+    )
+    attended = jnp.transpose(attended, (1, 2, 0, 3)).reshape(frame_total, width)
+    attended_both = pair(attended)
+    weight_expand, weight_contract, weight_output = joined(1)
+    frame_weights = (gains[0], weight_project, weight_output, gains[1], weight_expand, weight_contract)
+    frame_result, frame_saved = rear_pass(hidden, attended, frame_weights)
+    normed_two_both = pair(frame_saved[1])
+    activated_both = pair(frame_saved[3])
+    base = frame_result.astype(BF).astype(F32)
+
+    weight_project, table = joined(2)
+    embedded = table[codes.reshape(positions - 1, frame_total)].astype(F32)
+    codec_hidden = jnp.concatenate([base[None], base[None] + embedded], axis=0).reshape(
+        positions * frame_total, width
+    )
+    codec_normed, codec_projected = front_pass(codec_hidden, (gains[2], weight_project))
+    codec_normed_both = pair(codec_normed)
+    codec_packed = codec_projected.reshape(positions, frame_total, 3 * width)
+    codec_attended = codec_attend_call(codec_packed).reshape(positions * frame_total, width)
+    codec_attended_both = pair(codec_attended)
+    weight_expand, weight_contract, weight_output = joined(3)
+    codec_weights = (gains[2], weight_project, weight_output, gains[3], weight_expand, weight_contract)
+    codec_result, codec_saved = rear_pass(codec_hidden, codec_attended, codec_weights)
+    codec_normed_two_both = pair(codec_saved[1])
+    codec_activated_both = pair(codec_saved[3])
+    output = jnp.transpose(
+        (codec_result.reshape(positions, frame_total, width) * live).astype(BF), (1, 0, 2)
+    ).reshape(row_count, frames_dev, positions, width)
+
+    mixed_grad, attended_grad, codec_postnorm_grad, _, expand_in, output_in = rear_grads(
+        codec_grad, codec_saved, codec_weights
+    )
+    output_in = pair(output_in)
+    codec_one = grad_rows(codec_normed_two_both, pair(expand_in), order, True, 8, 0)
+    codec_one = grad_columns(codec_activated_both, contract_in, order, 8, 4, codec_one)
+    codec_one = reduce_blocks(*codec_one, True)
+    codec_projected_grad = codec_attend_grads_call(
+        codec_packed, attended_grad.reshape(positions, frame_total, width)
+    ).reshape(positions * frame_total, 3 * width)
+    codec_two = grad_rows(codec_normed_both, pair(codec_projected_grad), order, False, 6, 0)
+    codec_two = grad_rows(codec_attended_both, output_in, order, False, 6, 3, codec_two)
+    input_grad, codec_prenorm_grad = front_grads(
+        codec_hidden, codec_projected_grad, mixed_grad, codec_weights
+    )
+    input_grad = input_grad.reshape(positions, frame_total, width)
+    table_in = pair(input_grad[1:].reshape(-1, width).astype(BF))
+    codec_two = grad_table(codes_both, table_in, order, codebooks.shape[0], 6, 4, codec_two)
+    codec_two = reduce_blocks(*codec_two, False)
+    base_grad = jnp.sum(input_grad, axis=0).astype(BF).astype(F32)
+
+    (
+        frame_mixed_grad,
+        frame_attended_grad,
+        frame_postnorm_grad,
+        contract_in,
+        expand_in,
+        output_in,
+    ) = rear_grads(base_grad, frame_saved, frame_weights)
+    grads = lax.all_to_all(
+        jnp.transpose(
+            frame_attended_grad.reshape(row_count, frames_dev, count, LANES), (2, 0, 1, 3)
+        ),
+        "seq",
+        split_axis=0,
+        concat_axis=0,
+        tiled=True,
+    )
+    frame_one = grad_rows(normed_two_both, pair(expand_in), order, True, 8, 0)
+    frame_one = grad_columns(activated_both, pair(contract_in), order, 8, 4, frame_one)
+    frame_one = reduce_blocks(*frame_one, True)
+    packed_grad = lax.all_to_all(
+        frame_attend_grads_call(packed, grads, every_segment),
+        "seq",
+        split_axis=0,
+        concat_axis=0,
+        tiled=True,
+    )
+    frame_projected_grad = jnp.transpose(
+        packed_grad.reshape(count, row_count, frames_dev, 3, LANES), (1, 2, 3, 0, 4)
+    ).reshape(frame_total, 3 * width)
+    frame_two = grad_rows(normed_both, pair(frame_projected_grad), order, False, 4, 0)
+    frame_two = grad_rows(attended_both, pair(output_in), order, False, 4, 3, frame_two)
+    frame_two = reduce_blocks(*frame_two, False)
+    frames_grad, frame_prenorm_grad = front_grads(
+        hidden, frame_projected_grad, frame_mixed_grad, frame_weights
+    )
+    gain_sums = sum_everywhere(
+        jnp.stack(
+            [frame_prenorm_grad, frame_postnorm_grad, codec_prenorm_grad, codec_postnorm_grad]
+        ),
+        place,
+    )
+    height = frame_project.shape[0]
+    return (
+        output,
+        frames_grad.reshape(row_count, frames_dev, width),
+        rows_from_units(codec_two[4:], codebooks.shape[0]),
+        gain_sums[0],
+        rows_from_units(frame_two[:3], height),
+        rows_from_units(frame_two[3:], height),
+        gain_sums[1],
+        rows_from_units(frame_one[:4], height),
+        columns_from_units(frame_one[4:]),
+        gain_sums[2],
+        rows_from_units(codec_two[:3], height),
+        rows_from_units(codec_two[3:4], height),
+        gain_sums[3],
+        rows_from_units(codec_one[:4], height),
+        columns_from_units(codec_one[4:]),
+    )
+
+
 def solution(mesh):
     placed = (
         P("mp", "seq", None),
@@ -535,8 +1383,9 @@
         P("mp", None),
         P("mp", "seq", None, None),
     )
+    small = mesh.shape["seq"] == 8 and mesh.shape["mp"] == 4
     return jax.shard_map(
-        shards,
+        shards if small else shards_general,
         mesh=mesh,
         in_specs=placed,
         out_specs=(

time: 1410 us -> 949 us (0.67)
  local copies, waits for them, and re-layouts: 432 us -> 99.5 us
  matrix products: 314 us -> 125 us
  Pallas kernels: 0 us -> 155 us
  starting transfers between devices: 177 us -> 63.1 us
  other arithmetic: 111 us -> 47 us
  waiting for transfers between devices: 315 us -> 379 us
  blocking collectives: 38.5 us -> 66.4 us
    pallas_call x0 -> x17, Pallas kernels: none -> 155 us  [the longest x9 77.1 us: grad_call(): pl.pallas_call(kernel, grid_spec=pltpu.PrefetchScalarGridSpec(num_scalar_...]
    dot_general x70 -> x0, matrix products: 154 us -> none  [the longest x36 108 us: inner_left(): lax.dot_general(former, latter, (((0,), (0,)), ((), ())), preferred_eleme...]
    ppermute x36 -> x0, starting transfers between devices: 98.7 us -> none  [the longest x18 80.2 us: line_scatter(): up_in = lax.ppermute(up_out, 'seq', up_perm)]
    dynamic_slice x54 -> x4, local copies, waits for them, and re-layouts: 104 us -> 9.43 us  [start_pack(): lax.dynamic_slice(pack, (place.seq_low * half, 0), (half, pack.shape[1]))]
    dynamic_update_slice x54 -> x0, local copies, waits for them, and re-layouts: 80.9 us -> none  [the longest x36 65 us: gather_weight(): lax.dynamic_update_slice(whole, piece, ((place.mp ^ flip) * height, 0))]
    ppermute x68 -> x59, waiting for transfers between devices: 274 us -> 354 us  [swap(): lax.ppermute(values, axis, [(i, i ^ bit) for i in range(lax.axis_size(axi...]
    convert_element_type x31 -> x9, other arithmetic: 68.1 us -> 19.1 us  [the longest x4 10.2 us: reduce_blocks(): (keep[1].astype(F32) + first[1].astype(F32) + second.astype(F32)).astype(BF)]
    unnamed x499 -> x190, local copies, waits for them, and re-layouts: 91.4 us -> 47.8 us
  transfers between devices with their start and end apart: 108 -> 63, of which waited for: 33 -> 23; matrix products, arithmetic and copies ran while one was open for 44% -> 26% of each run, Pallas kernels for 0% -> 17%
where the time goes in v2:
time: 949 us; the launch traced here: 938 us
  waiting for transfers between devices  379 us (40%)
  Pallas kernels  155 us (16%)
  matrix products  125 us (13%)
  local copies, waits for them, and re-layouts  99.5 us (10%)
  blocking collectives  66.4 us (7%)
  starting transfers between devices  63.1 us (7%)
  other arithmetic  47 us (5%)
    ppermute x59, waiting for transfers between devices, swap(): lax.ppermute(values, axis, [(i, i ^ bit) for i in range(lax.axis_size(axi...  354 us
    pallas_call x9, Pallas kernels, grad_call(): pl.pallas_call(kernel, grid_spec=pltpu.PrefetchScalarGridSpec(num_scalar_...  77.1 us
    dot_general x8, matrix products, matmul(): return jnp.dot(former, latter, preferred_element_type=F32)  65.1 us
    dot_general x8, matrix products, inner_right(): lax.dot_general(former, latter, (((1,), (1,)), ((), ())), preferred_eleme...  60.2 us
    unnamed x190, local copies, waits for them, and re-layouts  47.8 us
    all_gather x1, blocking collectives, shards(): lax.all_gather(jnp.stack([frame_prenorm, frame_postnorm, codec_prenorm, c...  45.6 us
    ppermute x59, starting transfers between devices, swap(): lax.ppermute(values, axis, [(i, i ^ bit) for i in range(lax.axis_size(axi...  45 us
    pallas_call x4, Pallas kernels, join_weights(): pl.pallas_call(functools.partial(join_kernel, layout), in_specs=[pl.Block...  39.5 us
  transfers between devices with their start and end apart: 63, of which 23 were waited for; matrix products, arithmetic and copies ran while one was open for 26% of the time, Pallas kernels for 17%

profile of v2, /device:TPU:0, one launch (start us, length us, event | category | flops | bytes accessed | tf_op | source)
XLA Modules:
  0.0 937.6 jit_solution(12351330761480534807)
XLA Ops:
  16.9 3.4 constant_dynamic-slice_fusion.2
  31.1 45.6 %all_gather.6 = bf16[4,1024]{1,0:T(4,128)(2,1)S(1)} all-gather(bf16[4,256]{1,0:T(4,128)(2,1)S(1)} %pad_maximum_fusion.4), channel_id=1, replica_groups=mesh['seq'=8,'mp'=4] {'mp'}, dimensions={1}, use_global_device_ids=true | all-gather | bytes 10240 | tf_op jit(solution)/shard_map/all_gather | solution.py:1225
  83.3 5.8 join_weights.4
  89.1 4.6 fusion.24
  98.5 4.9 all-to-all-start
  103.4 7.2 collective-permute-done.11.refs_2_
  117.8 3.5 constant_dynamic-slice_fusion
  122.7 25.5 %collective-permute-done.7.refs_3_ = bf16[1152,1024]{1,0:T(8,128)(2,1)} collective-permute-done((bf16[1152,1024]{1,0:T(8,128)(2,1)}, bf16[1152,1024]{1,0:T(8,128)(2,1)}, u32[]{:S(2)}, u32[]{:S(2)}) %collective-permute-start.7) | collective-permute-done | bytes 2359328 | tf_op jit(solution)/shard_map/ppermute | solution.py:46
  148.8 31.3 %collective-permute-done.12.refs_3_ = bf16[640,1024]{1,0:T(8,128)(2,1)} collective-permute-done((bf16[640,1024]{1,0:T(8,128)(2,1)S(1)}, bf16[640,1024]{1,0:T(8,128)(2,1)}, u32[]{:S(2)}, u32[]{:S(2)}) %collective-permute-start.12) | collective-permute-done | bytes 1310752 | tf_op jit(solution)/shard_map/ppermute | solution.py:46
  181.3 20.8 %all_gather.7 = s32[2,1024]{1,0:T(2,128)S(1)} all-gather(s32[2,128]{1,0:T(2,128)S(1)} %copy-done.75), channel_id=1, replica_groups=mesh['seq'=8,'mp'=4] {'seq'}, dimensions={1}, use_global_device_ids=true | all-gather | bytes 9216 | tf_op jit(solution)/shard_map/all_gather | solution.py:1231
  202.5 3.1 copy.54
  205.7 9.4 frame_attend.1
  215.0 4.1 all-to-all-start.1
  225.1 5.3 all-to-all-done.1
  233.3 7.3 join_weights.6
  240.6 5.5 gather_fusion
  246.7 13.1 %join_weights.5 = (bf16[1024,4096]{1,0:T(8,128)(2,1)}, bf16[4096,1024]{1,0:T(8,128)(2,1)}, bf16[1024,1024]{1,0:T(8,128)(2,1)S(1)}) custom-call(s32[2]{0:T(128)S(1)} %pad_add_fusion.1.place_ref, bf16[2304,1024]{1,0:T(8,128)(2,1)} %constant_dynamic-update-slice_fusion.refs_0_, bf16[2304,1024]{1,0:T(8,128)(2,1)} %collective-permute-done.5.refs_1_, ...), custom_call_target="tpu_custom_call" | custom-call | bytes 37748736 | tf_op jit(solution)/shard_map/join_weights/pallas_call | solution.py:989
  260.9 9.8 %multiply_convert_fusion.1 = (bf16[256,4096]{1,0:T(8,128)(2,1)}, f32[256,4096]{1,0:T(8,128)}) fusion(bf16[256,1024]{1,0:T(8,128)(2,1)S(1)} %multiply_convert_fusion.5.far_own.own_own, bf16[1024,4096]{1,0:T(8,128)(2,1)} %get-tuple-element.50), kind=kOutput, calls=%fused_computation.29 | convolution fusion | flops 2156920832 | bytes 15204352 | tf_op jit(solution)/shard_map/dot_general | solution.py:30
  271.1 3.3 collective-permute-done.17.refs_3_
  274.4 3.9 fusion.26
  283.0 10.0 %convolution_convert_fusion = bf16[768,3072]{1,0:T(8,128)(2,1)} fusion(bf16[768,1024]{1,0:T(8,128)(2,1)S(1)} %multiply_convert_fusion.4.far_own.own_own, bf16[1024,3072]{1,0:T(8,128)(2,1)} %get-tuple-element.55), kind=kOutput, calls=%fused_computation.13 | convolution fusion | flops 4834197504 | bytes 12582912 | tf_op jit(solution)/shard_map/dot_general | solution.py:30
  293.0 6.0 codec_attend.1
  299.0 13.4 %join_weights.7 = (bf16[1024,4096]{1,0:T(8,128)(2,1)}, bf16[4096,1024]{1,0:T(8,128)(2,1)}, bf16[1024,1024]{1,0:T(8,128)(2,1)S(1)}) custom-call(s32[2]{0:T(128)S(1)} %pad_add_fusion.1.place_ref, bf16[2304,1024]{1,0:T(8,128)(2,1)} %constant_dynamic-update-slice_fusion.2.refs_0_, bf16[2304,1024]{1,0:T(8,128)(2,1)} %collective-permute-done.15.refs_1_, ...), custom_call_target="tpu_custom_call" | custom-call | bytes 37748736 | tf_op jit(solution)/shard_map/join_weights/pallas_call | solution.py:989
  316.9 9.2 fusion.56
  326.4 22.9 %fusion.6 = (bf16[768,4096]{1,0:T(8,128)(2,1)}, bf16[768,4096]{1,0:T(8,128)(2,1)}) fusion(f32[768,4096]{1,0:T(8,128)} %fusion.56, bf16[768,1024]{1,0:T(8,128)(2,1)S(1)} %multiply_convert_fusion.3.far_own.own_own, bf16[1024,4096]{1,0:T(8,128)(2,1)} %get-tuple-element.59), kind=kOutput, calls=%fused_computation.9 | convolution fusion | flops 6511656960 | bytes 35127296 | tf_op jit(solution)/shard_map/dot_general | solution.py:30
  349.3 12.8 %multiply_reduce_fusion = (f32[1024]{0:T(1024)S(1)}, f32[768]{0:T(1024)S(1)}, f32[768,1024]{1,0:T(8,128)}) fusion(f32[768,1024]{1,0:T(8,128)S(1)} %get-tuple-element.131, f32[768]{0:T(1024)S(1)} %fusion.44, f32[1024]{0:T(1024)S(1)} %bitcast.266, bf16[768,4096]{1,0:T(8,128)(2,1)} %get-tuple-element.104.latter_own, bf16[1024,4096]{1,0:T(8,128)(2,1)} %get-tuple-element.59), kind=kOutput, calls=%fused_computation.43 | convolution fusion | flops 6447167488 | bytes 20985856 | tf_op jit(solution)/shard_map/dot_general | solution.py:38
  362.2 4.8 fusion.49
  367.0 3.2 convolution_convert_fusion.2
  370.2 8.6 codec_attend_grads.1
  378.8 9.2 multiply_reduce_fusion.1
  392.7 11.7 %fusion.13.latter_own = bf16[256,4096]{1,0:T(8,128)(2,1)S(1)} fusion(f32[256,4096]{1,0:T(8,128)} %get-tuple-element.129, bf16[256,1024]{1,0:T(8,128)(2,1)S(1)} %reduce_sum.125.latter_own, bf16[4096,1024]{1,0:T(8,128)(2,1)} %get-tuple-element.51), kind=kOutput, calls=%fused_computation.22 | convolution fusion | flops 2168455168 | bytes 15204352 | tf_op jit(solution)/shard_map/dot_general | solution.py:38
  404.5 7.0 multiply_reduce_fusion.5
  415.2 4.6 all-to-all-start.2
  428.6 6.4 all-to-all-done.2.grad_ref
  437.7 14.7 %frame_attend_grads.1 = bf16[8,2,128,384]{3,2,1,0:T(8,128)(2,1)S(1)} custom-call(bf16[8,2,128,384]{3,2,1,0:T(8,128)(2,1)S(1)} %copy-done.5, bf16[8,2,128,128]{3,2,1,0:T(8,128)(2,1)} %all-to-all-done.2.grad_ref, s32[2,1024,1]{2,1,0:T(8,128)S(1)} %copy-done.15, s32[2,1,1024]{2,1,0:T(1,128)S(1)} %copy-done.23), custom_call_target="tpu_custom_call" | custom-call | flops 3221225472 | bytes 3932160 | tf_op jit(solution)/shard_map/frame_attend_grads/pallas_call | solution.py:480
  453.6 4.5 all-to-all-start.3
  466.1 8.3 grad_rows.10
  474.4 7.2 grad_columns.2
  482.1 12.6 %all-to-all-done.3 = bf16[8,2,128,384]{3,2,1,0:T(8,128)(2,1)} async-done(((bf16[8,2,128,384]{3,2,1,0:T(8,128)(2,1)}), bf16[8,2,128,384]{3,2,1,0:T(8,128)(2,1)}, u32[]{:S(2)}, u32[]{:S(2)}) %all-to-all-start.3) | async-done | bytes 1572896 | tf_op jit(solution)/shard_map/all_to_all | solution.py:1323
  500.1 3.7 reshape.370.latter_own
  503.9 6.4 multiply_reduce_fusion.6
  511.7 3.2 collective-permute-done.38.latter_rec
  515.2 7.8 grad_rows.8
  522.9 3.8 grad_rows.9
  527.1 47.3 %collective-permute-done.47 = bf16[2,4,8,256,128]{4,3,2,1,0:T(8,128)(2,1)} collective-permute-done((bf16[2,4,8,256,128]{4,3,2,1,0:T(8,128)(2,1)}, bf16[2,4,8,256,128]{4,3,2,1,0:T(8,128)(2,1)}, u32[]{:S(2)}, u32[]{:S(2)}) %collective-permute-start.47) | collective-permute-done | bytes 4194336 | tf_op jit(solution)/shard_map/ppermute | solution.py:46
  576.4 13.0 %grad_rows.6 = (bf16[2,4,6,256,128]{4,3,2,1,0:T(8,128)(2,1)}, bf16[2,4,6,256,128]{4,3,2,1,0:T(8,128)(2,1)}) custom-call(s32[11]{0:T(128)S(1)} %stack.89.order_ref, bf16[768,1024]{1,0:T(8,128)(2,1)S(1)} %copy-done.11, bf16[768,1024]{1,0:T(8,128)(2,1)} %collective-permute-done.24.far_rec.own_rec, bf16[768,1024]{1,0:T(8,128)(2,1)S(1)} %copy-done.11, ...), custom_call_target="tpu_custom_call" | custom-call | flops 4831838208 | bytes 15728640 | tf_op jit(solution)/shard_map/grad_rows/pallas_call | solution.py:731
  589.4 5.8 grad_rows.7
  595.2 6.3 grad_table.1
  601.5 3.1 fusion.20
  605.3 12.9 %grad_rows.11 = (bf16[2,4,8,256,128]{4,3,2,1,0:T(8,128)(2,1)}, bf16[2,4,8,256,128]{4,3,2,1,0:T(8,128)(2,1)}) custom-call(s32[11]{0:T(128)S(1)} %stack.89.order_ref, bf16[768,1024]{1,0:T(8,128)(2,1)S(1)} %copy-done.9, bf16[768,1024]{1,0:T(8,128)(2,1)S(1)} %collective-permute-done.53.far_rec.own_rec, bf16[768,1024]{1,0:T(8,128)(2,1)S(1)} %copy-done.9, ...), custom_call_target="tpu_custom_call" | custom-call | flops 6442450944 | bytes 18874368 | tf_op jit(solution)/shard_map/grad_rows/pallas_call | solution.py:731
  620.2 12.0 %grad_columns.3 = (bf16[2,4,8,256,128]{4,3,2,1,0:T(8,128)(2,1)}, bf16[2,4,8,256,128]{4,3,2,1,0:T(8,128)(2,1)}) custom-call(s32[11]{0:T(128)S(1)} %stack.89.order_ref, bf16[768,1024]{1,0:T(8,128)(2,1)S(1)} %copy-done.1, bf16[768,1024]{1,0:T(8,128)(2,1)S(1)} %collective-permute-done.51.latter_rec, ...), custom_call_target="tpu_custom_call", output_to_operand_aliasing={{0}: (5, {}), {1}: (6, {})} | custom-call | flops 6442450944 | bytes 15728640 | tf_op jit(solution)/shard_map/grad_columns/pallas_call | solution.py:731
  636.1 11.2 %convolution_add_fusion = f32[768,1024]{1,0:T(8,128)S(1)} fusion(f32[768,1024]{1,0:T(8,128)S(1)} %copy-done.37, bf16[768,4096]{1,0:T(8,128)(2,1)} %get-tuple-element.105.former_own, bf16[4096,1024]{1,0:T(8,128)(2,1)} %get-tuple-element.60), kind=kOutput, calls=%fused_computation.62 | convolution fusion | flops 6443237376 | bytes 20971520 | tf_op jit(solution)/shard_map/dot_general | solution.py:30
  649.2 85.1 %collective-permute-done.32 = f32[4,1024]{1,0:T(4,128)S(1)} collective-permute-done((f32[4,1024]{1,0:T(4,128)S(1)}, f32[4,1024]{1,0:T(4,128)S(1)}, u32[]{:S(2)}, u32[]{:S(2)}) %collective-permute-start.32) | collective-permute-done | bytes 16416 | tf_op jit(solution)/shard_map/ppermute | solution.py:46
  740.8 4.7 collective-permute-done.40
  753.3 3.2 fusion.15
  757.7 36.3 %collective-permute-done.41 = bf16[2,4,256,128]{3,2,1,0:T(8,128)(2,1)S(1)} collective-permute-done((bf16[2,4,256,128]{3,2,1,0:T(8,128)(2,1)S(1)}, bf16[2,4,256,128]{3,2,1,0:T(8,128)(2,1)S(1)}, u32[]{:S(2)}, u32[]{:S(2)}) %collective-permute-start.41) | collective-permute-done | bytes 524320 | tf_op jit(solution)/shard_map/ppermute | solution.py:46
  800.6 20.4 %collective-permute-done.42 = bf16[4,256,128]{2,1,0:T(8,128)(2,1)S(1)} collective-permute-done((bf16[4,256,128]{2,1,0:T(8,128)(2,1)S(1)}, bf16[4,256,128]{2,1,0:T(8,128)(2,1)S(1)}, u32[]{:S(2)}, u32[]{:S(2)}) %collective-permute-start.42) | collective-permute-done | bytes 262176 | tf_op jit(solution)/shard_map/ppermute | solution.py:46
  830.7 3.8 collective-permute-start.28
  834.4 9.9 %collective-permute-done.56 = bf16[4,8,256,128]{3,2,1,0:T(8,128)(2,1)} collective-permute-done((bf16[4,8,256,128]{3,2,1,0:T(8,128)(2,1)}, bf16[4,8,256,128]{3,2,1,0:T(8,128)(2,1)}, u32[]{:S(2)}, u32[]{:S(2)}) %collective-permute-start.56) | collective-permute-done | bytes 2097184 | tf_op jit(solution)/shard_map/ppermute | solution.py:46
  848.0 3.4 collective-permute-start.57
  855.5 36.9 %collective-permute-done.28 = bf16[2,6,256,128]{3,2,1,0:T(8,128)(2,1)} collective-permute-done((bf16[2,6,256,128]{3,2,1,0:T(8,128)(2,1)}, bf16[2,6,256,128]{3,2,1,0:T(8,128)(2,1)}, u32[]{:S(2)}, u32[]{:S(2)}) %collective-permute-start.28) | collective-permute-done | bytes 786464 | tf_op jit(solution)/shard_map/ppermute | solution.py:46
  894.2 20.1 %collective-permute-done.57 = bf16[2,8,256,128]{3,2,1,0:T(8,128)(2,1)} collective-permute-done((bf16[2,8,256,128]{3,2,1,0:T(8,128)(2,1)}, bf16[2,8,256,128]{3,2,1,0:T(8,128)(2,1)}, u32[]{:S(2)}, u32[]{:S(2)}) %collective-permute-start.57) | collective-permute-done | bytes 1048608 | tf_op jit(solution)/shard_map/ppermute | solution.py:46
  917.9 4.6 collective-permute-done.29
  926.8 6.9 collective-permute-done.58
  (395 shorter events, 168.8 us)
Async XLA Ops:
  2.4 20.7 %collective-permute-start.1 = (bf16[384,1024]{1,0:T(8,128)(2,1)S(1)}, bf16[384,1024]{1,0:T(8,128)(2,1)}, u32[]{:S(2)}, u32[]{:S(2)}) collective-permute-start(bf16[384,1024]{1,0:T(8,128)(2,1)S(1)} %constant_dynamic-slice_fusion.3), channel_id=1, source_target_pairs={{0,2},{1,3},{2,0},{3,1},{4,6},{5,7},{6,4},{7,5},{8,10},{9,11},{10,... | collective-permute-start | bytes 2359304 | tf_op jit(solution)/shard_map/ppermute | solution.py:46
  23.0 56.4 %collective-permute-start.6 = (bf16[1152,1024]{1,0:T(8,128)(2,1)}, bf16[1152,1024]{1,0:T(8,128)(2,1)}, u32[]{:S(2)}, u32[]{:S(2)}) collective-permute-start(bf16[1152,1024]{1,0:T(8,128)(2,1)} %constant_dynamic-slice_fusion.2), channel_id=1, source_target_pairs={{0,2},{1,3},{2,0},{3,1},{4,6},{5,7},{6,4},{7,5},{8,10},{9,11},{10,... | collective-permute-start | bytes 7077896 | tf_op jit(solution)/shard_map/ppermute | solution.py:46
  24.8 56.4 %collective-permute-start = (bf16[768,1024]{1,0:T(8,128)(2,1)S(1)}, bf16[768,1024]{1,0:T(8,128)(2,1)}, u32[]{:S(2)}, u32[]{:S(2)}) collective-permute-start(bf16[768,1024]{1,0:T(8,128)(2,1)S(1)} %pad_maximum_fusion.2.refs_0_), channel_id=1, source_target_pairs={{0,1},{1,0},{2,3},{3,2},{4,5},{5,4},{6,7},{7,6},{8,9},{9,8},{10,11... | collective-permute-start | bytes 4718600 | tf_op jit(solution)/shard_map/ppermute | solution.py:46
  26.7 52.5 %collective-permute-start.2 = (bf16[384,1024]{1,0:T(8,128)(2,1)}, bf16[384,1024]{1,0:T(8,128)(2,1)}, u32[]{:S(2)}, u32[]{:S(2)}) collective-permute-start(bf16[384,1024]{1,0:T(8,128)(2,1)} %collective-permute-done.1.refs_2_), channel_id=1, source_target_pairs={{0,4},{4,0},{8,12},{12,8},{16,20},{20,16},{24,28},{28,24},{1,5},{5... | collective-permute-start | bytes 2359304 | tf_op jit(solution)/shard_map/ppermute | solution.py:46
  30.8 51.9 %collective-permute-start.3 = (bf16[384,1024]{1,0:T(8,128)(2,1)}, bf16[384,1024]{1,0:T(8,128)(2,1)}, u32[]{:S(2)}, u32[]{:S(2)}) collective-permute-start(bf16[384,1024]{1,0:T(8,128)(2,1)} %collective-permute-done.1.refs_2_), channel_id=1, source_target_pairs={{0,1},{1,0},{2,3},{3,2},{4,5},{5,4},{6,7},{7,6},{8,9},{9,8},{10,11... | collective-permute-start | bytes 2359304 | tf_op jit(solution)/shard_map/ppermute | solution.py:46
  79.1 4.1 collective-permute-start.4
  79.5 31.1 %collective-permute-start.11 = (bf16[640,1024]{1,0:T(8,128)(2,1)}, bf16[640,1024]{1,0:T(8,128)(2,1)S(1)}, u32[]{:S(2)}, u32[]{:S(2)}) collective-permute-start(bf16[640,1024]{1,0:T(8,128)(2,1)} %constant_dynamic-slice_fusion.1), channel_id=1, source_target_pairs={{0,2},{1,3},{2,0},{3,1},{4,6},{5,7},{6,4},{7,5},{8,10},{9,11},{10,... | collective-permute-start | bytes 3932168 | tf_op jit(solution)/shard_map/ppermute | solution.py:46
  81.1 67.2 %collective-permute-start.10 = (bf16[1280,1024]{1,0:T(8,128)(2,1)}, bf16[1280,1024]{1,0:T(8,128)(2,1)}, u32[]{:S(2)}, u32[]{:S(2)}) collective-permute-start(bf16[1280,1024]{1,0:T(8,128)(2,1)} %pad_maximum_fusion.1.refs_0_), channel_id=1, source_target_pairs={{0,1},{1,0},{2,3},{3,2},{4,5},{5,4},{6,7},{7,6},{8,9},{9,8},{10,11... | collective-permute-start | bytes 7864328 | tf_op jit(solution)/shard_map/ppermute | solution.py:46
  81.2 67.1 %collective-permute-start.7 = (bf16[1152,1024]{1,0:T(8,128)(2,1)}, bf16[1152,1024]{1,0:T(8,128)(2,1)}, u32[]{:S(2)}, u32[]{:S(2)}) collective-permute-start(bf16[1152,1024]{1,0:T(8,128)(2,1)} %collective-permute-done.6.refs_2_), channel_id=1, source_target_pairs={{0,4},{4,0},{8,12},{12,8},{16,20},{20,16},{24,28},{28,24},{1,5},{5... | collective-permute-start | bytes 7077896 | tf_op jit(solution)/shard_map/ppermute | solution.py:46
  82.8 163.3 %collective-permute-start.5 = (bf16[2304,1024]{1,0:T(8,128)(2,1)}, bf16[2304,1024]{1,0:T(8,128)(2,1)}, u32[]{:S(2)}, u32[]{:S(2)}) collective-permute-start(bf16[2304,1024]{1,0:T(8,128)(2,1)} %constant_dynamic-update-slice_fusion.refs_0_), channel_id=1, source_target_pairs={{0,1},{1,0},{2,3},{3,2},{4,5},{5,4},{6,7},{7,6},{8,9},{9,8},{10,11... | collective-permute-start | bytes 14155784 | tf_op jit(solution)/shard_map/ppermute | solution.py:46
  98.5 107.1 %all-to-all-start = ((bf16[8,2,128,384]{3,2,1,0:T(8,128)(2,1)}), bf16[8,2,128,384]{3,2,1,0:T(8,128)(2,1)S(1)}, u32[]{:S(2)}, u32[]{:S(2)}) async-start(bf16[8,2,128,384]{3,2,1,0:T(8,128)(2,1)} %copy.51), calls=%async_computation | async-start | bytes 3145728 | tf_op jit(solution)/shard_map/all_to_all | solution.py:1250
  110.6 69.6 %collective-permute-start.12 = (bf16[640,1024]{1,0:T(8,128)(2,1)S(1)}, bf16[640,1024]{1,0:T(8,128)(2,1)}, u32[]{:S(2)}, u32[]{:S(2)}) collective-permute-start(bf16[640,1024]{1,0:T(8,128)(2,1)S(1)} %collective-permute-done.11.refs_2_), channel_id=1, source_target_pairs={{0,4},{4,0},{8,12},{12,8},{16,20},{20,16},{24,28},{28,24},{1,5},{5... | collective-permute-start | bytes 3932168 | tf_op jit(solution)/shard_map/ppermute | solution.py:46
  121.2 98.2 %collective-permute-start.16 = (bf16[1152,1024]{1,0:T(8,128)(2,1)}, bf16[1152,1024]{1,0:T(8,128)(2,1)}, u32[]{:S(2)}, u32[]{:S(2)}) collective-permute-start(bf16[1152,1024]{1,0:T(8,128)(2,1)} %constant_dynamic-slice_fusion), channel_id=1, source_target_pairs={{0,2},{1,3},{2,0},{3,1},{4,6},{5,7},{6,4},{7,5},{8,10},{9,11},{10,... | collective-permute-start | bytes 7077896 | tf_op jit(solution)/shard_map/ppermute | solution.py:46
  148.3 32.5 %collective-permute-start.13 = (bf16[640,1024]{1,0:T(8,128)(2,1)S(1)}, bf16[640,1024]{1,0:T(8,128)(2,1)}, u32[]{:S(2)}, u32[]{:S(2)}) collective-permute-start(bf16[640,1024]{1,0:T(8,128)(2,1)S(1)} %collective-permute-done.11.refs_2_), channel_id=1, source_target_pairs={{0,1},{1,0},{2,3},{3,2},{4,5},{5,4},{6,7},{7,6},{8,9},{9,8},{10,11... | collective-permute-start | bytes 3932168 | tf_op jit(solution)/shard_map/ppermute | solution.py:46
  148.3 98.3 %collective-permute-start.8 = (bf16[1152,1024]{1,0:T(8,128)(2,1)}, bf16[1152,1024]{1,0:T(8,128)(2,1)}, u32[]{:S(2)}, u32[]{:S(2)}) collective-permute-start(bf16[1152,1024]{1,0:T(8,128)(2,1)} %collective-permute-done.6.refs_2_), channel_id=1, source_target_pairs={{0,1},{1,0},{2,3},{3,2},{4,5},{5,4},{6,7},{7,6},{8,9},{9,8},{10,11... | collective-permute-start | bytes 7077896 | tf_op jit(solution)/shard_map/ppermute | solution.py:46
  180.1 66.6 %collective-permute-start.9 = (bf16[1152,1024]{1,0:T(8,128)(2,1)}, bf16[1152,1024]{1,0:T(8,128)(2,1)}, u32[]{:S(2)}, u32[]{:S(2)}) collective-permute-start(bf16[1152,1024]{1,0:T(8,128)(2,1)} %collective-permute-done.7.refs_3_), channel_id=1, source_target_pairs={{0,1},{1,0},{2,3},{3,2},{4,5},{5,4},{6,7},{7,6},{8,9},{9,8},{10,11... | collective-permute-start | bytes 7077896 | tf_op jit(solution)/shard_map/ppermute | solution.py:46
  180.7 51.1 %collective-permute-start.14 = (bf16[640,1024]{1,0:T(8,128)(2,1)}, bf16[640,1024]{1,0:T(8,128)(2,1)}, u32[]{:S(2)}, u32[]{:S(2)}) collective-permute-start(bf16[640,1024]{1,0:T(8,128)(2,1)} %collective-permute-done.12.refs_3_), channel_id=1, source_target_pairs={{0,1},{1,0},{2,3},{3,2},{4,5},{5,4},{6,7},{7,6},{8,9},{9,8},{10,11... | collective-permute-start | bytes 3932168 | tf_op jit(solution)/shard_map/ppermute | solution.py:46
  215.0 15.4 %all-to-all-start.1 = ((bf16[8,2,128,128]{3,2,1,0:T(8,128)(2,1)}), bf16[8,2,128,128]{3,2,1,0:T(8,128)(2,1)}, u32[]{:S(2)}, u32[]{:S(2)}) async-start(bf16[8,2,128,128]{3,2,1,0:T(8,128)(2,1)} %frame_attend.1), calls=%async_computation.1 | async-start | bytes 1048576 | tf_op jit(solution)/shard_map/all_to_all | solution.py:1251
  219.4 55.0 %collective-permute-start.17 = (bf16[1152,1024]{1,0:T(8,128)(2,1)}, bf16[1152,1024]{1,0:T(8,128)(2,1)}, u32[]{:S(2)}, u32[]{:S(2)}) collective-permute-start(bf16[1152,1024]{1,0:T(8,128)(2,1)} %collective-permute-done.16.refs_2_), channel_id=1, source_target_pairs={{0,4},{4,0},{8,12},{12,8},{16,20},{20,16},{24,28},{28,24},{1,5},{5... | collective-permute-start | bytes 7077896 | tf_op jit(solution)/shard_map/ppermute | solution.py:46
  231.8 193.2 %collective-permute-start.37 = (bf16[256,1024]{1,0:T(8,128)(2,1)}, bf16[256,1024]{1,0:T(8,128)(2,1)}, u32[]{:S(2)}, u32[]{:S(2)}) collective-permute-start(bf16[256,1024]{1,0:T(8,128)(2,1)} %copy-done.16), channel_id=1, source_target_pairs={{0,1},{1,0},{2,3},{3,2},{4,5},{5,4},{6,7},{7,6},{8,9},{9,8},{10,11... | collective-permute-start | bytes 1572872 | tf_op jit(solution)/shard_map/ppermute | solution.py:46
  246.1 52.9 %collective-permute-start.15 = (bf16[2304,1024]{1,0:T(8,128)(2,1)}, bf16[2304,1024]{1,0:T(8,128)(2,1)}, u32[]{:S(2)}, u32[]{:S(2)}) collective-permute-start(bf16[2304,1024]{1,0:T(8,128)(2,1)} %constant_dynamic-update-slice_fusion.2.refs_0_), channel_id=1, source_target_pairs={{0,1},{1,0},{2,3},{3,2},{4,5},{5,4},{6,7},{7,6},{8,9},{9,8},{10,11... | collective-permute-start | bytes 14155784 | tf_op jit(solution)/shard_map/ppermute | solution.py:46
  246.6 52.4 %collective-permute-start.18 = (bf16[1152,1024]{1,0:T(8,128)(2,1)}, bf16[1152,1024]{1,0:T(8,128)(2,1)}, u32[]{:S(2)}, u32[]{:S(2)}) collective-permute-start(bf16[1152,1024]{1,0:T(8,128)(2,1)} %collective-permute-done.16.refs_2_), channel_id=1, source_target_pairs={{0,1},{1,0},{2,3},{3,2},{4,5},{5,4},{6,7},{7,6},{8,9},{9,8},{10,11... | collective-permute-start | bytes 7077896 | tf_op jit(solution)/shard_map/ppermute | solution.py:46
  270.7 188.1 %collective-permute-start.44 = (bf16[256,4096]{1,0:T(8,128)(2,1)}, bf16[256,4096]{1,0:T(8,128)(2,1)}, u32[]{:S(2)}, u32[]{:S(2)}) collective-permute-start(bf16[256,4096]{1,0:T(8,128)(2,1)} %get-tuple-element.128.former_own), channel_id=1, source_target_pairs={{0,1},{1,0},{2,3},{3,2},{4,5},{5,4},{6,7},{7,6},{8,9},{9,8},{10,11... | collective-permute-start | bytes 6291464 | tf_op jit(solution)/shard_map/ppermute | solution.py:46
  274.4 24.6 %collective-permute-start.19 = (bf16[1152,1024]{1,0:T(8,128)(2,1)}, bf16[1152,1024]{1,0:T(8,128)(2,1)}, u32[]{:S(2)}, u32[]{:S(2)}) collective-permute-start(bf16[1152,1024]{1,0:T(8,128)(2,1)} %collective-permute-done.17.refs_3_), channel_id=1, source_target_pairs={{0,1},{1,0},{2,3},{3,2},{4,5},{5,4},{6,7},{7,6},{8,9},{9,8},{10,11... | collective-permute-start | bytes 7077896 | tf_op jit(solution)/shard_map/ppermute | solution.py:46
  415.2 19.8 %all-to-all-start.2 = ((bf16[8,2,128,128]{3,2,1,0:T(8,128)(2,1)}), bf16[8,2,128,128]{3,2,1,0:T(8,128)(2,1)}, u32[]{:S(2)}, u32[]{:S(2)}) async-start(bf16[8,2,128,128]{3,2,1,0:T(8,128)(2,1)} %bitcast.221), calls=%async_computation.2 | async-start | bytes 1048576 | tf_op jit(solution)/shard_map/all_to_all | solution.py:1311
  419.8 43.2 %collective-permute-start.46 = (bf16[256,4096]{1,0:T(8,128)(2,1)}, bf16[256,4096]{1,0:T(8,128)(2,1)}, u32[]{:S(2)}, u32[]{:S(2)}) collective-permute-start(bf16[256,4096]{1,0:T(8,128)(2,1)} %copy-done.24), channel_id=1, source_target_pairs={{0,1},{1,0},{2,3},{3,2},{4,5},{5,4},{6,7},{7,6},{8,9},{9,8},{10,11... | collective-permute-start | bytes 6291464 | tf_op jit(solution)/shard_map/ppermute | solution.py:46
  420.0 38.2 %collective-permute-start.22 = (bf16[768,1024]{1,0:T(8,128)(2,1)S(1)}, bf16[768,1024]{1,0:T(8,128)(2,1)}, u32[]{:S(2)}, u32[]{:S(2)}) collective-permute-start(bf16[768,1024]{1,0:T(8,128)(2,1)S(1)} %bitcast.223), channel_id=1, source_target_pairs={{0,1},{1,0},{2,3},{3,2},{4,5},{5,4},{6,7},{7,6},{8,9},{9,8},{10,11... | collective-permute-start | bytes 4718600 | tf_op jit(solution)/shard_map/ppermute | solution.py:46
  420.4 4.4 collective-permute-start.20
  424.8 2.9 collective-permute-start.35
  425.0 33.7 %collective-permute-start.24 = (bf16[768,1024]{1,0:T(8,128)(2,1)}, bf16[768,1024]{1,0:T(8,128)(2,1)}, u32[]{:S(2)}, u32[]{:S(2)}) collective-permute-start(bf16[768,1024]{1,0:T(8,128)(2,1)} %copy-done.10), channel_id=1, source_target_pairs={{0,1},{1,0},{2,3},{3,2},{4,5},{5,4},{6,7},{7,6},{8,9},{9,8},{10,11... | collective-permute-start | bytes 4718600 | tf_op jit(solution)/shard_map/ppermute | solution.py:46
  428.5 29.6 %collective-permute-start.45 = (bf16[256,1024]{1,0:T(8,128)(2,1)}, bf16[256,1024]{1,0:T(8,128)(2,1)}, u32[]{:S(2)}, u32[]{:S(2)}) collective-permute-start(bf16[256,1024]{1,0:T(8,128)(2,1)} %copy-done.18), channel_id=1, source_target_pairs={{0,1},{1,0},{2,3},{3,2},{4,5},{5,4},{6,7},{7,6},{8,9},{9,8},{10,11... | collective-permute-start | bytes 1572872 | tf_op jit(solution)/shard_map/ppermute | solution.py:46
  453.6 41.1 %all-to-all-start.3 = ((bf16[8,2,128,384]{3,2,1,0:T(8,128)(2,1)}), bf16[8,2,128,384]{3,2,1,0:T(8,128)(2,1)}, u32[]{:S(2)}, u32[]{:S(2)}) async-start(bf16[8,2,128,384]{3,2,1,0:T(8,128)(2,1)} %copy-done.6), calls=%async_computation.3 | async-start | bytes 3145728 | tf_op jit(solution)/shard_map/all_to_all | solution.py:1323
  458.1 3.9 collective-permute-start.43
  458.2 147.1 %collective-permute-start.54 = (bf16[768,4096]{1,0:T(8,128)(2,1)}, bf16[768,4096]{1,0:T(8,128)(2,1)}, u32[]{:S(2)}, u32[]{:S(2)}) collective-permute-start(bf16[768,4096]{1,0:T(8,128)(2,1)} %get-tuple-element.104.latter_own), channel_id=1, source_target_pairs={{0,1},{1,0},{2,3},{3,2},{4,5},{5,4},{6,7},{7,6},{8,9},{9,8},{10,11... | collective-permute-start | bytes 18874376 | tf_op jit(solution)/shard_map/ppermute | solution.py:46
  458.7 68.1 %collective-permute-start.25 = (bf16[768,3072]{1,0:T(8,128)(2,1)}, bf16[768,3072]{1,0:T(8,128)(2,1)}, u32[]{:S(2)}, u32[]{:S(2)}) collective-permute-start(bf16[768,3072]{1,0:T(8,128)(2,1)} %bitcast.239), channel_id=1, source_target_pairs={{0,1},{1,0},{2,3},{3,2},{4,5},{5,4},{6,7},{7,6},{8,9},{9,8},{10,11... | collective-permute-start | bytes 14155784 | tf_op jit(solution)/shard_map/ppermute | solution.py:46
  458.8 22.8 %collective-permute-start.36 = (bf16[256,1024]{1,0:T(8,128)(2,1)S(1)}, bf16[256,1024]{1,0:T(8,128)(2,1)}, u32[]{:S(2)}, u32[]{:S(2)}) collective-permute-start(bf16[256,1024]{1,0:T(8,128)(2,1)S(1)} %fusion.48.latter_own), channel_id=1, source_target_pairs={{0,1},{1,0},{2,3},{3,2},{4,5},{5,4},{6,7},{7,6},{8,9},{9,8},{10,11... | collective-permute-start | bytes 1572872 | tf_op jit(solution)/shard_map/ppermute | solution.py:46
  462.8 19.3 %collective-permute-start.21 = (bf16[512,1024]{1,0:T(8,128)(2,1)}, bf16[512,1024]{1,0:T(8,128)(2,1)}, u32[]{:S(2)}, u32[]{:S(2)}) collective-permute-start(bf16[512,1024]{1,0:T(8,128)(2,1)} %slice.371.latter_own), channel_id=1, source_target_pairs={{0,1},{1,0},{2,3},{3,2},{4,5},{5,4},{6,7},{7,6},{8,9},{9,8},{10,11... | collective-permute-start | bytes 3145736 | tf_op jit(solution)/shard_map/ppermute | solution.py:46
  463.0 157.2 %collective-permute-start.52 = (bf16[768,4096]{1,0:T(8,128)(2,1)}, bf16[768,4096]{1,0:T(8,128)(2,1)}, u32[]{:S(2)}, u32[]{:S(2)}) collective-permute-start(bf16[768,4096]{1,0:T(8,128)(2,1)} %get-tuple-element.105.former_own), channel_id=1, source_target_pairs={{0,1},{1,0},{2,3},{3,2},{4,5},{5,4},{6,7},{7,6},{8,9},{9,8},{10,11... | collective-permute-start | bytes 18874376 | tf_op jit(solution)/shard_map/ppermute | solution.py:46
  481.6 92.9 %collective-permute-start.47 = (bf16[2,4,8,256,128]{4,3,2,1,0:T(8,128)(2,1)}, bf16[2,4,8,256,128]{4,3,2,1,0:T(8,128)(2,1)}, u32[]{:S(2)}, u32[]{:S(2)}) collective-permute-start(bf16[2,4,8,256,128]{4,3,2,1,0:T(8,128)(2,1)} %get-tuple-element.74), channel_id=1, source_target_pairs={{0,2},{1,3},{2,0},{3,1},{4,6},{5,7},{6,4},{7,5},{8,10},{9,11},{10,... | collective-permute-start | bytes 12582920 | tf_op jit(solution)/shard_map/ppermute | solution.py:46
  482.1 28.2 %collective-permute-start.23 = (bf16[768,1024]{1,0:T(8,128)(2,1)}, bf16[768,1024]{1,0:T(8,128)(2,1)}, u32[]{:S(2)}, u32[]{:S(2)}) collective-permute-start(bf16[768,1024]{1,0:T(8,128)(2,1)} %get-tuple-element.102.latter_own), channel_id=1, source_target_pairs={{0,1},{1,0},{2,3},{3,2},{4,5},{5,4},{6,7},{7,6},{8,9},{9,8},{10,11... | collective-permute-start | bytes 4718600 | tf_op jit(solution)/shard_map/ppermute | solution.py:46
  510.3 1.2 collective-permute-start.30
  511.5 3.4 collective-permute-start.38
  515.0 89.7 %collective-permute-start.53 = (bf16[768,1024]{1,0:T(8,128)(2,1)S(1)}, bf16[768,1024]{1,0:T(8,128)(2,1)S(1)}, u32[]{:S(2)}, u32[]{:S(2)}) collective-permute-start(bf16[768,1024]{1,0:T(8,128)(2,1)S(1)} %copy-done.9), channel_id=1, source_target_pairs={{0,1},{1,0},{2,3},{3,2},{4,5},{5,4},{6,7},{7,6},{8,9},{9,8},{10,11... | collective-permute-start | bytes 4718600 | tf_op jit(solution)/shard_map/ppermute | solution.py:46
  526.8 91.4 %collective-permute-start.51 = (bf16[768,1024]{1,0:T(8,128)(2,1)S(1)}, bf16[768,1024]{1,0:T(8,128)(2,1)S(1)}, u32[]{:S(2)}, u32[]{:S(2)}) collective-permute-start(bf16[768,1024]{1,0:T(8,128)(2,1)S(1)} %copy-done.1), channel_id=1, source_target_pairs={{0,1},{1,0},{2,3},{3,2},{4,5},{5,4},{6,7},{7,6},{8,9},{9,8},{10,11... | collective-permute-start | bytes 4718600 | tf_op jit(solution)/shard_map/ppermute | solution.py:46
  574.5 59.3 %collective-permute-start.39 = (bf16[2,4,4,256,128]{4,3,2,1,0:T(8,128)(2,1)}, bf16[2,4,4,256,128]{4,3,2,1,0:T(8,128)(2,1)}, u32[]{:S(2)}, u32[]{:S(2)}) collective-permute-start(bf16[2,4,4,256,128]{4,3,2,1,0:T(8,128)(2,1)} %get-tuple-element.70), channel_id=1, source_target_pairs={{0,4},{4,0},{8,12},{12,8},{16,20},{20,16},{24,28},{28,24},{1,5},{5... | collective-permute-start | bytes 6291464 | tf_op jit(solution)/shard_map/ppermute | solution.py:46
  604.7 42.6 %collective-permute-start.31 = (f32[4,1024]{1,0:T(4,128)S(1)}, f32[4,1024]{1,0:T(4,128)S(1)}, u32[]{:S(2)}, u32[]{:S(2)}) collective-permute-start(f32[4,1024]{1,0:T(4,128)S(1)} %fusion.47), channel_id=1, source_target_pairs={{0,2},{1,3},{2,0},{3,1},{4,6},{5,7},{6,4},{7,5},{8,10},{9,11},{10,... | collective-permute-start | bytes 49160 | tf_op jit(solution)/shard_map/ppermute | solution.py:46
  605.2 144.4 %collective-permute-start.26 = (bf16[2,4,6,256,128]{4,3,2,1,0:T(8,128)(2,1)}, bf16[2,4,6,256,128]{4,3,2,1,0:T(8,128)(2,1)S(1)}, u32[]{:S(2)}, u32[]{:S(2)}) collective-permute-start(bf16[2,4,6,256,128]{4,3,2,1,0:T(8,128)(2,1)} %get-tuple-element.66), channel_id=1, source_target_pairs={{0,4},{4,0},{8,12},{12,8},{16,20},{20,16},{24,28},{28,24},{1,5},{5... | collective-permute-start | bytes 9437192 | tf_op jit(solution)/shard_map/ppermute | solution.py:46
  618.2 135.1 %collective-permute-start.48 = (bf16[4,8,256,128]{3,2,1,0:T(8,128)(2,1)S(1)}, bf16[4,8,256,128]{3,2,1,0:T(8,128)(2,1)}, u32[]{:S(2)}, u32[]{:S(2)}) collective-permute-start(bf16[4,8,256,128]{3,2,1,0:T(8,128)(2,1)S(1)} %fusion.20), channel_id=1, source_target_pairs={{0,4},{4,0},{8,12},{12,8},{16,20},{20,16},{24,28},{28,24},{1,5},{5... | collective-permute-start | bytes 6291464 | tf_op jit(solution)/shard_map/ppermute | solution.py:46
  632.2 162.0 %collective-permute-start.55 = (bf16[2,4,8,256,128]{4,3,2,1,0:T(8,128)(2,1)}, bf16[2,4,8,256,128]{4,3,2,1,0:T(8,128)(2,1)S(1)}, u32[]{:S(2)}, u32[]{:S(2)}) collective-permute-start(bf16[2,4,8,256,128]{4,3,2,1,0:T(8,128)(2,1)} %get-tuple-element.78), channel_id=1, source_target_pairs={{0,2},{1,3},{2,0},{3,1},{4,6},{5,7},{6,4},{7,5},{8,10},{9,11},{10,... | collective-permute-start | bytes 12582920 | tf_op jit(solution)/shard_map/ppermute | solution.py:46
  635.3 110.3 %collective-permute-start.40 = (bf16[4,4,256,128]{3,2,1,0:T(8,128)(2,1)S(1)}, bf16[4,4,256,128]{3,2,1,0:T(8,128)(2,1)S(1)}, u32[]{:S(2)}, u32[]{:S(2)}) collective-permute-start(bf16[4,4,256,128]{3,2,1,0:T(8,128)(2,1)S(1)} %fusion.30), channel_id=1, source_target_pairs={{0,2},{1,3},{2,0},{3,1},{4,6},{5,7},{6,4},{7,5},{8,10},{9,11},{10,... | collective-permute-start | bytes 3145736 | tf_op jit(solution)/shard_map/ppermute | solution.py:46
  647.3 87.0 %collective-permute-start.32 = (f32[4,1024]{1,0:T(4,128)S(1)}, f32[4,1024]{1,0:T(4,128)S(1)}, u32[]{:S(2)}, u32[]{:S(2)}) collective-permute-start(f32[4,1024]{1,0:T(4,128)S(1)} %fusion.88), channel_id=1, source_target_pairs={{0,4},{4,0},{8,12},{12,8},{16,20},{20,16},{24,28},{28,24},{1,5},{5... | collective-permute-start | bytes 49160 | tf_op jit(solution)/shard_map/ppermute | solution.py:46
  649.2 100.5 %copy-start.31 = (bf16[2,4,6,256,128]{4,3,2,1,0:T(8,128)(2,1)S(1)}, bf16[2,4,6,256,128]{4,3,2,1,0:T(8,128)(2,1)}, u32[]{:S(2)}) copy-start(bf16[2,4,6,256,128]{4,3,2,1,0:T(8,128)(2,1)} %get-tuple-element.65) | copy-start | bytes 9437188
  734.4 3.7 collective-permute-start.33
  738.1 61.9 %collective-permute-start.34 = (f32[4,1024]{1,0:T(4,128)S(1)}, f32[4,1024]{1,0:T(4,128)S(1)}, u32[]{:S(2)}, u32[]{:S(2)}) collective-permute-start(f32[4,1024]{1,0:T(4,128)S(1)} %add.282), channel_id=1, source_target_pairs={{0,16},{4,20},{8,24},{12,28},{16,0},{20,4},{24,8},{28,12},{1,17},{... | collective-permute-start | bytes 49160 | tf_op jit(solution)/shard_map/ppermute | solution.py:46
  747.2 46.8 %collective-permute-start.41 = (bf16[2,4,256,128]{3,2,1,0:T(8,128)(2,1)S(1)}, bf16[2,4,256,128]{3,2,1,0:T(8,128)(2,1)S(1)}, u32[]{:S(2)}, u32[]{:S(2)}) collective-permute-start(bf16[2,4,256,128]{3,2,1,0:T(8,128)(2,1)S(1)} %slice.282), channel_id=1, source_target_pairs={{0,16},{4,20},{8,24},{12,28},{16,0},{20,4},{24,8},{28,12},{1,17},{... | collective-permute-start | bytes 1572872 | tf_op jit(solution)/shard_map/ppermute | solution.py:46
  751.7 75.0 %collective-permute-start.27 = (bf16[4,6,256,128]{3,2,1,0:T(8,128)(2,1)}, bf16[4,6,256,128]{3,2,1,0:T(8,128)(2,1)}, u32[]{:S(2)}, u32[]{:S(2)}) collective-permute-start(bf16[4,6,256,128]{3,2,1,0:T(8,128)(2,1)} %fusion.23), channel_id=1, source_target_pairs={{0,2},{1,3},{2,0},{3,1},{4,6},{5,7},{6,4},{7,5},{8,10},{9,11},{10,... | collective-permute-start | bytes 4718600 | tf_op jit(solution)/shard_map/ppermute | solution.py:46
  757.6 67.2 %collective-permute-start.49 = (bf16[2,8,256,128]{3,2,1,0:T(8,128)(2,1)}, bf16[2,8,256,128]{3,2,1,0:T(8,128)(2,1)}, u32[]{:S(2)}, u32[]{:S(2)}) collective-permute-start(bf16[2,8,256,128]{3,2,1,0:T(8,128)(2,1)} %slice.291), channel_id=1, source_target_pairs={{0,16},{4,20},{8,24},{12,28},{16,0},{20,4},{24,8},{28,12},{1,17},{... | collective-permute-start | bytes 3145736 | tf_op jit(solution)/shard_map/ppermute | solution.py:46
  794.2 26.9 %collective-permute-start.42 = (bf16[4,256,128]{2,1,0:T(8,128)(2,1)S(1)}, bf16[4,256,128]{2,1,0:T(8,128)(2,1)S(1)}, u32[]{:S(2)}, u32[]{:S(2)}) collective-permute-start(bf16[4,256,128]{2,1,0:T(8,128)(2,1)S(1)} %fusion.40), channel_id=1, source_target_pairs={{0,8},{4,12},{8,0},{12,4},{16,24},{20,28},{24,16},{28,20},{1,9},{5... | collective-permute-start | bytes 786440 | tf_op jit(solution)/shard_map/ppermute | solution.py:46
  797.4 47.0 %collective-permute-start.56 = (bf16[4,8,256,128]{3,2,1,0:T(8,128)(2,1)}, bf16[4,8,256,128]{3,2,1,0:T(8,128)(2,1)}, u32[]{:S(2)}, u32[]{:S(2)}) collective-permute-start(bf16[4,8,256,128]{3,2,1,0:T(8,128)(2,1)} %fusion.21), channel_id=1, source_target_pairs={{0,4},{4,0},{8,12},{12,8},{16,20},{20,16},{24,28},{28,24},{1,5},{5... | collective-permute-start | bytes 6291464 | tf_op jit(solution)/shard_map/ppermute | solution.py:46
  826.7 24.7 %collective-permute-start.50 = (bf16[8,256,128]{2,1,0:T(8,128)(2,1)S(1)}, bf16[8,256,128]{2,1,0:T(8,128)(2,1)S(1)}, u32[]{:S(2)}, u32[]{:S(2)}) collective-permute-start(bf16[8,256,128]{2,1,0:T(8,128)(2,1)S(1)} %fusion.35), channel_id=1, source_target_pairs={{0,8},{4,12},{8,0},{12,4},{16,24},{20,28},{24,16},{28,20},{1,9},{5... | collective-permute-start | bytes 1572872 | tf_op jit(solution)/shard_map/ppermute | solution.py:46
  830.7 61.8 %collective-permute-start.28 = (bf16[2,6,256,128]{3,2,1,0:T(8,128)(2,1)}, bf16[2,6,256,128]{3,2,1,0:T(8,128)(2,1)}, u32[]{:S(2)}, u32[]{:S(2)}) collective-permute-start(bf16[2,6,256,128]{3,2,1,0:T(8,128)(2,1)} %slice.274), channel_id=1, source_target_pairs={{0,16},{4,20},{8,24},{12,28},{16,0},{20,4},{24,8},{28,12},{1,17},{... | collective-permute-start | bytes 2359304 | tf_op jit(solution)/shard_map/ppermute | solution.py:46
  848.0 66.3 %collective-permute-start.57 = (bf16[2,8,256,128]{3,2,1,0:T(8,128)(2,1)}, bf16[2,8,256,128]{3,2,1,0:T(8,128)(2,1)}, u32[]{:S(2)}, u32[]{:S(2)}) collective-permute-start(bf16[2,8,256,128]{3,2,1,0:T(8,128)(2,1)} %slice.303), channel_id=1, source_target_pairs={{0,16},{4,20},{8,24},{12,28},{16,0},{20,4},{24,8},{28,12},{1,17},{... | collective-permute-start | bytes 3145736 | tf_op jit(solution)/shard_map/ppermute | solution.py:46
  894.1 28.4 %collective-permute-start.29 = (bf16[6,256,128]{2,1,0:T(8,128)(2,1)S(1)}, bf16[6,256,128]{2,1,0:T(8,128)(2,1)S(1)}, u32[]{:S(2)}, u32[]{:S(2)}) collective-permute-start(bf16[6,256,128]{2,1,0:T(8,128)(2,1)S(1)} %fusion.39), channel_id=1, source_target_pairs={{0,8},{4,12},{8,0},{12,4},{16,24},{20,28},{24,16},{28,20},{1,9},{5... | collective-permute-start | bytes 1179656 | tf_op jit(solution)/shard_map/ppermute | solution.py:46
  917.9 15.9 %collective-permute-start.58 = (bf16[8,256,128]{2,1,0:T(8,128)(2,1)}, bf16[8,256,128]{2,1,0:T(8,128)(2,1)}, u32[]{:S(2)}, u32[]{:S(2)}) collective-permute-start(bf16[8,256,128]{2,1,0:T(8,128)(2,1)} %fusion.36), channel_id=1, source_target_pairs={{0,8},{4,12},{8,0},{12,4},{16,24},{20,28},{24,16},{28,20},{1,9},{5... | collective-permute-start | bytes 1572872 | tf_op jit(solution)/shard_map/ppermute | solution.py:46
  (83 other events, 1258.5 us)

commit v3 on v2

--- a/solution.py
+++ b/solution.py
@@ -1182,6 +1182,19 @@
     return (values, swap(values, "mp", 1))
 
 
+def hidden_grads(contract_in, expanded, weights):
+    active_grad = inner_right(contract_in, weights[5])
+    expand_in = jax.vjp(jax.nn.gelu, expanded)[1](active_grad)[0].astype(BF)
+    return expand_in, inner_right(expand_in, weights[4])
+
+
+def mixed_grads(result_grad, normed_grad, mixed_sum, weights):
+    mixed_part, postnorm_grad = jax.vjp(rms_scale, mixed_sum, weights[3].astype(F32))[1](normed_grad)
+    mixed_grad = result_grad + mixed_part
+    output_in = mixed_grad.astype(BF)
+    return mixed_grad, inner_right(output_in, weights[2]).astype(BF), postnorm_grad, output_in
+
+
 def shards(
     frames,
     segments,
@@ -1208,8 +1221,12 @@
     frame_total = row_count * frames_dev
     positions = cotangent.shape[2]
 
+    gain_rows = jnp.pad(
+        jnp.concatenate([frame_prenorm, frame_postnorm, codec_prenorm, codec_postnorm])[None],
+        ((0, 31), (0, 0)),
+    )
     packs = (
-        [frame_project],
+        [frame_project, gain_rows],
         [frame_expand, frame_contract, frame_output],
         [codec_project, codebooks],
         [codec_expand, codec_contract, codec_output],
@@ -1222,13 +1239,15 @@
     def joined(at):
         return join_weights(*pieces[at], pack_layout(packs[at])[0], place)
 
-    gains = lax.all_gather(
-        jnp.stack([frame_prenorm, frame_postnorm, codec_prenorm, codec_postnorm]),
-        "mp",
-        axis=1,
+    count = place.seq_count
+    every_segment = lax.all_to_all(
+        jnp.broadcast_to(segments[None], (count, row_count, frames_dev)),
+        "seq",
+        split_axis=0,
+        concat_axis=0,
         tiled=True,
     )
-    every_segment = lax.all_gather(segments, "seq", axis=1, tiled=True)
+    every_segment = jnp.transpose(every_segment, (1, 0, 2)).reshape(row_count, count * frames_dev)
     codes = codec_tokens.reshape(1, (positions - 1) * frame_total) + jnp.repeat(
         jnp.arange(positions - 1, dtype=jnp.int32) * CODES, frame_total
     )
@@ -1239,11 +1258,13 @@
     ).reshape(positions * frame_total, width)
     contract_in = pair(codec_grad.astype(BF))
 
-    (weight_project,) = joined(0)
+    weight_project, gains = joined(0)
+    gains = jnp.transpose(
+        gains.reshape(place.mp_count, 32, 4, -1)[:, 0], (1, 0, 2)
+    ).reshape(4, width)
     hidden = frames.astype(F32).reshape(frame_total, width)
     normed, projected = front_pass(hidden, (gains[0], weight_project))
     normed_both = pair(normed)
-    count = place.seq_count
     packed = jnp.transpose(
         projected.reshape(row_count, frames_dev, 3, count, LANES), (3, 0, 1, 2, 4)
     ).reshape(count, row_count, frames_dev, 3 * LANES)
@@ -1279,13 +1300,15 @@
         (codec_result.reshape(positions, frame_total, width) * live).astype(BF), (1, 0, 2)
     ).reshape(row_count, frames_dev, positions, width)
 
-    mixed_grad, attended_grad, codec_postnorm_grad, _, expand_in, output_in = rear_grads(
-        codec_grad, codec_saved, codec_weights
-    )
+    expand_in, normed_grad = hidden_grads(contract_in[0], codec_saved[2], codec_weights)
+    codec_one = grad_columns(codec_activated_both, contract_in, order, 8, 4)
+    codec_one = grad_rows(codec_normed_two_both, pair(expand_in), order, True, 8, 0, codec_one)
+    normed_grad = tie(normed_grad, *codec_one)
+    mixed_grad, attended_grad, codec_postnorm_grad, output_in = mixed_grads(
+        codec_grad, normed_grad, codec_saved[0], codec_weights
+    )
+    codec_one = reduce_blocks(*codec_one, True)
     output_in = pair(output_in)
-    codec_one = grad_rows(codec_normed_two_both, pair(expand_in), order, True, 8, 0)
-    codec_one = grad_columns(codec_activated_both, contract_in, order, 8, 4, codec_one)
-    codec_one = reduce_blocks(*codec_one, True)
     codec_projected_grad = codec_attend_grads_call(
         codec_packed, attended_grad.reshape(positions, frame_total, width)
     ).reshape(positions * frame_total, 3 * width)
@@ -1297,17 +1320,14 @@
     input_grad = input_grad.reshape(positions, frame_total, width)
     table_in = pair(input_grad[1:].reshape(-1, width).astype(BF))
     codec_two = grad_table(codes_both, table_in, order, codebooks.shape[0], 6, 4, codec_two)
+    base_grad = tie(jnp.sum(input_grad, axis=0).astype(BF), *codec_two).astype(F32)
     codec_two = reduce_blocks(*codec_two, False)
-    base_grad = jnp.sum(input_grad, axis=0).astype(BF).astype(F32)
-
-    (
-        frame_mixed_grad,
-        frame_attended_grad,
-        frame_postnorm_grad,
-        contract_in,
-        expand_in,
-        output_in,
-    ) = rear_grads(base_grad, frame_saved, frame_weights)
+
+    contract_in = pair(base_grad.astype(BF))
+    expand_in, normed_grad = hidden_grads(contract_in[0], frame_saved[2], frame_weights)
+    frame_mixed_grad, frame_attended_grad, frame_postnorm_grad, output_in = mixed_grads(
+        base_grad, normed_grad, frame_saved[0], frame_weights
+    )
     grads = lax.all_to_all(
         jnp.transpose(
             frame_attended_grad.reshape(row_count, frames_dev, count, LANES), (2, 0, 1, 3)
@@ -1317,8 +1337,9 @@
         concat_axis=0,
         tiled=True,
     )
-    frame_one = grad_rows(normed_two_both, pair(expand_in), order, True, 8, 0)
-    frame_one = grad_columns(activated_both, pair(contract_in), order, 8, 4, frame_one)
+    frame_one = grad_columns(activated_both, contract_in, order, 8, 4)
+    frame_one = grad_rows(normed_two_both, pair(expand_in), order, True, 8, 0, frame_one)
+    grads = tie(grads, *frame_one)
     frame_one = reduce_blocks(*frame_one, True)
     packed_grad = lax.all_to_all(
         frame_attend_grads_call(packed, grads, every_segment),

time: 949 us -> 886 us (0.934)
  blocking collectives: 66.4 us -> 0 us
    all_gather x2 -> x0, blocking collectives: 66.4 us -> none  [the longest x1 45.6 us: shards(): lax.all_gather(jnp.stack([frame_prenorm, frame_postnorm, codec_prenorm, c...]
    ppermute x59, waiting for transfers between devices: 354 us -> 368 us  [swap(): lax.ppermute(values, axis, [(i, i ^ bit) for i in range(lax.axis_size(axi...]
    all_to_all x1, waiting for transfers between devices: 12.6 us -> 2.22 us  [shards(): lax.all_to_all(frame_attend_grads_call(packed, grads, every_segment), 'se...]
    unnamed x190 -> x172, local copies, waits for them, and re-layouts: 47.8 us -> 44.1 us
  transfers between devices with their start and end apart: 63 -> 64, of which waited for: 23 -> 24; matrix products, arithmetic and copies ran while one was open for 26% -> 24% of each run, Pallas kernels for 17% -> 14%
where the time goes in v3:
time: 886 us; the launch traced here: 874 us
  waiting for transfers between devices  378 us (43%)
  Pallas kernels  157 us (18%)
  matrix products  121 us (14%)
  local copies, waits for them, and re-layouts  93.2 us (11%)
  starting transfers between devices  67.2 us (8%)
  other arithmetic  55.3 us (6%)
    ppermute x59, waiting for transfers between devices, swap(): lax.ppermute(values, axis, [(i, i ^ bit) for i in range(lax.axis_size(axi...  368 us
    pallas_call x9, Pallas kernels, grad_call(): pl.pallas_call(kernel, grid_spec=pltpu.PrefetchScalarGridSpec(num_scalar_...  79.9 us
    dot_general x8, matrix products, matmul(): return jnp.dot(former, latter, preferred_element_type=F32)  61.9 us
    dot_general x8, matrix products, inner_right(): lax.dot_general(former, latter, (((1,), (1,)), ((), ())), preferred_eleme...  58.9 us
    unnamed x172, local copies, waits for them, and re-layouts  44.1 us
    ppermute x59, starting transfers between devices, swap(): lax.ppermute(values, axis, [(i, i ^ bit) for i in range(lax.axis_size(axi...  40.5 us
    pallas_call x4, Pallas kernels, join_weights(): pl.pallas_call(functools.partial(join_kernel, layout), in_specs=[pl.Block...  38.9 us
  transfers between devices with their start and end apart: 64, of which 24 were waited for; matrix products, arithmetic and copies ran while one was open for 24% of the time, Pallas kernels for 14%

profile of v3, /device:TPU:0, one launch (start us, length us, event | category | flops | bytes accessed | tf_op | source)
XLA Modules:
  0.0 873.8 jit_solution(5056271218401623107)
XLA Ops:
  17.6 3.3 constant_dynamic-slice_fusion.2
  20.9 3.5 collective-permute-done.1.refs_2_
  26.8 5.8 all-to-all-start.1
  41.0 14.6 %collective-permute-done.2.refs_3_ = bf16[400,1024]{1,0:T(8,128)(2,1)} collective-permute-done((bf16[400,1024]{1,0:T(8,128)(2,1)}, bf16[400,1024]{1,0:T(8,128)(2,1)}, u32[]{:S(2)}, u32[]{:S(2)}) %collective-permute-start.2) | collective-permute-done | bytes 819232 | tf_op jit(solution)/shard_map/ppermute | solution.py:46
  57.4 19.9 %collective-permute-done.6.refs_2_ = bf16[1152,1024]{1,0:T(8,128)(2,1)} collective-permute-done((bf16[1152,1024]{1,0:T(8,128)(2,1)}, bf16[1152,1024]{1,0:T(8,128)(2,1)}, u32[]{:S(2)}, u32[]{:S(2)}) %collective-permute-start.6) | collective-permute-done | bytes 2359328 | tf_op jit(solution)/shard_map/ppermute | solution.py:46
  78.8 5.3 join_weights.4
  88.4 4.8 fusion.26
  97.9 8.5 collective-permute-done.11.refs_2_
  107.6 4.9 all-to-all-start
  114.4 3.1 constant_dynamic-update-slice_fusion.3
  118.3 3.3 constant_dynamic-slice_fusion
  123.1 28.8 %collective-permute-done.7.refs_3_ = bf16[1152,1024]{1,0:T(8,128)(2,1)} collective-permute-done((bf16[1152,1024]{1,0:T(8,128)(2,1)}, bf16[1152,1024]{1,0:T(8,128)(2,1)}, u32[]{:S(2)}, u32[]{:S(2)}) %collective-permute-start.7) | collective-permute-done | bytes 2359328 | tf_op jit(solution)/shard_map/ppermute | solution.py:46
  152.4 27.6 %collective-permute-done.12.refs_3_ = bf16[640,1024]{1,0:T(8,128)(2,1)} collective-permute-done((bf16[640,1024]{1,0:T(8,128)(2,1)S(1)}, bf16[640,1024]{1,0:T(8,128)(2,1)}, u32[]{:S(2)}, u32[]{:S(2)}) %collective-permute-start.12) | collective-permute-done | bytes 1310752 | tf_op jit(solution)/shard_map/ppermute | solution.py:46
  186.6 8.7 frame_attend.1
  196.1 5.8 all-to-all-start.2
  209.2 7.4 all-to-all-done.2
  218.1 7.2 join_weights.6
  225.3 5.8 gather_fusion
  231.7 13.0 %join_weights.5 = (bf16[1024,4096]{1,0:T(8,128)(2,1)}, bf16[4096,1024]{1,0:T(8,128)(2,1)}, bf16[1024,1024]{1,0:T(8,128)(2,1)S(1)}) custom-call(s32[2]{0:T(128)S(1)} %pad_add_fusion.1.place_ref, bf16[2304,1024]{1,0:T(8,128)(2,1)} %constant_dynamic-update-slice_fusion.refs_0_, bf16[2304,1024]{1,0:T(8,128)(2,1)} %collective-permute-done.5.refs_1_, ...), custom_call_target="tpu_custom_call" | custom-call | bytes 37748736 | tf_op jit(solution)/shard_map/join_weights/pallas_call | solution.py:989
  245.8 9.9 %multiply_convert_fusion.1 = (bf16[256,4096]{1,0:T(8,128)(2,1)}, f32[256,4096]{1,0:T(8,128)}) fusion(bf16[256,1024]{1,0:T(8,128)(2,1)S(1)} %multiply_convert_fusion.5.far_own.own_own, bf16[1024,4096]{1,0:T(8,128)(2,1)} %get-tuple-element.57), kind=kOutput, calls=%fused_computation.29 | convolution fusion | flops 2156920832 | bytes 15204352 | tf_op jit(solution)/shard_map/dot_general | solution.py:30
  255.7 5.0 collective-permute-done.17.refs_3_
  260.7 4.0 fusion.28
  267.3 9.0 %convolution_convert_fusion = bf16[768,3072]{1,0:T(8,128)(2,1)} fusion(bf16[768,1024]{1,0:T(8,128)(2,1)} %multiply_convert_fusion.4.far_own.own_own, bf16[1024,3072]{1,0:T(8,128)(2,1)} %get-tuple-element.62), kind=kOutput, calls=%fused_computation.13 | convolution fusion | flops 4834197504 | bytes 12582912 | tf_op jit(solution)/shard_map/dot_general | solution.py:30
  276.3 6.0 codec_attend.1
  282.4 13.4 %join_weights.7 = (bf16[1024,4096]{1,0:T(8,128)(2,1)}, bf16[4096,1024]{1,0:T(8,128)(2,1)}, bf16[1024,1024]{1,0:T(8,128)(2,1)S(1)}) custom-call(s32[2]{0:T(128)S(1)} %pad_add_fusion.1.place_ref, bf16[2304,1024]{1,0:T(8,128)(2,1)} %constant_dynamic-update-slice_fusion.2.refs_0_, bf16[2304,1024]{1,0:T(8,128)(2,1)} %collective-permute-done.15.refs_1_, ...), custom_call_target="tpu_custom_call" | custom-call | bytes 37748736 | tf_op jit(solution)/shard_map/join_weights/pallas_call | solution.py:989
  297.7 13.7 %fusion.58 = f32[768,4096]{1,0:T(8,128)} fusion(bf16[768,1024]{1,0:T(8,128)(2,1)} %bitcast_convert_fusion.latter_own, bf16[4096,1024]{1,0:T(8,128)(2,1)} %get-tuple-element.67), kind=kOutput, calls=%fused_computation.177 | convolution fusion | flops 6442450944 | bytes 22544384 | tf_op jit(solution)/shard_map/dot_general | solution.py:38
  311.8 20.0 %fusion.6 = (bf16[768,4096]{1,0:T(8,128)(2,1)}, bf16[768,4096]{1,0:T(8,128)(2,1)}) fusion(f32[768,4096]{1,0:T(8,128)} %fusion.58, bf16[768,1024]{1,0:T(8,128)(2,1)S(1)} %multiply_convert_fusion.3.far_own.own_own, bf16[1024,4096]{1,0:T(8,128)(2,1)S(1)} %bitcast.302), kind=kOutput, calls=%fused_computation.9 | convolution fusion | flops 6511656960 | bytes 35127296 | tf_op jit(solution)/shard_map/dot_general | solution.py:30
  333.0 11.0 %fusion.59 = f32[768,1024]{1,0:T(8,128)S(1)} fusion(bf16[768,4096]{1,0:T(8,128)(2,1)} %get-tuple-element.129.latter_own, bf16[1024,4096]{1,0:T(8,128)(2,1)} %get-tuple-element.66), kind=kOutput, calls=%fused_computation.178 | convolution fusion | flops 6442450944 | bytes 17825792 | tf_op jit(solution)/shard_map/dot_general | solution.py:38
  344.0 12.0 %collective-permute-done.22.latter_rec = bf16[768,1024]{1,0:T(8,128)(2,1)} collective-permute-done((bf16[768,1024]{1,0:T(8,128)(2,1)}, bf16[768,1024]{1,0:T(8,128)(2,1)}, u32[]{:S(2)}, u32[]{:S(2)}) %collective-permute-start.22) | collective-permute-done | bytes 1572896 | tf_op jit(solution)/shard_map/ppermute | solution.py:46
  355.9 13.2 %grad_columns.2 = (bf16[2,4,8,256,128]{4,3,2,1,0:T(8,128)(2,1)}, bf16[2,4,8,256,128]{4,3,2,1,0:T(8,128)(2,1)}) custom-call(s32[11]{0:T(128)S(1)} %stack.69.order_ref, bf16[768,1024]{1,0:T(8,128)(2,1)} %bitcast_convert_fusion.latter_own, bf16[768,1024]{1,0:T(8,128)(2,1)} %collective-permute-done.22.latter_rec, ...), custom_call_target="tpu_custom_call" | custom-call | flops 6442450944 | bytes 15728640 | tf_op jit(solution)/shard_map/grad_columns/pallas_call | solution.py:731
  369.2 13.2 %grad_rows.6 = (bf16[2,4,8,256,128]{4,3,2,1,0:T(8,128)(2,1)}, bf16[2,4,8,256,128]{4,3,2,1,0:T(8,128)(2,1)}) custom-call(s32[11]{0:T(128)S(1)} %stack.69.order_ref, bf16[768,1024]{1,0:T(8,128)(2,1)S(1)} %multiply_convert_fusion.3.far_own.own_own, ...), custom_call_target="tpu_custom_call", output_to_operand_aliasing={{0}: (7, {}), {1}: (8, {})} | custom-call | flops 6442450944 | bytes 18874368 | tf_op jit(solution)/shard_map/grad_rows/pallas_call | solution.py:731
  388.7 8.8 %codec_attend_grads.1 = bf16[3,256,3072]{2,1,0:T(8,128)(2,1)} custom-call(bf16[3,256,3072]{2,1,0:T(8,128)(2,1)} %bitcast.237, bf16[3,256,1024]{2,1,0:T(8,128)(2,1)S(1)} %bitcast.233, bf16[1024,128]{1,0:T(8,128)(2,1)S(1)} %fusion.40.marks_ref), custom_call_target="tpu_custom_call" | custom-call | flops 2348810240 | bytes 11796480 | tf_op jit(solution)/shard_map/codec_attend_grads/pallas_call | solution.py:631
  399.1 9.7 %multiply_reduce_fusion.1 = (f32[1024]{0:T(1024)S(1)}, f32[768]{0:T(1024)S(1)}, f32[768,1024]{1,0:T(8,128)S(1)}) fusion(f32[3,256,1024]{2,1,0:T(8,128)S(1)} %copy-done.25, f32[768]{0:T(1024)S(1)} %rsqrt.46, f32[1024]{0:T(1024)S(1)} %bitcast.276, bf16[768,3072]{1,0:T(8,128)(2,1)} %bitcast.245, bf16[1024,3072]{1,0:T(8,128)(2,1)} %get-tuple-element.62), kind=kOutput, calls=%fused_computation.46 | convolution fusion | flops 4836554752 | bytes 17315840 | tf_op jit(solution)/shard_map/dot_general | solution.py:38
  411.2 79.5 %collective-permute-done.55 = bf16[2,4,8,256,128]{4,3,2,1,0:T(8,128)(2,1)S(1)} collective-permute-done((bf16[2,4,8,256,128]{4,3,2,1,0:T(8,128)(2,1)}, bf16[2,4,8,256,128]{4,3,2,1,0:T(8,128)(2,1)S(1)}, u32[]{:S(2)}, u32[]{:S(2)}) %collective-permute-start.55) | collective-permute-done | bytes 4194336 | tf_op jit(solution)/shard_map/ppermute | solution.py:46
  495.8 4.5 fusion.22
  501.0 13.2 %grad_rows.7 = (bf16[2,4,6,256,128]{4,3,2,1,0:T(8,128)(2,1)}, bf16[2,4,6,256,128]{4,3,2,1,0:T(8,128)(2,1)}) custom-call(s32[11]{0:T(128)S(1)} %stack.69.order_ref, bf16[768,1024]{1,0:T(8,128)(2,1)} %multiply_convert_fusion.4.far_own.own_own, bf16[768,1024]{1,0:T(8,128)(2,1)} %collective-permute-done.28.far_rec.own_rec, ...), custom_call_target="tpu_custom_call" | custom-call | flops 4831838208 | bytes 15728640 | tf_op jit(solution)/shard_map/grad_rows/pallas_call | solution.py:731
  514.2 5.4 grad_rows.8
  521.5 6.3 grad_table.1
  528.0 11.7 %fusion.13.latter_own = bf16[256,4096]{1,0:T(8,128)(2,1)} fusion(f32[256,4096]{1,0:T(8,128)} %get-tuple-element.154, bf16[256,1024]{1,0:T(8,128)(2,1)} %reduce_sum.125.latter_own, bf16[4096,1024]{1,0:T(8,128)(2,1)} %get-tuple-element.58), kind=kOutput, calls=%fused_computation.22 | convolution fusion | flops 2168455168 | bytes 15204352 | tf_op jit(solution)/shard_map/dot_general | solution.py:38
  539.8 4.3 multiply_reduce_fusion.5
  548.5 5.7 all-to-all-start.3
  555.8 8.1 grad_columns.3
  566.0 3.5 fusion.14
  573.1 8.5 grad_rows.9
  584.7 14.7 %frame_attend_grads.1 = bf16[8,2,128,384]{3,2,1,0:T(8,128)(2,1)S(1)} custom-call(bf16[8,2,128,384]{3,2,1,0:T(8,128)(2,1)S(1)} %copy-done.8, bf16[8,2,128,128]{3,2,1,0:T(8,128)(2,1)} %all-to-all-done.3.grad_ref, s32[2,1024,1]{2,1,0:T(8,128)S(1)} %copy-done.11, s32[2,1,1024]{2,1,0:T(1,128)S(1)} %bitcast.235), custom_call_target="tpu_custom_call" | custom-call | flops 3221225472 | bytes 3932160 | tf_op jit(solution)/shard_map/frame_attend_grads/pallas_call | solution.py:480
  600.7 4.5 all-to-all-start.4
  605.3 11.5 %convolution_add_fusion = f32[768,1024]{1,0:T(8,128)S(1)} fusion(f32[768,1024]{1,0:T(8,128)} %copy-done.19, bf16[768,4096]{1,0:T(8,128)(2,1)} %get-tuple-element.130.former_own, bf16[4096,1024]{1,0:T(8,128)(2,1)} %get-tuple-element.67), kind=kOutput, calls=%fused_computation.64 | convolution fusion | flops 6443237376 | bytes 20971520 | tf_op jit(solution)/shard_map/dot_general | solution.py:30
  616.8 20.5 %collective-permute-done.57 = bf16[2,8,256,128]{3,2,1,0:T(8,128)(2,1)} collective-permute-done((bf16[2,8,256,128]{3,2,1,0:T(8,128)(2,1)}, bf16[2,8,256,128]{3,2,1,0:T(8,128)(2,1)}, u32[]{:S(2)}, u32[]{:S(2)}) %collective-permute-start.57) | collective-permute-done | bytes 1048608 | tf_op jit(solution)/shard_map/ppermute | solution.py:46
  642.1 5.7 collective-permute-done.34
  657.2 3.8 collective-permute-done.58
  662.4 5.9 multiply_reduce_fusion.6
  669.0 6.4 collective-permute-done.51
  675.4 3.8 fusion.21
  680.4 7.8 grad_rows.10
  688.1 4.2 grad_rows.11
  693.8 14.3 %collective-permute-done.35 = bf16[4,6,256,128]{3,2,1,0:T(8,128)(2,1)} collective-permute-done((bf16[4,6,256,128]{3,2,1,0:T(8,128)(2,1)}, bf16[4,6,256,128]{3,2,1,0:T(8,128)(2,1)}, u32[]{:S(2)}, u32[]{:S(2)}) %collective-permute-start.35) | collective-permute-done | bytes 1572896 | tf_op jit(solution)/shard_map/ppermute | solution.py:46
  720.0 52.7 %collective-permute-done.40 = f32[4,1024]{1,0:T(4,128)S(1)} collective-permute-done((f32[4,1024]{1,0:T(4,128)S(1)}, f32[4,1024]{1,0:T(4,128)S(1)}, u32[]{:S(2)}, u32[]{:S(2)}) %collective-permute-start.40) | collective-permute-done | bytes 16416 | tf_op jit(solution)/shard_map/ppermute | solution.py:46
  777.0 3.4 fusion.31
  791.7 25.1 %collective-permute-done.37 = bf16[6,256,128]{2,1,0:T(8,128)(2,1)S(1)} collective-permute-done((bf16[6,256,128]{2,1,0:T(8,128)(2,1)S(1)}, bf16[6,256,128]{2,1,0:T(8,128)(2,1)S(1)}, u32[]{:S(2)}, u32[]{:S(2)}) %collective-permute-start.37) | collective-permute-done | bytes 393248 | tf_op jit(solution)/shard_map/ppermute | solution.py:46
  817.0 14.9 %collective-permute-done.53 = bf16[2,8,256,128]{3,2,1,0:T(8,128)(2,1)S(1)} collective-permute-done((bf16[2,8,256,128]{3,2,1,0:T(8,128)(2,1)S(1)}, bf16[2,8,256,128]{3,2,1,0:T(8,128)(2,1)S(1)}, u32[]{:S(2)}, u32[]{:S(2)}) %collective-permute-start.53) | collective-permute-done | bytes 1048608 | tf_op jit(solution)/shard_map/ppermute | solution.py:46
  835.9 3.4 collective-permute-start.49
  844.5 10.3 %collective-permute-done.54 = bf16[8,256,128]{2,1,0:T(8,128)(2,1)} collective-permute-done((bf16[8,256,128]{2,1,0:T(8,128)(2,1)}, bf16[8,256,128]{2,1,0:T(8,128)(2,1)}, u32[]{:S(2)}, u32[]{:S(2)}) %collective-permute-start.54) | collective-permute-done | bytes 524320 | tf_op jit(solution)/shard_map/ppermute | solution.py:46
  855.9 6.8 collective-permute-done.49
  866.3 5.1 collective-permute-done.50
  (380 shorter events, 165.4 us)
Async XLA Ops:
  3.1 21.4 %collective-permute-start.1 = (bf16[400,1024]{1,0:T(8,128)(2,1)S(1)}, bf16[400,1024]{1,0:T(8,128)(2,1)}, u32[]{:S(2)}, u32[]{:S(2)}) collective-permute-start(bf16[400,1024]{1,0:T(8,128)(2,1)S(1)} %constant_dynamic-slice_fusion.3), channel_id=1, source_target_pairs={{0,2},{1,3},{2,0},{3,1},{4,6},{5,7},{6,4},{7,5},{8,10},{9,11},{10,... | collective-permute-start | bytes 2457608 | tf_op jit(solution)/shard_map/ppermute | solution.py:46
  24.5 52.7 %collective-permute-start.6 = (bf16[1152,1024]{1,0:T(8,128)(2,1)}, bf16[1152,1024]{1,0:T(8,128)(2,1)}, u32[]{:S(2)}, u32[]{:S(2)}) collective-permute-start(bf16[1152,1024]{1,0:T(8,128)(2,1)} %constant_dynamic-slice_fusion.2), channel_id=1, source_target_pairs={{0,2},{1,3},{2,0},{3,1},{4,6},{5,7},{6,4},{7,5},{8,10},{9,11},{10,... | collective-permute-start | bytes 7077896 | tf_op jit(solution)/shard_map/ppermute | solution.py:46
  26.2 52.5 %collective-permute-start = (bf16[800,1024]{1,0:T(8,128)(2,1)S(1)}, bf16[800,1024]{1,0:T(8,128)(2,1)}, u32[]{:S(2)}, u32[]{:S(2)}) collective-permute-start(bf16[800,1024]{1,0:T(8,128)(2,1)S(1)} %fusion.24.refs_0_), channel_id=1, source_target_pairs={{0,1},{1,0},{2,3},{3,2},{4,5},{5,4},{6,7},{7,6},{8,9},{9,8},{10,11... | collective-permute-start | bytes 4915208 | tf_op jit(solution)/shard_map/ppermute | solution.py:46
  26.8 80.7 %all-to-all-start.1 = ((s32[8,2,128]{2,1,0:T(2,128)}), s32[8,2,128]{2,1,0:T(2,128)S(1)}, u32[]{:S(2)}, u32[]{:S(2)}) async-start(s32[8,2,128]{2,1,0:T(2,128)} %broadcast_in_dim.19), calls=%async_computation.1 | async-start | bytes 16384 | tf_op jit(solution)/shard_map/all_to_all | solution.py:1243
  34.9 20.7 %collective-permute-start.2 = (bf16[400,1024]{1,0:T(8,128)(2,1)}, bf16[400,1024]{1,0:T(8,128)(2,1)}, u32[]{:S(2)}, u32[]{:S(2)}) collective-permute-start(bf16[400,1024]{1,0:T(8,128)(2,1)} %collective-permute-done.1.refs_2_), channel_id=1, source_target_pairs={{0,4},{4,0},{8,12},{12,8},{16,20},{20,16},{24,28},{28,24},{1,5},{5... | collective-permute-start | bytes 2457608 | tf_op jit(solution)/shard_map/ppermute | solution.py:46
  41.0 37.7 %collective-permute-start.3 = (bf16[400,1024]{1,0:T(8,128)(2,1)}, bf16[400,1024]{1,0:T(8,128)(2,1)S(1)}, u32[]{:S(2)}, u32[]{:S(2)}) collective-permute-start(bf16[400,1024]{1,0:T(8,128)(2,1)} %collective-permute-done.1.refs_2_), channel_id=1, source_target_pairs={{0,1},{1,0},{2,3},{3,2},{4,5},{5,4},{6,7},{7,6},{8,9},{9,8},{10,11... | collective-permute-start | bytes 2457608 | tf_op jit(solution)/shard_map/ppermute | solution.py:46
  55.7 23.1 %collective-permute-start.4 = (bf16[400,1024]{1,0:T(8,128)(2,1)}, bf16[400,1024]{1,0:T(8,128)(2,1)S(1)}, u32[]{:S(2)}, u32[]{:S(2)}) collective-permute-start(bf16[400,1024]{1,0:T(8,128)(2,1)} %collective-permute-done.2.refs_3_), channel_id=1, source_target_pairs={{0,1},{1,0},{2,3},{3,2},{4,5},{5,4},{6,7},{7,6},{8,9},{9,8},{10,11... | collective-permute-start | bytes 2457608 | tf_op jit(solution)/shard_map/ppermute | solution.py:46
  77.2 29.3 %collective-permute-start.11 = (bf16[640,1024]{1,0:T(8,128)(2,1)}, bf16[640,1024]{1,0:T(8,128)(2,1)S(1)}, u32[]{:S(2)}, u32[]{:S(2)}) collective-permute-start(bf16[640,1024]{1,0:T(8,128)(2,1)} %constant_dynamic-slice_fusion.1), channel_id=1, source_target_pairs={{0,2},{1,3},{2,0},{3,1},{4,6},{5,7},{6,4},{7,5},{8,10},{9,11},{10,... | collective-permute-start | bytes 3932168 | tf_op jit(solution)/shard_map/ppermute | solution.py:46
  78.7 152.4 %collective-permute-start.5 = (bf16[2304,1024]{1,0:T(8,128)(2,1)}, bf16[2304,1024]{1,0:T(8,128)(2,1)}, u32[]{:S(2)}, u32[]{:S(2)}) collective-permute-start(bf16[2304,1024]{1,0:T(8,128)(2,1)} %constant_dynamic-update-slice_fusion.refs_0_), channel_id=1, source_target_pairs={{0,1},{1,0},{2,3},{3,2},{4,5},{5,4},{6,7},{7,6},{8,9},{9,8},{10,11... | collective-permute-start | bytes 14155784 | tf_op jit(solution)/shard_map/ppermute | solution.py:46
  84.3 67.6 %collective-permute-start.10 = (bf16[1280,1024]{1,0:T(8,128)(2,1)}, bf16[1280,1024]{1,0:T(8,128)(2,1)}, u32[]{:S(2)}, u32[]{:S(2)}) collective-permute-start(bf16[1280,1024]{1,0:T(8,128)(2,1)} %copy-done.32), channel_id=1, source_target_pairs={{0,1},{1,0},{2,3},{3,2},{4,5},{5,4},{6,7},{7,6},{8,9},{9,8},{10,11... | collective-permute-start | bytes 7864328 | tf_op jit(solution)/shard_map/ppermute | solution.py:46
  84.8 67.1 %collective-permute-start.7 = (bf16[1152,1024]{1,0:T(8,128)(2,1)}, bf16[1152,1024]{1,0:T(8,128)(2,1)}, u32[]{:S(2)}, u32[]{:S(2)}) collective-permute-start(bf16[1152,1024]{1,0:T(8,128)(2,1)} %collective-permute-done.6.refs_2_), channel_id=1, source_target_pairs={{0,4},{4,0},{8,12},{12,8},{16,20},{20,16},{24,28},{28,24},{1,5},{5... | collective-permute-start | bytes 7077896 | tf_op jit(solution)/shard_map/ppermute | solution.py:46
  106.5 73.5 %collective-permute-start.12 = (bf16[640,1024]{1,0:T(8,128)(2,1)S(1)}, bf16[640,1024]{1,0:T(8,128)(2,1)}, u32[]{:S(2)}, u32[]{:S(2)}) collective-permute-start(bf16[640,1024]{1,0:T(8,128)(2,1)S(1)} %collective-permute-done.11.refs_2_), channel_id=1, source_target_pairs={{0,4},{4,0},{8,12},{12,8},{16,20},{20,16},{24,28},{28,24},{1,5},{5... | collective-permute-start | bytes 3932168 | tf_op jit(solution)/shard_map/ppermute | solution.py:46
  107.6 77.2 %all-to-all-start = ((bf16[8,2,128,384]{3,2,1,0:T(8,128)(2,1)}), bf16[8,2,128,384]{3,2,1,0:T(8,128)(2,1)S(1)}, u32[]{:S(2)}, u32[]{:S(2)}) async-start(bf16[8,2,128,384]{3,2,1,0:T(8,128)(2,1)} %copy.69), calls=%async_computation | async-start | bytes 3145728 | tf_op jit(solution)/shard_map/all_to_all | solution.py:1271
  121.6 80.5 %collective-permute-start.16 = (bf16[1152,1024]{1,0:T(8,128)(2,1)}, bf16[1152,1024]{1,0:T(8,128)(2,1)}, u32[]{:S(2)}, u32[]{:S(2)}) collective-permute-start(bf16[1152,1024]{1,0:T(8,128)(2,1)} %constant_dynamic-slice_fusion), channel_id=1, source_target_pairs={{0,2},{1,3},{2,0},{3,1},{4,6},{5,7},{6,4},{7,5},{8,10},{9,11},{10,... | collective-permute-start | bytes 7077896 | tf_op jit(solution)/shard_map/ppermute | solution.py:46
  151.9 28.2 %collective-permute-start.13 = (bf16[640,1024]{1,0:T(8,128)(2,1)S(1)}, bf16[640,1024]{1,0:T(8,128)(2,1)}, u32[]{:S(2)}, u32[]{:S(2)}) collective-permute-start(bf16[640,1024]{1,0:T(8,128)(2,1)S(1)} %collective-permute-done.11.refs_2_), channel_id=1, source_target_pairs={{0,1},{1,0},{2,3},{3,2},{4,5},{5,4},{6,7},{7,6},{8,9},{9,8},{10,11... | collective-permute-start | bytes 3932168 | tf_op jit(solution)/shard_map/ppermute | solution.py:46
  151.9 79.8 %collective-permute-start.8 = (bf16[1152,1024]{1,0:T(8,128)(2,1)}, bf16[1152,1024]{1,0:T(8,128)(2,1)}, u32[]{:S(2)}, u32[]{:S(2)}) collective-permute-start(bf16[1152,1024]{1,0:T(8,128)(2,1)} %collective-permute-done.6.refs_2_), channel_id=1, source_target_pairs={{0,1},{1,0},{2,3},{3,2},{4,5},{5,4},{6,7},{7,6},{8,9},{9,8},{10,11... | collective-permute-start | bytes 7077896 | tf_op jit(solution)/shard_map/ppermute | solution.py:46
  180.0 51.7 %collective-permute-start.9 = (bf16[1152,1024]{1,0:T(8,128)(2,1)}, bf16[1152,1024]{1,0:T(8,128)(2,1)}, u32[]{:S(2)}, u32[]{:S(2)}) collective-permute-start(bf16[1152,1024]{1,0:T(8,128)(2,1)} %collective-permute-done.7.refs_3_), channel_id=1, source_target_pairs={{0,1},{1,0},{2,3},{3,2},{4,5},{5,4},{6,7},{7,6},{8,9},{9,8},{10,11... | collective-permute-start | bytes 7077896 | tf_op jit(solution)/shard_map/ppermute | solution.py:46
  180.1 38.0 %collective-permute-start.14 = (bf16[640,1024]{1,0:T(8,128)(2,1)}, bf16[640,1024]{1,0:T(8,128)(2,1)}, u32[]{:S(2)}, u32[]{:S(2)}) collective-permute-start(bf16[640,1024]{1,0:T(8,128)(2,1)} %collective-permute-done.12.refs_3_), channel_id=1, source_target_pairs={{0,1},{1,0},{2,3},{3,2},{4,5},{5,4},{6,7},{7,6},{8,9},{9,8},{10,11... | collective-permute-start | bytes 3932168 | tf_op jit(solution)/shard_map/ppermute | solution.py:46
  196.1 20.6 %all-to-all-start.2 = ((bf16[8,2,128,128]{3,2,1,0:T(8,128)(2,1)}), bf16[8,2,128,128]{3,2,1,0:T(8,128)(2,1)}, u32[]{:S(2)}, u32[]{:S(2)}) async-start(bf16[8,2,128,128]{3,2,1,0:T(8,128)(2,1)} %copy-done.12), calls=%async_computation.2 | async-start | bytes 1048576 | tf_op jit(solution)/shard_map/all_to_all | solution.py:1272
  202.1 58.6 %collective-permute-start.17 = (bf16[1152,1024]{1,0:T(8,128)(2,1)}, bf16[1152,1024]{1,0:T(8,128)(2,1)}, u32[]{:S(2)}, u32[]{:S(2)}) collective-permute-start(bf16[1152,1024]{1,0:T(8,128)(2,1)} %collective-permute-done.16.refs_2_), channel_id=1, source_target_pairs={{0,4},{4,0},{8,12},{12,8},{16,20},{20,16},{24,28},{28,24},{1,5},{5... | collective-permute-start | bytes 7077896 | tf_op jit(solution)/shard_map/ppermute | solution.py:46
  218.1 64.3 %collective-permute-start.15 = (bf16[2304,1024]{1,0:T(8,128)(2,1)}, bf16[2304,1024]{1,0:T(8,128)(2,1)}, u32[]{:S(2)}, u32[]{:S(2)}) collective-permute-start(bf16[2304,1024]{1,0:T(8,128)(2,1)} %constant_dynamic-update-slice_fusion.2.refs_0_), channel_id=1, source_target_pairs={{0,1},{1,0},{2,3},{3,2},{4,5},{5,4},{6,7},{7,6},{8,9},{9,8},{10,11... | collective-permute-start | bytes 14155784 | tf_op jit(solution)/shard_map/ppermute | solution.py:46
  231.1 51.2 %collective-permute-start.18 = (bf16[1152,1024]{1,0:T(8,128)(2,1)}, bf16[1152,1024]{1,0:T(8,128)(2,1)}, u32[]{:S(2)}, u32[]{:S(2)}) collective-permute-start(bf16[1152,1024]{1,0:T(8,128)(2,1)} %collective-permute-done.16.refs_2_), channel_id=1, source_target_pairs={{0,1},{1,0},{2,3},{3,2},{4,5},{5,4},{6,7},{7,6},{8,9},{9,8},{10,11... | collective-permute-start | bytes 7077896 | tf_op jit(solution)/shard_map/ppermute | solution.py:46
  260.7 21.6 %collective-permute-start.19 = (bf16[1152,1024]{1,0:T(8,128)(2,1)}, bf16[1152,1024]{1,0:T(8,128)(2,1)}, u32[]{:S(2)}, u32[]{:S(2)}) collective-permute-start(bf16[1152,1024]{1,0:T(8,128)(2,1)} %collective-permute-done.17.refs_3_), channel_id=1, source_target_pairs={{0,1},{1,0},{2,3},{3,2},{4,5},{5,4},{6,7},{7,6},{8,9},{9,8},{10,11... | collective-permute-start | bytes 7077896 | tf_op jit(solution)/shard_map/ppermute | solution.py:46
  331.8 24.1 %collective-permute-start.23 = (bf16[768,4096]{1,0:T(8,128)(2,1)}, bf16[768,4096]{1,0:T(8,128)(2,1)}, u32[]{:S(2)}, u32[]{:S(2)}) collective-permute-start(bf16[768,4096]{1,0:T(8,128)(2,1)} %get-tuple-element.130.former_own), channel_id=1, source_target_pairs={{0,1},{1,0},{2,3},{3,2},{4,5},{5,4},{6,7},{7,6},{8,9},{9,8},{10,11... | collective-permute-start | bytes 18874376 | tf_op jit(solution)/shard_map/ppermute | solution.py:46
  332.3 36.9 %collective-permute-start.21 = (bf16[768,4096]{1,0:T(8,128)(2,1)}, bf16[768,4096]{1,0:T(8,128)(2,1)}, u32[]{:S(2)}, u32[]{:S(2)}) collective-permute-start(bf16[768,4096]{1,0:T(8,128)(2,1)} %get-tuple-element.129.latter_own), channel_id=1, source_target_pairs={{0,1},{1,0},{2,3},{3,2},{4,5},{5,4},{6,7},{7,6},{8,9},{9,8},{10,11... | collective-permute-start | bytes 18874376 | tf_op jit(solution)/shard_map/ppermute | solution.py:46
  332.3 23.6 %collective-permute-start.22 = (bf16[768,1024]{1,0:T(8,128)(2,1)}, bf16[768,1024]{1,0:T(8,128)(2,1)}, u32[]{:S(2)}, u32[]{:S(2)}) collective-permute-start(bf16[768,1024]{1,0:T(8,128)(2,1)} %bitcast_convert_fusion.latter_own), channel_id=1, source_target_pairs={{0,1},{1,0},{2,3},{3,2},{4,5},{5,4},{6,7},{7,6},{8,9},{9,8},{10,11... | collective-permute-start | bytes 4718600 | tf_op jit(solution)/shard_map/ppermute | solution.py:46
  332.9 36.3 %collective-permute-start.20 = (bf16[768,1024]{1,0:T(8,128)(2,1)S(1)}, bf16[768,1024]{1,0:T(8,128)(2,1)S(1)}, u32[]{:S(2)}, u32[]{:S(2)}) collective-permute-start(bf16[768,1024]{1,0:T(8,128)(2,1)S(1)} %multiply_convert_fusion.3.far_own.own_own), channel_id=1, source_target_pairs={{0,1},{1,0},{2,3},{3,2},{4,5},{5,4},{6,7},{7,6},{8,9},{9,8},{10,11... | collective-permute-start | bytes 4718600 | tf_op jit(solution)/shard_map/ppermute | solution.py:46
  397.5 102.9 %collective-permute-start.29 = (bf16[768,3072]{1,0:T(8,128)(2,1)}, bf16[768,3072]{1,0:T(8,128)(2,1)}, u32[]{:S(2)}, u32[]{:S(2)}) collective-permute-start(bf16[768,3072]{1,0:T(8,128)(2,1)} %bitcast.244), channel_id=1, source_target_pairs={{0,1},{1,0},{2,3},{3,2},{4,5},{5,4},{6,7},{7,6},{8,9},{9,8},{10,11... | collective-permute-start | bytes 14155784 | tf_op jit(solution)/shard_map/ppermute | solution.py:46
  397.9 92.8 %collective-permute-start.55 = (bf16[2,4,8,256,128]{4,3,2,1,0:T(8,128)(2,1)}, bf16[2,4,8,256,128]{4,3,2,1,0:T(8,128)(2,1)S(1)}, u32[]{:S(2)}, u32[]{:S(2)}) collective-permute-start(bf16[2,4,8,256,128]{4,3,2,1,0:T(8,128)(2,1)} %get-tuple-element.70), channel_id=1, source_target_pairs={{0,2},{1,3},{2,0},{3,1},{4,6},{5,7},{6,4},{7,5},{8,10},{9,11},{10,... | collective-permute-start | bytes 12582920 | tf_op jit(solution)/shard_map/ppermute | solution.py:46
  398.5 10.4 %collective-permute-start.24 = (s32[1,512]{1,0:T(1,128)S(1)}, s32[1,512]{1,0:T(1,128)S(1)}, u32[]{:S(2)}, u32[]{:S(2)}) collective-permute-start(s32[1,512]{1,0:T(1,128)S(1)} %add.272), channel_id=1, source_target_pairs={{0,1},{1,0},{2,3},{3,2},{4,5},{5,4},{6,7},{7,6},{8,9},{9,8},{10,11... | collective-permute-start | bytes 6152 | tf_op jit(solution)/shard_map/ppermute | solution.py:46
  398.5 115.7 %collective-permute-start.26 = (bf16[768,1024]{1,0:T(8,128)(2,1)S(1)}, bf16[768,1024]{1,0:T(8,128)(2,1)}, u32[]{:S(2)}, u32[]{:S(2)}) collective-permute-start(bf16[768,1024]{1,0:T(8,128)(2,1)S(1)} %bitcast.230), channel_id=1, source_target_pairs={{0,1},{1,0},{2,3},{3,2},{4,5},{5,4},{6,7},{7,6},{8,9},{9,8},{10,11... | collective-permute-start | bytes 4718600 | tf_op jit(solution)/shard_map/ppermute | solution.py:46
  399.0 101.3 %collective-permute-start.28 = (bf16[768,1024]{1,0:T(8,128)(2,1)}, bf16[768,1024]{1,0:T(8,128)(2,1)}, u32[]{:S(2)}, u32[]{:S(2)}) collective-permute-start(bf16[768,1024]{1,0:T(8,128)(2,1)} %multiply_convert_fusion.4.far_own.own_own), channel_id=1, source_target_pairs={{0,1},{1,0},{2,3},{3,2},{4,5},{5,4},{6,7},{7,6},{8,9},{9,8},{10,11... | collective-permute-start | bytes 4718600 | tf_op jit(solution)/shard_map/ppermute | solution.py:46
  408.8 105.4 %collective-permute-start.27 = (bf16[768,1024]{1,0:T(8,128)(2,1)S(1)}, bf16[768,1024]{1,0:T(8,128)(2,1)}, u32[]{:S(2)}, u32[]{:S(2)}) collective-permute-start(bf16[768,1024]{1,0:T(8,128)(2,1)S(1)} %get-tuple-element.127.latter_own), channel_id=1, source_target_pairs={{0,1},{1,0},{2,3},{3,2},{4,5},{5,4},{6,7},{7,6},{8,9},{9,8},{10,11... | collective-permute-start | bytes 4718600 | tf_op jit(solution)/shard_map/ppermute | solution.py:46
  490.7 28.9 %collective-permute-start.25 = (bf16[512,1024]{1,0:T(8,128)(2,1)}, bf16[512,1024]{1,0:T(8,128)(2,1)}, u32[]{:S(2)}, u32[]{:S(2)}) collective-permute-start(bf16[512,1024]{1,0:T(8,128)(2,1)} %slice.381.latter_own), channel_id=1, source_target_pairs={{0,1},{1,0},{2,3},{3,2},{4,5},{5,4},{6,7},{7,6},{8,9},{9,8},{10,11... | collective-permute-start | bytes 3145736 | tf_op jit(solution)/shard_map/ppermute | solution.py:46
  500.4 54.9 %collective-permute-start.33 = (bf16[256,4096]{1,0:T(8,128)(2,1)}, bf16[256,4096]{1,0:T(8,128)(2,1)}, u32[]{:S(2)}, u32[]{:S(2)}) collective-permute-start(bf16[256,4096]{1,0:T(8,128)(2,1)} %get-tuple-element.153.former_own), channel_id=1, source_target_pairs={{0,1},{1,0},{2,3},{3,2},{4,5},{5,4},{6,7},{7,6},{8,9},{9,8},{10,11... | collective-permute-start | bytes 6291464 | tf_op jit(solution)/shard_map/ppermute | solution.py:46
  500.4 63.5 %collective-permute-start.56 = (bf16[4,8,256,128]{3,2,1,0:T(8,128)(2,1)}, bf16[4,8,256,128]{3,2,1,0:T(8,128)(2,1)}, u32[]{:S(2)}, u32[]{:S(2)}) collective-permute-start(bf16[4,8,256,128]{3,2,1,0:T(8,128)(2,1)} %fusion.22), channel_id=1, source_target_pairs={{0,4},{4,0},{8,12},{12,8},{16,20},{20,16},{24,28},{28,24},{1,5},{5... | collective-permute-start | bytes 6291464 | tf_op jit(solution)/shard_map/ppermute | solution.py:46
  527.8 27.9 %collective-permute-start.32 = (bf16[256,1024]{1,0:T(8,128)(2,1)}, bf16[256,1024]{1,0:T(8,128)(2,1)}, u32[]{:S(2)}, u32[]{:S(2)}) collective-permute-start(bf16[256,1024]{1,0:T(8,128)(2,1)} %reduce_sum.125.latter_own), channel_id=1, source_target_pairs={{0,1},{1,0},{2,3},{3,2},{4,5},{5,4},{6,7},{7,6},{8,9},{9,8},{10,11... | collective-permute-start | bytes 1572872 | tf_op jit(solution)/shard_map/ppermute | solution.py:46
  539.6 33.4 %collective-permute-start.31 = (bf16[256,4096]{1,0:T(8,128)(2,1)}, bf16[256,4096]{1,0:T(8,128)(2,1)}, u32[]{:S(2)}, u32[]{:S(2)}) collective-permute-start(bf16[256,4096]{1,0:T(8,128)(2,1)} %fusion.13.latter_own), channel_id=1, source_target_pairs={{0,1},{1,0},{2,3},{3,2},{4,5},{5,4},{6,7},{7,6},{8,9},{9,8},{10,11... | collective-permute-start | bytes 6291464 | tf_op jit(solution)/shard_map/ppermute | solution.py:46
  548.5 33.6 %all-to-all-start.3 = ((bf16[8,2,128,128]{3,2,1,0:T(8,128)(2,1)}), bf16[8,2,128,128]{3,2,1,0:T(8,128)(2,1)}, u32[]{:S(2)}, u32[]{:S(2)}) async-start(bf16[8,2,128,128]{3,2,1,0:T(8,128)(2,1)} %bitcast.228), calls=%async_computation.3 | async-start | bytes 1048576 | tf_op jit(solution)/shard_map/all_to_all | solution.py:1331
  554.2 114.1 %collective-permute-start.45 = (bf16[256,1024]{1,0:T(8,128)(2,1)}, bf16[256,1024]{1,0:T(8,128)(2,1)}, u32[]{:S(2)}, u32[]{:S(2)}) collective-permute-start(bf16[256,1024]{1,0:T(8,128)(2,1)} %multiply_convert_fusion.6.far_own.own_own), channel_id=1, source_target_pairs={{0,1},{1,0},{2,3},{3,2},{4,5},{5,4},{6,7},{7,6},{8,9},{9,8},{10,11... | collective-permute-start | bytes 1572872 | tf_op jit(solution)/shard_map/ppermute | solution.py:46
  555.3 132.8 %collective-permute-start.43 = (bf16[256,1024]{1,0:T(8,128)(2,1)}, bf16[256,1024]{1,0:T(8,128)(2,1)}, u32[]{:S(2)}, u32[]{:S(2)}) collective-permute-start(bf16[256,1024]{1,0:T(8,128)(2,1)} %bitcast.227.far_own.own_own), channel_id=1, source_target_pairs={{0,1},{1,0},{2,3},{3,2},{4,5},{5,4},{6,7},{7,6},{8,9},{9,8},{10,11... | collective-permute-start | bytes 1572872 | tf_op jit(solution)/shard_map/ppermute | solution.py:46
  555.7 15.0 %collective-permute-start.30 = (bf16[256,1024]{1,0:T(8,128)(2,1)}, bf16[256,1024]{1,0:T(8,128)(2,1)S(1)}, u32[]{:S(2)}, u32[]{:S(2)}) collective-permute-start(bf16[256,1024]{1,0:T(8,128)(2,1)} %copy-done.3), channel_id=1, source_target_pairs={{0,1},{1,0},{2,3},{3,2},{4,5},{5,4},{6,7},{7,6},{8,9},{9,8},{10,11... | collective-permute-start | bytes 1572872 | tf_op jit(solution)/shard_map/ppermute | solution.py:46
  563.9 83.8 %collective-permute-start.34 = (bf16[2,4,6,256,128]{4,3,2,1,0:T(8,128)(2,1)S(1)}, bf16[2,4,6,256,128]{4,3,2,1,0:T(8,128)(2,1)}, u32[]{:S(2)}, u32[]{:S(2)}) collective-permute-start(bf16[2,4,6,256,128]{4,3,2,1,0:T(8,128)(2,1)S(1)} %copy-done.2), channel_id=1, source_target_pairs={{0,4},{4,0},{8,12},{12,8},{16,20},{20,16},{24,28},{28,24},{1,5},{5... | collective-permute-start | bytes 9437192 | tf_op jit(solution)/shard_map/ppermute | solution.py:46
  570.7 66.6 %collective-permute-start.57 = (bf16[2,8,256,128]{3,2,1,0:T(8,128)(2,1)}, bf16[2,8,256,128]{3,2,1,0:T(8,128)(2,1)}, u32[]{:S(2)}, u32[]{:S(2)}) collective-permute-start(bf16[2,8,256,128]{3,2,1,0:T(8,128)(2,1)} %slice.312), channel_id=1, source_target_pairs={{0,16},{4,20},{8,24},{12,28},{16,0},{20,4},{24,8},{28,12},{1,17},{... | collective-permute-start | bytes 3145736 | tf_op jit(solution)/shard_map/ppermute | solution.py:46
  581.6 93.8 %collective-permute-start.51 = (bf16[2,4,8,256,128]{4,3,2,1,0:T(8,128)(2,1)}, bf16[2,4,8,256,128]{4,3,2,1,0:T(8,128)(2,1)}, u32[]{:S(2)}, u32[]{:S(2)}) collective-permute-start(bf16[2,4,8,256,128]{4,3,2,1,0:T(8,128)(2,1)} %get-tuple-element.82), channel_id=1, source_target_pairs={{0,2},{1,3},{2,0},{3,1},{4,6},{5,7},{6,4},{7,5},{8,10},{9,11},{10,... | collective-permute-start | bytes 12582920 | tf_op jit(solution)/shard_map/ppermute | solution.py:46
  600.7 52.8 %all-to-all-start.4 = ((bf16[8,2,128,384]{3,2,1,0:T(8,128)(2,1)}), bf16[8,2,128,384]{3,2,1,0:T(8,128)(2,1)}, u32[]{:S(2)}, u32[]{:S(2)}) async-start(bf16[8,2,128,384]{3,2,1,0:T(8,128)(2,1)} %copy-done.9), calls=%async_computation.4 | async-start | bytes 3145728 | tf_op jit(solution)/shard_map/all_to_all | solution.py:1344
  639.8 21.1 %collective-permute-start.58 = (bf16[8,256,128]{2,1,0:T(8,128)(2,1)}, bf16[8,256,128]{2,1,0:T(8,128)(2,1)}, u32[]{:S(2)}, u32[]{:S(2)}) collective-permute-start(bf16[8,256,128]{2,1,0:T(8,128)(2,1)} %fusion.38), channel_id=1, source_target_pairs={{0,8},{4,12},{8,0},{12,4},{16,24},{20,28},{24,16},{28,20},{1,9},{5... | collective-permute-start | bytes 1572872 | tf_op jit(solution)/shard_map/ppermute | solution.py:46
  650.8 57.4 %collective-permute-start.35 = (bf16[4,6,256,128]{3,2,1,0:T(8,128)(2,1)}, bf16[4,6,256,128]{3,2,1,0:T(8,128)(2,1)}, u32[]{:S(2)}, u32[]{:S(2)}) collective-permute-start(bf16[4,6,256,128]{3,2,1,0:T(8,128)(2,1)} %fusion.25), channel_id=1, source_target_pairs={{0,2},{1,3},{2,0},{3,1},{4,6},{5,7},{6,4},{7,5},{8,10},{9,11},{10,... | collective-permute-start | bytes 4718600 | tf_op jit(solution)/shard_map/ppermute | solution.py:46
  660.9 18.8 %collective-permute-start.46 = (bf16[256,3072]{1,0:T(8,128)(2,1)S(1)}, bf16[256,3072]{1,0:T(8,128)(2,1)S(1)}, u32[]{:S(2)}, u32[]{:S(2)}) collective-permute-start(bf16[256,3072]{1,0:T(8,128)(2,1)S(1)} %reshape.413.latter_own), channel_id=1, source_target_pairs={{0,1},{1,0},{2,3},{3,2},{4,5},{5,4},{6,7},{7,6},{8,9},{9,8},{10,11... | collective-permute-start | bytes 4718600 | tf_op jit(solution)/shard_map/ppermute | solution.py:46
  668.4 19.7 %collective-permute-start.44 = (bf16[256,1024]{1,0:T(8,128)(2,1)S(1)}, bf16[256,1024]{1,0:T(8,128)(2,1)S(1)}, u32[]{:S(2)}, u32[]{:S(2)}) collective-permute-start(bf16[256,1024]{1,0:T(8,128)(2,1)S(1)} %copy-done.6), channel_id=1, source_target_pairs={{0,1},{1,0},{2,3},{3,2},{4,5},{5,4},{6,7},{7,6},{8,9},{9,8},{10,11... | collective-permute-start | bytes 1572872 | tf_op jit(solution)/shard_map/ppermute | solution.py:46
  675.4 3.8 collective-permute-start.38
  679.2 103.3 %collective-permute-start.52 = (bf16[4,8,256,128]{3,2,1,0:T(8,128)(2,1)}, bf16[4,8,256,128]{3,2,1,0:T(8,128)(2,1)}, u32[]{:S(2)}, u32[]{:S(2)}) collective-permute-start(bf16[4,8,256,128]{3,2,1,0:T(8,128)(2,1)} %fusion.21), channel_id=1, source_target_pairs={{0,4},{4,0},{8,12},{12,8},{16,20},{20,16},{24,28},{28,24},{1,5},{5... | collective-permute-start | bytes 6291464 | tf_op jit(solution)/shard_map/ppermute | solution.py:46
  679.8 32.6 %collective-permute-start.39 = (f32[4,1024]{1,0:T(4,128)S(1)}, f32[4,1024]{1,0:T(4,128)S(1)}, u32[]{:S(2)}, u32[]{:S(2)}) collective-permute-start(f32[4,1024]{1,0:T(4,128)S(1)} %fusion.49), channel_id=1, source_target_pairs={{0,2},{1,3},{2,0},{3,1},{4,6},{5,7},{6,4},{7,5},{8,10},{9,11},{10,... | collective-permute-start | bytes 49160 | tf_op jit(solution)/shard_map/ppermute | solution.py:46
  692.4 96.6 %collective-permute-start.47 = (bf16[2,4,4,256,128]{4,3,2,1,0:T(8,128)(2,1)}, bf16[2,4,4,256,128]{4,3,2,1,0:T(8,128)(2,1)}, u32[]{:S(2)}, u32[]{:S(2)}) collective-permute-start(bf16[2,4,4,256,128]{4,3,2,1,0:T(8,128)(2,1)} %get-tuple-element.88), channel_id=1, source_target_pairs={{0,4},{4,0},{8,12},{12,8},{16,20},{20,16},{24,28},{28,24},{1,5},{5... | collective-permute-start | bytes 6291464 | tf_op jit(solution)/shard_map/ppermute | solution.py:46
  711.9 69.3 %collective-permute-start.36 = (bf16[2,6,256,128]{3,2,1,0:T(8,128)(2,1)}, bf16[2,6,256,128]{3,2,1,0:T(8,128)(2,1)}, u32[]{:S(2)}, u32[]{:S(2)}) collective-permute-start(bf16[2,6,256,128]{3,2,1,0:T(8,128)(2,1)} %slice.283), channel_id=1, source_target_pairs={{0,16},{4,20},{8,24},{12,28},{16,0},{20,4},{24,8},{28,12},{1,17},{... | collective-permute-start | bytes 2359304 | tf_op jit(solution)/shard_map/ppermute | solution.py:46
  712.4 60.3 %collective-permute-start.40 = (f32[4,1024]{1,0:T(4,128)S(1)}, f32[4,1024]{1,0:T(4,128)S(1)}, u32[]{:S(2)}, u32[]{:S(2)}) collective-permute-start(f32[4,1024]{1,0:T(4,128)S(1)} %fusion.91), channel_id=1, source_target_pairs={{0,4},{4,0},{8,12},{12,8},{16,20},{20,16},{24,28},{28,24},{1,5},{5... | collective-permute-start | bytes 49160 | tf_op jit(solution)/shard_map/ppermute | solution.py:46
  772.7 3.7 collective-permute-start.41
  776.5 4.6 collective-permute-start.42
  785.7 46.2 %collective-permute-start.53 = (bf16[2,8,256,128]{3,2,1,0:T(8,128)(2,1)S(1)}, bf16[2,8,256,128]{3,2,1,0:T(8,128)(2,1)S(1)}, u32[]{:S(2)}, u32[]{:S(2)}) collective-permute-start(bf16[2,8,256,128]{3,2,1,0:T(8,128)(2,1)S(1)} %slice.300), channel_id=1, source_target_pairs={{0,16},{4,20},{8,24},{12,28},{16,0},{20,4},{24,8},{28,12},{1,17},{... | collective-permute-start | bytes 3145736 | tf_op jit(solution)/shard_map/ppermute | solution.py:46
  787.5 29.4 %collective-permute-start.37 = (bf16[6,256,128]{2,1,0:T(8,128)(2,1)S(1)}, bf16[6,256,128]{2,1,0:T(8,128)(2,1)S(1)}, u32[]{:S(2)}, u32[]{:S(2)}) collective-permute-start(bf16[6,256,128]{2,1,0:T(8,128)(2,1)S(1)} %fusion.41), channel_id=1, source_target_pairs={{0,8},{4,12},{8,0},{12,4},{16,24},{20,28},{24,16},{28,20},{1,9},{5... | collective-permute-start | bytes 1179656 | tf_op jit(solution)/shard_map/ppermute | solution.py:46
  790.5 42.9 %collective-permute-start.48 = (bf16[4,4,256,128]{3,2,1,0:T(8,128)(2,1)S(1)}, bf16[4,4,256,128]{3,2,1,0:T(8,128)(2,1)S(1)}, u32[]{:S(2)}, u32[]{:S(2)}) collective-permute-start(bf16[4,4,256,128]{3,2,1,0:T(8,128)(2,1)S(1)} %fusion.32), channel_id=1, source_target_pairs={{0,2},{1,3},{2,0},{3,1},{4,6},{5,7},{6,4},{7,5},{8,10},{9,11},{10,... | collective-permute-start | bytes 3145736 | tf_op jit(solution)/shard_map/ppermute | solution.py:46
  833.0 21.7 %collective-permute-start.54 = (bf16[8,256,128]{2,1,0:T(8,128)(2,1)}, bf16[8,256,128]{2,1,0:T(8,128)(2,1)}, u32[]{:S(2)}, u32[]{:S(2)}) collective-permute-start(bf16[8,256,128]{2,1,0:T(8,128)(2,1)} %fusion.37), channel_id=1, source_target_pairs={{0,8},{4,12},{8,0},{12,4},{16,24},{20,28},{24,16},{28,20},{1,9},{5... | collective-permute-start | bytes 1572872 | tf_op jit(solution)/shard_map/ppermute | solution.py:46
  835.9 26.8 %collective-permute-start.49 = (bf16[2,4,256,128]{3,2,1,0:T(8,128)(2,1)}, bf16[2,4,256,128]{3,2,1,0:T(8,128)(2,1)}, u32[]{:S(2)}, u32[]{:S(2)}) collective-permute-start(bf16[2,4,256,128]{3,2,1,0:T(8,128)(2,1)} %slice.291), channel_id=1, source_target_pairs={{0,16},{4,20},{8,24},{12,28},{16,0},{20,4},{24,8},{28,12},{1,17},{... | collective-permute-start | bytes 1572872 | tf_op jit(solution)/shard_map/ppermute | solution.py:46
  864.0 7.4 collective-permute-start.50
  (75 other events, 1294.3 us)

commit v4 on v3

--- a/solution.py
+++ b/solution.py
@@ -646,12 +646,29 @@
     )(packed, grads, head_marks(width))
 
 
+BITS = {"y": ("mp", 2), "x": ("seq", 1), "n": ("seq", 2), "f": ("seq", 4)}
+
+
 def grad_order(place):
-    seqs = [place.seq ^ (2 * spot + 1 - side) for side in range(2) for spot in range(4)]
-    return jnp.stack([place.mp ^ 2, place.mp] + seqs + [place.seq]).astype(jnp.int32)
-
-
-def grad_rows_kernel(mp_first, wide, order_ref, far_own, far_rec, own_own, own_rec, latter_own, latter_rec, *refs):
+    flips = []
+    for bits in ((1, 2, 4), (2, 1, 4), (1, 2, 4)):
+        for step in range(8):
+            flips.append(sum(bit for at, bit in enumerate(bits) if not (step >> (2 - at)) & 1))
+    return jnp.stack(
+        [place.mp ^ 2, place.mp] + [place.seq ^ flip for flip in flips] + [place.seq]
+    ).astype(jnp.int32)
+
+
+STEPS = {"y": (2, "xnf"), "n": (10, "nxf"), "x": (18, "xnf")}
+OWN_SEQ = 26
+
+
+def keep_flags(order_ref, seq):
+    change = order_ref[OWN_SEQ] ^ seq
+    return {"x": 1 - (change & 1), "n": 1 - ((change >> 1) & 1), "f": 1 - ((change >> 2) & 1)}
+
+
+def grad_rows_kernel(stages, wide, order_ref, far_own, far_rec, own_own, own_rec, latter_own, latter_rec, *refs):
     send_ref, keep_ref, turned = refs[-3:]
     rows = latter_own.shape[0]
     height = far_own.shape[1]
@@ -663,62 +680,51 @@
             turned[height * at : height * (at + 1), rows:] = rec[...].T
 
     total = matmul(turned[:, :rows], latter_own[...]) + matmul(turned[:, rows:], latter_rec[...])
-    grad_rows_store(mp_first, wide, order_ref, total.astype(BF), height, send_ref, keep_ref)
-
-
-def grad_rows_store(mp_first, wide, order_ref, total, height, send_ref, keep_ref):
+    store = grad_store_wide if wide else grad_store
+    store(stages, order_ref, total.astype(BF), height, send_ref, keep_ref)
+
+
+def grad_store_wide(stages, order_ref, total, height, send_ref, keep_ref):
     units = height // TILE
-    if wide:
-        chunks = total.shape[1] // 8 // LANES
-        for seq in range(8):
-            change = order_ref[10] ^ seq
-            side = 1 - (change & 1)
-            spot = change >> 1
-            for chunk in range(chunks):
-                first = (seq * chunks + chunk) * LANES
-                value = total[:, first : first + LANES]
-                for unit in range(units):
-                    given = value[unit * TILE : (unit + 1) * TILE]
-                    kept = value[height + unit * TILE : height + (unit + 1) * TILE]
-                    at = chunk * units + unit
-                    if mp_first:
-                        send_ref[side, spot, at] = given
-                        keep_ref[side, spot, at] = kept
-                    else:
-
-                        @pl.when(side == 0)
-                        def _(given=given, kept=kept, at=at, spot=spot):
-                            send_ref[0, spot, at] = given
-                            send_ref[1, spot, at] = kept
-
-                        @pl.when(side == 1)
-                        def _(given=given, kept=kept, at=at, spot=spot):
-                            keep_ref[0, spot, at] = given
-                            keep_ref[1, spot, at] = kept
-
-        return
+    chunks = total.shape[1] // 8 // LANES
+    for seq in range(8):
+        flags = keep_flags(order_ref, seq)
+        for chunk in range(chunks):
+            first = (seq * chunks + chunk) * LANES
+            for unit in range(units):
+                at = chunk * units + unit
+                for kept in range(2):
+                    start = height * kept + unit * TILE
+                    value = total[start : start + TILE, first : first + LANES]
+                    spot = {**flags, "y": kept}
+                    where = tuple(spot[stage] for stage in stages[1:])
+                    for target, when in ((send_ref, 0), (keep_ref, 1)):
+
+                        @pl.when(spot[stages[0]] == when)
+                        def _(target=target, where=where, at=at, value=value):
+                            target[(*where, at)] = value
+
+
+def grad_store(stages, order_ref, total, height, send_ref, keep_ref):
     chunks = total.shape[1] // LANES
     for chunk in range(chunks):
         value = total[:, chunk * LANES : (chunk + 1) * LANES]
         given, kept = value[:height], value[height:]
-        if mp_first:
-            send_ref[0, 0, chunk] = given
-            keep_ref[0, 0, chunk] = kept
+        if stages[0] == "y":
+            send_ref[0, 0, 0, chunk] = given
+            keep_ref[0, 0, 0, chunk] = kept
         else:
-
-            @pl.when(pl.program_id(0) < 4)
-            def _(given=given, kept=kept, chunk=chunk):
-                send_ref[0, 0, chunk] = given
-                send_ref[1, 0, chunk] = kept
-
-            @pl.when(pl.program_id(0) >= 4)
-            def _(given=given, kept=kept, chunk=chunk):
-                keep_ref[0, 0, chunk] = given
-                keep_ref[1, 0, chunk] = kept
+            spots = [tuple(side if stage == "y" else 0 for stage in stages[1:]) for side in range(2)]
+            for target, when in ((send_ref, pl.program_id(0) < 4), (keep_ref, pl.program_id(0) >= 4)):
+
+                @pl.when(when)
+                def _(target=target, given=given, kept=kept, chunk=chunk):
+                    target[(*spots[0], chunk)] = given
+                    target[(*spots[1], chunk)] = kept
 
 
 def grad_buffers(units):
-    return [jax.ShapeDtypeStruct((2, 4, units, TILE, LANES), BF)] * 2
+    return [jax.ShapeDtypeStruct((2, 2, 2, units, TILE, LANES), BF)] * 2
 
 
 def grad_call(kernel, order, arrays, in_specs, out_specs, units, into, steps, scratch, flops, name):
@@ -745,7 +751,7 @@
     )(order, *arrays)
 
 
-def grad_rows(former, latter, order, mp_first, units, offset, into=None):
+def grad_rows(former, latter, order, stages, units, offset, into=None):
     rows, breadth = latter[0].shape
     height = former[0].shape[1] // 4
     wide = breadth // 8 == LANES
@@ -758,22 +764,36 @@
     ]
     if wide:
         latter_specs = [whole_block((rows, breadth))] * 2
-        block = (2, 4, 1, TILE, LANES)
-        out_specs = [pl.BlockSpec(block, lambda j, t: (0, 0, offset, 0, 0))] * 2
+        block = (2, 2, 2, 1, TILE, LANES)
+        out_specs = [pl.BlockSpec(block, lambda j, t: (0, 0, 0, offset, 0, 0))] * 2
     else:
-        latter_specs = [pl.BlockSpec((rows, breadth // 8), lambda j, t: (0, t[2 + j]))] * 2
         base = offset // chunks
-        if mp_first:
-            block = (1, 1, chunks, TILE, LANES)
-            out_specs = [pl.BlockSpec(block, lambda j, t: (j // 4, j % 4, base, 0, 0))] * 2
+        table, names = STEPS[stages[0]]
+        bits = {name: 2 - at for at, name in enumerate(names)}
+        if stages[0] == "y":
+            block = (1, 1, 1, chunks, TILE, LANES)
+
+            def where(j):
+                return tuple((j >> bits[stage]) & 1 for stage in stages[1:]) + (base, 0, 0)
+
+            out_specs = [pl.BlockSpec(block, lambda j, t: where(j))] * 2
         else:
-            block = (2, 1, chunks, TILE, LANES)
+            block = tuple(2 if stage == "y" else 1 for stage in stages[1:]) + (chunks, TILE, LANES)
+
+            def where(j):
+                return tuple(
+                    0 if stage == "y" else (j >> bits[stage]) & 1 for stage in stages[1:]
+                ) + (base, 0, 0)
+
             out_specs = [
-                pl.BlockSpec(block, lambda j, t: (0, jnp.minimum(j, 3), base, 0, 0)),
-                pl.BlockSpec(block, lambda j, t: (0, jnp.maximum(j - 4, 0), base, 0, 0)),
+                pl.BlockSpec(block, lambda j, t: where(jnp.minimum(j, 3))),
+                pl.BlockSpec(block, lambda j, t: where(jnp.maximum(j - 4, 0))),
             ]
+        latter_specs = [
+            pl.BlockSpec((rows, breadth // 8), lambda j, t: (0, t[table + j]))
+        ] * 2
     return grad_call(
-        functools.partial(grad_rows_kernel, mp_first, wide),
+        functools.partial(grad_rows_kernel, stages, wide),
         order,
         arrays,
         former_specs + latter_specs,
@@ -787,7 +807,7 @@
     )
 
 
-def grad_columns_kernel(order_ref, latter_own, latter_rec, former_own, former_rec, *refs):
+def grad_columns_kernel(stages, order_ref, latter_own, latter_rec, former_own, former_rec, *refs):
     send_ref, keep_ref, turned = refs[-3:]
     rows = latter_own.shape[0]
     step = pl.program_id(0)
@@ -805,32 +825,32 @@
         @pl.when(when)
         def _(target=target):
             for seq in range(8):
-                change = order_ref[10] ^ seq
-                side = 1 - (change & 1)
-                spot = change >> 1
+                flags = keep_flags(order_ref, seq)
+                where = tuple(flags[stage] for stage in stages[1:])
                 for chunk in range(chunks):
-                    target[side, spot, chunk // 2, (chunk % 2) * LANES : (chunk % 2 + 1) * LANES] = total[
+                    half = (chunk % 2) * LANES
+                    target[(*where, chunk // 2, slice(half, half + LANES))] = total[
                         seq * LANES : (seq + 1) * LANES, chunk * LANES : (chunk + 1) * LANES
                     ]
 
 
-def grad_columns(former, latter, order, units, offset, into=None):
+def grad_columns(former, latter, order, stages, units, offset, into=None):
     rows, breadth = latter[0].shape
     height = former[0].shape[1] // 4
     step = min(512, height)
     per = height // step
-    block = (2, 4, step // TILE, TILE, LANES)
+    block = (2, 2, 2, step // TILE, TILE, LANES)
     base = offset // (step // TILE)
     latter_specs = [
         pl.BlockSpec((rows, breadth), lambda j, t: (0, 0), pipeline_mode=pl.Buffered(1))
     ] * 2
     former_specs = [pl.BlockSpec((rows, step), lambda j, t: (0, t[j // per] * per + j % per))] * 2
     out_specs = [
-        pl.BlockSpec(block, lambda j, t: (0, 0, base + jnp.minimum(j, per - 1), 0, 0)),
-        pl.BlockSpec(block, lambda j, t: (0, 0, base + jnp.maximum(j - per, 0), 0, 0)),
+        pl.BlockSpec(block, lambda j, t: (0, 0, 0, base + jnp.minimum(j, per - 1), 0, 0)),
+        pl.BlockSpec(block, lambda j, t: (0, 0, 0, base + jnp.maximum(j - per, 0), 0, 0)),
     ]
     return grad_call(
-        grad_columns_kernel,
+        functools.partial(grad_columns_kernel, stages),
         order,
         [latter[0], latter[1], former[0], former[1]],
         latter_specs + former_specs,
@@ -844,7 +864,7 @@
     )
 
 
-def grad_table_kernel(height, order_ref, codes_ref, latter_own, latter_rec, *refs):
+def grad_table_kernel(stages, height, order_ref, codes_ref, latter_own, latter_rec, *refs):
     send_ref, keep_ref, _ = refs[-3:]
     rows = latter_own.shape[0]
     parts = []
@@ -853,19 +873,19 @@
         parts.append((entry == codes_ref[...]).astype(F32).astype(BF))
     chosen = jnp.concatenate(parts, axis=0)
     total = matmul(chosen[:, :rows], latter_own[...]) + matmul(chosen[:, rows:], latter_rec[...])
-    grad_rows_store(False, True, order_ref, total.astype(BF), height, send_ref, keep_ref)
-
-
-def grad_table(codes, latter, order, height, units, offset, into=None):
+    grad_store_wide(stages, order_ref, total.astype(BF), height, send_ref, keep_ref)
+
+
+def grad_table(codes, latter, order, stages, height, units, offset, into=None):
     rows, breadth = latter[0].shape
-    block = (2, 4, height // TILE, TILE, LANES)
+    block = (2, 2, 2, height // TILE, TILE, LANES)
     base = offset // (height // TILE)
     return grad_call(
-        functools.partial(grad_table_kernel, height),
+        functools.partial(grad_table_kernel, stages, height),
         order,
         [codes, latter[0], latter[1]],
         [whole_block(codes.shape), whole_block((rows, breadth)), whole_block((rows, breadth))],
-        [pl.BlockSpec(block, lambda j, t: (0, 0, base, 0, 0))] * 2,
+        [pl.BlockSpec(block, lambda j, t: (0, 0, 0, base, 0, 0))] * 2,
         units,
         into,
         1,
@@ -875,18 +895,6 @@
     )
 
 
-def reduce_blocks(send, keep, mp_first):
-    stages = (("mp", 2), ("seq", 1)) if mp_first else (("seq", 1), ("mp", 2))
-    first = swap(send, *stages[0])
-    given = (keep[0].astype(F32) + first[0].astype(F32)).astype(BF)
-    second = swap(given, *stages[1])
-    total = (keep[1].astype(F32) + first[1].astype(F32) + second.astype(F32)).astype(BF)
-    far = swap(total[2:], "seq", 4)
-    total = total[:2].astype(F32) + far.astype(F32)
-    near = swap(total[1].astype(BF), "seq", 2)
-    return total[0] + near.astype(F32)
-
-
 def rows_from_units(units, height):
     tiles = height // TILE
     chunks = units.shape[0] // tiles
@@ -900,114 +908,129 @@
     return jnp.transpose(units.reshape(2 * count, LANES, LANES), (0, 2, 1)).reshape(count * TILE, LANES)
 
 
-def join_kernel(layout, place_ref, *refs):
-    count = len(layout)
-    own, other, first, second, first_other, second_other = refs[:6]
-    outs = refs[6 : 6 + count]
-    held = refs[6 + count : 6 + 2 * count]
-    sems, out_sems = refs[-2:]
-    half = first.shape[0]
-    width = own.shape[1]
-    me = place_ref[0]
-    low = place_ref[1]
+PACK = 1024
+
+
+def pack_rows(members):
+    return sum(member.shape[0] * (member.shape[1] // PACK) for member in members)
+
+
+def pack_pieces(shapes):
+    found, start = [], 0
+    for at, (height, breadth) in enumerate(shapes):
+        for column in range(breadth // PACK):
+            found.append((at, column, height, start))
+            start += height
+    return found
+
+
+def columns_of(column):
+    return pl.ds(column * PACK, PACK)
+
+
+def pack_kernel(place_ref, *refs):
+    members, (pack_ref, quarter_ref, held, sems, out_sems) = refs[:-5], refs[-5:]
+    rows = held.shape[0] // 4
     copies = []
-    for at, (height, breadth, start) in enumerate(layout):
-        for column in range(breadth // width):
-            row = start + column * height
-            columns = pl.ds(column * width, width)
-            for flip, source in ((0, own), (1, other)):
-                target = held[at].at[pl.ds(pl.multiple_of((me ^ flip) * height, height), height), columns]
-                copies.append((at, None, source.at[pl.ds(row, height)], target))
-            for flip, sources in ((2, (first, second)), (3, (first_other, second_other))):
-                for side in range(2):
-                    begin, end = max(row, side * half), min(row + height, (side + 1) * half)
-                    if begin >= end:
-                        continue
-                    rows = pl.ds(begin - side * half, end - begin)
-                    target = held[at].at[
-                        pl.ds(pl.multiple_of((me ^ flip) * height + begin - row, 16), end - begin), columns
-                    ]
-                    copies.append((at, side, sources[0].at[rows], target))
-                    copies.append((at, 1 - side, sources[1].at[rows], target))
-
-    def act(action, number):
-        _, when, source, target = copies[number]
-        copy = pltpu.make_async_copy(source, target, sems.at[number])
-        if when is None:
-            getattr(copy, action)()
-        else:
-
-            @pl.when(low == when)
-            def _():
-                getattr(copy, action)()
-
-    for number in range(len(copies)):
-        act("start", number)
-    for at in range(count):
-        for number in range(len(copies)):
-            if copies[number][0] == at:
-                act("wait", number)
-        pltpu.make_async_copy(held[at], outs[at], out_sems.at[at]).start()
-    for at in range(count):
-        pltpu.make_async_copy(held[at], outs[at], out_sems.at[at]).wait()
-
-
-def join_count(layout, half, width):
-    count = 0
-    for height, breadth, start in layout:
-        for column in range(breadth // width):
-            row = start + column * height
-            count += 2
-            for side in range(2):
-                if max(row, side * half) < min(row + height, (side + 1) * half):
-                    count += 4
-    return count
-
-
-def pack_weights(shards):
-    width = 1024
-    pieces = []
-    for shard in shards:
-        for column in range(shard.shape[1] // width):
-            pieces.append(shard[:, column * width : (column + 1) * width])
-    return pieces[0] if len(pieces) == 1 else jnp.concatenate(pieces, axis=0)
-
-
-def pack_layout(shards):
-    layout, start = [], 0
-    for shard in shards:
-        height, breadth = shard.shape
-        layout.append((height, breadth, start))
-        start += height * (breadth // 1024)
-    return tuple(layout), start
-
-
-def join_weights(pack, other, first, second, first_other, second_other, layout, place):
-    half, width = first.shape
+    for number, (at, column, height, start) in enumerate(pack_pieces([m.shape for m in members])):
+        copies.append(
+            pltpu.make_async_copy(
+                members[at].at[:, columns_of(column)], held.at[pl.ds(start, height)], sems.at[number]
+            )
+        )
+    for copy in copies:
+        copy.start()
+    for copy in copies:
+        copy.wait()
+    mine = pl.ds(pl.multiple_of(place_ref[1] * rows, 16), rows)
+    whole = pltpu.make_async_copy(held, pack_ref, out_sems.at[0])
+    part = pltpu.make_async_copy(held.at[mine], quarter_ref, out_sems.at[1])
+    part.start()
+    whole.start()
+    part.wait()
+    whole.wait()
+
+
+def pack_call(members, spots):
+    rows = pack_rows(members)
     any_spec = pl.BlockSpec(memory_space=pl.ANY)
-    outs = [jax.ShapeDtypeStruct((4 * height, breadth), BF) for height, breadth, _ in layout]
+    count = len(pack_pieces([m.shape for m in members]))
     return pl.pallas_call(
-        functools.partial(join_kernel, layout),
-        in_specs=[pl.BlockSpec(memory_space=pltpu.SMEM)] + [any_spec] * 6,
+        pack_kernel,
+        in_specs=[pl.BlockSpec(memory_space=pltpu.SMEM)] + [any_spec] * len(members),
+        out_specs=[any_spec] * 2,
+        out_shape=[
+            jax.ShapeDtypeStruct((rows, PACK), BF),
+            jax.ShapeDtypeStruct((rows // 4, PACK), BF),
+        ],
+        scratch_shapes=[
+            pltpu.VMEM((rows, PACK), BF),
+            pltpu.SemaphoreType.DMA((count,)),
+            pltpu.SemaphoreType.DMA((2,)),
+        ],
+        compiler_params=pltpu.CompilerParams(vmem_limit_bytes=VMEM_LIMIT),
+        cost_estimate=pl.CostEstimate(flops=0, bytes_accessed=4 * rows * PACK, transcendentals=0),
+        name="pack_weights",
+    )(spots, *members)
+
+
+def join_kernel(shapes, parts, place_ref, *refs):
+    count = len(parts)
+    sources = refs[:count]
+    outs = refs[count : count + len(shapes)]
+    held, sems, out_sems = refs[-3:]
+    rows = held.shape[0] // 4
+    quarter = rows // 4
+    copies = []
+    for number, (source, (flip, change, offset)) in enumerate(zip(sources, parts)):
+        start = (place_ref[0] ^ flip) * rows + offset
+        if change is not None:
+            start = start + (place_ref[1] ^ change) * quarter
+        size = source.shape[0]
+        copies.append(
+            pltpu.make_async_copy(
+                source, held.at[pl.ds(pl.multiple_of(start, 16), size)], sems.at[number]
+            )
+        )
+    for copy in copies:
+        copy.start()
+    for copy in copies:
+        copy.wait()
+    copies = []
+    for at, column, height, start in pack_pieces(shapes):
+        for block in range(4):
+            copies.append(
+                pltpu.make_async_copy(
+                    held.at[pl.ds(block * rows + start, height)],
+                    outs[at].at[pl.ds(block * height, height), columns_of(column)],
+                    out_sems.at[len(copies)],
+                )
+            )
+    for copy in copies:
+        copy.start()
+    for copy in copies:
+        copy.wait()
+
+
+def join_weights(members, pieces, parts, spots):
+    shapes = [member.shape for member in members]
+    rows = pack_rows(members)
+    any_spec = pl.BlockSpec(memory_space=pl.ANY)
+    outs = [jax.ShapeDtypeStruct((4 * height, breadth), BF) for height, breadth in shapes]
+    return pl.pallas_call(
+        functools.partial(join_kernel, shapes, parts),
+        in_specs=[pl.BlockSpec(memory_space=pltpu.SMEM)] + [any_spec] * len(pieces),
         out_specs=[any_spec] * len(outs),
         out_shape=outs,
-        scratch_shapes=[pltpu.VMEM(out.shape, BF) for out in outs]
-        + [
-            pltpu.SemaphoreType.DMA((join_count(layout, half, width),)),
-            pltpu.SemaphoreType.DMA((len(outs),)),
+        scratch_shapes=[
+            pltpu.VMEM((4 * rows, PACK), BF),
+            pltpu.SemaphoreType.DMA((len(pieces),)),
+            pltpu.SemaphoreType.DMA((4 * len(pack_pieces(shapes)),)),
         ],
         compiler_params=pltpu.CompilerParams(vmem_limit_bytes=VMEM_LIMIT),
-        cost_estimate=pl.CostEstimate(flops=0, bytes_accessed=16 * pack.size, transcendentals=0),
+        cost_estimate=pl.CostEstimate(flops=0, bytes_accessed=16 * rows * PACK, transcendentals=0),
         name="join_weights",
-    )(
-        jnp.stack([place.mp, place.seq_low]).astype(jnp.int32),
-        pack,
-        other,
-        first,
-        second,
-        first_other,
-        second_other,
-    )
+    )(spots, *pieces)
 
 
 def shards_general(
@@ -1161,21 +1184,89 @@
     )
 
 
-def tie(values, *after):
-    flat, tree = jax.tree.flatten(values)
-    held = lax.optimization_barrier(tuple(flat) + tuple(after))
-    return jax.tree.unflatten(tree, held[: len(flat)])
-
-
-def start_pack(pack, place, *after):
-    half = pack.shape[0] // 2
-    mine = lax.dynamic_slice(pack, (place.seq_low * half, 0), (half, pack.shape[1]))
-    if after:
-        pack, mine = tie((pack, mine), *after)
-    first = swap(mine, "mp", 2)
-    other = swap(pack, "mp", 1)
-    second = swap(first, "seq", 1)
-    return [pack, other, first, second, swap(first, "mp", 1), swap(second, "mp", 1)]
+class Chain:
+    def __init__(self):
+        self.last = ()
+
+    def enter(self, *values):
+        held = lax.optimization_barrier(tuple(values) + self.last)
+        return held[0] if len(values) == 1 else held[: len(values)]
+
+    def leave(self, *values):
+        self.last = values
+
+
+class Gather:
+    def __init__(self, members, spots, whole=False):
+        self.members = members
+        self.spots = spots
+        self.whole = whole
+        self.pack, self.quarter = pack_call(members, spots)
+        self.pieces = [self.pack]
+        self.parts = [(0, None, 0)]
+
+    def add(self, piece, change, offset):
+        self.pieces += [piece, swap(piece, "mp", 1)]
+        self.parts += [(2, change, offset), (3, change, offset)]
+
+    def start(self, chain):
+        self.far = swap(chain.enter(self.pack if self.whole else self.quarter), "mp", 2)
+        self.pieces.append(swap(self.pack, "mp", 1))
+        self.parts.append((1, None, 0))
+
+    def spread(self, chain):
+        far = chain.enter(self.far)
+        chain.leave(far)
+        if self.whole:
+            self.add(far, None, 0)
+            return
+        self.over_x = swap(far, "seq", 1)
+        self.over_n = swap(far, "seq", 2)
+        self.add(far, 0, 0)
+
+    def cross(self, chain):
+        over_x, over_n = chain.enter(self.over_x, self.over_n)
+        chain.leave(over_x, over_n)
+        half = over_x.shape[0] // 2
+        self.ends = (swap(over_n[:half], "seq", 1), swap(over_x[half:], "seq", 2))
+        self.add(over_x, 1, 0)
+        self.add(over_n, 2, 0)
+
+    def close(self, chain):
+        ends = chain.enter(*self.ends)
+        chain.leave(*ends)
+        self.add(ends[0], 3, 0)
+        self.add(ends[1], 3, ends[0].shape[0])
+
+    def join(self, chain):
+        pieces = chain.enter(*self.pieces)
+        outs = join_weights(self.members, pieces, tuple(self.parts), self.spots)
+        chain.leave(*outs)
+        return outs
+
+
+class Reduce:
+    def __init__(self, stages, blocks):
+        self.stages = stages
+        self.keep = blocks[1]
+        self.came = [swap(blocks[0], *BITS[stages[0]])]
+
+    def total(self, last):
+        at = len(self.came) - 1
+        spot = (1,) * at + ((0,) if not last else ())
+        value = self.keep[spot].astype(F32) if spot else self.keep.astype(F32)
+        for level, came in enumerate(self.came):
+            value = value + came[spot[level:]].astype(F32)
+        return value
+
+    def step(self, chain):
+        self.keep, *self.came = chain.enter(self.keep, *self.came)
+        given = self.total(False).astype(BF)
+        chain.leave(given)
+        self.came.append(swap(given, *BITS[self.stages[len(self.came)]]))
+
+    def result(self):
+        return self.total(True)
 
 
 def pair(values):
@@ -1184,8 +1275,7 @@
 
 def hidden_grads(contract_in, expanded, weights):
     active_grad = inner_right(contract_in, weights[5])
-    expand_in = jax.vjp(jax.nn.gelu, expanded)[1](active_grad)[0].astype(BF)
-    return expand_in, inner_right(expand_in, weights[4])
+    return jax.vjp(jax.nn.gelu, expanded)[1](active_grad)[0].astype(BF)
 
 
 def mixed_grads(result_grad, normed_grad, mixed_sum, weights):
@@ -1216,30 +1306,21 @@
     cotangent,
 ):
     place = Place()
+    chain = Chain()
     order = grad_order(place)
+    spots = jnp.stack([place.mp, place.seq % 4]).astype(jnp.int32)
     row_count, frames_dev, width = frames.shape
     frame_total = row_count * frames_dev
     positions = cotangent.shape[2]
+    count = place.seq_count
 
     gain_rows = jnp.pad(
         jnp.concatenate([frame_prenorm, frame_postnorm, codec_prenorm, codec_postnorm])[None],
-        ((0, 31), (0, 0)),
-    )
-    packs = (
-        [frame_project, gain_rows],
-        [frame_expand, frame_contract, frame_output],
-        [codec_project, codebooks],
-        [codec_expand, codec_contract, codec_output],
-    )
-    pieces = []
-    for members in packs:
-        pack = pack_weights(members)
-        pieces.append(start_pack(pack, place, *([pieces[-1][2]] if pieces else [])))
-
-    def joined(at):
-        return join_weights(*pieces[at], pack_layout(packs[at])[0], place)
-
-    count = place.seq_count
+        ((0, 127), (0, 0)),
+    )
+    first = Gather([frame_project, gain_rows], spots)
+    first.start(chain)
+    chain.leave(first.quarter)
     every_segment = lax.all_to_all(
         jnp.broadcast_to(segments[None], (count, row_count, frames_dev)),
         "seq",
@@ -1253,133 +1334,209 @@
     )
     codes_both = jnp.concatenate(pair(codes), axis=1)
     live = padding.reshape(frame_total).astype(F32)[None, :, None]
+    second = Gather([frame_expand, frame_contract, frame_output], spots)
+    first.spread(chain)
+    second.start(chain)
     codec_grad = (
-        jnp.transpose(cotangent.reshape(frame_total, positions, width), (1, 0, 2)).astype(F32) * live
+        jnp.transpose(
+            chain.enter(cotangent).reshape(frame_total, positions, width), (1, 0, 2)
+        ).astype(F32)
+        * live
     ).reshape(positions * frame_total, width)
     contract_in = pair(codec_grad.astype(BF))
-
-    weight_project, gains = joined(0)
+    chain.leave(contract_in[0])
+    first.cross(chain)
+    third = Gather([codec_project, codebooks], spots, True)
+    fourth = Gather([codec_expand, codec_contract, codec_output], spots)
+    first.close(chain)
+
+    weight_project, gains = first.join(chain)
     gains = jnp.transpose(
-        gains.reshape(place.mp_count, 32, 4, -1)[:, 0], (1, 0, 2)
+        gains.reshape(place.mp_count, -1, 4, width // 4)[:, 0], (1, 0, 2)
     ).reshape(4, width)
     hidden = frames.astype(F32).reshape(frame_total, width)
     normed, projected = front_pass(hidden, (gains[0], weight_project))
-    normed_both = pair(normed)
     packed = jnp.transpose(
         projected.reshape(row_count, frames_dev, 3, count, LANES), (3, 0, 1, 2, 4)
     ).reshape(count, row_count, frames_dev, 3 * LANES)
+    chain.leave(packed)
     packed = lax.all_to_all(packed, "seq", split_axis=0, concat_axis=0, tiled=True)
-    attended = lax.all_to_all(
-        frame_attend_call(packed, every_segment), "seq", split_axis=0, concat_axis=0, tiled=True
-    )
-    attended = jnp.transpose(attended, (1, 2, 0, 3)).reshape(frame_total, width)
+    second.spread(chain)
+    fourth.start(chain)
+    second.cross(chain)
+    third.start(chain)
+    packed = chain.enter(packed)
+    attended = frame_attend_call(packed, every_segment)
+    chain.leave(attended)
+    attended = lax.all_to_all(attended, "seq", split_axis=0, concat_axis=0, tiled=True)
+    fourth.spread(chain)
+    second.close(chain)
+    weight_expand, weight_contract, weight_output = second.join(chain)
+    frame_weights = (gains[0], weight_project, weight_output, gains[1], weight_expand, weight_contract)
+    attended = jnp.transpose(chain.enter(attended), (1, 2, 0, 3)).reshape(frame_total, width)
+    frame_result, frame_saved = rear_pass(hidden, attended, frame_weights)
+    base_low = frame_result.astype(BF)
+    chain.leave(base_low)
+    normed_both = pair(normed)
     attended_both = pair(attended)
-    weight_expand, weight_contract, weight_output = joined(1)
-    frame_weights = (gains[0], weight_project, weight_output, gains[1], weight_expand, weight_contract)
-    frame_result, frame_saved = rear_pass(hidden, attended, frame_weights)
     normed_two_both = pair(frame_saved[1])
     activated_both = pair(frame_saved[3])
-    base = frame_result.astype(BF).astype(F32)
-
-    weight_project, table = joined(2)
+
+    third.spread(chain)
+    fourth.cross(chain)
+    weight_project, table = third.join(chain)
     embedded = table[codes.reshape(positions - 1, frame_total)].astype(F32)
+    base = chain.enter(base_low).astype(F32)
     codec_hidden = jnp.concatenate([base[None], base[None] + embedded], axis=0).reshape(
         positions * frame_total, width
     )
     codec_normed, codec_projected = front_pass(codec_hidden, (gains[2], weight_project))
+    codec_packed = codec_projected.reshape(positions, frame_total, 3 * width)
+    chain.leave(codec_packed)
+    fourth.close(chain)
+    codec_attended = codec_attend_call(chain.enter(codec_packed)).reshape(
+        positions * frame_total, width
+    )
+    chain.leave(codec_attended)
     codec_normed_both = pair(codec_normed)
-    codec_packed = codec_projected.reshape(positions, frame_total, 3 * width)
-    codec_attended = codec_attend_call(codec_packed).reshape(positions * frame_total, width)
     codec_attended_both = pair(codec_attended)
-    weight_expand, weight_contract, weight_output = joined(3)
+    weight_expand, weight_contract, weight_output = fourth.join(chain)
     codec_weights = (gains[2], weight_project, weight_output, gains[3], weight_expand, weight_contract)
-    codec_result, codec_saved = rear_pass(codec_hidden, codec_attended, codec_weights)
-    codec_normed_two_both = pair(codec_saved[1])
-    codec_activated_both = pair(codec_saved[3])
+    mixed_sum = codec_hidden + matmul(chain.enter(codec_attended), weight_output)
+    normed_two = rms_scale(mixed_sum, gains[3].astype(F32)).astype(BF)
+    expanded = matmul(normed_two, weight_expand)
+    activated = jax.nn.gelu(expanded).astype(BF)
+
+    expand_in = hidden_grads(contract_in[0], expanded, codec_weights)
+    chain.leave(activated, expand_in)
+    activated_pair = pair(activated)
+    expand_pair = pair(expand_in)
+    codec_normed_two_both = pair(normed_two)
+    normed_grad = inner_right(chain.enter(expand_in), weight_expand)
+    chain.leave(normed_grad)
+    stages = tuple("ynxf")
+    blocks = grad_columns(chain.enter(*activated_pair), contract_in, order, stages, 4, 0)
+    chain.leave(*blocks)
+    contract_sum = Reduce(stages, blocks)
+    stages = tuple("xynf")
+    blocks = grad_rows(codec_normed_two_both, chain.enter(*expand_pair), order, stages, 4, 0)
+    chain.leave(*blocks)
+    expand_sum = Reduce(stages, blocks)
+    mixed_grad, attended_grad, codec_postnorm_grad, output_in = mixed_grads(
+        codec_grad, chain.enter(normed_grad), mixed_sum, codec_weights
+    )
+    chain.leave(attended_grad)
+    output_pair = pair(output_in)
+    codec_projected_grad = codec_attend_grads_call(
+        codec_packed, chain.enter(attended_grad).reshape(positions, frame_total, width)
+    ).reshape(positions * frame_total, 3 * width)
+    chain.leave(codec_projected_grad)
+    projected_pair = pair(codec_projected_grad)
+    input_grad, codec_prenorm_grad = front_grads(
+        codec_hidden, chain.enter(codec_projected_grad), mixed_grad, codec_weights
+    )
+    input_grad = input_grad.reshape(positions, frame_total, width)
+    base_grad = jnp.sum(input_grad, axis=0).astype(BF)
+    table_in = input_grad[1:].reshape(-1, width).astype(BF)
+    chain.leave(base_grad, table_in)
+    table_pair = pair(table_in)
+
+    base_grad = chain.enter(base_grad)
+    contract_in = pair(base_grad)
+    base_grad = base_grad.astype(F32)
+    frame_expand_in = hidden_grads(contract_in[0], frame_saved[2], frame_weights)
+    chain.leave(frame_expand_in)
+    frame_expand_pair = pair(frame_expand_in)
+    contract_sum.step(chain)
+    normed_grad = inner_right(chain.enter(frame_expand_in), frame_weights[4])
+    frame_mixed_grad, frame_attended_grad, frame_postnorm_grad, output_in = mixed_grads(
+        base_grad, normed_grad, frame_saved[0], frame_weights
+    )
+    grads = jnp.transpose(
+        frame_attended_grad.reshape(row_count, frames_dev, count, LANES), (2, 0, 1, 3)
+    )
+    chain.leave(grads)
+    grads = lax.all_to_all(grads, "seq", split_axis=0, concat_axis=0, tiled=True)
+    frame_output_pair = pair(output_in)
+    expand_sum.step(chain)
+    stages = tuple("yxnf")
+    blocks = grad_columns(chain.enter(*activated_both), contract_in, order, stages, 4, 0)
+    chain.leave(*blocks)
+    frame_contract_sum = Reduce(stages, blocks)
+    stages = tuple("xynf")
+    blocks = grad_rows(normed_two_both, chain.enter(*frame_expand_pair), order, stages, 5, 0)
+    blocks = grad_rows(attended_both, frame_output_pair, order, stages, 5, 4, blocks)
+    chain.leave(*blocks)
+    frame_expand_sum = Reduce(stages, blocks)
+    contract_sum.step(chain)
+    packed_grad = frame_attend_grads_call(packed, chain.enter(grads), every_segment)
+    chain.leave(packed_grad)
+    packed_grad = lax.all_to_all(packed_grad, "seq", split_axis=0, concat_axis=0, tiled=True)
+    expand_sum.step(chain)
+    contract_sum.step(chain)
+    stages = tuple("nyxf")
+    blocks = grad_rows(codec_normed_both, chain.enter(*projected_pair), order, stages, 6, 0)
+    blocks = grad_rows(codec_attended_both, output_pair, order, stages, 6, 3, blocks)
+    blocks = grad_table(codes_both, table_pair, order, stages, codebooks.shape[0], 6, 4, blocks)
+    chain.leave(*blocks)
+    codec_sum = Reduce(stages, blocks)
+    frame_contract_sum.step(chain)
+    expand_sum.step(chain)
+    codec_result = mixed_sum + matmul(chain.enter(activated), weight_contract)
     output = jnp.transpose(
         (codec_result.reshape(positions, frame_total, width) * live).astype(BF), (1, 0, 2)
     ).reshape(row_count, frames_dev, positions, width)
-
-    expand_in, normed_grad = hidden_grads(contract_in[0], codec_saved[2], codec_weights)
-    codec_one = grad_columns(codec_activated_both, contract_in, order, 8, 4)
-    codec_one = grad_rows(codec_normed_two_both, pair(expand_in), order, True, 8, 0, codec_one)
-    normed_grad = tie(normed_grad, *codec_one)
-    mixed_grad, attended_grad, codec_postnorm_grad, output_in = mixed_grads(
-        codec_grad, normed_grad, codec_saved[0], codec_weights
-    )
-    codec_one = reduce_blocks(*codec_one, True)
-    output_in = pair(output_in)
-    codec_projected_grad = codec_attend_grads_call(
-        codec_packed, attended_grad.reshape(positions, frame_total, width)
-    ).reshape(positions * frame_total, 3 * width)
-    codec_two = grad_rows(codec_normed_both, pair(codec_projected_grad), order, False, 6, 0)
-    codec_two = grad_rows(codec_attended_both, output_in, order, False, 6, 3, codec_two)
-    input_grad, codec_prenorm_grad = front_grads(
-        codec_hidden, codec_projected_grad, mixed_grad, codec_weights
-    )
-    input_grad = input_grad.reshape(positions, frame_total, width)
-    table_in = pair(input_grad[1:].reshape(-1, width).astype(BF))
-    codec_two = grad_table(codes_both, table_in, order, codebooks.shape[0], 6, 4, codec_two)
-    base_grad = tie(jnp.sum(input_grad, axis=0).astype(BF), *codec_two).astype(F32)
-    codec_two = reduce_blocks(*codec_two, False)
-
-    contract_in = pair(base_grad.astype(BF))
-    expand_in, normed_grad = hidden_grads(contract_in[0], frame_saved[2], frame_weights)
-    frame_mixed_grad, frame_attended_grad, frame_postnorm_grad, output_in = mixed_grads(
-        base_grad, normed_grad, frame_saved[0], frame_weights
-    )
-    grads = lax.all_to_all(
-        jnp.transpose(
-            frame_attended_grad.reshape(row_count, frames_dev, count, LANES), (2, 0, 1, 3)
-        ),
-        "seq",
-        split_axis=0,
-        concat_axis=0,
-        tiled=True,
-    )
-    frame_one = grad_columns(activated_both, contract_in, order, 8, 4)
-    frame_one = grad_rows(normed_two_both, pair(expand_in), order, True, 8, 0, frame_one)
-    grads = tie(grads, *frame_one)
-    frame_one = reduce_blocks(*frame_one, True)
-    packed_grad = lax.all_to_all(
-        frame_attend_grads_call(packed, grads, every_segment),
-        "seq",
-        split_axis=0,
-        concat_axis=0,
-        tiled=True,
-    )
+    chain.leave(output)
+    frame_expand_sum.step(chain)
     frame_projected_grad = jnp.transpose(
-        packed_grad.reshape(count, row_count, frames_dev, 3, LANES), (1, 2, 3, 0, 4)
+        chain.enter(packed_grad).reshape(count, row_count, frames_dev, 3, LANES), (1, 2, 3, 0, 4)
     ).reshape(frame_total, 3 * width)
-    frame_two = grad_rows(normed_both, pair(frame_projected_grad), order, False, 4, 0)
-    frame_two = grad_rows(attended_both, pair(output_in), order, False, 4, 3, frame_two)
-    frame_two = reduce_blocks(*frame_two, False)
+    frame_projected_pair = pair(frame_projected_grad)
+    chain.leave(frame_projected_grad)
     frames_grad, frame_prenorm_grad = front_grads(
-        hidden, frame_projected_grad, frame_mixed_grad, frame_weights
-    )
+        hidden, chain.enter(frame_projected_grad), frame_mixed_grad, frame_weights
+    )
+    chain.leave(frames_grad)
+    stages = tuple("nxyf")
+    blocks = grad_rows(normed_both, chain.enter(*frame_projected_pair), order, stages, 3, 0)
+    chain.leave(*blocks)
+    frame_project_sum = Reduce(stages, blocks)
     gain_sums = sum_everywhere(
         jnp.stack(
             [frame_prenorm_grad, frame_postnorm_grad, codec_prenorm_grad, codec_postnorm_grad]
         ),
         place,
     )
+    frame_contract_sum.step(chain)
+    codec_sum.step(chain)
+    frame_expand_sum.step(chain)
+    frame_contract_sum.step(chain)
+    codec_sum.step(chain)
+    frame_project_sum.step(chain)
+    frame_expand_sum.step(chain)
+    frame_project_sum.step(chain)
+    codec_sum.step(chain)
+    frame_project_sum.step(chain)
+
     height = frame_project.shape[0]
+    codec_two = codec_sum.result()
+    frame_one = frame_expand_sum.result()
     return (
         output,
         frames_grad.reshape(row_count, frames_dev, width),
         rows_from_units(codec_two[4:], codebooks.shape[0]),
         gain_sums[0],
-        rows_from_units(frame_two[:3], height),
-        rows_from_units(frame_two[3:], height),
+        rows_from_units(frame_project_sum.result(), height),
+        rows_from_units(frame_one[4:], height),
         gain_sums[1],
         rows_from_units(frame_one[:4], height),
-        columns_from_units(frame_one[4:]),
+        columns_from_units(frame_contract_sum.result()),
         gain_sums[2],
         rows_from_units(codec_two[:3], height),
         rows_from_units(codec_two[3:4], height),
         gain_sums[3],
-        rows_from_units(codec_one[:4], height),
-        columns_from_units(codec_one[4:]),
+        rows_from_units(expand_sum.result(), height),
+        columns_from_units(contract_sum.result()),
     )
 
 

time: 886 us -> 808 us (0.912)
  waiting for transfers between devices: 378 us -> 276 us
  local copies, waits for them, and re-layouts: 93.2 us -> 68.4 us
  starting transfers between devices: 67.2 us -> 89.3 us
  other arithmetic: 55.3 us -> 70.5 us
  Pallas kernels: 157 us -> 169 us
    ppermute x59 -> x83, waiting for transfers between devices: 368 us -> 276 us  [swap(): lax.ppermute(values, axis, [(i, i ^ bit) for i in range(lax.axis_size(axi...]
    ppermute x59 -> x83, starting transfers between devices: 40.5 us -> 63.2 us  [swap(): lax.ppermute(values, axis, [(i, i ^ bit) for i in range(lax.axis_size(axi...]
    pallas_call x4 -> x8, Pallas kernels: 38.9 us -> 52.8 us  [the longest x4 41.2 us: join_weights(): pl.pallas_call(functools.partial(join_kernel, shapes, parts), in_specs=[p...]
    unnamed x172 -> x195, local copies, waits for them, and re-layouts: 44.1 us -> 31.3 us
    convert_element_type x8 -> x20, other arithmetic: 23.8 us -> 36.3 us  [the longest x18 35.3 us: step(): given = self.total(False).astype(BF)]
    all_to_all x3, waiting for transfers between devices: 9.66 us -> 0.01 us  [the longest x1 0.01 us: shards(): lax.all_to_all(attended, 'seq', split_axis=0, concat_axis=0, tiled=True)]
  transfers between devices with their start and end apart: 64 -> 88, of which waited for: 24 -> 28; matrix products, arithmetic and copies ran while one was open for 24% -> 24% of each run, Pallas kernels for 14% -> 19%
where the time goes in v4:
time: 808 us; the launch traced here: 797 us
  waiting for transfers between devices  276 us (34%)
  Pallas kernels  169 us (21%)
  matrix products  121 us (15%)
  starting transfers between devices  89.3 us (11%)
  other arithmetic  70.5 us (9%)
  local copies, waits for them, and re-layouts  68.4 us (8%)
    ppermute x83, waiting for transfers between devices, swap(): lax.ppermute(values, axis, [(i, i ^ bit) for i in range(lax.axis_size(axi...  276 us
    pallas_call x9, Pallas kernels, grad_call(): pl.pallas_call(kernel, grid_spec=pltpu.PrefetchScalarGridSpec(num_scalar_...  77 us
    dot_general x8, matrix products, matmul(): return jnp.dot(former, latter, preferred_element_type=F32)  65.1 us
    ppermute x83, starting transfers between devices, swap(): lax.ppermute(values, axis, [(i, i ^ bit) for i in range(lax.axis_size(axi...  63.2 us
    dot_general x8, matrix products, inner_right(): lax.dot_general(former, latter, (((1,), (1,)), ((), ())), preferred_eleme...  56.1 us
    pallas_call x4, Pallas kernels, join_weights(): pl.pallas_call(functools.partial(join_kernel, shapes, parts), in_specs=[p...  41.2 us
    convert_element_type x18, other arithmetic, step(): given = self.total(False).astype(BF)  35.3 us
    unnamed x195, local copies, waits for them, and re-layouts  31.3 us
  transfers between devices with their start and end apart: 88, of which 28 were waited for; matrix products, arithmetic and copies ran while one was open for 24% of the time, Pallas kernels for 19%

profile of v4, /device:TPU:0, one launch (start us, length us, event | category | flops | bytes accessed | tf_op | source)
XLA Modules:
  0.0 796.9 jit_solution(3008299183430539731)
XLA Ops:
  9.0 10.5 %collective-permute-done.1.refs_2_ = bf16[224,1024]{1,0:T(8,128)(2,1)} collective-permute-done((bf16[224,1024]{1,0:T(8,128)(2,1)S(1)}, bf16[224,1024]{1,0:T(8,128)(2,1)}, u32[]{:S(2)}, u32[]{:S(2)}) %collective-permute-start.1) | collective-permute-done | bytes 458784 | tf_op jit(solution)/shard_map/ppermute | solution.py:46
  26.3 5.7 collective-permute-done.3.refs_4_
  36.2 3.3 collective-permute-done.7.refs_8_
  40.1 4.9 all-to-all-start.1
  48.4 3.5 pack_weights.5
  54.2 6.5 join_weights.4
  63.0 4.8 fusion.19
  70.0 2.7 copy.66
  72.7 5.8 all-to-all-start
  87.2 3.4 pack_weights.6
  92.1 31.1 %collective-permute-done.12.refs_4_ = bf16[576,1024]{1,0:T(8,128)(2,1)S(1)} collective-permute-done((bf16[576,1024]{1,0:T(8,128)(2,1)}, bf16[576,1024]{1,0:T(8,128)(2,1)S(1)}, u32[]{:S(2)}, u32[]{:S(2)}) %collective-permute-start.12) | collective-permute-done | bytes 1179680 | tf_op jit(solution)/shard_map/ppermute | solution.py:46
  123.3 8.6 %collective-permute-done.13.refs_6_ = bf16[576,1024]{1,0:T(8,128)(2,1)} collective-permute-done((bf16[576,1024]{1,0:T(8,128)(2,1)}, bf16[576,1024]{1,0:T(8,128)(2,1)}, u32[]{:S(2)}, u32[]{:S(2)}) %collective-permute-start.13) | collective-permute-done | bytes 1179680 | tf_op jit(solution)/shard_map/ppermute | solution.py:46
  136.8 10.5 %collective-permute-done.18.refs_8_ = bf16[288,1024]{1,0:T(8,128)(2,1)S(1)} collective-permute-done((bf16[288,1024]{1,0:T(8,128)(2,1)S(1)}, bf16[288,1024]{1,0:T(8,128)(2,1)S(1)}, u32[]{:S(2)}, u32[]{:S(2)}) %collective-permute-start.18) | collective-permute-done | bytes 589856 | tf_op jit(solution)/shard_map/ppermute | solution.py:46
  150.0 9.6 %frame_attend.1 = bf16[8,2,128,128]{3,2,1,0:T(8,128)(2,1)S(1)} custom-call(bf16[8,2,128,384]{3,2,1,0:T(8,128)(2,1)} %all-to-all-done.packed_ref, s32[2,1024,1]{2,1,0:T(8,128)S(1)} %copy-done.24, s32[2,1,1024]{2,1,0:T(1,128)S(1)} %bitcast.328), custom_call_target="tpu_custom_call" | custom-call | flops 1342177280 | bytes 2359296 | tf_op jit(solution)/shard_map/frame_attend/pallas_call | solution.py:461
  160.5 4.9 all-to-all-start.2
  170.4 13.0 %join_weights.5 = (bf16[1024,4096]{1,0:T(8,128)(2,1)}, bf16[4096,1024]{1,0:T(8,128)(2,1)}, bf16[1024,1024]{1,0:T(8,128)(2,1)}) custom-call(s32[2]{0:T(128)S(1)} %pad_add_fusion.1.place_ref, bf16[2304,1024]{1,0:T(8,128)(2,1)} %get-tuple-element.224.refs_0_, bf16[2304,1024]{1,0:T(8,128)(2,1)} %collective-permute-done.14.refs_1_, ...), custom_call_target="tpu_custom_call" | custom-call | bytes 37748736 | tf_op jit(solution)/shard_map/join_weights/pallas_call | solution.py:1020
  188.5 9.5 %multiply_convert_fusion.1 = (bf16[256,4096]{1,0:T(8,128)(2,1)S(1)}, f32[256,4096]{1,0:T(8,128)}) fusion(bf16[256,1024]{1,0:T(8,128)(2,1)} %multiply_convert_fusion.5.far_own.own_own, bf16[1024,4096]{1,0:T(8,128)(2,1)} %get-tuple-element.236), kind=kOutput, calls=%fused_computation.23 | convolution fusion | flops 2156920832 | bytes 15204352 | tf_op jit(solution)/shard_map/dot_general | solution.py:30
  200.4 28.8 %collective-permute-done.24.refs_2_ = bf16[1280,1024]{1,0:T(8,128)(2,1)} collective-permute-done((bf16[1280,1024]{1,0:T(8,128)(2,1)}, bf16[1280,1024]{1,0:T(8,128)(2,1)}, u32[]{:S(2)}, u32[]{:S(2)}) %collective-permute-start.24) | collective-permute-done | bytes 2621472 | tf_op jit(solution)/shard_map/ppermute | solution.py:46
  233.1 24.8 %collective-permute-done.26.refs_4_ = bf16[576,1024]{1,0:T(8,128)(2,1)S(1)} collective-permute-done((bf16[576,1024]{1,0:T(8,128)(2,1)}, bf16[576,1024]{1,0:T(8,128)(2,1)S(1)}, u32[]{:S(2)}, u32[]{:S(2)}) %collective-permute-start.26) | collective-permute-done | bytes 1179680 | tf_op jit(solution)/shard_map/ppermute | solution.py:46
  262.3 8.7 %join_weights.6 = (bf16[1024,3072]{1,0:T(8,128)(2,1)}, bf16[2048,1024]{1,0:T(8,128)(2,1)}) custom-call(s32[2]{0:T(128)S(1)} %pad_add_fusion.1.place_ref, bf16[1280,1024]{1,0:T(8,128)(2,1)} %get-tuple-element.245.refs_0_, bf16[1280,1024]{1,0:T(8,128)(2,1)} %collective-permute-done.23.refs_1_, bf16[1280,1024]{1,0:T(8,128)(2,1)} %collective-permute-done.24.refs_2_, ...), custom_call_target="tpu_custom_call" | custom-call | bytes 20971520 | tf_op jit(solution)/shard_map/join_weights/pallas_call | solution.py:1020
  271.1 5.5 gather_fusion
  279.0 3.4 multiply_convert_fusion.4.far_own.own_own
  284.0 9.2 %convolution_convert_fusion = bf16[768,3072]{1,0:T(8,128)(2,1)} fusion(bf16[768,1024]{1,0:T(8,128)(2,1)} %multiply_convert_fusion.4.far_own.own_own, bf16[1024,3072]{1,0:T(8,128)(2,1)} %get-tuple-element.249), kind=kOutput, calls=%fused_computation.13 | convolution fusion | flops 4834197504 | bytes 12582912 | tf_op jit(solution)/shard_map/dot_general | solution.py:30
  293.2 4.4 collective-permute-done.29.refs_10_
  298.4 6.0 codec_attend.1
  304.4 13.0 %join_weights.7 = (bf16[1024,4096]{1,0:T(8,128)(2,1)}, bf16[4096,1024]{1,0:T(8,128)(2,1)}, bf16[1024,1024]{1,0:T(8,128)(2,1)}) custom-call(s32[2]{0:T(128)S(1)} %pad_add_fusion.1.place_ref, bf16[2304,1024]{1,0:T(8,128)(2,1)} %get-tuple-element.256.refs_0_, bf16[2304,1024]{1,0:T(8,128)(2,1)} %collective-permute-done.30.refs_1_, ...), custom_call_target="tpu_custom_call" | custom-call | bytes 37748736 | tf_op jit(solution)/shard_map/join_weights/pallas_call | solution.py:1020
  317.4 12.7 %fusion.61 = f32[768,4096]{1,0:T(8,128)} fusion(bf16[768,1024]{1,0:T(8,128)(2,1)S(1)} %copy-done.17, bf16[4096,1024]{1,0:T(8,128)(2,1)} %get-tuple-element.269), kind=kOutput, calls=%fused_computation.177 | convolution fusion | flops 6442450944 | bytes 22544384 | tf_op jit(solution)/shard_map/dot_general | solution.py:38
  332.4 23.7 %fusion.6 = (bf16[768,4096]{1,0:T(8,128)(2,1)}, bf16[768,4096]{1,0:T(8,128)(2,1)}) fusion(f32[768,4096]{1,0:T(8,128)} %fusion.61, bf16[768,1024]{1,0:T(8,128)(2,1)S(1)} %multiply_convert_fusion.3.far_own.own_own, bf16[1024,4096]{1,0:T(8,128)(2,1)} %get-tuple-element.268), kind=kOutput, calls=%fused_computation.9 | convolution fusion | flops 6511656960 | bytes 35127296 | tf_op jit(solution)/shard_map/dot_general | solution.py:30
  357.4 11.4 %fusion.62 = f32[768,1024]{1,0:T(8,128)S(1)} fusion(bf16[768,4096]{1,0:T(8,128)(2,1)} %get-tuple-element.277.latter_own, bf16[1024,4096]{1,0:T(8,128)(2,1)} %get-tuple-element.268), kind=kOutput, calls=%fused_computation.178 | convolution fusion | flops 6442450944 | bytes 17825792 | tf_op jit(solution)/shard_map/dot_general | solution.py:38
  370.0 12.0 %grad_columns.2 = (bf16[2,2,2,4,256,128]{5,4,3,2,1,0:T(8,128)(2,1)}, bf16[2,2,2,4,256,128]{5,4,3,2,1,0:T(8,128)(2,1)}) custom-call(s32[27]{0:T(128)S(1)} %stack.76.order_ref, bf16[768,1024]{1,0:T(8,128)(2,1)S(1)} %copy-done.18, bf16[768,1024]{1,0:T(8,128)(2,1)S(1)} %collective-permute-done.38.latter_rec, bf16[768,4096]{1,0:T(8,128)(2,1)} %get-tuple-element.324.former_own, ...), custom_call_target="tpu_custom_call" | custom-call | flops 6442450944 | bytes 15728640 | tf_op jit(solution)/shard_map/grad_columns/pallas_call | solution.py:737
  382.5 13.9 %grad_rows.6 = (bf16[2,2,2,4,256,128]{5,4,3,2,1,0:T(8,128)(2,1)}, bf16[2,2,2,4,256,128]{5,4,3,2,1,0:T(8,128)(2,1)}) custom-call(s32[27]{0:T(128)S(1)} %stack.76.order_ref, bf16[768,1024]{1,0:T(8,128)(2,1)S(1)} %copy-done.20, bf16[768,1024]{1,0:T(8,128)(2,1)S(1)} %collective-permute-done.36.far_rec.own_rec, bf16[768,1024]{1,0:T(8,128)(2,1)S(1)} %copy-done.20, ...), custom_call_target="tpu_custom_call" | custom-call | flops 6442450944 | bytes 18874368 | tf_op jit(solution)/shard_map/grad_rows/pallas_call | solution.py:737
  404.0 8.7 %codec_attend_grads.1 = bf16[3,256,3072]{2,1,0:T(8,128)(2,1)} custom-call(bf16[3,256,3072]{2,1,0:T(8,128)(2,1)} %bitcast.331, bf16[3,256,1024]{2,1,0:T(8,128)(2,1)S(1)} %bitcast.327, bf16[1024,128]{1,0:T(8,128)(2,1)S(1)} %fusion.46.marks_ref), custom_call_target="tpu_custom_call" | custom-call | flops 2348810240 | bytes 11796480 | tf_op jit(solution)/shard_map/codec_attend_grads/pallas_call | solution.py:631
  412.8 9.3 %multiply_reduce_fusion.1 = (f32[1024]{0:T(1024)S(1)}, f32[768]{0:T(1024)S(1)}, f32[768,1024]{1,0:T(8,128)S(1)}) fusion(f32[3,256,1024]{2,1,0:T(8,128)S(1)} %copy-done.39, f32[768]{0:T(1024)S(1)} %rsqrt.46, f32[1024]{0:T(1024)S(1)} %bitcast.370, bf16[768,3072]{1,0:T(8,128)(2,1)} %bitcast.339, bf16[1024,3072]{1,0:T(8,128)(2,1)} %get-tuple-element.249), kind=kOutput, calls=%fused_computation.36 | convolution fusion | flops 4836554752 | bytes 17315840 | tf_op jit(solution)/shard_map/dot_general | solution.py:38
  425.7 3.1 reduce_sum.125.latter_own
  428.8 10.6 %fusion.13.latter_own = bf16[256,4096]{1,0:T(8,128)(2,1)} fusion(f32[256,4096]{1,0:T(8,128)} %get-tuple-element.422, bf16[256,1024]{1,0:T(8,128)(2,1)} %reduce_sum.125.latter_own, bf16[4096,1024]{1,0:T(8,128)(2,1)} %get-tuple-element.237), kind=kOutput, calls=%fused_computation.22 | convolution fusion | flops 2168455168 | bytes 15204352 | tf_op jit(solution)/shard_map/dot_general | solution.py:38
  443.4 4.2 multiply_reduce_fusion.5
  453.1 4.4 all-to-all-start.3
  460.0 7.3 grad_columns.3
  470.2 9.4 %grad_rows.7 = (bf16[2,2,2,5,256,128]{5,4,3,2,1,0:T(8,128)(2,1)}, bf16[2,2,2,5,256,128]{5,4,3,2,1,0:T(8,128)(2,1)}) custom-call(s32[27]{0:T(128)S(1)} %stack.76.order_ref, bf16[256,1024]{1,0:T(8,128)(2,1)} %multiply_convert_fusion.5.far_own.own_own, bf16[256,1024]{1,0:T(8,128)(2,1)} %collective-permute-done.46.far_rec.own_rec, ...), custom_call_target="tpu_custom_call" | custom-call | flops 2147483648 | bytes 6291456 | tf_op jit(solution)/shard_map/grad_rows/pallas_call | solution.py:737
  493.9 7.0 collective-permute-done.58
  502.9 14.9 %frame_attend_grads.1 = bf16[8,2,128,384]{3,2,1,0:T(8,128)(2,1)S(1)} custom-call(bf16[8,2,128,384]{3,2,1,0:T(8,128)(2,1)} %all-to-all-done.packed_ref, bf16[8,2,128,128]{3,2,1,0:T(8,128)(2,1)} %all-to-all-done.3.grad_ref, s32[2,1024,1]{2,1,0:T(8,128)S(1)} %copy-done.25, s32[2,1,1024]{2,1,0:T(1,128)S(1)} %bitcast.329), custom_call_target="tpu_custom_call" | custom-call | flops 3221225472 | bytes 3932160 | tf_op jit(solution)/shard_map/frame_attend_grads/pallas_call | solution.py:480
  519.0 6.2 all-to-all-start.4
  531.1 13.2 %grad_rows.9 = (bf16[2,2,2,6,256,128]{5,4,3,2,1,0:T(8,128)(2,1)}, bf16[2,2,2,6,256,128]{5,4,3,2,1,0:T(8,128)(2,1)}) custom-call(s32[27]{0:T(128)S(1)} %stack.76.order_ref, bf16[768,1024]{1,0:T(8,128)(2,1)} %multiply_convert_fusion.4.far_own.own_own, bf16[768,1024]{1,0:T(8,128)(2,1)} %collective-permute-done.56.far_rec.own_rec, ...), custom_call_target="tpu_custom_call" | custom-call | flops 4831838208 | bytes 15728640 | tf_op jit(solution)/shard_map/grad_rows/pallas_call | solution.py:737
  545.8 5.4 grad_rows.10
  551.2 4.8 grad_table.1
  556.6 2.9 fusion.28
  559.4 6.8 collective-permute-done.50
  569.0 11.1 %convolution_add_fusion = f32[768,1024]{1,0:T(8,128)S(1)} fusion(f32[768,1024]{1,0:T(8,128)S(1)} %copy-done.37, bf16[768,4096]{1,0:T(8,128)(2,1)} %get-tuple-element.324.former_own, bf16[4096,1024]{1,0:T(8,128)(2,1)} %get-tuple-element.269), kind=kOutput, calls=%fused_computation.50 | convolution fusion | flops 6443237376 | bytes 20971520 | tf_op jit(solution)/shard_map/dot_general | solution.py:30
  581.7 18.7 %collective-permute-done.59 = bf16[2,2,2,5,256,128]{5,4,3,2,1,0:T(8,128)(2,1)S(1)} collective-permute-done((bf16[2,2,2,5,256,128]{5,4,3,2,1,0:T(8,128)(2,1)S(1)}, bf16[2,2,2,5,256,128]{5,4,3,2,1,0:T(8,128)(2,1)S(1)}, u32[]{:S(2)}, u32[]{:S(2)}) %collective-permute-start.59) | collective-permute-done | bytes 2621472 | tf_op jit(solution)/shard_map/ppermute | solution.py:46
  606.0 2.9 copy.73
  608.9 3.7 reshape.519.latter_own
  616.2 5.3 multiply_reduce_fusion.6
  621.6 2.7 fusion.25
  625.4 8.5 %grad_rows.11 = (bf16[2,2,2,3,256,128]{5,4,3,2,1,0:T(8,128)(2,1)}, bf16[2,2,2,3,256,128]{5,4,3,2,1,0:T(8,128)(2,1)S(1)}) custom-call(s32[27]{0:T(128)S(1)} %stack.76.order_ref, bf16[256,1024]{1,0:T(8,128)(2,1)S(1)} %copy-done.29, bf16[256,1024]{1,0:T(8,128)(2,1)S(1)} %collective-permute-done.62.far_rec.own_rec, bf16[256,1024]{1,0:T(8,128)(2,1)S(1)} %copy-done.29, ...), custom_call_target="tpu_custom_call" | custom-call | flops 1610612736 | bytes 5242880 | tf_op jit(solution)/shard_map/grad_rows/pallas_call | solution.py:737
  634.0 6.6 collective-permute-done.61
  643.1 3.1 fusion.17
  650.2 38.6 %collective-permute-done.73 = f32[4,1024]{1,0:T(4,128)S(1)} collective-permute-done((f32[4,1024]{1,0:T(4,128)S(1)}, f32[4,1024]{1,0:T(4,128)S(1)}, u32[]{:S(2)}, u32[]{:S(2)}) %collective-permute-start.73) | collective-permute-done | bytes 16416 | tf_op jit(solution)/shard_map/ppermute | solution.py:46
  697.0 2.8 copy.80
  702.2 3.6 collective-permute-done.81
  712.3 11.4 %collective-permute-done.65 = bf16[2,4,256,128]{3,2,1,0:T(8,128)(2,1)} collective-permute-done((bf16[2,4,256,128]{3,2,1,0:T(8,128)(2,1)}, bf16[2,4,256,128]{3,2,1,0:T(8,128)(2,1)}, u32[]{:S(2)}, u32[]{:S(2)}) %collective-permute-start.65) | collective-permute-done | bytes 524320 | tf_op jit(solution)/shard_map/ppermute | solution.py:46
  730.7 7.2 collective-permute-done.70
  744.6 11.0 %collective-permute-done.79 = bf16[5,256,128]{2,1,0:T(8,128)(2,1)} collective-permute-done((bf16[5,256,128]{2,1,0:T(8,128)(2,1)}, bf16[5,256,128]{2,1,0:T(8,128)(2,1)}, u32[]{:S(2)}, u32[]{:S(2)}) %collective-permute-start.79) | collective-permute-done | bytes 327712 | tf_op jit(solution)/shard_map/ppermute | solution.py:46
  765.4 14.6 %collective-permute-done.71 = bf16[6,256,128]{2,1,0:T(8,128)(2,1)S(1)} collective-permute-done((bf16[6,256,128]{2,1,0:T(8,128)(2,1)S(1)}, bf16[6,256,128]{2,1,0:T(8,128)(2,1)S(1)}, u32[]{:S(2)}, u32[]{:S(2)}) %collective-permute-start.71) | collective-permute-done | bytes 393248 | tf_op jit(solution)/shard_map/ppermute | solution.py:46
  785.4 8.9 %collective-permute-done.78 = bf16[3,256,128]{2,1,0:T(8,128)(2,1)S(1)} collective-permute-done((bf16[3,256,128]{2,1,0:T(8,128)(2,1)S(1)}, bf16[3,256,128]{2,1,0:T(8,128)(2,1)S(1)}, u32[]{:S(2)}, u32[]{:S(2)}) %collective-permute-start.78) | collective-permute-done | bytes 196640 | tf_op jit(solution)/shard_map/ppermute | solution.py:46
  (451 shorter events, 200.1 us)
Async XLA Ops:
  5.2 49.0 %collective-permute-start = (bf16[896,1024]{1,0:T(8,128)(2,1)}, bf16[896,1024]{1,0:T(8,128)(2,1)}, u32[]{:S(2)}, u32[]{:S(2)}) collective-permute-start(bf16[896,1024]{1,0:T(8,128)(2,1)} %get-tuple-element.198.refs_0_), channel_id=1, source_target_pairs={{0,1},{1,0},{2,3},{3,2},{4,5},{5,4},{6,7},{7,6},{8,9},{9,8},{10,11... | collective-permute-start | bytes 5505032 | tf_op jit(solution)/shard_map/ppermute | solution.py:46
  22.8 22.4 %collective-permute-start.2 = (bf16[224,1024]{1,0:T(8,128)(2,1)}, bf16[224,1024]{1,0:T(8,128)(2,1)}, u32[]{:S(2)}, u32[]{:S(2)}) collective-permute-start(bf16[224,1024]{1,0:T(8,128)(2,1)} %collective-permute-done.1.refs_2_), channel_id=1, source_target_pairs={{0,1},{1,0},{2,3},{3,2},{4,5},{5,4},{6,7},{7,6},{8,9},{9,8},{10,11... | collective-permute-start | bytes 1376264 | tf_op jit(solution)/shard_map/ppermute | solution.py:46
  36.1 18.0 %collective-permute-start.5 = (bf16[224,1024]{1,0:T(8,128)(2,1)S(1)}, bf16[224,1024]{1,0:T(8,128)(2,1)}, u32[]{:S(2)}, u32[]{:S(2)}) collective-permute-start(bf16[224,1024]{1,0:T(8,128)(2,1)S(1)} %collective-permute-done.3.refs_4_), channel_id=1, source_target_pairs={{0,1},{1,0},{2,3},{3,2},{4,5},{5,4},{6,7},{7,6},{8,9},{9,8},{10,11... | collective-permute-start | bytes 1376264 | tf_op jit(solution)/shard_map/ppermute | solution.py:46
  40.1 32.6 %all-to-all-start.1 = ((s32[8,2,128]{2,1,0:T(2,128)}), s32[8,2,128]{2,1,0:T(2,128)S(1)}, u32[]{:S(2)}, u32[]{:S(2)}) async-start(s32[8,2,128]{2,1,0:T(2,128)} %broadcast_in_dim.19), calls=%async_computation.1 | async-start | bytes 16384 | tf_op jit(solution)/shard_map/all_to_all | solution.py:1324
  52.4 118.0 %collective-permute-start.14 = (bf16[2304,1024]{1,0:T(8,128)(2,1)}, bf16[2304,1024]{1,0:T(8,128)(2,1)}, u32[]{:S(2)}, u32[]{:S(2)}) collective-permute-start(bf16[2304,1024]{1,0:T(8,128)(2,1)} %get-tuple-element.224.refs_0_), channel_id=1, source_target_pairs={{0,1},{1,0},{2,3},{3,2},{4,5},{5,4},{6,7},{7,6},{8,9},{9,8},{10,11... | collective-permute-start | bytes 14155784 | tf_op jit(solution)/shard_map/ppermute | solution.py:46
  52.7 28.5 %collective-permute-start.11 = (bf16[576,1024]{1,0:T(8,128)(2,1)}, bf16[576,1024]{1,0:T(8,128)(2,1)}, u32[]{:S(2)}, u32[]{:S(2)}) collective-permute-start(bf16[576,1024]{1,0:T(8,128)(2,1)} %get-tuple-element.213), channel_id=1, source_target_pairs={{0,2},{1,3},{2,0},{3,1},{4,6},{5,7},{6,4},{7,5},{8,10},{9,11},{10,... | collective-permute-start | bytes 3538952 | tf_op jit(solution)/shard_map/ppermute | solution.py:46
  72.7 76.0 %all-to-all-start = ((bf16[8,2,128,384]{3,2,1,0:T(8,128)(2,1)}), bf16[8,2,128,384]{3,2,1,0:T(8,128)(2,1)}, u32[]{:S(2)}, u32[]{:S(2)}) async-start(bf16[8,2,128,384]{3,2,1,0:T(8,128)(2,1)} %copy.66), calls=%async_computation | async-start | bytes 3145728 | tf_op jit(solution)/shard_map/all_to_all | solution.py:1363
  81.1 42.2 %collective-permute-start.12 = (bf16[576,1024]{1,0:T(8,128)(2,1)}, bf16[576,1024]{1,0:T(8,128)(2,1)S(1)}, u32[]{:S(2)}, u32[]{:S(2)}) collective-permute-start(bf16[576,1024]{1,0:T(8,128)(2,1)} %collective-permute-done.11.refs_2_), channel_id=1, source_target_pairs={{0,4},{4,0},{8,12},{12,8},{16,20},{20,16},{24,28},{28,24},{1,5},{5... | collective-permute-start | bytes 3538952 | tf_op jit(solution)/shard_map/ppermute | solution.py:46
  83.1 48.8 %collective-permute-start.13 = (bf16[576,1024]{1,0:T(8,128)(2,1)}, bf16[576,1024]{1,0:T(8,128)(2,1)}, u32[]{:S(2)}, u32[]{:S(2)}) collective-permute-start(bf16[576,1024]{1,0:T(8,128)(2,1)} %collective-permute-done.11.refs_2_), channel_id=1, source_target_pairs={{0,8},{4,12},{8,0},{12,4},{16,24},{20,28},{24,16},{28,20},{1,9},{5... | collective-permute-start | bytes 3538952 | tf_op jit(solution)/shard_map/ppermute | solution.py:46
  90.6 45.3 %collective-permute-start.20 = (bf16[576,1024]{1,0:T(8,128)(2,1)S(1)}, bf16[576,1024]{1,0:T(8,128)(2,1)}, u32[]{:S(2)}, u32[]{:S(2)}) collective-permute-start(bf16[576,1024]{1,0:T(8,128)(2,1)S(1)} %get-tuple-element.220), channel_id=1, source_target_pairs={{0,2},{1,3},{2,0},{3,1},{4,6},{5,7},{6,4},{7,5},{8,10},{9,11},{10,... | collective-permute-start | bytes 3538952 | tf_op jit(solution)/shard_map/ppermute | solution.py:46
  134.5 31.2 %collective-permute-start.15 = (bf16[576,1024]{1,0:T(8,128)(2,1)}, bf16[576,1024]{1,0:T(8,128)(2,1)}, u32[]{:S(2)}, u32[]{:S(2)}) collective-permute-start(bf16[576,1024]{1,0:T(8,128)(2,1)} %collective-permute-done.11.refs_2_), channel_id=1, source_target_pairs={{0,1},{1,0},{2,3},{3,2},{4,5},{5,4},{6,7},{7,6},{8,9},{9,8},{10,11... | collective-permute-start | bytes 3538952 | tf_op jit(solution)/shard_map/ppermute | solution.py:46
  134.5 35.3 %collective-permute-start.16 = (bf16[576,1024]{1,0:T(8,128)(2,1)S(1)}, bf16[576,1024]{1,0:T(8,128)(2,1)}, u32[]{:S(2)}, u32[]{:S(2)}) collective-permute-start(bf16[576,1024]{1,0:T(8,128)(2,1)S(1)} %collective-permute-done.12.refs_4_), channel_id=1, source_target_pairs={{0,1},{1,0},{2,3},{3,2},{4,5},{5,4},{6,7},{7,6},{8,9},{9,8},{10,11... | collective-permute-start | bytes 3538952 | tf_op jit(solution)/shard_map/ppermute | solution.py:46
  135.8 29.6 %collective-permute-start.19 = (bf16[288,1024]{1,0:T(8,128)(2,1)}, bf16[288,1024]{1,0:T(8,128)(2,1)}, u32[]{:S(2)}, u32[]{:S(2)}) collective-permute-start(bf16[288,1024]{1,0:T(8,128)(2,1)} %slice.311), channel_id=1, source_target_pairs={{0,8},{4,12},{8,0},{12,4},{16,24},{20,28},{24,16},{28,20},{1,9},{5... | collective-permute-start | bytes 1769480 | tf_op jit(solution)/shard_map/ppermute | solution.py:46
  147.3 23.0 %collective-permute-start.17 = (bf16[576,1024]{1,0:T(8,128)(2,1)}, bf16[576,1024]{1,0:T(8,128)(2,1)}, u32[]{:S(2)}, u32[]{:S(2)}) collective-permute-start(bf16[576,1024]{1,0:T(8,128)(2,1)} %collective-permute-done.13.refs_6_), channel_id=1, source_target_pairs={{0,1},{1,0},{2,3},{3,2},{4,5},{5,4},{6,7},{7,6},{8,9},{9,8},{10,11... | collective-permute-start | bytes 3538952 | tf_op jit(solution)/shard_map/ppermute | solution.py:46
  160.5 23.0 %all-to-all-start.2 = ((bf16[8,2,128,128]{3,2,1,0:T(8,128)(2,1)}), bf16[8,2,128,128]{3,2,1,0:T(8,128)(2,1)}, u32[]{:S(2)}, u32[]{:S(2)}) async-start(bf16[8,2,128,128]{3,2,1,0:T(8,128)(2,1)} %copy-done.30), calls=%async_computation.2 | async-start | bytes 1048576 | tf_op jit(solution)/shard_map/all_to_all | solution.py:1371
  169.8 59.4 %collective-permute-start.24 = (bf16[1280,1024]{1,0:T(8,128)(2,1)}, bf16[1280,1024]{1,0:T(8,128)(2,1)}, u32[]{:S(2)}, u32[]{:S(2)}) collective-permute-start(bf16[1280,1024]{1,0:T(8,128)(2,1)} %get-tuple-element.245.refs_0_), channel_id=1, source_target_pairs={{0,2},{1,3},{2,0},{3,1},{4,6},{5,7},{6,4},{7,5},{8,10},{9,11},{10,... | collective-permute-start | bytes 7864328 | tf_op jit(solution)/shard_map/ppermute | solution.py:46
  170.4 91.1 %collective-permute-start.23 = (bf16[1280,1024]{1,0:T(8,128)(2,1)}, bf16[1280,1024]{1,0:T(8,128)(2,1)}, u32[]{:S(2)}, u32[]{:S(2)}) collective-permute-start(bf16[1280,1024]{1,0:T(8,128)(2,1)} %get-tuple-element.245.refs_0_), channel_id=1, source_target_pairs={{0,1},{1,0},{2,3},{3,2},{4,5},{5,4},{6,7},{7,6},{8,9},{9,8},{10,11... | collective-permute-start | bytes 7864328 | tf_op jit(solution)/shard_map/ppermute | solution.py:46
  229.2 32.8 %collective-permute-start.25 = (bf16[1280,1024]{1,0:T(8,128)(2,1)}, bf16[1280,1024]{1,0:T(8,128)(2,1)}, u32[]{:S(2)}, u32[]{:S(2)}) collective-permute-start(bf16[1280,1024]{1,0:T(8,128)(2,1)} %collective-permute-done.24.refs_2_), channel_id=1, source_target_pairs={{0,1},{1,0},{2,3},{3,2},{4,5},{5,4},{6,7},{7,6},{8,9},{9,8},{10,11... | collective-permute-start | bytes 7864328 | tf_op jit(solution)/shard_map/ppermute | solution.py:46
  229.2 68.5 %collective-permute-start.30 = (bf16[2304,1024]{1,0:T(8,128)(2,1)}, bf16[2304,1024]{1,0:T(8,128)(2,1)}, u32[]{:S(2)}, u32[]{:S(2)}) collective-permute-start(bf16[2304,1024]{1,0:T(8,128)(2,1)} %get-tuple-element.256.refs_0_), channel_id=1, source_target_pairs={{0,1},{1,0},{2,3},{3,2},{4,5},{5,4},{6,7},{7,6},{8,9},{9,8},{10,11... | collective-permute-start | bytes 14155784 | tf_op jit(solution)/shard_map/ppermute | solution.py:46
  229.7 28.2 %collective-permute-start.26 = (bf16[576,1024]{1,0:T(8,128)(2,1)}, bf16[576,1024]{1,0:T(8,128)(2,1)S(1)}, u32[]{:S(2)}, u32[]{:S(2)}) collective-permute-start(bf16[576,1024]{1,0:T(8,128)(2,1)} %collective-permute-done.20.refs_2_), channel_id=1, source_target_pairs={{0,4},{4,0},{8,12},{12,8},{16,20},{20,16},{24,28},{28,24},{1,5},{5... | collective-permute-start | bytes 3538952 | tf_op jit(solution)/shard_map/ppermute | solution.py:46
  231.6 27.9 %collective-permute-start.27 = (bf16[576,1024]{1,0:T(8,128)(2,1)}, bf16[576,1024]{1,0:T(8,128)(2,1)}, u32[]{:S(2)}, u32[]{:S(2)}) collective-permute-start(bf16[576,1024]{1,0:T(8,128)(2,1)} %collective-permute-done.20.refs_2_), channel_id=1, source_target_pairs={{0,8},{4,12},{8,0},{12,4},{16,24},{20,28},{24,16},{28,20},{1,9},{5... | collective-permute-start | bytes 3538952 | tf_op jit(solution)/shard_map/ppermute | solution.py:46
  257.9 46.4 %collective-permute-start.31 = (bf16[576,1024]{1,0:T(8,128)(2,1)}, bf16[576,1024]{1,0:T(8,128)(2,1)}, u32[]{:S(2)}, u32[]{:S(2)}) collective-permute-start(bf16[576,1024]{1,0:T(8,128)(2,1)} %collective-permute-done.20.refs_2_), channel_id=1, source_target_pairs={{0,1},{1,0},{2,3},{3,2},{4,5},{5,4},{6,7},{7,6},{8,9},{9,8},{10,11... | collective-permute-start | bytes 3538952 | tf_op jit(solution)/shard_map/ppermute | solution.py:46
  259.5 44.8 %collective-permute-start.32 = (bf16[576,1024]{1,0:T(8,128)(2,1)S(1)}, bf16[576,1024]{1,0:T(8,128)(2,1)}, u32[]{:S(2)}, u32[]{:S(2)}) collective-permute-start(bf16[576,1024]{1,0:T(8,128)(2,1)S(1)} %collective-permute-done.26.refs_4_), channel_id=1, source_target_pairs={{0,1},{1,0},{2,3},{3,2},{4,5},{5,4},{6,7},{7,6},{8,9},{9,8},{10,11... | collective-permute-start | bytes 3538952 | tf_op jit(solution)/shard_map/ppermute | solution.py:46
  261.5 42.9 %collective-permute-start.33 = (bf16[576,1024]{1,0:T(8,128)(2,1)}, bf16[576,1024]{1,0:T(8,128)(2,1)}, u32[]{:S(2)}, u32[]{:S(2)}) collective-permute-start(bf16[576,1024]{1,0:T(8,128)(2,1)} %collective-permute-done.27.refs_6_), channel_id=1, source_target_pairs={{0,1},{1,0},{2,3},{3,2},{4,5},{5,4},{6,7},{7,6},{8,9},{9,8},{10,11... | collective-permute-start | bytes 3538952 | tf_op jit(solution)/shard_map/ppermute | solution.py:46
  262.0 20.3 %collective-permute-start.28 = (bf16[288,1024]{1,0:T(8,128)(2,1)}, bf16[288,1024]{1,0:T(8,128)(2,1)}, u32[]{:S(2)}, u32[]{:S(2)}) collective-permute-start(bf16[288,1024]{1,0:T(8,128)(2,1)} %slice.314), channel_id=1, source_target_pairs={{0,4},{4,0},{8,12},{12,8},{16,20},{20,16},{24,28},{28,24},{1,5},{5... | collective-permute-start | bytes 1769480 | tf_op jit(solution)/shard_map/ppermute | solution.py:46
  282.3 15.3 %collective-permute-start.29 = (bf16[288,1024]{1,0:T(8,128)(2,1)S(1)}, bf16[288,1024]{1,0:T(8,128)(2,1)S(1)}, u32[]{:S(2)}, u32[]{:S(2)}) collective-permute-start(bf16[288,1024]{1,0:T(8,128)(2,1)S(1)} %slice.315), channel_id=1, source_target_pairs={{0,8},{4,12},{8,0},{12,4},{16,24},{20,28},{24,16},{28,20},{1,9},{5... | collective-permute-start | bytes 1769480 | tf_op jit(solution)/shard_map/ppermute | solution.py:46
  356.2 26.3 %collective-permute-start.37 = (bf16[768,4096]{1,0:T(8,128)(2,1)}, bf16[768,4096]{1,0:T(8,128)(2,1)}, u32[]{:S(2)}, u32[]{:S(2)}) collective-permute-start(bf16[768,4096]{1,0:T(8,128)(2,1)} %get-tuple-element.277.latter_own), channel_id=1, source_target_pairs={{0,1},{1,0},{2,3},{3,2},{4,5},{5,4},{6,7},{7,6},{8,9},{9,8},{10,11... | collective-permute-start | bytes 18874376 | tf_op jit(solution)/shard_map/ppermute | solution.py:46
  356.9 90.7 %collective-permute-start.49 = (bf16[256,4096]{1,0:T(8,128)(2,1)}, bf16[256,4096]{1,0:T(8,128)(2,1)}, u32[]{:S(2)}, u32[]{:S(2)}) collective-permute-start(bf16[256,4096]{1,0:T(8,128)(2,1)} %copy-done.84), channel_id=1, source_target_pairs={{0,1},{1,0},{2,3},{3,2},{4,5},{5,4},{6,7},{7,6},{8,9},{9,8},{10,11... | collective-permute-start | bytes 6291464 | tf_op jit(solution)/shard_map/ppermute | solution.py:46
  357.4 25.1 %collective-permute-start.36 = (bf16[768,1024]{1,0:T(8,128)(2,1)}, bf16[768,1024]{1,0:T(8,128)(2,1)S(1)}, u32[]{:S(2)}, u32[]{:S(2)}) collective-permute-start(bf16[768,1024]{1,0:T(8,128)(2,1)} %copy-done.19), channel_id=1, source_target_pairs={{0,1},{1,0},{2,3},{3,2},{4,5},{5,4},{6,7},{7,6},{8,9},{9,8},{10,11... | collective-permute-start | bytes 4718600 | tf_op jit(solution)/shard_map/ppermute | solution.py:46
  382.0 58.8 %collective-permute-start.41 = (bf16[2,2,2,4,256,128]{5,4,3,2,1,0:T(8,128)(2,1)}, bf16[2,2,2,4,256,128]{5,4,3,2,1,0:T(8,128)(2,1)}, u32[]{:S(2)}, u32[]{:S(2)}) collective-permute-start(bf16[2,2,2,4,256,128]{5,4,3,2,1,0:T(8,128)(2,1)} %get-tuple-element.275), channel_id=1, source_target_pairs={{0,2},{1,3},{2,0},{3,1},{4,6},{5,7},{6,4},{7,5},{8,10},{9,11},{10,... | collective-permute-start | bytes 6291464 | tf_op jit(solution)/shard_map/ppermute | solution.py:46
  396.5 54.1 %collective-permute-start.40 = (bf16[2,2,2,4,256,128]{5,4,3,2,1,0:T(8,128)(2,1)}, bf16[2,2,2,4,256,128]{5,4,3,2,1,0:T(8,128)(2,1)}, u32[]{:S(2)}, u32[]{:S(2)}) collective-permute-start(bf16[2,2,2,4,256,128]{5,4,3,2,1,0:T(8,128)(2,1)} %get-tuple-element.280), channel_id=1, source_target_pairs={{0,4},{4,0},{8,12},{12,8},{16,20},{20,16},{24,28},{28,24},{1,5},{5... | collective-permute-start | bytes 6291464 | tf_op jit(solution)/shard_map/ppermute | solution.py:46
  412.8 112.5 %collective-permute-start.57 = (bf16[768,3072]{1,0:T(8,128)(2,1)}, bf16[768,3072]{1,0:T(8,128)(2,1)}, u32[]{:S(2)}, u32[]{:S(2)}) collective-permute-start(bf16[768,3072]{1,0:T(8,128)(2,1)} %bitcast.338), channel_id=1, source_target_pairs={{0,1},{1,0},{2,3},{3,2},{4,5},{5,4},{6,7},{7,6},{8,9},{9,8},{10,11... | collective-permute-start | bytes 14155784 | tf_op jit(solution)/shard_map/ppermute | solution.py:46
  439.4 18.3 %collective-permute-start.47 = (bf16[256,4096]{1,0:T(8,128)(2,1)}, bf16[256,4096]{1,0:T(8,128)(2,1)}, u32[]{:S(2)}, u32[]{:S(2)}) collective-permute-start(bf16[256,4096]{1,0:T(8,128)(2,1)} %fusion.13.latter_own), channel_id=1, source_target_pairs={{0,1},{1,0},{2,3},{3,2},{4,5},{5,4},{6,7},{7,6},{8,9},{9,8},{10,11... | collective-permute-start | bytes 6291464 | tf_op jit(solution)/shard_map/ppermute | solution.py:46
  440.8 16.7 %collective-permute-start.48 = (bf16[256,1024]{1,0:T(8,128)(2,1)}, bf16[256,1024]{1,0:T(8,128)(2,1)}, u32[]{:S(2)}, u32[]{:S(2)}) collective-permute-start(bf16[256,1024]{1,0:T(8,128)(2,1)} %reduce_sum.125.latter_own), channel_id=1, source_target_pairs={{0,1},{1,0},{2,3},{3,2},{4,5},{5,4},{6,7},{7,6},{8,9},{9,8},{10,11... | collective-permute-start | bytes 1572872 | tf_op jit(solution)/shard_map/ppermute | solution.py:46
  447.6 37.8 %collective-permute-start.43 = (bf16[2,2,4,256,128]{4,3,2,1,0:T(8,128)(2,1)}, bf16[2,2,4,256,128]{4,3,2,1,0:T(8,128)(2,1)}, u32[]{:S(2)}, u32[]{:S(2)}) collective-permute-start(bf16[2,2,4,256,128]{4,3,2,1,0:T(8,128)(2,1)} %fusion.26), channel_id=1, source_target_pairs={{0,8},{4,12},{8,0},{12,4},{16,24},{20,28},{24,16},{28,20},{1,9},{5... | collective-permute-start | bytes 3145736 | tf_op jit(solution)/shard_map/ppermute | solution.py:46
  450.5 18.1 %collective-permute-start.46 = (bf16[256,1024]{1,0:T(8,128)(2,1)}, bf16[256,1024]{1,0:T(8,128)(2,1)}, u32[]{:S(2)}, u32[]{:S(2)}) collective-permute-start(bf16[256,1024]{1,0:T(8,128)(2,1)} %multiply_convert_fusion.5.far_own.own_own), channel_id=1, source_target_pairs={{0,1},{1,0},{2,3},{3,2},{4,5},{5,4},{6,7},{7,6},{8,9},{9,8},{10,11... | collective-permute-start | bytes 1572872 | tf_op jit(solution)/shard_map/ppermute | solution.py:46
  453.1 48.6 %all-to-all-start.3 = ((bf16[8,2,128,128]{3,2,1,0:T(8,128)(2,1)}), bf16[8,2,128,128]{3,2,1,0:T(8,128)(2,1)}, u32[]{:S(2)}, u32[]{:S(2)}) async-start(bf16[8,2,128,128]{3,2,1,0:T(8,128)(2,1)} %bitcast.347), calls=%async_computation.3 | async-start | bytes 1048576 | tf_op jit(solution)/shard_map/all_to_all | solution.py:1459
  457.5 22.1 %collective-permute-start.44 = (bf16[256,1024]{1,0:T(8,128)(2,1)}, bf16[256,1024]{1,0:T(8,128)(2,1)S(1)}, u32[]{:S(2)}, u32[]{:S(2)}) collective-permute-start(bf16[256,1024]{1,0:T(8,128)(2,1)} %bitcast.324), channel_id=1, source_target_pairs={{0,1},{1,0},{2,3},{3,2},{4,5},{5,4},{6,7},{7,6},{8,9},{9,8},{10,11... | collective-permute-start | bytes 1572872 | tf_op jit(solution)/shard_map/ppermute | solution.py:46
  457.7 21.9 %collective-permute-start.45 = (bf16[256,1024]{1,0:T(8,128)(2,1)}, bf16[256,1024]{1,0:T(8,128)(2,1)S(1)}, u32[]{:S(2)}, u32[]{:S(2)}) collective-permute-start(bf16[256,1024]{1,0:T(8,128)(2,1)} %copy-done.11), channel_id=1, source_target_pairs={{0,1},{1,0},{2,3},{3,2},{4,5},{5,4},{6,7},{7,6},{8,9},{9,8},{10,11... | collective-permute-start | bytes 1572872 | tf_op jit(solution)/shard_map/ppermute | solution.py:46
  468.7 25.2 %collective-permute-start.42 = (bf16[2,2,4,256,128]{4,3,2,1,0:T(8,128)(2,1)S(1)}, bf16[2,2,4,256,128]{4,3,2,1,0:T(8,128)(2,1)S(1)}, u32[]{:S(2)}, u32[]{:S(2)}) collective-permute-start(bf16[2,2,4,256,128]{4,3,2,1,0:T(8,128)(2,1)S(1)} %fusion.27), channel_id=1, source_target_pairs={{0,2},{1,3},{2,0},{3,1},{4,6},{5,7},{6,4},{7,5},{8,10},{9,11},{10,... | collective-permute-start | bytes 3145736 | tf_op jit(solution)/shard_map/ppermute | solution.py:46
  489.0 40.1 %collective-permute-start.56 = (bf16[768,1024]{1,0:T(8,128)(2,1)}, bf16[768,1024]{1,0:T(8,128)(2,1)}, u32[]{:S(2)}, u32[]{:S(2)}) collective-permute-start(bf16[768,1024]{1,0:T(8,128)(2,1)} %multiply_convert_fusion.4.far_own.own_own), channel_id=1, source_target_pairs={{0,1},{1,0},{2,3},{3,2},{4,5},{5,4},{6,7},{7,6},{8,9},{9,8},{10,11... | collective-permute-start | bytes 4718600 | tf_op jit(solution)/shard_map/ppermute | solution.py:46
  492.0 64.5 %collective-permute-start.51 = (bf16[2,2,2,4,256,128]{5,4,3,2,1,0:T(8,128)(2,1)}, bf16[2,2,2,4,256,128]{5,4,3,2,1,0:T(8,128)(2,1)}, u32[]{:S(2)}, u32[]{:S(2)}) collective-permute-start(bf16[2,2,2,4,256,128]{5,4,3,2,1,0:T(8,128)(2,1)} %get-tuple-element.291), channel_id=1, source_target_pairs={{0,2},{1,3},{2,0},{3,1},{4,6},{5,7},{6,4},{7,5},{8,10},{9,11},{10,... | collective-permute-start | bytes 6291464 | tf_op jit(solution)/shard_map/ppermute | solution.py:46
  493.9 50.4 %collective-permute-start.54 = (bf16[768,1024]{1,0:T(8,128)(2,1)S(1)}, bf16[768,1024]{1,0:T(8,128)(2,1)}, u32[]{:S(2)}, u32[]{:S(2)}) collective-permute-start(bf16[768,1024]{1,0:T(8,128)(2,1)S(1)} %bitcast.321), channel_id=1, source_target_pairs={{0,1},{1,0},{2,3},{3,2},{4,5},{5,4},{6,7},{7,6},{8,9},{9,8},{10,11... | collective-permute-start | bytes 4718600 | tf_op jit(solution)/shard_map/ppermute | solution.py:46
  500.9 45.0 %collective-permute-start.55 = (bf16[768,1024]{1,0:T(8,128)(2,1)S(1)}, bf16[768,1024]{1,0:T(8,128)(2,1)}, u32[]{:S(2)}, u32[]{:S(2)}) collective-permute-start(bf16[768,1024]{1,0:T(8,128)(2,1)S(1)} %get-tuple-element.403.latter_own), channel_id=1, source_target_pairs={{0,1},{1,0},{2,3},{3,2},{4,5},{5,4},{6,7},{7,6},{8,9},{9,8},{10,11... | collective-permute-start | bytes 4718600 | tf_op jit(solution)/shard_map/ppermute | solution.py:46
  519.0 84.5 %all-to-all-start.4 = ((bf16[8,2,128,384]{3,2,1,0:T(8,128)(2,1)}), bf16[8,2,128,384]{3,2,1,0:T(8,128)(2,1)}, u32[]{:S(2)}, u32[]{:S(2)}) async-start(bf16[8,2,128,384]{3,2,1,0:T(8,128)(2,1)} %copy-done.14), calls=%async_computation.4 | async-start | bytes 3145728 | tf_op jit(solution)/shard_map/all_to_all | solution.py:1474
  525.2 26.0 %collective-permute-start.53 = (bf16[512,1024]{1,0:T(8,128)(2,1)}, bf16[512,1024]{1,0:T(8,128)(2,1)S(1)}, u32[]{:S(2)}, u32[]{:S(2)}) collective-permute-start(bf16[512,1024]{1,0:T(8,128)(2,1)} %slice.510.latter_own), channel_id=1, source_target_pairs={{0,1},{1,0},{2,3},{3,2},{4,5},{5,4},{6,7},{7,6},{8,9},{9,8},{10,11... | collective-permute-start | bytes 3145736 | tf_op jit(solution)/shard_map/ppermute | solution.py:46
  529.1 71.3 %collective-permute-start.59 = (bf16[2,2,2,5,256,128]{5,4,3,2,1,0:T(8,128)(2,1)S(1)}, bf16[2,2,2,5,256,128]{5,4,3,2,1,0:T(8,128)(2,1)S(1)}, u32[]{:S(2)}, u32[]{:S(2)}) collective-permute-start(bf16[2,2,2,5,256,128]{5,4,3,2,1,0:T(8,128)(2,1)S(1)} %copy-done.4), channel_id=1, source_target_pairs={{0,4},{4,0},{8,12},{12,8},{16,20},{20,16},{24,28},{28,24},{1,5},{5... | collective-permute-start | bytes 7864328 | tf_op jit(solution)/shard_map/ppermute | solution.py:46
  544.3 22.0 %collective-permute-start.50 = (bf16[2,4,256,128]{3,2,1,0:T(8,128)(2,1)S(1)}, bf16[2,4,256,128]{3,2,1,0:T(8,128)(2,1)S(1)}, u32[]{:S(2)}, u32[]{:S(2)}) collective-permute-start(bf16[2,4,256,128]{3,2,1,0:T(8,128)(2,1)S(1)} %fusion.30), channel_id=1, source_target_pairs={{0,8},{4,12},{8,0},{12,4},{16,24},{20,28},{24,16},{28,20},{1,9},{5... | collective-permute-start | bytes 1572872 | tf_op jit(solution)/shard_map/ppermute | solution.py:46
  556.0 87.1 %collective-permute-start.60 = (bf16[2,2,2,6,256,128]{5,4,3,2,1,0:T(8,128)(2,1)}, bf16[2,2,2,6,256,128]{5,4,3,2,1,0:T(8,128)(2,1)}, u32[]{:S(2)}, u32[]{:S(2)}) collective-permute-start(bf16[2,2,2,6,256,128]{5,4,3,2,1,0:T(8,128)(2,1)} %get-tuple-element.316), channel_id=1, source_target_pairs={{0,8},{4,12},{8,0},{12,4},{16,24},{20,28},{24,16},{28,20},{1,9},{5... | collective-permute-start | bytes 9437192 | tf_op jit(solution)/shard_map/ppermute | solution.py:46
  613.2 79.8 %collective-permute-start.82 = (bf16[4,256,128]{2,1,0:T(8,128)(2,1)S(1)}, bf16[4,256,128]{2,1,0:T(8,128)(2,1)S(1)}, u32[]{:S(2)}, u32[]{:S(2)}) collective-permute-start(bf16[4,256,128]{2,1,0:T(8,128)(2,1)S(1)} %copy-done.63), channel_id=1, source_target_pairs={{0,16},{4,20},{8,24},{12,28},{16,0},{20,4},{24,8},{28,12},{1,17},{... | collective-permute-start | bytes 786440 | tf_op jit(solution)/shard_map/ppermute | solution.py:46
  615.6 25.1 %collective-permute-start.61 = (bf16[2,2,4,256,128]{4,3,2,1,0:T(8,128)(2,1)}, bf16[2,2,4,256,128]{4,3,2,1,0:T(8,128)(2,1)S(1)}, u32[]{:S(2)}, u32[]{:S(2)}) collective-permute-start(bf16[2,2,4,256,128]{4,3,2,1,0:T(8,128)(2,1)} %fusion.28), channel_id=1, source_target_pairs={{0,4},{4,0},{8,12},{12,8},{16,20},{20,16},{24,28},{28,24},{1,5},{5... | collective-permute-start | bytes 3145736 | tf_op jit(solution)/shard_map/ppermute | solution.py:46
  624.3 84.1 %collective-permute-start.66 = (bf16[2,2,5,256,128]{4,3,2,1,0:T(8,128)(2,1)}, bf16[2,2,5,256,128]{4,3,2,1,0:T(8,128)(2,1)}, u32[]{:S(2)}, u32[]{:S(2)}) collective-permute-start(bf16[2,2,5,256,128]{4,3,2,1,0:T(8,128)(2,1)} %fusion.20), channel_id=1, source_target_pairs={{0,2},{1,3},{2,0},{3,1},{4,6},{5,7},{6,4},{7,5},{8,10},{9,11},{10,... | collective-permute-start | bytes 3932168 | tf_op jit(solution)/shard_map/ppermute | solution.py:46
  624.8 22.0 %collective-permute-start.72 = (f32[4,1024]{1,0:T(4,128)S(1)}, f32[4,1024]{1,0:T(4,128)S(1)}, u32[]{:S(2)}, u32[]{:S(2)}) collective-permute-start(f32[4,1024]{1,0:T(4,128)S(1)} %pad_maximum_fusion.1), channel_id=1, source_target_pairs={{0,1},{1,0},{2,3},{3,2},{4,5},{5,4},{6,7},{7,6},{8,9},{9,8},{10,11... | collective-permute-start | bytes 49160 | tf_op jit(solution)/shard_map/ppermute | solution.py:46
  646.2 78.8 %collective-permute-start.64 = (bf16[2,2,6,256,128]{4,3,2,1,0:T(8,128)(2,1)}, bf16[2,2,6,256,128]{4,3,2,1,0:T(8,128)(2,1)}, u32[]{:S(2)}, u32[]{:S(2)}) collective-permute-start(bf16[2,2,6,256,128]{4,3,2,1,0:T(8,128)(2,1)} %fusion.17), channel_id=1, source_target_pairs={{0,2},{1,3},{2,0},{3,1},{4,6},{5,7},{6,4},{7,5},{8,10},{9,11},{10,... | collective-permute-start | bytes 4718600 | tf_op jit(solution)/shard_map/ppermute | solution.py:46
  646.8 41.9 %collective-permute-start.73 = (f32[4,1024]{1,0:T(4,128)S(1)}, f32[4,1024]{1,0:T(4,128)S(1)}, u32[]{:S(2)}, u32[]{:S(2)}) collective-permute-start(f32[4,1024]{1,0:T(4,128)S(1)} %fusion.56), channel_id=1, source_target_pairs={{0,2},{1,3},{2,0},{3,1},{4,6},{5,7},{6,4},{7,5},{8,10},{9,11},{10,... | collective-permute-start | bytes 49160 | tf_op jit(solution)/shard_map/ppermute | solution.py:46
  648.4 78.6 %collective-permute-start.68 = (bf16[2,2,2,3,256,128]{5,4,3,2,1,0:T(8,128)(2,1)}, bf16[2,2,2,3,256,128]{5,4,3,2,1,0:T(8,128)(2,1)}, u32[]{:S(2)}, u32[]{:S(2)}) collective-permute-start(bf16[2,2,2,3,256,128]{5,4,3,2,1,0:T(8,128)(2,1)} %get-tuple-element.331), channel_id=1, source_target_pairs={{0,8},{4,12},{8,0},{12,4},{16,24},{20,28},{24,16},{28,20},{1,9},{5... | collective-permute-start | bytes 4718600 | tf_op jit(solution)/shard_map/ppermute | solution.py:46
  705.8 18.0 %collective-permute-start.65 = (bf16[2,4,256,128]{3,2,1,0:T(8,128)(2,1)}, bf16[2,4,256,128]{3,2,1,0:T(8,128)(2,1)}, u32[]{:S(2)}, u32[]{:S(2)}) collective-permute-start(bf16[2,4,256,128]{3,2,1,0:T(8,128)(2,1)} %fusion.29), channel_id=1, source_target_pairs={{0,8},{4,12},{8,0},{12,4},{16,24},{20,28},{24,16},{28,20},{1,9},{5... | collective-permute-start | bytes 1572872 | tf_op jit(solution)/shard_map/ppermute | solution.py:46
  710.2 27.6 %collective-permute-start.70 = (bf16[2,5,256,128]{3,2,1,0:T(8,128)(2,1)S(1)}, bf16[2,5,256,128]{3,2,1,0:T(8,128)(2,1)S(1)}, u32[]{:S(2)}, u32[]{:S(2)}) collective-permute-start(bf16[2,5,256,128]{3,2,1,0:T(8,128)(2,1)S(1)} %fusion.21), channel_id=1, source_target_pairs={{0,8},{4,12},{8,0},{12,4},{16,24},{20,28},{24,16},{28,20},{1,9},{5... | collective-permute-start | bytes 1966088 | tf_op jit(solution)/shard_map/ppermute | solution.py:46
  725.0 17.3 %collective-permute-start.80 = (bf16[4,256,128]{2,1,0:T(8,128)(2,1)S(1)}, bf16[4,256,128]{2,1,0:T(8,128)(2,1)S(1)}, u32[]{:S(2)}, u32[]{:S(2)}) collective-permute-start(bf16[4,256,128]{2,1,0:T(8,128)(2,1)S(1)} %fusion.43), channel_id=1, source_target_pairs={{0,16},{4,20},{8,24},{12,28},{16,0},{20,4},{24,8},{28,12},{1,17},{... | collective-permute-start | bytes 786440 | tf_op jit(solution)/shard_map/ppermute | solution.py:46
  729.3 27.9 %collective-permute-start.69 = (bf16[2,2,3,256,128]{4,3,2,1,0:T(8,128)(2,1)}, bf16[2,2,3,256,128]{4,3,2,1,0:T(8,128)(2,1)}, u32[]{:S(2)}, u32[]{:S(2)}) collective-permute-start(bf16[2,2,3,256,128]{4,3,2,1,0:T(8,128)(2,1)} %fusion.33), channel_id=1, source_target_pairs={{0,4},{4,0},{8,12},{12,8},{16,20},{20,16},{24,28},{28,24},{1,5},{5... | collective-permute-start | bytes 2359304 | tf_op jit(solution)/shard_map/ppermute | solution.py:46
  740.1 15.4 %collective-permute-start.79 = (bf16[5,256,128]{2,1,0:T(8,128)(2,1)}, bf16[5,256,128]{2,1,0:T(8,128)(2,1)}, u32[]{:S(2)}, u32[]{:S(2)}) collective-permute-start(bf16[5,256,128]{2,1,0:T(8,128)(2,1)} %fusion.38), channel_id=1, source_target_pairs={{0,16},{4,20},{8,24},{12,28},{16,0},{20,4},{24,8},{28,12},{1,17},{... | collective-permute-start | bytes 983048 | tf_op jit(solution)/shard_map/ppermute | solution.py:46
  741.0 18.8 %collective-permute-start.67 = (bf16[2,6,256,128]{3,2,1,0:T(8,128)(2,1)S(1)}, bf16[2,6,256,128]{3,2,1,0:T(8,128)(2,1)}, u32[]{:S(2)}, u32[]{:S(2)}) collective-permute-start(bf16[2,6,256,128]{3,2,1,0:T(8,128)(2,1)S(1)} %fusion.18), channel_id=1, source_target_pairs={{0,4},{4,0},{8,12},{12,8},{16,20},{20,16},{24,28},{28,24},{1,5},{5... | collective-permute-start | bytes 2359304 | tf_op jit(solution)/shard_map/ppermute | solution.py:46
  761.4 18.6 %collective-permute-start.71 = (bf16[6,256,128]{2,1,0:T(8,128)(2,1)S(1)}, bf16[6,256,128]{2,1,0:T(8,128)(2,1)S(1)}, u32[]{:S(2)}, u32[]{:S(2)}) collective-permute-start(bf16[6,256,128]{2,1,0:T(8,128)(2,1)S(1)} %fusion.34), channel_id=1, source_target_pairs={{0,16},{4,20},{8,24},{12,28},{16,0},{20,4},{24,8},{28,12},{1,17},{... | collective-permute-start | bytes 1179656 | tf_op jit(solution)/shard_map/ppermute | solution.py:46
  764.9 17.5 %collective-permute-start.77 = (bf16[2,3,256,128]{3,2,1,0:T(8,128)(2,1)S(1)}, bf16[2,3,256,128]{3,2,1,0:T(8,128)(2,1)S(1)}, u32[]{:S(2)}, u32[]{:S(2)}) collective-permute-start(bf16[2,3,256,128]{3,2,1,0:T(8,128)(2,1)S(1)} %fusion.36), channel_id=1, source_target_pairs={{0,2},{1,3},{2,0},{3,1},{4,6},{5,7},{6,4},{7,5},{8,10},{9,11},{10,... | collective-permute-start | bytes 1179656 | tf_op jit(solution)/shard_map/ppermute | solution.py:46
  (116 other events, 1181.8 us)

commit v5 on v4

--- a/solution.py
+++ b/solution.py
@@ -370,6 +370,7 @@
 LANES = 128
 TILE = 256
 VMEM_LIMIT = 48 * 1024 * 1024
+HINT = pl.CostEstimate(flops=1, bytes_accessed=1, transcendentals=0)
 
 
 def whole_block(shape):
@@ -465,11 +466,7 @@
         out_specs=row_spec(chunks, own, LANES),
         out_shape=jax.ShapeDtypeStruct((chunks, rows, own, LANES), BF),
         compiler_params=pltpu.CompilerParams(vmem_limit_bytes=VMEM_LIMIT),
-        cost_estimate=pl.CostEstimate(
-            flops=rows * length * length * LANES * 5,
-            bytes_accessed=packed.size * 3,
-            transcendentals=rows * length * length,
-        ),
+        cost_estimate=HINT,
         name="frame_attend",
     )(packed, segments[:, :, None], segments[:, None, :])
 
@@ -489,11 +486,7 @@
         out_shape=jax.ShapeDtypeStruct((chunks, rows, own, 3 * LANES), BF),
         scratch_shapes=[pltpu.VMEM((length, LANES), F32), pltpu.VMEM((length, LANES), F32)],
         compiler_params=pltpu.CompilerParams(vmem_limit_bytes=VMEM_LIMIT),
-        cost_estimate=pl.CostEstimate(
-            flops=rows * length * length * LANES * 12,
-            bytes_accessed=packed.size * 5,
-            transcendentals=rows * length * length,
-        ),
+        cost_estimate=HINT,
         name="frame_attend_grads",
     )(packed, grads, segments[:, :, None], segments[:, None, :])
 
@@ -617,9 +610,7 @@
         out_specs=codec_spec(positions, tile, width),
         out_shape=jax.ShapeDtypeStruct((positions, total, width), BF),
         compiler_params=pltpu.CompilerParams(vmem_limit_bytes=VMEM_LIMIT),
-        cost_estimate=pl.CostEstimate(
-            flops=total * width * LANES * 30, bytes_accessed=packed.size * 3, transcendentals=0
-        ),
+        cost_estimate=HINT,
         name="codec_attend",
     )(packed, head_marks(width))
 
@@ -639,9 +630,7 @@
         out_specs=codec_spec(positions, tile, triple),
         out_shape=jax.ShapeDtypeStruct((positions, total, triple), BF),
         compiler_params=pltpu.CompilerParams(vmem_limit_bytes=VMEM_LIMIT),
-        cost_estimate=pl.CostEstimate(
-            flops=total * width * LANES * 70, bytes_accessed=packed.size * 5, transcendentals=0
-        ),
+        cost_estimate=HINT,
         name="codec_attend_grads",
     )(packed, grads, head_marks(width))
 
@@ -746,24 +735,29 @@
         out_shape=grad_buffers(units),
         input_output_aliases=aliases,
         compiler_params=pltpu.CompilerParams(vmem_limit_bytes=VMEM_LIMIT),
-        cost_estimate=pl.CostEstimate(flops=flops, bytes_accessed=moved, transcendentals=0),
+        cost_estimate=HINT,
         name=name,
     )(order, *arrays)
 
 
 def grad_rows(former, latter, order, stages, units, offset, into=None):
-    rows, breadth = latter[0].shape
-    height = former[0].shape[1] // 4
+    former, skip, height = former
+    latter, latter_skip, breadth = latter
+    rows = latter[0].shape[0]
+    height = height // 4
+    skip = skip // height
     wide = breadth // 8 == LANES
     chunks = breadth // 8 // LANES
     steps = 1 if wide else 8
     arrays = [former[0], former[1], former[0], former[1], latter[0], latter[1]]
     former_specs = [
-        pl.BlockSpec((rows, height), lambda j, t, at=at: (0, t[at]), pipeline_mode=pl.Buffered(1))
+        pl.BlockSpec((rows, height), lambda j, t, at=at: (0, skip + t[at]), pipeline_mode=pl.Buffered(1))
         for at in (0, 0, 1, 1)
     ]
     if wide:
-        latter_specs = [whole_block((rows, breadth))] * 2
+        latter_specs = [
+            pl.BlockSpec((rows, breadth), lambda j, t: (0, latter_skip // breadth))
+        ] * 2
         block = (2, 2, 2, 1, TILE, LANES)
         out_specs = [pl.BlockSpec(block, lambda j, t: (0, 0, 0, offset, 0, 0))] * 2
     else:
@@ -790,7 +784,10 @@
                 pl.BlockSpec(block, lambda j, t: where(jnp.maximum(j - 4, 0))),
             ]
         latter_specs = [
-            pl.BlockSpec((rows, breadth // 8), lambda j, t: (0, t[table + j]))
+            pl.BlockSpec(
+                (rows, breadth // 8),
+                lambda j, t: (0, latter_skip // (breadth // 8) + t[table + j]),
+            )
         ] * 2
     return grad_call(
         functools.partial(grad_rows_kernel, stages, wide),
@@ -835,16 +832,22 @@
 
 
 def grad_columns(former, latter, order, stages, units, offset, into=None):
-    rows, breadth = latter[0].shape
-    height = former[0].shape[1] // 4
+    former, skip, height = former
+    latter, latter_skip, breadth = latter
+    rows = latter[0].shape[0]
+    height = height // 4
     step = min(512, height)
     per = height // step
     block = (2, 2, 2, step // TILE, TILE, LANES)
     base = offset // (step // TILE)
     latter_specs = [
-        pl.BlockSpec((rows, breadth), lambda j, t: (0, 0), pipeline_mode=pl.Buffered(1))
+        pl.BlockSpec(
+            (rows, breadth), lambda j, t: (0, latter_skip // breadth), pipeline_mode=pl.Buffered(1)
+        )
     ] * 2
-    former_specs = [pl.BlockSpec((rows, step), lambda j, t: (0, t[j // per] * per + j % per))] * 2
+    former_specs = [
+        pl.BlockSpec((rows, step), lambda j, t: (0, skip // step + t[j // per] * per + j % per))
+    ] * 2
     out_specs = [
         pl.BlockSpec(block, lambda j, t: (0, 0, 0, base + jnp.minimum(j, per - 1), 0, 0)),
         pl.BlockSpec(block, lambda j, t: (0, 0, 0, base + jnp.maximum(j - per, 0), 0, 0)),
@@ -969,29 +972,59 @@
             pltpu.SemaphoreType.DMA((2,)),
         ],
         compiler_params=pltpu.CompilerParams(vmem_limit_bytes=VMEM_LIMIT),
-        cost_estimate=pl.CostEstimate(flops=0, bytes_accessed=4 * rows * PACK, transcendentals=0),
+        cost_estimate=HINT,
         name="pack_weights",
     )(spots, *members)
 
 
-def join_kernel(shapes, parts, place_ref, *refs):
-    count = len(parts)
-    sources = refs[:count]
-    outs = refs[count : count + len(shapes)]
+def far_kernel(parts, place_ref, *refs):
+    pieces, (out_ref, held, sems, out_sem) = refs[:-4], refs[-4:]
+    quarter = held.shape[0] // 4
+    copies = []
+    for number, (piece, (change, offset)) in enumerate(zip(pieces, parts)):
+        start = (place_ref[1] ^ change) * quarter + offset
+        copies.append(
+            pltpu.make_async_copy(
+                piece, held.at[pl.ds(pl.multiple_of(start, 16), piece.shape[0])], sems.at[number]
+            )
+        )
+    for copy in copies:
+        copy.start()
+    for copy in copies:
+        copy.wait()
+    whole = pltpu.make_async_copy(held, out_ref, out_sem.at[0])
+    whole.start()
+    whole.wait()
+
+
+def far_pack(pieces, parts, spots):
+    rows = sum(piece.shape[0] for piece in pieces)
+    any_spec = pl.BlockSpec(memory_space=pl.ANY)
+    return pl.pallas_call(
+        functools.partial(far_kernel, parts),
+        in_specs=[pl.BlockSpec(memory_space=pltpu.SMEM)] + [any_spec] * len(pieces),
+        out_specs=any_spec,
+        out_shape=jax.ShapeDtypeStruct((rows, PACK), BF),
+        scratch_shapes=[
+            pltpu.VMEM((rows, PACK), BF),
+            pltpu.SemaphoreType.DMA((len(pieces),)),
+            pltpu.SemaphoreType.DMA((1,)),
+        ],
+        compiler_params=pltpu.CompilerParams(vmem_limit_bytes=VMEM_LIMIT),
+        cost_estimate=HINT,
+        name="far_pack",
+    )(spots, *pieces)
+
+
+def join_kernel(shapes, place_ref, *refs):
+    packs = refs[:4]
+    outs = refs[4 : 4 + len(shapes)]
     held, sems, out_sems = refs[-3:]
     rows = held.shape[0] // 4
-    quarter = rows // 4
     copies = []
-    for number, (source, (flip, change, offset)) in enumerate(zip(sources, parts)):
-        start = (place_ref[0] ^ flip) * rows + offset
-        if change is not None:
-            start = start + (place_ref[1] ^ change) * quarter
-        size = source.shape[0]
-        copies.append(
-            pltpu.make_async_copy(
-                source, held.at[pl.ds(pl.multiple_of(start, 16), size)], sems.at[number]
-            )
-        )
+    for flip, pack in enumerate(packs):
+        start = pl.multiple_of((place_ref[0] ^ flip) * rows, 16)
+        copies.append(pltpu.make_async_copy(pack, held.at[pl.ds(start, rows)], sems.at[flip]))
     for copy in copies:
         copy.start()
     for copy in copies:
@@ -1012,25 +1045,524 @@
         copy.wait()
 
 
-def join_weights(members, pieces, parts, spots):
+def join_weights(members, packs, spots):
     shapes = [member.shape for member in members]
     rows = pack_rows(members)
     any_spec = pl.BlockSpec(memory_space=pl.ANY)
     outs = [jax.ShapeDtypeStruct((4 * height, breadth), BF) for height, breadth in shapes]
     return pl.pallas_call(
-        functools.partial(join_kernel, shapes, parts),
-        in_specs=[pl.BlockSpec(memory_space=pltpu.SMEM)] + [any_spec] * len(pieces),
+        functools.partial(join_kernel, shapes),
+        in_specs=[pl.BlockSpec(memory_space=pltpu.SMEM)] + [any_spec] * 4,
         out_specs=[any_spec] * len(outs),
         out_shape=outs,
         scratch_shapes=[
             pltpu.VMEM((4 * rows, PACK), BF),
-            pltpu.SemaphoreType.DMA((len(pieces),)),
+            pltpu.SemaphoreType.DMA((4,)),
             pltpu.SemaphoreType.DMA((4 * len(pack_pieces(shapes)),)),
         ],
         compiler_params=pltpu.CompilerParams(vmem_limit_bytes=VMEM_LIMIT),
-        cost_estimate=pl.CostEstimate(flops=0, bytes_accessed=16 * rows * PACK, transcendentals=0),
+        cost_estimate=HINT,
         name="join_weights",
-    )(spots, *pieces)
+    )(spots, *packs)
+
+
+WIDE_LIMIT = 58 * 1024 * 1024
+GELU_A = 0.7978845608028654
+GELU_B = 0.044715
+
+
+def gelu_pair(values):
+    square = values * values
+    bent = jnp.tanh(GELU_A * values * (1.0 + GELU_B * square))
+    half = 0.5 * (1.0 + bent)
+    slope = half + 0.5 * values * (1.0 - bent * bent) * (GELU_A * (1.0 + 3.0 * GELU_B * square))
+    return values * half, slope
+
+
+def rms_grads(values, gain, grad):
+    inverse = lax.rsqrt(jnp.mean(values * values, axis=-1, keepdims=True) + EPSILON)
+    scaled = values * inverse
+    inner = grad * gain
+    part = inverse * (inner - scaled * jnp.mean(inner * scaled, axis=-1, keepdims=True))
+    return part, jnp.sum(grad * scaled, axis=0, keepdims=True)
+
+
+def held(shape):
+    return pl.BlockSpec(
+        shape, lambda *_: (0,) * len(shape), pipeline_mode=pl.Buffered(1)
+    )
+
+
+def dense_call(kernel, steps, in_specs, out_specs, out_shape, scratch, name):
+    return pl.pallas_call(
+        kernel,
+        grid=(steps,),
+        in_specs=in_specs,
+        out_specs=out_specs,
+        out_shape=out_shape,
+        scratch_shapes=scratch,
+        compiler_params=pltpu.CompilerParams(vmem_limit_bytes=WIDE_LIMIT),
+        cost_estimate=HINT,
+        name=name,
+    )
+
+
+def frame_front_kernel(hidden_ref, gain_ref, weight_ref, normed_ref, packed_ref):
+    groups, rows, own, _ = packed_ref.shape
+
+    @pl.when(pl.program_id(0) == 0)
+    def _():
+        normed_ref[...] = rms_scale(hidden_ref[...].astype(F32), gain_ref[...]).astype(BF)
+
+    total = matmul(normed_ref[...], weight_ref[...]).astype(BF)
+    for part in range(3):
+
+        @pl.when(pl.program_id(0) == part)
+        def _(part=part):
+            for group in range(groups):
+                packed_ref[group, :, :, LANES * part : LANES * (part + 1)] = total[
+                    :, LANES * group : LANES * (group + 1)
+                ].reshape(rows, own, LANES)
+
+
+def frame_front(hidden, gain, weight, rows):
+    total, width = hidden.shape
+    groups = width // LANES
+    shape = (groups, rows, total // rows, 3 * LANES)
+    return dense_call(
+        frame_front_kernel,
+        3,
+        [held(hidden.shape), held(gain.shape), pl.BlockSpec((width, width), lambda j: (0, j))],
+        [whole_block((total, width)), whole_block(shape)],
+        [jax.ShapeDtypeStruct((total, width), BF), jax.ShapeDtypeStruct(shape, BF)],
+        [],
+        "frame_front",
+    )(hidden, gain, weight)
+
+
+def frame_rear_kernel(
+    hidden_ref, front_ref, packed_ref, gain_ref, output_ref, expand_ref, contract_ref,
+    kept_ref, mixed_ref, slope_ref, base_ref, total, normed_ref,
+):
+    groups, rows, own, _ = packed_ref.shape
+    width = groups * LANES
+    tile = slope_ref.shape[1]
+
+    @pl.when(pl.program_id(0) == 0)
+    def _():
+        for group in range(groups):
+            kept_ref[:, width + LANES * group : width + LANES * (group + 1)] = packed_ref[
+                group
+            ].reshape(rows * own, LANES)
+        attended = kept_ref[:, width : 2 * width]
+        mixed = hidden_ref[...].astype(F32) + matmul(attended, output_ref[...])
+        mixed_ref[...] = mixed
+        total[...] = mixed
+        normed_ref[...] = rms_scale(mixed, gain_ref[...]).astype(BF)
+        kept_ref[:, :width] = front_ref[...]
+        kept_ref[:, 2 * width : 3 * width] = normed_ref[...]
+
+    active, slope = gelu_pair(matmul(normed_ref[...], expand_ref[...]))
+    active = active.astype(BF)
+    for step in range(4 * width // tile):
+
+        @pl.when(pl.program_id(0) == step)
+        def _(step=step):
+            kept_ref[:, 3 * width + step * tile : 3 * width + (step + 1) * tile] = active
+
+    slope_ref[...] = slope.astype(BF)
+    total[...] += matmul(active, contract_ref[...])
+
+    @pl.when(pl.program_id(0) == pl.num_programs(0) - 1)
+    def _():
+        base_ref[...] = total[...].astype(BF)
+
+
+FF_TILE = 512
+FRAME_TILE = 1024
+
+
+def frame_rear(hidden, front, packed, gain, output, expand, contract):
+    total, width = hidden.shape
+    inner = expand.shape[1]
+    tile = FRAME_TILE
+    full = whole_block((total, width))
+    kept = (total, 3 * width + inner)
+    return dense_call(
+        frame_rear_kernel,
+        inner // tile,
+        [
+            held(hidden.shape),
+            held(front.shape),
+            held(packed.shape),
+            held(gain.shape),
+            held(output.shape),
+            pl.BlockSpec((width, tile), lambda j: (0, j)),
+            pl.BlockSpec((tile, width), lambda j: (j, 0)),
+        ],
+        [whole_block(kept), full, pl.BlockSpec((total, tile), lambda j: (0, j)), full],
+        [
+            jax.ShapeDtypeStruct(kept, BF),
+            jax.ShapeDtypeStruct((total, width), F32),
+            jax.ShapeDtypeStruct((total, inner), BF),
+            jax.ShapeDtypeStruct((total, width), BF),
+        ],
+        [pltpu.VMEM((total, width), F32), pltpu.VMEM((total, width), BF)],
+        "frame_rear",
+    )(hidden, front, packed, gain, output, expand, contract)
+
+
+def frame_rear_grads_kernel(
+    grad_ref, slope_ref, mixed_ref, gain_ref, output_ref, expand_ref, contract_ref,
+    kept_ref, mixed_grad_ref, packed_ref, gain_grad_ref, total,
+):
+    groups, rows, own, _ = packed_ref.shape
+    width = groups * LANES
+    tile = slope_ref.shape[1]
+    grad = grad_ref[...]
+    expand_in = (slope_ref[...].astype(F32) * inner_right(grad, contract_ref[...])).astype(BF)
+    for step in range(4 * width // tile):
+
+        @pl.when(pl.program_id(0) == step)
+        def _(step=step):
+            kept_ref[:, width + step * tile : width + (step + 1) * tile] = expand_in
+
+    @pl.when(pl.program_id(0) == 0)
+    def _():
+        total[...] = jnp.zeros_like(total)
+        kept_ref[:, :width] = grad
+
+    total[...] += inner_right(expand_in, expand_ref[...])
+
+    @pl.when(pl.program_id(0) == pl.num_programs(0) - 1)
+    def _():
+        part, gain_grad = rms_grads(mixed_ref[...], gain_ref[...], total[...])
+        mixed_grad = grad.astype(F32) + part
+        mixed_grad_ref[...] = mixed_grad
+        gain_grad_ref[...] = gain_grad
+        output_in = mixed_grad.astype(BF)
+        kept_ref[:, 5 * width :] = output_in
+        attended_grad = inner_right(output_in, output_ref[...]).astype(BF)
+        for group in range(groups):
+            packed_ref[group] = attended_grad[:, LANES * group : LANES * (group + 1)].reshape(
+                rows, own, LANES
+            )
+
+
+def frame_rear_grads(grad, slope, mixed, gain, output, expand, contract, rows):
+    total, width = grad.shape
+    inner = expand.shape[1]
+    tile = FRAME_TILE
+    shape = (width // LANES, rows, total // rows, LANES)
+    kept = (total, 2 * width + inner)
+    full = whole_block((total, width))
+    part = pl.BlockSpec((total, tile), lambda j: (0, j))
+    return dense_call(
+        frame_rear_grads_kernel,
+        inner // tile,
+        [
+            held(grad.shape),
+            part,
+            held(mixed.shape),
+            held(gain.shape),
+            held(output.shape),
+            pl.BlockSpec((width, tile), lambda j: (0, j)),
+            pl.BlockSpec((tile, width), lambda j: (j, 0)),
+        ],
+        [whole_block(kept), full, whole_block(shape), whole_block((1, width))],
+        [
+            jax.ShapeDtypeStruct(kept, BF),
+            jax.ShapeDtypeStruct((total, width), F32),
+            jax.ShapeDtypeStruct(shape, BF),
+            jax.ShapeDtypeStruct((1, width), F32),
+        ],
+        [pltpu.VMEM((total, width), F32)],
+        "frame_rear_grads",
+    )(grad, slope, mixed, gain, output, expand, contract)
+
+
+def frame_front_grads_kernel(
+    packed_ref, hidden_ref, gain_ref, mixed_grad_ref, weight_ref,
+    projected_ref, grad_ref, gain_grad_ref, total,
+):
+    groups, rows, own, _ = packed_ref.shape
+
+    @pl.when(pl.program_id(0) == 0)
+    def _():
+        total[...] = jnp.zeros_like(total)
+
+    for part in range(3):
+
+        @pl.when(pl.program_id(0) == part)
+        def _(part=part):
+            for group in range(groups):
+                projected_ref[:, LANES * group : LANES * (group + 1)] = packed_ref[
+                    group, :, :, LANES * part : LANES * (part + 1)
+                ].reshape(rows * own, LANES)
+
+    total[...] += inner_right(projected_ref[...], weight_ref[...])
+
+    @pl.when(pl.program_id(0) == 2)
+    def _():
+        part, gain_grad = rms_grads(hidden_ref[...].astype(F32), gain_ref[...], total[...])
+        grad_ref[...] = mixed_grad_ref[...] + part
+        gain_grad_ref[...] = gain_grad
+
+
+def frame_front_grads(packed, hidden, gain, mixed_grad, weight):
+    total, width = hidden.shape
+    return dense_call(
+        frame_front_grads_kernel,
+        3,
+        [
+            held(packed.shape),
+            held(hidden.shape),
+            held(gain.shape),
+            held(mixed_grad.shape),
+            pl.BlockSpec((width, width), lambda j: (0, j)),
+        ],
+        [
+            pl.BlockSpec((total, width), lambda j: (0, j)),
+            whole_block((total, width)),
+            whole_block((1, width)),
+        ],
+        [
+            jax.ShapeDtypeStruct((total, 3 * width), BF),
+            jax.ShapeDtypeStruct((total, width), F32),
+            jax.ShapeDtypeStruct((1, width), F32),
+        ],
+        [pltpu.VMEM((total, width), F32)],
+        "frame_front_grads",
+    )(packed, hidden, gain, mixed_grad, weight)
+
+
+def codec_front_kernel(base_ref, entries_ref, gain_ref, weight_ref, normed_ref, packed_ref, normed):
+    positions = packed_ref.shape[0]
+
+    @pl.when(pl.program_id(0) == 0)
+    def _():
+        base = base_ref[...].astype(F32)
+        size = base.shape[0]
+        for t in range(positions):
+            hidden = base if t == 0 else base + entries_ref[t - 1].astype(F32)
+            normed[size * t : size * (t + 1)] = rms_scale(hidden, gain_ref[...]).astype(BF)
+        normed_ref[...] = normed[...]
+
+    total = matmul(normed[...], weight_ref[...]).astype(BF)
+    packed_ref[...] = total.reshape(packed_ref.shape)
+
+
+def codec_front(base, entries, gain, weight):
+    total, width = base.shape
+    positions = entries.shape[0] + 1
+    return dense_call(
+        codec_front_kernel,
+        6,
+        [
+            held(base.shape),
+            held(entries.shape),
+            held(gain.shape),
+            pl.BlockSpec((width, width // 2), lambda j: (0, j)),
+        ],
+        [
+            whole_block((positions * total, width)),
+            pl.BlockSpec((positions, total, width // 2), lambda j: (0, 0, j)),
+        ],
+        [
+            jax.ShapeDtypeStruct((positions * total, width), BF),
+            jax.ShapeDtypeStruct((positions, total, 3 * width), BF),
+        ],
+        [pltpu.VMEM((positions * total, width), BF)],
+        "codec_front",
+    )(base, entries, gain, weight)
+
+
+def codec_rear_kernel(
+    base_ref, entries_ref, front_ref, attended_ref, grad_ref, gain_ref, output_ref, expand_ref,
+    contract_ref, mixed_ref, active_ref, expand_kept_ref, kept_ref, mixed_grad_ref,
+    attended_grad_ref, gain_grad_ref, total,
+):
+    width = total.shape[1]
+    positions = entries_ref.shape[0] + 1
+    size = base_ref.shape[0]
+
+    @pl.when(pl.program_id(0) == 0)
+    def _():
+        base = base_ref[...].astype(F32)
+        for t in range(positions):
+            own = slice(size * t, size * (t + 1))
+            hidden = base if t == 0 else base + entries_ref[t - 1].astype(F32)
+            mixed = hidden + matmul(attended_ref[own], output_ref[...])
+            mixed_ref[own] = mixed
+            expand_kept_ref[own, :width] = rms_scale(mixed, gain_ref[...]).astype(BF)
+        total[...] = jnp.zeros_like(total)
+        kept_ref[:, :width] = front_ref[...]
+        kept_ref[:, width : 2 * width] = attended_ref[...]
+
+    active, slope = gelu_pair(matmul(expand_kept_ref[:, :width], expand_ref[...]))
+    active_ref[...] = active.astype(BF)
+    expand_in = (slope * inner_right(grad_ref[...], contract_ref[...])).astype(BF)
+    tile = expand_in.shape[1]
+    for step in range(4 * width // tile):
+
+        @pl.when(pl.program_id(0) == step)
+        def _(step=step):
+            expand_kept_ref[:, width + step * tile : width + (step + 1) * tile] = expand_in
+
+    total[...] += inner_right(expand_in, expand_ref[...])
+
+    @pl.when(pl.program_id(0) == pl.num_programs(0) - 1)
+    def _():
+        gain_grads = jnp.zeros_like(gain_grad_ref)
+        for t in range(positions):
+            own = slice(size * t, size * (t + 1))
+            part, gain_grad = rms_grads(mixed_ref[own], gain_ref[...], total[own])
+            gain_grads = gain_grads + gain_grad
+            mixed_grad = grad_ref[own].astype(F32) + part
+            mixed_grad_ref[own] = mixed_grad
+            output_in = mixed_grad.astype(BF)
+            kept_ref[own, 2 * width :] = output_in
+            attended_grad_ref[t] = inner_right(output_in, output_ref[...]).astype(BF)
+        gain_grad_ref[...] = gain_grads
+
+
+def codec_rear(base, entries, front, attended, grad, gain, output, expand, contract):
+    size, width = base.shape
+    total = attended.shape[0]
+    inner = expand.shape[1]
+    tile = FF_TILE
+    full = whole_block((total, width))
+    wide, triple = (total, width + inner), (total, 3 * width)
+    high = jax.ShapeDtypeStruct((total, width), F32)
+    return dense_call(
+        codec_rear_kernel,
+        inner // tile,
+        [
+            held(base.shape),
+            held(entries.shape),
+            held(front.shape),
+            held(attended.shape),
+            held(grad.shape),
+            held(gain.shape),
+            held(output.shape),
+            pl.BlockSpec((width, tile), lambda j: (0, j)),
+            pl.BlockSpec((tile, width), lambda j: (j, 0)),
+        ],
+        [
+            held((total, width)),
+            pl.BlockSpec((total, tile), lambda j: (0, j)),
+            held(wide),
+            held(triple),
+            held((total, width)),
+            held((total // size, size, width)),
+            whole_block((1, width)),
+        ],
+        [
+            high,
+            jax.ShapeDtypeStruct((total, inner), BF),
+            jax.ShapeDtypeStruct(wide, BF),
+            jax.ShapeDtypeStruct(triple, BF),
+            high,
+            jax.ShapeDtypeStruct((total // size, size, width), BF),
+            jax.ShapeDtypeStruct((1, width), F32),
+        ],
+        [pltpu.VMEM((total, width), F32)],
+        "codec_rear",
+    )(base, entries, front, attended, grad, gain, output, expand, contract)
+
+
+def codec_result_kernel(mixed_ref, active_ref, live_ref, contract_ref, out_ref, total):
+    positions, size, _ = out_ref.shape
+
+    @pl.when(pl.program_id(0) == 0)
+    def _():
+        total[...] = mixed_ref[...]
+
+    total[...] += matmul(active_ref[...], contract_ref[...])
+
+    @pl.when(pl.program_id(0) == pl.num_programs(0) - 1)
+    def _():
+        for t in range(positions):
+            out_ref[t] = (total[size * t : size * (t + 1)] * live_ref[...]).astype(BF)
+
+
+def codec_result(mixed, active, live, contract):
+    total, width = mixed.shape
+    size = live.shape[0]
+    inner = active.shape[1]
+    tile = FF_TILE
+    shape = (total // size, size, width)
+    return dense_call(
+        codec_result_kernel,
+        inner // tile,
+        [
+            held(mixed.shape),
+            pl.BlockSpec((total, tile), lambda j: (0, j)),
+            held(live.shape),
+            pl.BlockSpec((tile, width), lambda j: (j, 0)),
+        ],
+        whole_block(shape),
+        jax.ShapeDtypeStruct(shape, BF),
+        [pltpu.VMEM((total, width), F32)],
+        "codec_result",
+    )(mixed, active, live, contract)
+
+
+def codec_front_grads_kernel(
+    grad_ref, base_ref, entries_ref, gain_ref, mixed_grad_ref, weight_ref,
+    base_grad_ref, entry_grad_ref, gain_grad_ref, total,
+):
+    positions = entries_ref.shape[0] + 1
+    size = base_ref.shape[0]
+
+    @pl.when(pl.program_id(0) == 0)
+    def _():
+        total[...] = jnp.zeros_like(total)
+
+    total[...] += inner_right(grad_ref[...], weight_ref[...])
+
+    @pl.when(pl.program_id(0) == pl.num_programs(0) - 1)
+    def _():
+        base = base_ref[...].astype(F32)
+        gain_grads = jnp.zeros_like(gain_grad_ref)
+        base_grad = jnp.zeros_like(base)
+        for t in range(positions):
+            own = slice(size * t, size * (t + 1))
+            hidden = base if t == 0 else base + entries_ref[t - 1].astype(F32)
+            part, gain_grad = rms_grads(hidden, gain_ref[...], total[own])
+            gain_grads = gain_grads + gain_grad
+            grad = mixed_grad_ref[own] + part
+            base_grad = base_grad + grad
+            if t > 0:
+                entry_grad_ref[size * (t - 1) : size * t] = grad.astype(BF)
+        base_grad_ref[...] = base_grad.astype(BF)
+        gain_grad_ref[...] = gain_grads
+
+
+def codec_front_grads(grad, base, entries, gain, mixed_grad, weight):
+    size, width = base.shape
+    total = grad.shape[0]
+    tile = width // 2
+    return dense_call(
+        codec_front_grads_kernel,
+        grad.shape[1] // tile,
+        [
+            pl.BlockSpec((total, tile), lambda j: (0, j)),
+            held(base.shape),
+            held(entries.shape),
+            held(gain.shape),
+            held(mixed_grad.shape),
+            pl.BlockSpec((width, tile), lambda j: (0, j)),
+        ],
+        [whole_block((size, width)), whole_block((total - size, width)), whole_block((1, width))],
+        [
+            jax.ShapeDtypeStruct((size, width), BF),
+            jax.ShapeDtypeStruct((total - size, width), BF),
+            jax.ShapeDtypeStruct((1, width), F32),
+        ],
+        [pltpu.VMEM((total, width), F32)],
+        "codec_front_grads",
+    )(grad, base, entries, gain, mixed_grad, weight)
 
 
 def shards_general(
@@ -1184,12 +1716,35 @@
     )
 
 
+class Pair:
+    def __init__(self, own):
+        self.own = own
+        self.other = swap(own, "mp", 1)
+        self.age = 0
+
+    def both(self):
+        return (self.own, self.other)
+
+
 class Chain:
     def __init__(self):
         self.last = ()
+        self.pending = []
+
+    def pair(self, own):
+        made = Pair(own)
+        self.pending.append(made)
+        return made
 
     def enter(self, *values):
-        held = lax.optimization_barrier(tuple(values) + self.last)
+        due = [made for made in self.pending if made.age >= 3]
+        self.pending = [made for made in self.pending if made.age < 3]
+        for made in self.pending:
+            made.age += 1
+        came = tuple(made.other for made in due)
+        held = lax.optimization_barrier(tuple(values) + came + self.last)
+        for made, other in zip(due, held[len(values) :]):
+            made.other = other
         return held[0] if len(values) == 1 else held[: len(values)]
 
     def leave(self, *values):
@@ -1202,54 +1757,80 @@
         self.spots = spots
         self.whole = whole
         self.pack, self.quarter = pack_call(members, spots)
-        self.pieces = [self.pack]
-        self.parts = [(0, None, 0)]
-
-    def add(self, piece, change, offset):
-        self.pieces += [piece, swap(piece, "mp", 1)]
-        self.parts += [(2, change, offset), (3, change, offset)]
 
     def start(self, chain):
-        self.far = swap(chain.enter(self.pack if self.whole else self.quarter), "mp", 2)
-        self.pieces.append(swap(self.pack, "mp", 1))
-        self.parts.append((1, None, 0))
+        self.came = swap(chain.enter(self.pack if self.whole else self.quarter), "mp", 2)
+        self.near = chain.pair(self.pack)
 
     def spread(self, chain):
-        far = chain.enter(self.far)
-        chain.leave(far)
+        self.came = chain.enter(self.came)
+        chain.leave(self.came)
         if self.whole:
-            self.add(far, None, 0)
+            self.far = chain.pair(self.came)
             return
-        self.over_x = swap(far, "seq", 1)
-        self.over_n = swap(far, "seq", 2)
-        self.add(far, 0, 0)
+        self.over_x = swap(self.came, "seq", 1)
+        self.over_n = swap(self.came, "seq", 2)
 
     def cross(self, chain):
-        over_x, over_n = chain.enter(self.over_x, self.over_n)
-        chain.leave(over_x, over_n)
-        half = over_x.shape[0] // 2
-        self.ends = (swap(over_n[:half], "seq", 1), swap(over_x[half:], "seq", 2))
-        self.add(over_x, 1, 0)
-        self.add(over_n, 2, 0)
+        self.over_x, self.over_n = chain.enter(self.over_x, self.over_n)
+        chain.leave(self.over_x, self.over_n)
+        half = self.over_x.shape[0] // 2
+        self.ends = (swap(self.over_n[:half], "seq", 1), swap(self.over_x[half:], "seq", 2))
 
     def close(self, chain):
         ends = chain.enter(*self.ends)
-        chain.leave(*ends)
-        self.add(ends[0], 3, 0)
-        self.add(ends[1], 3, ends[0].shape[0])
+        parts = ((0, 0), (1, 0), (2, 0), (3, 0), (3, ends[0].shape[0]))
+        far = far_pack([self.came, self.over_x, self.over_n, *ends], parts, self.spots)
+        chain.leave(far)
+        self.far = far
+
+    def send(self, chain):
+        self.far = Pair(chain.enter(self.far))
 
     def join(self, chain):
-        pieces = chain.enter(*self.pieces)
-        outs = join_weights(self.members, pieces, tuple(self.parts), self.spots)
+        packs = chain.enter(*self.near.both(), *self.far.both())
+        outs = join_weights(self.members, packs, self.spots)
         chain.leave(*outs)
         return outs
 
 
+def load(block, riders):
+    if riders is None:
+        return block
+    high = riders.astype(BF)
+    low = (riders - high.astype(F32)).astype(BF)
+    return jnp.concatenate(
+        [part.reshape(-1, LANES) for part in (block, high, low)], axis=0
+    )
+
+
+def unload(message, shape, riders):
+    if riders is None:
+        return message, None
+    rows = message.shape[0] - 2 * riders.size // LANES
+    high, low = (
+        part.astype(F32).reshape(riders.shape) for part in jnp.split(message[rows:], 2, axis=0)
+    )
+    return message[:rows].reshape(shape), riders + (high + low)
+
+
 class Reduce:
-    def __init__(self, stages, blocks):
+    def __init__(self, stages, blocks, riders=None):
         self.stages = stages
         self.keep = blocks[1]
-        self.came = [swap(blocks[0], *BITS[stages[0]])]
+        self.riders = riders
+        self.came = []
+        self.shape = blocks[0].shape
+        self.coming = swap(load(blocks[0], riders), *BITS[stages[0]])
+
+    def arrive(self, chain):
+        self.coming = chain.enter(self.coming)
+        chain.leave(self.coming)
+
+    def take(self, chain):
+        self.keep, self.coming, *self.came = chain.enter(self.keep, self.coming, *self.came)
+        block, self.riders = unload(self.coming, self.shape, self.riders)
+        self.came.append(block)
 
     def total(self, last):
         at = len(self.came) - 1
@@ -1259,30 +1840,39 @@
             value = value + came[spot[level:]].astype(F32)
         return value
 
+    def give(self, chain):
+        self.take(chain)
+        given = self.total(False).astype(BF)
+        self.shape = given.shape
+        return given
+
     def step(self, chain):
-        self.keep, *self.came = chain.enter(self.keep, *self.came)
-        given = self.total(False).astype(BF)
-        chain.leave(given)
-        self.came.append(swap(given, *BITS[self.stages[len(self.came)]]))
+        given = self.give(chain)
+        message = load(given, self.riders)
+        chain.leave(message)
+        self.coming = swap(message, *BITS[self.stages[len(self.came)]])
 
     def result(self):
         return self.total(True)
 
 
-def pair(values):
-    return (values, swap(values, "mp", 1))
-
-
-def hidden_grads(contract_in, expanded, weights):
-    active_grad = inner_right(contract_in, weights[5])
-    return jax.vjp(jax.nn.gelu, expanded)[1](active_grad)[0].astype(BF)
-
-
-def mixed_grads(result_grad, normed_grad, mixed_sum, weights):
-    mixed_part, postnorm_grad = jax.vjp(rms_scale, mixed_sum, weights[3].astype(F32))[1](normed_grad)
-    mixed_grad = result_grad + mixed_part
-    output_in = mixed_grad.astype(BF)
-    return mixed_grad, inner_right(output_in, weights[2]).astype(BF), postnorm_grad, output_in
+def finish(sums, chain):
+    given = jnp.concatenate([one.give(chain) for one in sums], axis=0)
+    riders = sums[-1].riders
+    message = load(given, riders)
+    chain.leave(message)
+    message = swap(message, *BITS["f"])
+
+    def take():
+        came, total = unload(message, given.shape, riders)
+        start = 0
+        for one in sums:
+            size = one.shape[-3]
+            one.came.append(came[start : start + size])
+            start += size
+        sums[-1].riders = total
+
+    return take
 
 
 def shards(
@@ -1321,6 +1911,9 @@
     first = Gather([frame_project, gain_rows], spots)
     first.start(chain)
     chain.leave(first.quarter)
+    second = Gather([frame_expand, frame_contract, frame_output], spots)
+    second.quarter = chain.enter(second.quarter)
+    chain.leave(second.quarter)
     every_segment = lax.all_to_all(
         jnp.broadcast_to(segments[None], (count, row_count, frames_dev)),
         "seq",
@@ -1332,208 +1925,279 @@
     codes = codec_tokens.reshape(1, (positions - 1) * frame_total) + jnp.repeat(
         jnp.arange(positions - 1, dtype=jnp.int32) * CODES, frame_total
     )
-    codes_both = jnp.concatenate(pair(codes), axis=1)
-    live = padding.reshape(frame_total).astype(F32)[None, :, None]
-    second = Gather([frame_expand, frame_contract, frame_output], spots)
+    codes_pair = chain.pair(codes)
+    every_segment = chain.enter(every_segment)
+    chain.leave(every_segment)
+    live = padding.reshape(frame_total).astype(F32)[:, None]
     first.spread(chain)
     second.start(chain)
-    codec_grad = (
-        jnp.transpose(
-            chain.enter(cotangent).reshape(frame_total, positions, width), (1, 0, 2)
-        ).astype(F32)
-        * live
+    contract_in = (
+        jnp.transpose(chain.enter(cotangent).reshape(frame_total, positions, width), (1, 0, 2))
+        * live.astype(BF)[None]
     ).reshape(positions * frame_total, width)
-    contract_in = pair(codec_grad.astype(BF))
-    chain.leave(contract_in[0])
+    chain.leave(contract_in)
     first.cross(chain)
+    fourth = Gather([codec_expand, codec_contract, codec_output], spots)
+    fourth.quarter = chain.enter(fourth.quarter)
+    chain.leave(fourth.quarter)
+    second.spread(chain)
+    fourth.start(chain)
     third = Gather([codec_project, codebooks], spots, True)
-    fourth = Gather([codec_expand, codec_contract, codec_output], spots)
+    third.pack = chain.enter(third.pack)
+    chain.leave(third.pack)
+    third.start(chain)
     first.close(chain)
-
-    weight_project, gains = first.join(chain)
+    first.send(chain)
+
+    frame_project_all, gains = first.join(chain)
     gains = jnp.transpose(
         gains.reshape(place.mp_count, -1, 4, width // 4)[:, 0], (1, 0, 2)
-    ).reshape(4, width)
-    hidden = frames.astype(F32).reshape(frame_total, width)
-    normed, projected = front_pass(hidden, (gains[0], weight_project))
-    packed = jnp.transpose(
-        projected.reshape(row_count, frames_dev, 3, count, LANES), (3, 0, 1, 2, 4)
-    ).reshape(count, row_count, frames_dev, 3 * LANES)
+    ).reshape(4, 1, width).astype(F32)
+    hidden = frames.reshape(frame_total, width)
+    normed, packed = frame_front(hidden, chain.enter(gains[0]), frame_project_all, row_count)
+    packed, second.over_x, second.over_n, fourth.came = chain.enter(
+        packed, second.over_x, second.over_n, fourth.came
+    )
     chain.leave(packed)
     packed = lax.all_to_all(packed, "seq", split_axis=0, concat_axis=0, tiled=True)
-    second.spread(chain)
-    fourth.start(chain)
     second.cross(chain)
-    third.start(chain)
+    packed, *second.ends = chain.enter(packed, *second.ends)
+    chain.leave(packed)
+    second.close(chain)
+    second.send(chain)
+    fourth.spread(chain)
+    contract_pair = Pair(contract_in)
     packed = chain.enter(packed)
     attended = frame_attend_call(packed, every_segment)
     chain.leave(attended)
+    attended, second.far.other = chain.enter(attended, second.far.other)
+    chain.leave(attended)
     attended = lax.all_to_all(attended, "seq", split_axis=0, concat_axis=0, tiled=True)
-    fourth.spread(chain)
-    second.close(chain)
-    weight_expand, weight_contract, weight_output = second.join(chain)
-    frame_weights = (gains[0], weight_project, weight_output, gains[1], weight_expand, weight_contract)
-    attended = jnp.transpose(chain.enter(attended), (1, 2, 0, 3)).reshape(frame_total, width)
-    frame_result, frame_saved = rear_pass(hidden, attended, frame_weights)
-    base_low = frame_result.astype(BF)
-    chain.leave(base_low)
-    normed_both = pair(normed)
-    attended_both = pair(attended)
-    normed_two_both = pair(frame_saved[1])
-    activated_both = pair(frame_saved[3])
-
+    frame_expand_all, frame_contract_all, frame_output_all = second.join(chain)
+    attended, fourth.over_x, fourth.over_n = chain.enter(attended, fourth.over_x, fourth.over_n)
+    chain.leave(attended)
+    fourth.cross(chain)
+    frame_kept, mixed, slope, base = frame_rear(
+        hidden,
+        normed,
+        chain.enter(attended),
+        gains[1],
+        frame_output_all,
+        frame_expand_all,
+        frame_contract_all,
+    )
+    chain.leave(base)
+
+    base, third.came, *fourth.ends = chain.enter(base, third.came, *fourth.ends)
+    chain.leave(base)
     third.spread(chain)
-    fourth.cross(chain)
-    weight_project, table = third.join(chain)
-    embedded = table[codes.reshape(positions - 1, frame_total)].astype(F32)
-    base = chain.enter(base_low).astype(F32)
-    codec_hidden = jnp.concatenate([base[None], base[None] + embedded], axis=0).reshape(
-        positions * frame_total, width
-    )
-    codec_normed, codec_projected = front_pass(codec_hidden, (gains[2], weight_project))
-    codec_packed = codec_projected.reshape(positions, frame_total, 3 * width)
+    fourth.close(chain)
+    codec_project_all, table = third.join(chain)
+    fourth.send(chain)
+    frame_kept = Pair(chain.enter(frame_kept))
+    entries = table[codes.reshape(positions - 1, frame_total)]
+    codec_normed, codec_packed = codec_front(chain.enter(base), entries, gains[2], codec_project_all)
     chain.leave(codec_packed)
-    fourth.close(chain)
-    codec_attended = codec_attend_call(chain.enter(codec_packed)).reshape(
-        positions * frame_total, width
-    )
+    codec_packed, contract_pair.other = chain.enter(codec_packed, contract_pair.other)
+    codec_attended = codec_attend_call(codec_packed).reshape(positions * frame_total, width)
     chain.leave(codec_attended)
-    codec_normed_both = pair(codec_normed)
-    codec_attended_both = pair(codec_attended)
-    weight_expand, weight_contract, weight_output = fourth.join(chain)
-    codec_weights = (gains[2], weight_project, weight_output, gains[3], weight_expand, weight_contract)
-    mixed_sum = codec_hidden + matmul(chain.enter(codec_attended), weight_output)
-    normed_two = rms_scale(mixed_sum, gains[3].astype(F32)).astype(BF)
-    expanded = matmul(normed_two, weight_expand)
-    activated = jax.nn.gelu(expanded).astype(BF)
-
-    expand_in = hidden_grads(contract_in[0], expanded, codec_weights)
-    chain.leave(activated, expand_in)
-    activated_pair = pair(activated)
-    expand_pair = pair(expand_in)
-    codec_normed_two_both = pair(normed_two)
-    normed_grad = inner_right(chain.enter(expand_in), weight_expand)
-    chain.leave(normed_grad)
-    stages = tuple("ynxf")
-    blocks = grad_columns(chain.enter(*activated_pair), contract_in, order, stages, 4, 0)
-    chain.leave(*blocks)
-    contract_sum = Reduce(stages, blocks)
-    stages = tuple("xynf")
-    blocks = grad_rows(codec_normed_two_both, chain.enter(*expand_pair), order, stages, 4, 0)
-    chain.leave(*blocks)
-    expand_sum = Reduce(stages, blocks)
-    mixed_grad, attended_grad, codec_postnorm_grad, output_in = mixed_grads(
-        codec_grad, chain.enter(normed_grad), mixed_sum, codec_weights
-    )
-    chain.leave(attended_grad)
-    output_pair = pair(output_in)
-    codec_projected_grad = codec_attend_grads_call(
-        codec_packed, chain.enter(attended_grad).reshape(positions, frame_total, width)
-    ).reshape(positions * frame_total, 3 * width)
-    chain.leave(codec_projected_grad)
-    projected_pair = pair(codec_projected_grad)
-    input_grad, codec_prenorm_grad = front_grads(
-        codec_hidden, chain.enter(codec_projected_grad), mixed_grad, codec_weights
-    )
-    input_grad = input_grad.reshape(positions, frame_total, width)
-    base_grad = jnp.sum(input_grad, axis=0).astype(BF)
-    table_in = input_grad[1:].reshape(-1, width).astype(BF)
-    chain.leave(base_grad, table_in)
-    table_pair = pair(table_in)
-
-    base_grad = chain.enter(base_grad)
-    contract_in = pair(base_grad)
-    base_grad = base_grad.astype(F32)
-    frame_expand_in = hidden_grads(contract_in[0], frame_saved[2], frame_weights)
-    chain.leave(frame_expand_in)
-    frame_expand_pair = pair(frame_expand_in)
-    contract_sum.step(chain)
-    normed_grad = inner_right(chain.enter(frame_expand_in), frame_weights[4])
-    frame_mixed_grad, frame_attended_grad, frame_postnorm_grad, output_in = mixed_grads(
-        base_grad, normed_grad, frame_saved[0], frame_weights
-    )
-    grads = jnp.transpose(
-        frame_attended_grad.reshape(row_count, frames_dev, count, LANES), (2, 0, 1, 3)
+    codec_expand_all, codec_contract_all, codec_output_all = fourth.join(chain)
+    codec_attended, frame_kept.other = chain.enter(codec_attended, frame_kept.other)
+    chain.leave(codec_attended)
+    (
+        codec_mixed,
+        codec_activated,
+        codec_expand_kept,
+        codec_kept,
+        mixed_grad,
+        attended_grad,
+        codec_postnorm_grad,
+    ) = codec_rear(
+        base,
+        entries,
+        codec_normed,
+        chain.enter(codec_attended),
+        contract_in,
+        gains[3],
+        codec_output_all,
+        codec_expand_all,
+        codec_contract_all,
+    )
+    chain.leave(codec_activated)
+
+    inner = codec_activated.shape[1]
+    activated_pair = chain.pair(codec_activated)
+    codec_expand_kept = chain.pair(codec_expand_kept)
+    projected_grad = codec_attend_grads_call(codec_packed, chain.enter(attended_grad)).reshape(
+        positions * frame_total, 3 * width
+    )
+    chain.leave(projected_grad)
+    base_grad, table_in, codec_prenorm_grad = codec_front_grads(
+        chain.enter(projected_grad), base, entries, gains[2], mixed_grad, codec_project_all
+    )
+    chain.leave(base_grad)
+    frame_grads_kept, frame_mixed_grad, grads, frame_postnorm_grad = frame_rear_grads(
+        chain.enter(base_grad),
+        slope,
+        mixed,
+        gains[1],
+        frame_output_all,
+        frame_expand_all,
+        frame_contract_all,
+        row_count,
+    )
+    chain.leave(grads)
+
+    activated_pair.other, codec_expand_kept.other, grads, frame_grads_kept = chain.enter(
+        activated_pair.other, codec_expand_kept.other, grads, frame_grads_kept
     )
     chain.leave(grads)
     grads = lax.all_to_all(grads, "seq", split_axis=0, concat_axis=0, tiled=True)
-    frame_output_pair = pair(output_in)
-    expand_sum.step(chain)
-    stages = tuple("yxnf")
-    blocks = grad_columns(chain.enter(*activated_both), contract_in, order, stages, 4, 0)
-    chain.leave(*blocks)
-    frame_contract_sum = Reduce(stages, blocks)
-    stages = tuple("xynf")
-    blocks = grad_rows(normed_two_both, chain.enter(*frame_expand_pair), order, stages, 5, 0)
-    blocks = grad_rows(attended_both, frame_output_pair, order, stages, 5, 4, blocks)
-    chain.leave(*blocks)
-    frame_expand_sum = Reduce(stages, blocks)
-    contract_sum.step(chain)
+    frame_grads_kept = Pair(frame_grads_kept)
+    contract_stages = tuple("ynxf")
+    contract_blocks = grad_columns(
+        (chain.enter(*activated_pair.both()), 0, inner),
+        (contract_pair.both(), 0, width),
+        order,
+        contract_stages,
+        4,
+        0,
+    )
+    chain.leave(*contract_blocks)
+    expand_stages = tuple("xnyf")
+    arrays = chain.enter(*codec_expand_kept.both())
+    expand_blocks = grad_rows((arrays, 0, width), (arrays, width, inner), order, expand_stages, 4, 0)
+    chain.leave(*expand_blocks)
+
+    grads, frame_grads_kept.other = chain.enter(grads, frame_grads_kept.other)
+    chain.leave(grads)
+    contract_sum = Reduce(contract_stages, chain.enter(*contract_blocks))
+    expand_sum = Reduce(expand_stages, chain.enter(*expand_blocks))
+    codec_kept = Pair(chain.enter(codec_kept))
+    projected_pair = Pair(chain.enter(projected_grad))
     packed_grad = frame_attend_grads_call(packed, chain.enter(grads), every_segment)
     chain.leave(packed_grad)
+    kept, arrays = frame_kept.both(), chain.enter(*frame_grads_kept.both())
+    frame_contract_blocks = grad_columns(
+        (kept, 3 * width, inner), (arrays, 0, width), order, contract_stages, 4, 0
+    )
+    chain.leave(*frame_contract_blocks)
+    frame_expand_stages = tuple("xynf")
+    arrays = chain.enter(*arrays)
+    blocks = grad_rows(
+        (kept, 2 * width, width), (arrays, width, inner), order, frame_expand_stages, 5, 0
+    )
+    frame_expand_blocks = grad_rows(
+        (kept, width, width), (arrays, width + inner, width), order, frame_expand_stages, 5, 4, blocks
+    )
+    chain.leave(*frame_expand_blocks)
+
+    packed_grad, codec_kept.other, projected_pair.other = chain.enter(
+        packed_grad, codec_kept.other, projected_pair.other
+    )
+    chain.leave(packed_grad)
+    contract_sum.arrive(chain)
+    expand_sum.arrive(chain)
     packed_grad = lax.all_to_all(packed_grad, "seq", split_axis=0, concat_axis=0, tiled=True)
+    contract_sum.step(chain)
     expand_sum.step(chain)
+    frame_contract_sum = Reduce(contract_stages, chain.enter(*frame_contract_blocks))
+    frame_expand_sum = Reduce(frame_expand_stages, chain.enter(*frame_expand_blocks))
+    table_pair = Pair(chain.enter(table_in))
+    project_stages = tuple("yxnf")
+    arrays = chain.enter(*codec_kept.both())
+    blocks = grad_rows(
+        (arrays, 0, width), (projected_pair.both(), 0, 3 * width), order, project_stages, 4, 0
+    )
+    project_blocks = grad_rows(
+        (arrays, width, width), (arrays, 2 * width, width), order, project_stages, 4, 3, blocks
+    )
+    chain.leave(*project_blocks)
+    table_stages = tuple("xynf")
+    table_blocks = grad_table(
+        jnp.concatenate(codes_pair.both(), axis=1),
+        chain.enter(*table_pair.both()),
+        order,
+        table_stages,
+        codebooks.shape[0],
+        2,
+        0,
+    )
+    chain.leave(*table_blocks)
+    output = codec_result(codec_mixed, chain.enter(codec_activated), live, codec_contract_all)
+    chain.leave(output)
+    output = jnp.transpose(output, (1, 0, 2)).reshape(row_count, frames_dev, positions, width)
+
+    packed_grad, contract_sum.coming, expand_sum.coming, frame_contract_sum.coming = chain.enter(
+        packed_grad, contract_sum.coming, expand_sum.coming, frame_contract_sum.coming
+    )
+    packed_grad, frame_expand_sum.coming = chain.enter(packed_grad, frame_expand_sum.coming)
+    chain.leave(packed_grad)
+    frame_contract_sum.step(chain)
+    frame_expand_sum.step(chain)
+    frame_projected_grad, frames_grad, frame_prenorm_grad = frame_front_grads(
+        chain.enter(packed_grad), hidden, gains[0], frame_mixed_grad, frame_project_all
+    )
+    chain.leave(frames_grad)
+    frame_projected_pair = Pair(frame_projected_grad)
+    gain_pair = Pair(
+        jnp.concatenate(
+            [frame_prenorm_grad, frame_postnorm_grad, codec_prenorm_grad, codec_postnorm_grad]
+        )
+    )
+    frame_projected_pair.other, gain_pair.other = chain.enter(
+        frame_projected_pair.other, gain_pair.other
+    )
+    chain.leave(gain_pair.other)
+    blocks = grad_rows(
+        (kept, 0, width),
+        (chain.enter(*frame_projected_pair.both()), 0, 3 * width),
+        order,
+        table_stages,
+        3,
+        0,
+    )
+    chain.leave(*blocks)
+    riders = gain_pair.own + gain_pair.other
+    frame_project_sum = Reduce(table_stages, blocks, chain.enter(riders))
+    project_sum = Reduce(project_stages, chain.enter(*project_blocks))
     contract_sum.step(chain)
-    stages = tuple("nyxf")
-    blocks = grad_rows(codec_normed_both, chain.enter(*projected_pair), order, stages, 6, 0)
-    blocks = grad_rows(codec_attended_both, output_pair, order, stages, 6, 3, blocks)
-    blocks = grad_table(codes_both, table_pair, order, stages, codebooks.shape[0], 6, 4, blocks)
-    chain.leave(*blocks)
-    codec_sum = Reduce(stages, blocks)
+    expand_sum.step(chain)
     frame_contract_sum.step(chain)
-    expand_sum.step(chain)
-    codec_result = mixed_sum + matmul(chain.enter(activated), weight_contract)
-    output = jnp.transpose(
-        (codec_result.reshape(positions, frame_total, width) * live).astype(BF), (1, 0, 2)
-    ).reshape(row_count, frames_dev, positions, width)
-    chain.leave(output)
     frame_expand_sum.step(chain)
-    frame_projected_grad = jnp.transpose(
-        chain.enter(packed_grad).reshape(count, row_count, frames_dev, 3, LANES), (1, 2, 3, 0, 4)
-    ).reshape(frame_total, 3 * width)
-    frame_projected_pair = pair(frame_projected_grad)
-    chain.leave(frame_projected_grad)
-    frames_grad, frame_prenorm_grad = front_grads(
-        hidden, chain.enter(frame_projected_grad), frame_mixed_grad, frame_weights
-    )
-    chain.leave(frames_grad)
-    stages = tuple("nxyf")
-    blocks = grad_rows(normed_both, chain.enter(*frame_projected_pair), order, stages, 3, 0)
-    chain.leave(*blocks)
-    frame_project_sum = Reduce(stages, blocks)
-    gain_sums = sum_everywhere(
-        jnp.stack(
-            [frame_prenorm_grad, frame_postnorm_grad, codec_prenorm_grad, codec_postnorm_grad]
-        ),
-        place,
-    )
-    frame_contract_sum.step(chain)
-    codec_sum.step(chain)
-    frame_expand_sum.step(chain)
-    frame_contract_sum.step(chain)
-    codec_sum.step(chain)
+    table_sum = Reduce(table_stages, chain.enter(*table_blocks))
+    take_first = finish([contract_sum, expand_sum], chain)
     frame_project_sum.step(chain)
-    frame_expand_sum.step(chain)
+    take_second = finish([frame_contract_sum, frame_expand_sum], chain)
+    project_sum.step(chain)
+    table_sum.step(chain)
     frame_project_sum.step(chain)
-    codec_sum.step(chain)
-    frame_project_sum.step(chain)
+    project_sum.step(chain)
+    table_sum.step(chain)
+    take_third = finish([frame_project_sum], chain)
+    take_fourth = finish([project_sum, table_sum], chain)
+    take_first()
+    take_second()
+    take_third()
+    take_fourth()
 
     height = frame_project.shape[0]
-    codec_two = codec_sum.result()
-    frame_one = frame_expand_sum.result()
+    project_units = project_sum.result()
+    frame_expand_units = frame_expand_sum.result()
+    gain_sums = frame_project_sum.riders
     return (
         output,
         frames_grad.reshape(row_count, frames_dev, width),
-        rows_from_units(codec_two[4:], codebooks.shape[0]),
+        rows_from_units(table_sum.result(), codebooks.shape[0]),
         gain_sums[0],
         rows_from_units(frame_project_sum.result(), height),
-        rows_from_units(frame_one[4:], height),
+        rows_from_units(frame_expand_units[4:], height),
         gain_sums[1],
-        rows_from_units(frame_one[:4], height),
+        rows_from_units(frame_expand_units[:4], height),
         columns_from_units(frame_contract_sum.result()),
         gain_sums[2],
-        rows_from_units(codec_two[:3], height),
-        rows_from_units(codec_two[3:4], height),
+        rows_from_units(project_units[:3], height),
+        rows_from_units(project_units[3:], height),
         gain_sums[3],
         rows_from_units(expand_sum.result(), height),
         columns_from_units(contract_sum.result()),

time: 808 us -> 738 us (0.913)
  Pallas kernels: 169 us -> 303 us
  matrix products: 121 us -> 0 us
  waiting for transfers between devices: 276 us -> 193 us
  local copies, waits for them, and re-layouts: 68.4 us -> 83.1 us
  starting transfers between devices: 89.3 us -> 80.1 us
    pallas_call x4 -> x15, Pallas kernels: 41.2 us -> 177 us  [the longest x1 41.9 us: codec_rear(): dense_call(codec_rear_kernel, inner // tile, [held(base.shape), held(entr...]
    dot_general x16 -> x0, matrix products: 121 us -> none  [the longest x8 65.1 us: matmul(): return jnp.dot(former, latter, preferred_element_type=F32)]
    ppermute x83 -> x60, waiting for transfers between devices: 276 us -> 182 us  [swap(): lax.ppermute(values, axis, [(i, i ^ bit) for i in range(lax.axis_size(axi...]
    unnamed x195 -> x149, local copies, waits for them, and re-layouts: 31.3 us -> 45.6 us
    concatenate x1 -> x9, other arithmetic: 0.01 us -> 8.4 us  [the longest x4 5.18 us: load(): jnp.concatenate([part.reshape(-1, LANES) for part in (block, high, low)],...]
    ppermute x83 -> x60, starting transfers between devices: 63.2 us -> 54.8 us  [swap(): lax.ppermute(values, axis, [(i, i ^ bit) for i in range(lax.axis_size(axi...]
    convert_element_type x28 -> x26, other arithmetic: 48.9 us -> 40.8 us  [the longest x20 39.5 us: give(): given = self.total(False).astype(BF)]
  transfers between devices with their start and end apart: 88 -> 65, of which waited for: 28 -> 28; matrix products, arithmetic and copies ran while one was open for 24% -> 14% of each run, Pallas kernels for 19% -> 32%
where the time goes in v5:
time: 738 us; the launch traced here: 728 us
  Pallas kernels  303 us (41%)
  waiting for transfers between devices  193 us (26%)
  local copies, waits for them, and re-layouts  83.1 us (11%)
  starting transfers between devices  80.1 us (11%)
  other arithmetic  66.4 us (9%)
    ppermute x60, waiting for transfers between devices, swap(): lax.ppermute(values, axis, [(i, i ^ bit) for i in range(lax.axis_size(axi...  182 us
    pallas_call x9, Pallas kernels, grad_call(): pl.pallas_call(kernel, grid_spec=pltpu.PrefetchScalarGridSpec(num_scalar_...  77.8 us
    ppermute x60, starting transfers between devices, swap(): lax.ppermute(values, axis, [(i, i ^ bit) for i in range(lax.axis_size(axi...  54.8 us
    unnamed x149, local copies, waits for them, and re-layouts  45.6 us
    pallas_call x1, Pallas kernels, codec_rear(): dense_call(codec_rear_kernel, inner // tile, [held(base.shape), held(entr...  41.9 us
    pallas_call x4, Pallas kernels, join_weights(): pl.pallas_call(functools.partial(join_kernel, shapes), in_specs=[pl.Block...  41.2 us
    convert_element_type x20, other arithmetic, give(): given = self.total(False).astype(BF)  39.5 us
    pallas_call x1, Pallas kernels, frame_rear(): dense_call(frame_rear_kernel, inner // tile, [held(hidden.shape), held(fr...  15.5 us
  transfers between devices with their start and end apart: 65, of which 28 were waited for; matrix products, arithmetic and copies ran while one was open for 14% of the time, Pallas kernels for 32%

profile of v5, /device:TPU:0, one launch (start us, length us, event | category | flops | bytes accessed | tf_op | source)
XLA Modules:
  0.0 727.5 jit_solution(18066507337650115720)
XLA Ops:
  5.0 3.4 pack_weights.5
  9.0 3.5 pack_weights.7
  15.7 2.6 collective-permute-start.1
  18.8 5.8 all-to-all-start
  24.6 6.5 all-to-all-done
  34.5 2.5 pack_weights.6
  40.2 10.0 %collective-permute-done.2.refs_1_ = bf16[224,1024]{1,0:T(8,128)(2,1)S(1)} collective-permute-done((bf16[224,1024]{1,0:T(8,128)(2,1)}, bf16[224,1024]{1,0:T(8,128)(2,1)S(1)}, u32[]{:S(2)}, u32[]{:S(2)}) %collective-permute-start.2) | collective-permute-done | bytes 458784 | tf_op jit(solution)/shard_map/ppermute | solution.py:46
  51.0 7.2 collective-permute-done.7.refs_0_
  60.8 5.5 collective-permute-done.5.refs_3_
  74.1 6.1 join_weights.4
  83.1 6.4 frame_front.1
  89.4 8.2 %collective-permute-done.14.refs_0_ = bf16[576,1024]{1,0:T(8,128)(2,1)} collective-permute-done((bf16[576,1024]{1,0:T(8,128)(2,1)}, bf16[576,1024]{1,0:T(8,128)(2,1)}, u32[]{:S(2)}, u32[]{:S(2)}) %collective-permute-start.14) | collective-permute-done | bytes 1179680 | tf_op jit(solution)/shard_map/ppermute | solution.py:46
  99.1 5.8 all-to-all-start.1
  110.8 25.2 %collective-permute-done.15.refs_3_ = bf16[288,1024]{1,0:T(8,128)(2,1)S(1)} collective-permute-done((bf16[288,1024]{1,0:T(8,128)(2,1)S(1)}, bf16[288,1024]{1,0:T(8,128)(2,1)S(1)}, u32[]{:S(2)}, u32[]{:S(2)}) %collective-permute-start.15) | collective-permute-done | bytes 589856 | tf_op jit(solution)/shard_map/ppermute | solution.py:46
  136.8 7.7 %collective-permute-done.16.refs_4_ = bf16[288,1024]{1,0:T(8,128)(2,1)S(1)} collective-permute-done((bf16[288,1024]{1,0:T(8,128)(2,1)S(1)}, bf16[288,1024]{1,0:T(8,128)(2,1)S(1)}, u32[]{:S(2)}, u32[]{:S(2)}) %collective-permute-start.16) | collective-permute-done | bytes 589856 | tf_op jit(solution)/shard_map/ppermute | solution.py:46
  147.4 4.7 far_pack.4.refs_2_
  157.4 8.7 %frame_attend.1 = bf16[8,2,128,128]{3,2,1,0:T(8,128)(2,1)S(1)} custom-call(bf16[8,2,128,384]{3,2,1,0:T(8,128)(2,1)S(1)} %all-to-all-done.1.packed_ref, s32[2,1024,1]{2,1,0:T(8,128)S(1)} %copy-done.2, s32[2,1,1024]{2,1,0:T(1,128)S(1)} %broadcast_in_dim.16.seg_row_ref), custom_call_target="tpu_custom_call" | custom-call | flops 1 | bytes 1 | tf_op jit(solution)/shard_map/frame_attend/pallas_call | solution.py:462
  166.8 4.8 all-to-all-start.2
  171.7 13.2 %join_weights.5 = (bf16[1024,4096]{1,0:T(8,128)(2,1)}, bf16[4096,1024]{1,0:T(8,128)(2,1)}, bf16[1024,1024]{1,0:T(8,128)(2,1)S(1)}) custom-call(s32[2]{0:T(128)S(1)} %pad_add_fusion.1.place_ref, bf16[2304,1024]{1,0:T(8,128)(2,1)} %get-tuple-element.313.refs_0_, bf16[2304,1024]{1,0:T(8,128)(2,1)} %collective-permute-done.8.refs_1_, ...), custom_call_target="tpu_custom_call" | custom-call | flops 1 | bytes 1 | tf_op jit(solution)/shard_map/join_weights/pallas_call | solution.py:1053
  187.1 4.7 all-to-all-done.2.packed_ref
  196.8 15.5 %frame_rear.1 = (bf16[256,7168]{1,0:T(8,128)(2,1)}, f32[256,1024]{1,0:T(8,128)}, bf16[256,4096]{1,0:T(8,128)(2,1)}, bf16[256,1024]{1,0:T(8,128)(2,1)}) custom-call(bf16[256,1024]{1,0:T(8,128)(2,1)} %bitcast.263, bf16[256,1024]{1,0:T(8,128)(2,1)} %get-tuple-element.293.front_ref, bf16[8,2,128,128]{3,2,1,0:T(8,128)(2,1)} %all-to-all-done.2.packed_ref, ...), custom_call_target="tpu_custom_call" | custom-call | flops 1 | bytes 1 | tf_op jit(solution)/shard_map/frame_rear/pallas_call | solution.py:1191
  212.4 4.7 far_pack.5.refs_2_
  219.1 8.7 %join_weights.6 = (bf16[1024,3072]{1,0:T(8,128)(2,1)}, bf16[2048,1024]{1,0:T(8,128)(2,1)}) custom-call(s32[2]{0:T(128)S(1)} %pad_add_fusion.1.place_ref, bf16[1280,1024]{1,0:T(8,128)(2,1)} %get-tuple-element.336.refs_0_, bf16[1280,1024]{1,0:T(8,128)(2,1)} %collective-permute-done.11.refs_1_, bf16[1280,1024]{1,0:T(8,128)(2,1)} %collective-permute-done.20.refs_2_, ...), custom_call_target="tpu_custom_call" | custom-call | flops 1 | bytes 1 | tf_op jit(solution)/shard_map/join_weights/pallas_call | solution.py:1053
  230.1 6.2 gather_fusion
  236.3 10.5 %codec_front.1 = (bf16[768,1024]{1,0:T(8,128)(2,1)}, bf16[3,256,3072]{2,1,0:T(8,128)(2,1)}) custom-call(bf16[256,1024]{1,0:T(8,128)(2,1)} %get-tuple-element.342.base_ref, bf16[2,256,1024]{2,1,0:T(8,128)(2,1)} %bitcast.258, f32[1,1024]{1,0:T(1,128)} %bitcast.283, bf16[1024,3072]{1,0:T(8,128)(2,1)} %get-tuple-element.341.weight_ref), custom_call_target="tpu_custom_call" | custom-call | flops 1 | bytes 1 | tf_op jit(solution)/shard_map/codec_front/pallas_call | solution.py:1358
  246.8 6.0 codec_attend.1
  253.9 13.2 %join_weights.7 = (bf16[1024,4096]{1,0:T(8,128)(2,1)}, bf16[4096,1024]{1,0:T(8,128)(2,1)}, bf16[1024,1024]{1,0:T(8,128)(2,1)S(1)}) custom-call(s32[2]{0:T(128)S(1)} %pad_add_fusion.1.place_ref, bf16[2304,1024]{1,0:T(8,128)(2,1)} %get-tuple-element.350.refs_0_, bf16[2304,1024]{1,0:T(8,128)(2,1)} %collective-permute-done.9.refs_1_, ...), custom_call_target="tpu_custom_call" | custom-call | flops 1 | bytes 1 | tf_op jit(solution)/shard_map/join_weights/pallas_call | solution.py:1053
  268.4 41.9 %codec_rear.1 = (f32[768,1024]{1,0:T(8,128)}, bf16[768,4096]{1,0:T(8,128)(2,1)}, bf16[768,5120]{1,0:T(8,128)(2,1)}, bf16[768,3072]{1,0:T(8,128)(2,1)}, f32[768,1...) custom-call(bf16[256,1024]{1,0:T(8,128)(2,1)} %get-tuple-element.342.base_ref, ...), custom_call_target="tpu_custom_call" | custom-call | flops 1 | bytes 1 | tf_op jit(solution)/shard_map/codec_rear/pallas_call | solution.py:1437
  312.4 8.5 %codec_attend_grads.1 = bf16[3,256,3072]{2,1,0:T(8,128)(2,1)} custom-call(bf16[3,256,3072]{2,1,0:T(8,128)(2,1)} %get-tuple-element.345.packed_ref, bf16[3,256,1024]{2,1,0:T(8,128)(2,1)S(1)} %copy-done.28, bf16[1024,128]{1,0:T(8,128)(2,1)S(1)} %fusion.25.marks_ref), custom_call_target="tpu_custom_call" | custom-call | flops 1 | bytes 1 | tf_op jit(solution)/shard_map/codec_attend_grads/pallas_call | solution.py:622
  320.9 13.3 %codec_front_grads.1 = (bf16[256,1024]{1,0:T(8,128)(2,1)}, bf16[512,1024]{1,0:T(8,128)(2,1)}, f32[1,1024]{1,0:T(1,128)}) custom-call(bf16[768,3072]{1,0:T(8,128)(2,1)} %bitcast.255, bf16[256,1024]{1,0:T(8,128)(2,1)} %get-tuple-element.342.base_ref, bf16[2,256,1024]{2,1,0:T(8,128)(2,1)} %bitcast.260, f32[1,1024]{1,0:T(1,128)} %bitcast.284, ...), custom_call_target="tpu_custom_call" | custom-call | flops 1 | bytes 1 | tf_op jit(solution)/shard_map/codec_front_grads/pallas_call | solution.py:1546
  334.2 14.8 %frame_rear_grads.1 = (bf16[256,6144]{1,0:T(8,128)(2,1)}, f32[256,1024]{1,0:T(8,128)}, bf16[8,2,128,128]{3,2,1,0:T(8,128)(2,1)}, f32[1,1024]{1,0:T(1,128)}) custom-call(bf16[256,1024]{1,0:T(8,128)(2,1)} %get-tuple-element.367.grad_ref, bf16[256,4096]{1,0:T(8,128)(2,1)} %get-tuple-element.368.slope_ref, f32[256,1024]{1,0:T(8,128)} %get-tuple-element.369.mixed_ref, ...), custom_call_target="tpu_custom_call" | custom-call | flops 1 | bytes 1 | tf_op jit(solution)/shard_map/frame_rear_grads/pallas_call | solution.py:1260
  349.5 4.3 all-to-all-start.3
  353.9 12.3 %grad_columns.2 = (bf16[2,2,2,4,256,128]{5,4,3,2,1,0:T(8,128)(2,1)S(1)}, bf16[2,2,2,4,256,128]{5,4,3,2,1,0:T(8,128)(2,1)}) custom-call(s32[27]{0:T(128)S(1)} %stack.69.order_ref, bf16[768,1024]{1,0:T(8,128)(2,1)S(1)} %bitcast.252, bf16[768,1024]{1,0:T(8,128)(2,1)} %collective-permute-done.24.latter_rec, ...), custom_call_target="tpu_custom_call" | custom-call | flops 1 | bytes 1 | tf_op jit(solution)/shard_map/grad_columns/pallas_call | solution.py:726
  367.5 12.9 %grad_rows.6 = (bf16[2,2,2,4,256,128]{5,4,3,2,1,0:T(8,128)(2,1)S(1)}, bf16[2,2,2,4,256,128]{5,4,3,2,1,0:T(8,128)(2,1)S(1)}) custom-call(s32[27]{0:T(128)S(1)} %stack.69.order_ref, bf16[768,5120]{1,0:T(8,128)(2,1)} %get-tuple-element.380.far_own.own_own.latter_own, bf16[768,5120]{1,0:T(8,128)(2,1)} %collective-permute-done.28.far_rec.own_rec.latter_rec, ...), custom_call_target="tpu_custom_call" | custom-call | flops 1 | bytes 1 | tf_op jit(solution)/shard_map/grad_rows/pallas_call | solution.py:726
  387.1 14.7 %frame_attend_grads.1 = bf16[8,2,128,384]{3,2,1,0:T(8,128)(2,1)S(1)} custom-call(bf16[8,2,128,384]{3,2,1,0:T(8,128)(2,1)S(1)} %all-to-all-done.1.packed_ref, bf16[8,2,128,128]{3,2,1,0:T(8,128)(2,1)} %all-to-all-done.3.grad_ref, s32[2,1024,1]{2,1,0:T(8,128)S(1)} %copy-done.3, s32[2,1,1024]{2,1,0:T(1,128)S(1)} %broadcast_in_dim.16.seg_row_ref), custom_call_target="tpu_custom_call" | custom-call | flops 1 | bytes 1 | tf_op jit(solution)/shard_map/frame_attend_grads/pallas_call | solution.py:477
  403.0 7.3 %grad_columns.3 = (bf16[2,2,2,4,256,128]{5,4,3,2,1,0:T(8,128)(2,1)}, bf16[2,2,2,4,256,128]{5,4,3,2,1,0:T(8,128)(2,1)S(1)}) custom-call(s32[27]{0:T(128)S(1)} %stack.69.order_ref, bf16[256,6144]{1,0:T(8,128)(2,1)} %get-tuple-element.399.latter_own, bf16[256,6144]{1,0:T(8,128)(2,1)} %collective-permute-done.29.latter_rec, ...), custom_call_target="tpu_custom_call" | custom-call | flops 1 | bytes 1 | tf_op jit(solution)/shard_map/grad_columns/pallas_call | solution.py:726
  411.7 9.3 %grad_rows.7 = (bf16[2,2,2,5,256,128]{5,4,3,2,1,0:T(8,128)(2,1)}, bf16[2,2,2,5,256,128]{5,4,3,2,1,0:T(8,128)(2,1)S(1)}) custom-call(s32[27]{0:T(128)S(1)} %stack.69.order_ref, bf16[256,7168]{1,0:T(8,128)(2,1)} %get-tuple-element.347.former_own.far_own.own_own, bf16[256,7168]{1,0:T(8,128)(2,1)} %collective-permute-done.25.former_rec.far_rec.own_rec, ...), custom_call_target="tpu_custom_call" | custom-call | flops 1 | bytes 1 | tf_op jit(solution)/shard_map/grad_rows/pallas_call | solution.py:726
  421.0 3.9 grad_rows.8
  424.8 4.6 all-to-all-start.4
  431.6 9.1 %collective-permute-done.30 = bf16[2,2,2,4,256,128]{5,4,3,2,1,0:T(8,128)(2,1)} collective-permute-done((bf16[2,2,2,4,256,128]{5,4,3,2,1,0:T(8,128)(2,1)}, bf16[2,2,2,4,256,128]{5,4,3,2,1,0:T(8,128)(2,1)}, u32[]{:S(2)}, u32[]{:S(2)}) %collective-permute-start.30) | collective-permute-done | bytes 2097184 | tf_op jit(solution)/shard_map/ppermute | solution.py:46
  440.8 2.8 fusion.3
  443.5 2.5 fusion.4
  446.0 3.0 collective-permute-start.38
  452.5 12.4 %grad_rows.9 = (bf16[2,2,2,4,256,128]{5,4,3,2,1,0:T(8,128)(2,1)}, bf16[2,2,2,4,256,128]{5,4,3,2,1,0:T(8,128)(2,1)S(1)}) custom-call(s32[27]{0:T(128)S(1)} %stack.69.order_ref, bf16[768,3072]{1,0:T(8,128)(2,1)} %get-tuple-element.415.far_own.own_own.latter_own, bf16[768,3072]{1,0:T(8,128)(2,1)} %collective-permute-done.32.far_rec.own_rec.latter_rec, ...), custom_call_target="tpu_custom_call" | custom-call | flops 1 | bytes 1 | tf_op jit(solution)/shard_map/grad_rows/pallas_call | solution.py:726
  464.9 5.6 grad_rows.10
  471.8 5.9 grad_table.1
  478.8 13.7 %codec_result.1 = bf16[3,256,1024]{2,1,0:T(8,128)(2,1)} custom-call(f32[768,1024]{1,0:T(8,128)} %get-tuple-element.358.mixed_ref, bf16[768,4096]{1,0:T(8,128)(2,1)} %get-tuple-element.426.former_own.active_ref, f32[256,1]{1,0:T(8,128)} %copy.63.live_ref, bf16[4096,1024]{1,0:T(8,128)(2,1)} %get-tuple-element.355.contract_ref), custom_call_target="tpu_custom_call" | custom-call | flops 1 | bytes 1 | tf_op jit(solution)/shard_map/codec_result/pallas_call | solution.py:1495
  492.6 12.7 %collective-permute-done.35 = bf16[2,2,4,256,128]{4,3,2,1,0:T(8,128)(2,1)} collective-permute-done((bf16[2,2,4,256,128]{4,3,2,1,0:T(8,128)(2,1)}, bf16[2,2,4,256,128]{4,3,2,1,0:T(8,128)(2,1)}, u32[]{:S(2)}, u32[]{:S(2)}) %collective-permute-start.35) | collective-permute-done | bytes 1048608 | tf_op jit(solution)/shard_map/ppermute | solution.py:46
  506.5 2.8 fusion.5
  509.4 2.8 fusion.1
  512.2 7.8 %frame_front_grads.1 = (bf16[256,3072]{1,0:T(8,128)(2,1)}, f32[256,1024]{1,0:T(8,128)}, f32[1,1024]{1,0:T(1,128)}) custom-call(bf16[8,2,128,384]{3,2,1,0:T(8,128)(2,1)} %all-to-all-done.4.packed_ref, bf16[256,1024]{1,0:T(8,128)(2,1)} %bitcast.264, f32[1,1024]{1,0:T(1,128)} %bitcast.286, f32[256,1024]{1,0:T(8,128)} %get-tuple-element.440.mixed_grad_ref, ...), custom_call_target="tpu_custom_call" | custom-call | flops 1 | bytes 1 | tf_op jit(solution)/shard_map/frame_front_grads/pallas_call | solution.py:1314
  521.3 6.9 collective-permute-start.40
  531.3 8.1 %grad_rows.11 = (bf16[2,2,2,3,256,128]{5,4,3,2,1,0:T(8,128)(2,1)S(1)}, bf16[2,2,2,3,256,128]{5,4,3,2,1,0:T(8,128)(2,1)S(1)}) custom-call(s32[27]{0:T(128)S(1)} %stack.69.order_ref, bf16[256,7168]{1,0:T(8,128)(2,1)} %get-tuple-element.347.former_own.far_own.own_own, bf16[256,7168]{1,0:T(8,128)(2,1)} %collective-permute-done.25.former_rec.far_rec.own_rec, ...), custom_call_target="tpu_custom_call" | custom-call | flops 1 | bytes 1 | tf_op jit(solution)/shard_map/grad_rows/pallas_call | solution.py:726
  554.3 5.9 collective-permute-done.39
  560.2 2.4 fusion.2
  562.6 29.7 %collective-permute-done.47 = bf16[2,4,256,128]{3,2,1,0:T(8,128)(2,1)S(1)} collective-permute-done((bf16[2,4,256,128]{3,2,1,0:T(8,128)(2,1)S(1)}, bf16[2,4,256,128]{3,2,1,0:T(8,128)(2,1)S(1)}, u32[]{:S(2)}, u32[]{:S(2)}) %collective-permute-start.47) | collective-permute-done | bytes 524320 | tf_op jit(solution)/shard_map/ppermute | solution.py:46
  598.5 2.5 fusion
  608.8 25.4 %collective-permute-done.59 = bf16[8,256,128]{2,1,0:T(8,128)(2,1)} collective-permute-done((bf16[8,256,128]{2,1,0:T(8,128)(2,1)}, bf16[8,256,128]{2,1,0:T(8,128)(2,1)}, u32[]{:S(2)}, u32[]{:S(2)}) %collective-permute-start.59) | collective-permute-done | bytes 524320 | tf_op jit(solution)/shard_map/ppermute | solution.py:46
  634.1 2.6 fusion.15
  644.9 3.1 fusion.6
  656.6 6.2 collective-permute-done.52
  677.9 8.6 %collective-permute-done.54 = bf16[1600,128]{1,0:T(8,128)(2,1)S(1)} collective-permute-done((bf16[1600,128]{1,0:T(8,128)(2,1)S(1)}, bf16[1600,128]{1,0:T(8,128)(2,1)S(1)}, u32[]{:S(2)}, u32[]{:S(2)}) %collective-permute-start.54) | collective-permute-done | bytes 409632 | tf_op jit(solution)/shard_map/ppermute | solution.py:46
  698.8 2.5 collective-permute-done.57
  712.9 9.3 %collective-permute-done.56 = bf16[6,256,128]{2,1,0:T(8,128)(2,1)S(1)} collective-permute-done((bf16[6,256,128]{2,1,0:T(8,128)(2,1)}, bf16[6,256,128]{2,1,0:T(8,128)(2,1)S(1)}, u32[]{:S(2)}, u32[]{:S(2)}) %collective-permute-start.56) | collective-permute-done | bytes 393248 | tf_op jit(solution)/shard_map/ppermute | solution.py:46
  (353 shorter events, 176.1 us)
Async XLA Ops:
  8.4 49.7 %collective-permute-start.8 = (bf16[2304,1024]{1,0:T(8,128)(2,1)}, bf16[2304,1024]{1,0:T(8,128)(2,1)}, u32[]{:S(2)}, u32[]{:S(2)}) collective-permute-start(bf16[2304,1024]{1,0:T(8,128)(2,1)} %get-tuple-element.313.refs_0_), channel_id=1, source_target_pairs={{0,1},{1,0},{2,3},{3,2},{4,5},{5,4},{6,7},{7,6},{8,9},{9,8},{10,11... | collective-permute-start | bytes 14155784 | tf_op jit(solution)/shard_map/ppermute | solution.py:46
  12.5 56.3 %collective-permute-start.9 = (bf16[2304,1024]{1,0:T(8,128)(2,1)}, bf16[2304,1024]{1,0:T(8,128)(2,1)}, u32[]{:S(2)}, u32[]{:S(2)}) collective-permute-start(bf16[2304,1024]{1,0:T(8,128)(2,1)} %get-tuple-element.350.refs_0_), channel_id=1, source_target_pairs={{0,1},{1,0},{2,3},{3,2},{4,5},{5,4},{6,7},{7,6},{8,9},{9,8},{10,11... | collective-permute-start | bytes 14155784 | tf_op jit(solution)/shard_map/ppermute | solution.py:46
  13.9 17.3 %collective-permute-start = (bf16[896,1024]{1,0:T(8,128)(2,1)S(1)}, bf16[896,1024]{1,0:T(8,128)(2,1)}, u32[]{:S(2)}, u32[]{:S(2)}) collective-permute-start(bf16[896,1024]{1,0:T(8,128)(2,1)S(1)} %get-tuple-element.286.refs_0_), channel_id=1, source_target_pairs={{0,1},{1,0},{2,3},{3,2},{4,5},{5,4},{6,7},{7,6},{8,9},{9,8},{10,11... | collective-permute-start | bytes 5505032 | tf_op jit(solution)/shard_map/ppermute | solution.py:46
  15.7 15.5 %collective-permute-start.1 = (bf16[224,1024]{1,0:T(8,128)(2,1)S(1)}, bf16[224,1024]{1,0:T(8,128)(2,1)}, u32[]{:S(2)}, u32[]{:S(2)}) collective-permute-start(bf16[224,1024]{1,0:T(8,128)(2,1)S(1)} %get-tuple-element.267), channel_id=1, source_target_pairs={{0,2},{1,3},{2,0},{3,1},{4,6},{5,7},{6,4},{7,5},{8,10},{9,11},{10,... | collective-permute-start | bytes 1376264 | tf_op jit(solution)/shard_map/ppermute | solution.py:46
  18.8 12.3 %all-to-all-start = ((s32[8,2,128]{2,1,0:T(2,128)}), s32[8,2,128]{2,1,0:T(2,128)S(1)}, u32[]{:S(2)}, u32[]{:S(2)}) async-start(s32[8,2,128]{2,1,0:T(2,128)} %broadcast_in_dim.13), calls=%async_computation | async-start | bytes 16384 | tf_op jit(solution)/shard_map/all_to_all | solution.py:1917
  31.2 27.0 %collective-permute-start.7 = (bf16[576,1024]{1,0:T(8,128)(2,1)}, bf16[576,1024]{1,0:T(8,128)(2,1)}, u32[]{:S(2)}, u32[]{:S(2)}) collective-permute-start(bf16[576,1024]{1,0:T(8,128)(2,1)} %copy-done.41), channel_id=1, source_target_pairs={{0,2},{1,3},{2,0},{3,1},{4,6},{5,7},{6,4},{7,5},{8,10},{9,11},{10,... | collective-permute-start | bytes 3538952 | tf_op jit(solution)/shard_map/ppermute | solution.py:46
  31.8 6.3 collective-permute-start.4
  37.0 13.2 %collective-permute-start.2 = (bf16[224,1024]{1,0:T(8,128)(2,1)}, bf16[224,1024]{1,0:T(8,128)(2,1)S(1)}, u32[]{:S(2)}, u32[]{:S(2)}) collective-permute-start(bf16[224,1024]{1,0:T(8,128)(2,1)} %collective-permute-done.1.refs_0_), channel_id=1, source_target_pairs={{0,4},{4,0},{8,12},{12,8},{16,20},{20,16},{24,28},{28,24},{1,5},{5... | collective-permute-start | bytes 1376264 | tf_op jit(solution)/shard_map/ppermute | solution.py:46
  38.1 12.8 %collective-permute-start.3 = (bf16[224,1024]{1,0:T(8,128)(2,1)}, bf16[224,1024]{1,0:T(8,128)(2,1)S(1)}, u32[]{:S(2)}, u32[]{:S(2)}) collective-permute-start(bf16[224,1024]{1,0:T(8,128)(2,1)} %collective-permute-done.1.refs_0_), channel_id=1, source_target_pairs={{0,8},{4,12},{8,0},{12,4},{16,24},{20,28},{24,16},{28,20},{1,9},{5... | collective-permute-start | bytes 1376264 | tf_op jit(solution)/shard_map/ppermute | solution.py:46
  58.1 24.9 %collective-permute-start.11 = (bf16[1280,1024]{1,0:T(8,128)(2,1)}, bf16[1280,1024]{1,0:T(8,128)(2,1)}, u32[]{:S(2)}, u32[]{:S(2)}) collective-permute-start(bf16[1280,1024]{1,0:T(8,128)(2,1)} %get-tuple-element.336.refs_0_), channel_id=1, source_target_pairs={{0,1},{1,0},{2,3},{3,2},{4,5},{5,4},{6,7},{7,6},{8,9},{9,8},{10,11... | collective-permute-start | bytes 7864328 | tf_op jit(solution)/shard_map/ppermute | solution.py:46
  58.2 8.1 %collective-permute-start.5 = (bf16[112,1024]{1,0:T(8,128)(2,1)S(1)}, bf16[112,1024]{1,0:T(8,128)(2,1)S(1)}, u32[]{:S(2)}, u32[]{:S(2)}) collective-permute-start(bf16[112,1024]{1,0:T(8,128)(2,1)S(1)} %slice.385), channel_id=1, source_target_pairs={{0,4},{4,0},{8,12},{12,8},{16,20},{20,16},{24,28},{28,24},{1,5},{5... | collective-permute-start | bytes 688136 | tf_op jit(solution)/shard_map/ppermute | solution.py:46
  59.2 7.7 %collective-permute-start.6 = (bf16[112,1024]{1,0:T(8,128)(2,1)S(1)}, bf16[112,1024]{1,0:T(8,128)(2,1)S(1)}, u32[]{:S(2)}, u32[]{:S(2)}) collective-permute-start(bf16[112,1024]{1,0:T(8,128)(2,1)S(1)} %slice.386), channel_id=1, source_target_pairs={{0,8},{4,12},{8,0},{12,4},{16,24},{20,28},{24,16},{28,20},{1,9},{5... | collective-permute-start | bytes 688136 | tf_op jit(solution)/shard_map/ppermute | solution.py:46
  68.9 28.7 %collective-permute-start.14 = (bf16[576,1024]{1,0:T(8,128)(2,1)}, bf16[576,1024]{1,0:T(8,128)(2,1)}, u32[]{:S(2)}, u32[]{:S(2)}) collective-permute-start(bf16[576,1024]{1,0:T(8,128)(2,1)} %get-tuple-element.295), channel_id=1, source_target_pairs={{0,2},{1,3},{2,0},{3,1},{4,6},{5,7},{6,4},{7,5},{8,10},{9,11},{10,... | collective-permute-start | bytes 3538952 | tf_op jit(solution)/shard_map/ppermute | solution.py:46
  70.5 28.4 %collective-permute-start.12 = (bf16[576,1024]{1,0:T(8,128)(2,1)}, bf16[576,1024]{1,0:T(8,128)(2,1)}, u32[]{:S(2)}, u32[]{:S(2)}) collective-permute-start(bf16[576,1024]{1,0:T(8,128)(2,1)} %collective-permute-done.7.refs_0_), channel_id=1, source_target_pairs={{0,4},{4,0},{8,12},{12,8},{16,20},{20,16},{24,28},{28,24},{1,5},{5... | collective-permute-start | bytes 3538952 | tf_op jit(solution)/shard_map/ppermute | solution.py:46
  71.0 28.1 %collective-permute-start.13 = (bf16[576,1024]{1,0:T(8,128)(2,1)}, bf16[576,1024]{1,0:T(8,128)(2,1)}, u32[]{:S(2)}, u32[]{:S(2)}) collective-permute-start(bf16[576,1024]{1,0:T(8,128)(2,1)} %collective-permute-done.7.refs_0_), channel_id=1, source_target_pairs={{0,8},{4,12},{8,0},{12,4},{16,24},{20,28},{24,16},{28,20},{1,9},{5... | collective-permute-start | bytes 3538952 | tf_op jit(solution)/shard_map/ppermute | solution.py:46
  99.1 46.1 %all-to-all-start.1 = ((bf16[8,2,128,384]{3,2,1,0:T(8,128)(2,1)}), bf16[8,2,128,384]{3,2,1,0:T(8,128)(2,1)S(1)}, u32[]{:S(2)}, u32[]{:S(2)}) async-start(bf16[8,2,128,384]{3,2,1,0:T(8,128)(2,1)} %get-tuple-element.296), calls=%async_computation.1 | async-start | bytes 3145728 | tf_op jit(solution)/shard_map/all_to_all | solution.py:1962
  106.0 29.9 %collective-permute-start.15 = (bf16[288,1024]{1,0:T(8,128)(2,1)S(1)}, bf16[288,1024]{1,0:T(8,128)(2,1)S(1)}, u32[]{:S(2)}, u32[]{:S(2)}) collective-permute-start(bf16[288,1024]{1,0:T(8,128)(2,1)S(1)} %slice.389), channel_id=1, source_target_pairs={{0,4},{4,0},{8,12},{12,8},{16,20},{20,16},{24,28},{28,24},{1,5},{5... | collective-permute-start | bytes 1769480 | tf_op jit(solution)/shard_map/ppermute | solution.py:46
  109.2 35.2 %collective-permute-start.16 = (bf16[288,1024]{1,0:T(8,128)(2,1)S(1)}, bf16[288,1024]{1,0:T(8,128)(2,1)S(1)}, u32[]{:S(2)}, u32[]{:S(2)}) collective-permute-start(bf16[288,1024]{1,0:T(8,128)(2,1)S(1)} %slice.390), channel_id=1, source_target_pairs={{0,8},{4,12},{8,0},{12,4},{16,24},{20,28},{24,16},{28,20},{1,9},{5... | collective-permute-start | bytes 1769480 | tf_op jit(solution)/shard_map/ppermute | solution.py:46
  152.1 14.7 %collective-permute-start.17 = (bf16[2304,1024]{1,0:T(8,128)(2,1)}, bf16[2304,1024]{1,0:T(8,128)(2,1)}, u32[]{:S(2)}, u32[]{:S(2)}) collective-permute-start(bf16[2304,1024]{1,0:T(8,128)(2,1)} %far_pack.4.refs_2_), channel_id=1, source_target_pairs={{0,1},{1,0},{2,3},{3,2},{4,5},{5,4},{6,7},{7,6},{8,9},{9,8},{10,11... | collective-permute-start | bytes 14155784 | tf_op jit(solution)/shard_map/ppermute | solution.py:46
  152.2 60.1 %collective-permute-start.20 = (bf16[1280,1024]{1,0:T(8,128)(2,1)}, bf16[1280,1024]{1,0:T(8,128)(2,1)}, u32[]{:S(2)}, u32[]{:S(2)}) collective-permute-start(bf16[1280,1024]{1,0:T(8,128)(2,1)} %get-tuple-element.336.refs_0_), channel_id=1, source_target_pairs={{0,2},{1,3},{2,0},{3,1},{4,6},{5,7},{6,4},{7,5},{8,10},{9,11},{10,... | collective-permute-start | bytes 7864328 | tf_op jit(solution)/shard_map/ppermute | solution.py:46
  152.8 33.4 %collective-permute-start.18 = (bf16[576,1024]{1,0:T(8,128)(2,1)}, bf16[576,1024]{1,0:T(8,128)(2,1)}, u32[]{:S(2)}, u32[]{:S(2)}) collective-permute-start(bf16[576,1024]{1,0:T(8,128)(2,1)} %collective-permute-done.14.refs_0_), channel_id=1, source_target_pairs={{0,4},{4,0},{8,12},{12,8},{16,20},{20,16},{24,28},{28,24},{1,5},{5... | collective-permute-start | bytes 3538952 | tf_op jit(solution)/shard_map/ppermute | solution.py:46
  154.2 32.9 %collective-permute-start.19 = (bf16[576,1024]{1,0:T(8,128)(2,1)}, bf16[576,1024]{1,0:T(8,128)(2,1)}, u32[]{:S(2)}, u32[]{:S(2)}) collective-permute-start(bf16[576,1024]{1,0:T(8,128)(2,1)} %collective-permute-done.14.refs_0_), channel_id=1, source_target_pairs={{0,8},{4,12},{8,0},{12,4},{16,24},{20,28},{24,16},{28,20},{1,9},{5... | collective-permute-start | bytes 3538952 | tf_op jit(solution)/shard_map/ppermute | solution.py:46
  166.8 25.0 %all-to-all-start.2 = ((bf16[8,2,128,128]{3,2,1,0:T(8,128)(2,1)}), bf16[8,2,128,128]{3,2,1,0:T(8,128)(2,1)}, u32[]{:S(2)}, u32[]{:S(2)}) async-start(bf16[8,2,128,128]{3,2,1,0:T(8,128)(2,1)} %copy-done.18), calls=%async_computation.2 | async-start | bytes 1048576 | tf_op jit(solution)/shard_map/all_to_all | solution.py:1975
  192.9 19.4 %collective-permute-start.21 = (bf16[288,1024]{1,0:T(8,128)(2,1)S(1)}, bf16[288,1024]{1,0:T(8,128)(2,1)S(1)}, u32[]{:S(2)}, u32[]{:S(2)}) collective-permute-start(bf16[288,1024]{1,0:T(8,128)(2,1)S(1)} %slice.392), channel_id=1, source_target_pairs={{0,4},{4,0},{8,12},{12,8},{16,20},{20,16},{24,28},{28,24},{1,5},{5... | collective-permute-start | bytes 1769480 | tf_op jit(solution)/shard_map/ppermute | solution.py:46
  194.1 18.2 %collective-permute-start.22 = (bf16[288,1024]{1,0:T(8,128)(2,1)S(1)}, bf16[288,1024]{1,0:T(8,128)(2,1)S(1)}, u32[]{:S(2)}, u32[]{:S(2)}) collective-permute-start(bf16[288,1024]{1,0:T(8,128)(2,1)S(1)} %slice.393), channel_id=1, source_target_pairs={{0,8},{4,12},{8,0},{12,4},{16,24},{20,28},{24,16},{28,20},{1,9},{5... | collective-permute-start | bytes 1769480 | tf_op jit(solution)/shard_map/ppermute | solution.py:46
  212.3 5.2 collective-permute-start.23
  227.9 26.0 %collective-permute-start.26 = (bf16[2304,1024]{1,0:T(8,128)(2,1)}, bf16[2304,1024]{1,0:T(8,128)(2,1)}, u32[]{:S(2)}, u32[]{:S(2)}) collective-permute-start(bf16[2304,1024]{1,0:T(8,128)(2,1)} %far_pack.5.refs_2_), channel_id=1, source_target_pairs={{0,1},{1,0},{2,3},{3,2},{4,5},{5,4},{6,7},{7,6},{8,9},{9,8},{10,11... | collective-permute-start | bytes 14155784 | tf_op jit(solution)/shard_map/ppermute | solution.py:46
  228.1 40.3 %collective-permute-start.25 = (bf16[256,7168]{1,0:T(8,128)(2,1)}, bf16[256,7168]{1,0:T(8,128)(2,1)}, u32[]{:S(2)}, u32[]{:S(2)}) collective-permute-start(bf16[256,7168]{1,0:T(8,128)(2,1)} %get-tuple-element.347.former_own.far_own.own_own), channel_id=1, source_target_pairs={{0,1},{1,0},{2,3},{3,2},{4,5},{5,4},{6,7},{7,6},{8,9},{9,8},{10,11... | collective-permute-start | bytes 11010056 | tf_op jit(solution)/shard_map/ppermute | solution.py:46
  228.5 18.3 %collective-permute-start.24 = (bf16[768,1024]{1,0:T(8,128)(2,1)S(1)}, bf16[768,1024]{1,0:T(8,128)(2,1)}, u32[]{:S(2)}, u32[]{:S(2)}) collective-permute-start(bf16[768,1024]{1,0:T(8,128)(2,1)S(1)} %bitcast.250), channel_id=1, source_target_pairs={{0,1},{1,0},{2,3},{3,2},{4,5},{5,4},{6,7},{7,6},{8,9},{9,8},{10,11... | collective-permute-start | bytes 4718600 | tf_op jit(solution)/shard_map/ppermute | solution.py:46
  310.4 38.6 %collective-permute-start.28 = (bf16[768,5120]{1,0:T(8,128)(2,1)}, bf16[768,5120]{1,0:T(8,128)(2,1)}, u32[]{:S(2)}, u32[]{:S(2)}) collective-permute-start(bf16[768,5120]{1,0:T(8,128)(2,1)} %get-tuple-element.380.far_own.own_own.latter_own), channel_id=1, source_target_pairs={{0,1},{1,0},{2,3},{3,2},{4,5},{5,4},{6,7},{7,6},{8,9},{9,8},{10,11... | collective-permute-start | bytes 23592968 | tf_op jit(solution)/shard_map/ppermute | solution.py:46
  310.8 38.2 %collective-permute-start.27 = (bf16[768,4096]{1,0:T(8,128)(2,1)}, bf16[768,4096]{1,0:T(8,128)(2,1)}, u32[]{:S(2)}, u32[]{:S(2)}) collective-permute-start(bf16[768,4096]{1,0:T(8,128)(2,1)} %get-tuple-element.426.former_own.active_ref), channel_id=1, source_target_pairs={{0,1},{1,0},{2,3},{3,2},{4,5},{5,4},{6,7},{7,6},{8,9},{9,8},{10,11... | collective-permute-start | bytes 18874376 | tf_op jit(solution)/shard_map/ppermute | solution.py:46
  349.0 34.1 %collective-permute-start.29 = (bf16[256,6144]{1,0:T(8,128)(2,1)}, bf16[256,6144]{1,0:T(8,128)(2,1)}, u32[]{:S(2)}, u32[]{:S(2)}) collective-permute-start(bf16[256,6144]{1,0:T(8,128)(2,1)} %get-tuple-element.399.latter_own), channel_id=1, source_target_pairs={{0,1},{1,0},{2,3},{3,2},{4,5},{5,4},{6,7},{7,6},{8,9},{9,8},{10,11... | collective-permute-start | bytes 9437192 | tf_op jit(solution)/shard_map/ppermute | solution.py:46
  349.5 33.7 %all-to-all-start.3 = ((bf16[8,2,128,128]{3,2,1,0:T(8,128)(2,1)}), bf16[8,2,128,128]{3,2,1,0:T(8,128)(2,1)}, u32[]{:S(2)}, u32[]{:S(2)}) async-start(bf16[8,2,128,128]{3,2,1,0:T(8,128)(2,1)} %get-tuple-element.375), calls=%async_computation.3 | async-start | bytes 1048576 | tf_op jit(solution)/shard_map/all_to_all | solution.py:2055
  383.1 41.7 %collective-permute-start.33 = (bf16[768,3072]{1,0:T(8,128)(2,1)}, bf16[768,3072]{1,0:T(8,128)(2,1)}, u32[]{:S(2)}, u32[]{:S(2)}) collective-permute-start(bf16[768,3072]{1,0:T(8,128)(2,1)} %bitcast.256), channel_id=1, source_target_pairs={{0,1},{1,0},{2,3},{3,2},{4,5},{5,4},{6,7},{7,6},{8,9},{9,8},{10,11... | collective-permute-start | bytes 14155784 | tf_op jit(solution)/shard_map/ppermute | solution.py:46
  383.3 41.6 %collective-permute-start.32 = (bf16[768,3072]{1,0:T(8,128)(2,1)}, bf16[768,3072]{1,0:T(8,128)(2,1)}, u32[]{:S(2)}, u32[]{:S(2)}) collective-permute-start(bf16[768,3072]{1,0:T(8,128)(2,1)} %get-tuple-element.415.far_own.own_own.latter_own), channel_id=1, source_target_pairs={{0,1},{1,0},{2,3},{3,2},{4,5},{5,4},{6,7},{7,6},{8,9},{9,8},{10,11... | collective-permute-start | bytes 14155784 | tf_op jit(solution)/shard_map/ppermute | solution.py:46
  383.6 48.0 %collective-permute-start.31 = (bf16[2,2,2,4,256,128]{5,4,3,2,1,0:T(8,128)(2,1)}, bf16[2,2,2,4,256,128]{5,4,3,2,1,0:T(8,128)(2,1)}, u32[]{:S(2)}, u32[]{:S(2)}) collective-permute-start(bf16[2,2,2,4,256,128]{5,4,3,2,1,0:T(8,128)(2,1)} %copy-done.39), channel_id=1, source_target_pairs={{0,2},{1,3},{2,0},{3,1},{4,6},{5,7},{6,4},{7,5},{8,10},{9,11},{10,... | collective-permute-start | bytes 6291464 | tf_op jit(solution)/shard_map/ppermute | solution.py:46
  385.2 55.6 %collective-permute-start.30 = (bf16[2,2,2,4,256,128]{5,4,3,2,1,0:T(8,128)(2,1)}, bf16[2,2,2,4,256,128]{5,4,3,2,1,0:T(8,128)(2,1)}, u32[]{:S(2)}, u32[]{:S(2)}) collective-permute-start(bf16[2,2,2,4,256,128]{5,4,3,2,1,0:T(8,128)(2,1)} %copy-done.40), channel_id=1, source_target_pairs={{0,4},{4,0},{8,12},{12,8},{16,20},{20,16},{24,28},{28,24},{1,5},{5... | collective-permute-start | bytes 6291464 | tf_op jit(solution)/shard_map/ppermute | solution.py:46
  424.8 80.5 %all-to-all-start.4 = ((bf16[8,2,128,384]{3,2,1,0:T(8,128)(2,1)}), bf16[8,2,128,384]{3,2,1,0:T(8,128)(2,1)}, u32[]{:S(2)}, u32[]{:S(2)}) async-start(bf16[8,2,128,384]{3,2,1,0:T(8,128)(2,1)} %copy-done.9), calls=%async_computation.4 | async-start | bytes 3145728 | tf_op jit(solution)/shard_map/all_to_all | solution.py:2101
  446.0 60.5 %collective-permute-start.38 = (bf16[2,2,2,5,256,128]{5,4,3,2,1,0:T(8,128)(2,1)}, bf16[2,2,2,5,256,128]{5,4,3,2,1,0:T(8,128)(2,1)}, u32[]{:S(2)}, u32[]{:S(2)}) collective-permute-start(bf16[2,2,2,5,256,128]{5,4,3,2,1,0:T(8,128)(2,1)} %get-tuple-element.429), channel_id=1, source_target_pairs={{0,4},{4,0},{8,12},{12,8},{16,20},{20,16},{24,28},{28,24},{1,5},{5... | collective-permute-start | bytes 7864328 | tf_op jit(solution)/shard_map/ppermute | solution.py:46
  449.0 56.3 %collective-permute-start.37 = (bf16[2,2,2,4,256,128]{5,4,3,2,1,0:T(8,128)(2,1)}, bf16[2,2,2,4,256,128]{5,4,3,2,1,0:T(8,128)(2,1)}, u32[]{:S(2)}, u32[]{:S(2)}) collective-permute-start(bf16[2,2,2,4,256,128]{5,4,3,2,1,0:T(8,128)(2,1)} %get-tuple-element.427), channel_id=1, source_target_pairs={{0,2},{1,3},{2,0},{3,1},{4,6},{5,7},{6,4},{7,5},{8,10},{9,11},{10,... | collective-permute-start | bytes 6291464 | tf_op jit(solution)/shard_map/ppermute | solution.py:46
  449.5 22.3 %collective-permute-start.34 = (bf16[512,1024]{1,0:T(8,128)(2,1)}, bf16[512,1024]{1,0:T(8,128)(2,1)}, u32[]{:S(2)}, u32[]{:S(2)}) collective-permute-start(bf16[512,1024]{1,0:T(8,128)(2,1)} %get-tuple-element.422.latter_own), channel_id=1, source_target_pairs={{0,1},{1,0},{2,3},{3,2},{4,5},{5,4},{6,7},{7,6},{8,9},{9,8},{10,11... | collective-permute-start | bytes 3145736 | tf_op jit(solution)/shard_map/ppermute | solution.py:46
  449.5 43.1 %collective-permute-start.36 = (bf16[2,2,4,256,128]{4,3,2,1,0:T(8,128)(2,1)}, bf16[2,2,4,256,128]{4,3,2,1,0:T(8,128)(2,1)}, u32[]{:S(2)}, u32[]{:S(2)}) collective-permute-start(bf16[2,2,4,256,128]{4,3,2,1,0:T(8,128)(2,1)} %fusion.4), channel_id=1, source_target_pairs={{0,8},{4,12},{8,0},{12,4},{16,24},{20,28},{24,16},{28,20},{1,9},{5... | collective-permute-start | bytes 3145736 | tf_op jit(solution)/shard_map/ppermute | solution.py:46
  451.6 53.6 %collective-permute-start.35 = (bf16[2,2,4,256,128]{4,3,2,1,0:T(8,128)(2,1)}, bf16[2,2,4,256,128]{4,3,2,1,0:T(8,128)(2,1)}, u32[]{:S(2)}, u32[]{:S(2)}) collective-permute-start(bf16[2,2,4,256,128]{4,3,2,1,0:T(8,128)(2,1)} %fusion.3), channel_id=1, source_target_pairs={{0,8},{4,12},{8,0},{12,4},{16,24},{20,28},{24,16},{28,20},{1,9},{5... | collective-permute-start | bytes 3145736 | tf_op jit(solution)/shard_map/ppermute | solution.py:46
  520.0 8.7 %collective-permute-start.41 = (bf16[256,3072]{1,0:T(8,128)(2,1)}, bf16[256,3072]{1,0:T(8,128)(2,1)S(1)}, u32[]{:S(2)}, u32[]{:S(2)}) collective-permute-start(bf16[256,3072]{1,0:T(8,128)(2,1)} %get-tuple-element.451.latter_own), channel_id=1, source_target_pairs={{0,1},{1,0},{2,3},{3,2},{4,5},{5,4},{6,7},{7,6},{8,9},{9,8},{10,11... | collective-permute-start | bytes 4718600 | tf_op jit(solution)/shard_map/ppermute | solution.py:46
  520.7 8.0 %collective-permute-start.42 = (f32[4,1024]{1,0:T(4,128)S(1)}, f32[4,1024]{1,0:T(4,128)S(1)}, u32[]{:S(2)}, u32[]{:S(2)}) collective-permute-start(f32[4,1024]{1,0:T(4,128)S(1)} %pad_maximum_fusion.7), channel_id=1, source_target_pairs={{0,1},{1,0},{2,3},{3,2},{4,5},{5,4},{6,7},{7,6},{8,9},{9,8},{10,11... | collective-permute-start | bytes 49160 | tf_op jit(solution)/shard_map/ppermute | solution.py:46
  521.3 30.6 %collective-permute-start.40 = (bf16[2,2,4,256,128]{4,3,2,1,0:T(8,128)(2,1)}, bf16[2,2,4,256,128]{4,3,2,1,0:T(8,128)(2,1)}, u32[]{:S(2)}, u32[]{:S(2)}) collective-permute-start(bf16[2,2,4,256,128]{4,3,2,1,0:T(8,128)(2,1)} %fusion.5), channel_id=1, source_target_pairs={{0,8},{4,12},{8,0},{12,4},{16,24},{20,28},{24,16},{28,20},{1,9},{5... | collective-permute-start | bytes 3145736 | tf_op jit(solution)/shard_map/ppermute | solution.py:46
  528.2 32.0 %collective-permute-start.39 = (bf16[2,2,5,256,128]{4,3,2,1,0:T(8,128)(2,1)}, bf16[2,2,5,256,128]{4,3,2,1,0:T(8,128)(2,1)}, u32[]{:S(2)}, u32[]{:S(2)}) collective-permute-start(bf16[2,2,5,256,128]{4,3,2,1,0:T(8,128)(2,1)} %fusion.1), channel_id=1, source_target_pairs={{0,2},{1,3},{2,0},{3,1},{4,6},{5,7},{6,4},{7,5},{8,10},{9,11},{10,... | collective-permute-start | bytes 3932168 | tf_op jit(solution)/shard_map/ppermute | solution.py:46
  543.4 53.2 %collective-permute-start.46 = (bf16[6208,128]{1,0:T(8,128)(2,1)S(1)}, bf16[6208,128]{1,0:T(8,128)(2,1)S(1)}, u32[]{:S(2)}, u32[]{:S(2)}) collective-permute-start(bf16[6208,128]{1,0:T(8,128)(2,1)S(1)} %pad_maximum_fusion), channel_id=1, source_target_pairs={{0,4},{4,0},{8,12},{12,8},{16,20},{20,16},{24,28},{28,24},{1,5},{5... | collective-permute-start | bytes 4767752 | tf_op jit(solution)/shard_map/ppermute | solution.py:46
  546.4 45.9 %collective-permute-start.47 = (bf16[2,4,256,128]{3,2,1,0:T(8,128)(2,1)S(1)}, bf16[2,4,256,128]{3,2,1,0:T(8,128)(2,1)S(1)}, u32[]{:S(2)}, u32[]{:S(2)}) collective-permute-start(bf16[2,4,256,128]{3,2,1,0:T(8,128)(2,1)S(1)} %fusion.10), channel_id=1, source_target_pairs={{0,4},{4,0},{8,12},{12,8},{16,20},{20,16},{24,28},{28,24},{1,5},{5... | collective-permute-start | bytes 1572872 | tf_op jit(solution)/shard_map/ppermute | solution.py:46
  549.9 43.9 %collective-permute-start.48 = (bf16[2,4,256,128]{3,2,1,0:T(8,128)(2,1)S(1)}, bf16[2,4,256,128]{3,2,1,0:T(8,128)(2,1)S(1)}, u32[]{:S(2)}, u32[]{:S(2)}) collective-permute-start(bf16[2,4,256,128]{3,2,1,0:T(8,128)(2,1)S(1)} %fusion.9), channel_id=1, source_target_pairs={{0,2},{1,3},{2,0},{3,1},{4,6},{5,7},{6,4},{7,5},{8,10},{9,11},{10,... | collective-permute-start | bytes 1572872 | tf_op jit(solution)/shard_map/ppermute | solution.py:46
  554.3 49.4 %collective-permute-start.45 = (bf16[2,4,256,128]{3,2,1,0:T(8,128)(2,1)}, bf16[2,4,256,128]{3,2,1,0:T(8,128)(2,1)}, u32[]{:S(2)}, u32[]{:S(2)}) collective-permute-start(bf16[2,4,256,128]{3,2,1,0:T(8,128)(2,1)} %fusion.8), channel_id=1, source_target_pairs={{0,4},{4,0},{8,12},{12,8},{16,20},{20,16},{24,28},{28,24},{1,5},{5... | collective-permute-start | bytes 1572872 | tf_op jit(solution)/shard_map/ppermute | solution.py:46
  562.6 42.4 %collective-permute-start.49 = (bf16[2,5,256,128]{3,2,1,0:T(8,128)(2,1)}, bf16[2,5,256,128]{3,2,1,0:T(8,128)(2,1)}, u32[]{:S(2)}, u32[]{:S(2)}) collective-permute-start(bf16[2,5,256,128]{3,2,1,0:T(8,128)(2,1)} %fusion.2), channel_id=1, source_target_pairs={{0,8},{4,12},{8,0},{12,4},{16,24},{20,28},{24,16},{28,20},{1,9},{5... | collective-permute-start | bytes 1966088 | tf_op jit(solution)/shard_map/ppermute | solution.py:46
  592.3 52.5 %collective-permute-start.44 = (bf16[2,2,2,4,256,128]{5,4,3,2,1,0:T(8,128)(2,1)}, bf16[2,2,2,4,256,128]{5,4,3,2,1,0:T(8,128)(2,1)}, u32[]{:S(2)}, u32[]{:S(2)}) collective-permute-start(bf16[2,2,2,4,256,128]{5,4,3,2,1,0:T(8,128)(2,1)} %get-tuple-element.470), channel_id=1, source_target_pairs={{0,2},{1,3},{2,0},{3,1},{4,6},{5,7},{6,4},{7,5},{8,10},{9,11},{10,... | collective-permute-start | bytes 6291464 | tf_op jit(solution)/shard_map/ppermute | solution.py:46
  593.9 55.5 %collective-permute-start.43 = (bf16[2,2,2,2,256,128]{5,4,3,2,1,0:T(8,128)(2,1)}, bf16[2,2,2,2,256,128]{5,4,3,2,1,0:T(8,128)(2,1)}, u32[]{:S(2)}, u32[]{:S(2)}) collective-permute-start(bf16[2,2,2,2,256,128]{5,4,3,2,1,0:T(8,128)(2,1)} %get-tuple-element.468), channel_id=1, source_target_pairs={{0,4},{4,0},{8,12},{12,8},{16,20},{20,16},{24,28},{28,24},{1,5},{5... | collective-permute-start | bytes 3145736 | tf_op jit(solution)/shard_map/ppermute | solution.py:46
  596.5 37.6 %collective-permute-start.59 = (bf16[8,256,128]{2,1,0:T(8,128)(2,1)}, bf16[8,256,128]{2,1,0:T(8,128)(2,1)}, u32[]{:S(2)}, u32[]{:S(2)}) collective-permute-start(bf16[8,256,128]{2,1,0:T(8,128)(2,1)} %pad_maximum_fusion.3), channel_id=1, source_target_pairs={{0,16},{4,20},{8,24},{12,28},{16,0},{20,4},{24,8},{28,12},{1,17},{... | collective-permute-start | bytes 1572872 | tf_op jit(solution)/shard_map/ppermute | solution.py:46
  607.3 44.8 %collective-permute-start.58 = (bf16[9,256,128]{2,1,0:T(8,128)(2,1)}, bf16[9,256,128]{2,1,0:T(8,128)(2,1)}, u32[]{:S(2)}, u32[]{:S(2)}) collective-permute-start(bf16[9,256,128]{2,1,0:T(8,128)(2,1)} %pad_maximum_fusion.2), channel_id=1, source_target_pairs={{0,16},{4,20},{8,24},{12,28},{16,0},{20,4},{24,8},{28,12},{1,17},{... | collective-permute-start | bytes 1769480 | tf_op jit(solution)/shard_map/ppermute | solution.py:46
  641.8 21.0 %collective-permute-start.52 = (bf16[3136,128]{1,0:T(8,128)(2,1)}, bf16[3136,128]{1,0:T(8,128)(2,1)S(1)}, u32[]{:S(2)}, u32[]{:S(2)}) collective-permute-start(bf16[3136,128]{1,0:T(8,128)(2,1)} %pad_maximum_fusion.1), channel_id=1, source_target_pairs={{0,2},{1,3},{2,0},{3,1},{4,6},{5,7},{6,4},{7,5},{8,10},{9,11},{10,... | collective-permute-start | bytes 2408456 | tf_op jit(solution)/shard_map/ppermute | solution.py:46
  648.0 23.8 %collective-permute-start.51 = (bf16[2,2,4,256,128]{4,3,2,1,0:T(8,128)(2,1)}, bf16[2,2,4,256,128]{4,3,2,1,0:T(8,128)(2,1)}, u32[]{:S(2)}, u32[]{:S(2)}) collective-permute-start(bf16[2,2,4,256,128]{4,3,2,1,0:T(8,128)(2,1)} %fusion.6), channel_id=1, source_target_pairs={{0,4},{4,0},{8,12},{12,8},{16,20},{20,16},{24,28},{28,24},{1,5},{5... | collective-permute-start | bytes 3145736 | tf_op jit(solution)/shard_map/ppermute | solution.py:46
  651.4 24.6 %collective-permute-start.50 = (bf16[2,2,2,256,128]{4,3,2,1,0:T(8,128)(2,1)}, bf16[2,2,2,256,128]{4,3,2,1,0:T(8,128)(2,1)}, u32[]{:S(2)}, u32[]{:S(2)}) collective-permute-start(bf16[2,2,2,256,128]{4,3,2,1,0:T(8,128)(2,1)} %fusion.14), channel_id=1, source_target_pairs={{0,2},{1,3},{2,0},{3,1},{4,6},{5,7},{6,4},{7,5},{8,10},{9,11},{10,... | collective-permute-start | bytes 1572872 | tf_op jit(solution)/shard_map/ppermute | solution.py:46
  671.7 14.8 %collective-permute-start.54 = (bf16[1600,128]{1,0:T(8,128)(2,1)S(1)}, bf16[1600,128]{1,0:T(8,128)(2,1)S(1)}, u32[]{:S(2)}, u32[]{:S(2)}) collective-permute-start(bf16[1600,128]{1,0:T(8,128)(2,1)S(1)} %pad_maximum_fusion.4), channel_id=1, source_target_pairs={{0,8},{4,12},{8,0},{12,4},{16,24},{20,28},{24,16},{28,20},{1,9},{5... | collective-permute-start | bytes 1228808 | tf_op jit(solution)/shard_map/ppermute | solution.py:46
  674.0 33.1 %collective-permute-start.55 = (bf16[2,4,256,128]{3,2,1,0:T(8,128)(2,1)}, bf16[2,4,256,128]{3,2,1,0:T(8,128)(2,1)}, u32[]{:S(2)}, u32[]{:S(2)}) collective-permute-start(bf16[2,4,256,128]{3,2,1,0:T(8,128)(2,1)} %fusion.7), channel_id=1, source_target_pairs={{0,8},{4,12},{8,0},{12,4},{16,24},{20,28},{24,16},{28,20},{1,9},{5... | collective-permute-start | bytes 1572872 | tf_op jit(solution)/shard_map/ppermute | solution.py:46
  677.9 28.1 %collective-permute-start.53 = (bf16[2,2,256,128]{3,2,1,0:T(8,128)(2,1)}, bf16[2,2,256,128]{3,2,1,0:T(8,128)(2,1)}, u32[]{:S(2)}, u32[]{:S(2)}) collective-permute-start(bf16[2,2,256,128]{3,2,1,0:T(8,128)(2,1)} %fusion.21), channel_id=1, source_target_pairs={{0,8},{4,12},{8,0},{12,4},{16,24},{20,28},{24,16},{28,20},{1,9},{5... | collective-permute-start | bytes 786440 | tf_op jit(solution)/shard_map/ppermute | solution.py:46
  691.0 10.2 %collective-permute-start.57 = (bf16[832,128]{1,0:T(8,128)(2,1)}, bf16[832,128]{1,0:T(8,128)(2,1)S(1)}, u32[]{:S(2)}, u32[]{:S(2)}) collective-permute-start(bf16[832,128]{1,0:T(8,128)(2,1)} %pad_maximum_fusion.6), channel_id=1, source_target_pairs={{0,16},{4,20},{8,24},{12,28},{16,0},{20,4},{24,8},{28,12},{1,17},{... | collective-permute-start | bytes 638984 | tf_op jit(solution)/shard_map/ppermute | solution.py:46
  709.2 13.1 %collective-permute-start.56 = (bf16[6,256,128]{2,1,0:T(8,128)(2,1)}, bf16[6,256,128]{2,1,0:T(8,128)(2,1)S(1)}, u32[]{:S(2)}, u32[]{:S(2)}) collective-permute-start(bf16[6,256,128]{2,1,0:T(8,128)(2,1)} %pad_maximum_fusion.5), channel_id=1, source_target_pairs={{0,16},{4,20},{8,24},{12,28},{16,0},{20,4},{24,8},{28,12},{1,17},{... | collective-permute-start | bytes 1179656 | tf_op jit(solution)/shard_map/ppermute | solution.py:46
  (70 other events, 615.2 us)

commit v6 on v5

--- a/solution.py
+++ b/solution.py
@@ -535,17 +535,18 @@
     ]
 
 
-def codec_attend_kernel(packed_ref, marks_ref, out_ref):
-    positions, _, width = out_ref.shape
+def codec_attend_kernel(packed_ref, normed_ref, marks_ref, out_ref):
+    positions, _, width = normed_ref.shape
+    out_ref[:, :, :width] = normed_ref[...]
     queries, keys, values = codec_parts(packed_ref, width)
     marks = marks_ref[...]
     pairs = position_pairs(positions)
     portions = codec_portions(queries, keys, marks, pairs)
     wide = dict(zip(pairs, codec_spread([portions[pair] for pair in pairs], marks)))
-    out_ref[0] = values[0]
+    out_ref[0, :, width:] = values[0]
     for later in range(1, positions):
         terms = [wide[later, e] * values[e].astype(F32) for e in range(later + 1)]
-        out_ref[later] = functools.reduce(jnp.add, terms).astype(BF)
+        out_ref[later, :, width:] = functools.reduce(jnp.add, terms).astype(BF)
 
 
 def codec_attend_grads_kernel(packed_ref, grad_ref, marks_ref, out_ref):
@@ -599,20 +600,24 @@
     ).astype(BF)
 
 
-def codec_attend_call(packed):
+def codec_attend_call(packed, normed):
     positions, total, triple = packed.shape
     width = triple // 3
     tile = codec_tile(total)
     return pl.pallas_call(
         codec_attend_kernel,
         grid=(total // tile,),
-        in_specs=[codec_spec(positions, tile, triple), whole_block((width, LANES))],
-        out_specs=codec_spec(positions, tile, width),
-        out_shape=jax.ShapeDtypeStruct((positions, total, width), BF),
+        in_specs=[
+            codec_spec(positions, tile, triple),
+            codec_spec(positions, tile, width),
+            whole_block((width, LANES)),
+        ],
+        out_specs=codec_spec(positions, tile, 2 * width),
+        out_shape=jax.ShapeDtypeStruct((positions, total, 2 * width), BF),
         compiler_params=pltpu.CompilerParams(vmem_limit_bytes=VMEM_LIMIT),
         cost_estimate=HINT,
         name="codec_attend",
-    )(packed, head_marks(width))
+    )(packed, normed.reshape(positions, total, width), head_marks(width))
 
 
 def codec_attend_grads_call(packed, grads):
@@ -1016,54 +1021,54 @@
     )(spots, *pieces)
 
 
-def join_kernel(shapes, place_ref, *refs):
-    packs = refs[:4]
-    outs = refs[4 : 4 + len(shapes)]
-    held, sems, out_sems = refs[-3:]
-    rows = held.shape[0] // 4
+def join_kernel(shapes, flips, place_ref, *refs):
+    count = len(flips)
+    packs = refs[:count]
+    outs, (held, sems, out_sems) = refs[-3 - len(shapes) : -3], refs[-3:]
+    rows = held.shape[0] // count
+    for number, pack in enumerate(packs):
+        pltpu.make_async_copy(pack, held.at[pl.ds(number * rows, rows)], sems.at[number]).start()
     copies = []
-    for flip, pack in enumerate(packs):
-        start = pl.multiple_of((place_ref[0] ^ flip) * rows, 16)
-        copies.append(pltpu.make_async_copy(pack, held.at[pl.ds(start, rows)], sems.at[flip]))
-    for copy in copies:
-        copy.start()
-    for copy in copies:
-        copy.wait()
-    copies = []
-    for at, column, height, start in pack_pieces(shapes):
-        for block in range(4):
+    for number, flip in enumerate(flips):
+        pltpu.make_async_copy(
+            packs[number], held.at[pl.ds(number * rows, rows)], sems.at[number]
+        ).wait()
+        for at, column, height, start in pack_pieces(shapes):
+            target = pl.multiple_of((place_ref[0] ^ flip) * height, height)
             copies.append(
                 pltpu.make_async_copy(
-                    held.at[pl.ds(block * rows + start, height)],
-                    outs[at].at[pl.ds(block * height, height), columns_of(column)],
+                    held.at[pl.ds(number * rows + start, height)],
+                    outs[at].at[pl.ds(target, height), columns_of(column)],
                     out_sems.at[len(copies)],
                 )
             )
-    for copy in copies:
-        copy.start()
+            copies[-1].start()
     for copy in copies:
         copy.wait()
 
 
-def join_weights(members, packs, spots):
+def join_weights(members, packs, flips, spots, into=None):
     shapes = [member.shape for member in members]
     rows = pack_rows(members)
     any_spec = pl.BlockSpec(memory_space=pl.ANY)
     outs = [jax.ShapeDtypeStruct((4 * height, breadth), BF) for height, breadth in shapes]
+    count = len(flips)
+    held = [] if into is None else list(into)
     return pl.pallas_call(
-        functools.partial(join_kernel, shapes),
-        in_specs=[pl.BlockSpec(memory_space=pltpu.SMEM)] + [any_spec] * 4,
+        functools.partial(join_kernel, shapes, flips),
+        in_specs=[pl.BlockSpec(memory_space=pltpu.SMEM)] + [any_spec] * (count + len(held)),
         out_specs=[any_spec] * len(outs),
         out_shape=outs,
+        input_output_aliases={1 + count + at: at for at in range(len(held))},
         scratch_shapes=[
-            pltpu.VMEM((4 * rows, PACK), BF),
-            pltpu.SemaphoreType.DMA((4,)),
-            pltpu.SemaphoreType.DMA((4 * len(pack_pieces(shapes)),)),
+            pltpu.VMEM((count * rows, PACK), BF),
+            pltpu.SemaphoreType.DMA((count,)),
+            pltpu.SemaphoreType.DMA((count * len(pack_pieces(shapes)),)),
         ],
         compiler_params=pltpu.CompilerParams(vmem_limit_bytes=VMEM_LIMIT),
         cost_estimate=HINT,
         name="join_weights",
-    )(spots, *packs)
+    )(spots, *packs, *held)
 
 
 WIDE_LIMIT = 58 * 1024 * 1024
@@ -1378,8 +1383,8 @@
 
 
 def codec_rear_kernel(
-    base_ref, entries_ref, front_ref, attended_ref, grad_ref, gain_ref, output_ref, expand_ref,
-    contract_ref, mixed_ref, active_ref, expand_kept_ref, kept_ref, mixed_grad_ref,
+    base_ref, entries_ref, attended_ref, grad_ref, gain_ref, output_ref, expand_ref, contract_ref,
+    mixed_ref, active_ref, expand_kept_ref, kept_ref, mixed_grad_ref,
     attended_grad_ref, gain_grad_ref, total,
 ):
     width = total.shape[1]
@@ -1396,8 +1401,6 @@
             mixed_ref[own] = mixed
             expand_kept_ref[own, :width] = rms_scale(mixed, gain_ref[...]).astype(BF)
         total[...] = jnp.zeros_like(total)
-        kept_ref[:, :width] = front_ref[...]
-        kept_ref[:, width : 2 * width] = attended_ref[...]
 
     active, slope = gelu_pair(matmul(expand_kept_ref[:, :width], expand_ref[...]))
     active_ref[...] = active.astype(BF)
@@ -1421,18 +1424,18 @@
             mixed_grad = grad_ref[own].astype(F32) + part
             mixed_grad_ref[own] = mixed_grad
             output_in = mixed_grad.astype(BF)
-            kept_ref[own, 2 * width :] = output_in
+            kept_ref[own] = output_in
             attended_grad_ref[t] = inner_right(output_in, output_ref[...]).astype(BF)
         gain_grad_ref[...] = gain_grads
 
 
-def codec_rear(base, entries, front, attended, grad, gain, output, expand, contract):
+def codec_rear(base, entries, kept, grad, gain, output, expand, contract):
     size, width = base.shape
-    total = attended.shape[0]
+    total = kept.shape[0]
     inner = expand.shape[1]
     tile = FF_TILE
     full = whole_block((total, width))
-    wide, triple = (total, width + inner), (total, 3 * width)
+    wide = (total, width + inner)
     high = jax.ShapeDtypeStruct((total, width), F32)
     return dense_call(
         codec_rear_kernel,
@@ -1440,8 +1443,7 @@
         [
             held(base.shape),
             held(entries.shape),
-            held(front.shape),
-            held(attended.shape),
+            pl.BlockSpec((total, width), lambda j: (0, 1), pipeline_mode=pl.Buffered(1)),
             held(grad.shape),
             held(gain.shape),
             held(output.shape),
@@ -1452,7 +1454,7 @@
             held((total, width)),
             pl.BlockSpec((total, tile), lambda j: (0, j)),
             held(wide),
-            held(triple),
+            held((total, width)),
             held((total, width)),
             held((total // size, size, width)),
             whole_block((1, width)),
@@ -1461,14 +1463,14 @@
             high,
             jax.ShapeDtypeStruct((total, inner), BF),
             jax.ShapeDtypeStruct(wide, BF),
-            jax.ShapeDtypeStruct(triple, BF),
+            jax.ShapeDtypeStruct((total, width), BF),
             high,
             jax.ShapeDtypeStruct((total // size, size, width), BF),
             jax.ShapeDtypeStruct((1, width), F32),
         ],
         [pltpu.VMEM((total, width), F32)],
         "codec_rear",
-    )(base, entries, front, attended, grad, gain, output, expand, contract)
+    )(base, entries, kept, grad, gain, output, expand, contract)
 
 
 def codec_result_kernel(mixed_ref, active_ref, live_ref, contract_ref, out_ref, total):
@@ -1787,9 +1789,14 @@
     def send(self, chain):
         self.far = Pair(chain.enter(self.far))
 
+    def join_near(self, chain):
+        packs = chain.enter(*self.near.both())
+        self.outs = join_weights(self.members, packs, (0, 1), self.spots)
+        chain.leave(*self.outs)
+
     def join(self, chain):
-        packs = chain.enter(*self.near.both(), *self.far.both())
-        outs = join_weights(self.members, packs, self.spots)
+        packs = chain.enter(*self.far.both())
+        outs = join_weights(self.members, packs, (2, 3), self.spots, self.outs)
         chain.leave(*outs)
         return outs
 
@@ -1864,7 +1871,9 @@
     message = swap(message, *BITS["f"])
 
     def take():
-        came, total = unload(message, given.shape, riders)
+        held = chain.enter(message)
+        chain.leave(held)
+        came, total = unload(held, given.shape, riders)
         start = 0
         for one in sums:
             size = one.shape[-3]
@@ -1936,6 +1945,7 @@
         * live.astype(BF)[None]
     ).reshape(positions * frame_total, width)
     chain.leave(contract_in)
+    first.join_near(chain)
     first.cross(chain)
     fourth = Gather([codec_expand, codec_contract, codec_output], spots)
     fourth.quarter = chain.enter(fourth.quarter)
@@ -1960,6 +1970,9 @@
     )
     chain.leave(packed)
     packed = lax.all_to_all(packed, "seq", split_axis=0, concat_axis=0, tiled=True)
+    second.join_near(chain)
+    third.join_near(chain)
+    fourth.join_near(chain)
     second.cross(chain)
     packed, *second.ends = chain.enter(packed, *second.ends)
     chain.leave(packed)
@@ -1999,24 +2012,25 @@
     codec_normed, codec_packed = codec_front(chain.enter(base), entries, gains[2], codec_project_all)
     chain.leave(codec_packed)
     codec_packed, contract_pair.other = chain.enter(codec_packed, contract_pair.other)
-    codec_attended = codec_attend_call(codec_packed).reshape(positions * frame_total, width)
-    chain.leave(codec_attended)
+    codec_kept = codec_attend_call(codec_packed, codec_normed).reshape(
+        positions * frame_total, 2 * width
+    )
+    chain.leave(codec_kept)
     codec_expand_all, codec_contract_all, codec_output_all = fourth.join(chain)
-    codec_attended, frame_kept.other = chain.enter(codec_attended, frame_kept.other)
-    chain.leave(codec_attended)
+    codec_kept, frame_kept.other = chain.enter(codec_kept, frame_kept.other)
+    chain.leave(codec_kept)
     (
         codec_mixed,
         codec_activated,
         codec_expand_kept,
-        codec_kept,
+        codec_output_in,
         mixed_grad,
         attended_grad,
         codec_postnorm_grad,
     ) = codec_rear(
         base,
         entries,
-        codec_normed,
-        chain.enter(codec_attended),
+        chain.enter(codec_kept),
         contract_in,
         gains[3],
         codec_output_all,
@@ -2074,15 +2088,17 @@
     contract_sum = Reduce(contract_stages, chain.enter(*contract_blocks))
     expand_sum = Reduce(expand_stages, chain.enter(*expand_blocks))
     codec_kept = Pair(chain.enter(codec_kept))
+    output_pair = Pair(chain.enter(codec_output_in))
     projected_pair = Pair(chain.enter(projected_grad))
     packed_grad = frame_attend_grads_call(packed, chain.enter(grads), every_segment)
     chain.leave(packed_grad)
     kept, arrays = frame_kept.both(), chain.enter(*frame_grads_kept.both())
+    frame_contract_stages = tuple("yxnf")
     frame_contract_blocks = grad_columns(
-        (kept, 3 * width, inner), (arrays, 0, width), order, contract_stages, 4, 0
+        (kept, 3 * width, inner), (arrays, 0, width), order, frame_contract_stages, 4, 0
     )
     chain.leave(*frame_contract_blocks)
-    frame_expand_stages = tuple("xynf")
+    frame_expand_stages = tuple("xnyf")
     arrays = chain.enter(*arrays)
     blocks = grad_rows(
         (kept, 2 * width, width), (arrays, width, inner), order, frame_expand_stages, 5, 0
@@ -2092,8 +2108,8 @@
     )
     chain.leave(*frame_expand_blocks)
 
-    packed_grad, codec_kept.other, projected_pair.other = chain.enter(
-        packed_grad, codec_kept.other, projected_pair.other
+    packed_grad, codec_kept.other, projected_pair.other, output_pair.other = chain.enter(
+        packed_grad, codec_kept.other, projected_pair.other, output_pair.other
     )
     chain.leave(packed_grad)
     contract_sum.arrive(chain)
@@ -2101,16 +2117,16 @@
     packed_grad = lax.all_to_all(packed_grad, "seq", split_axis=0, concat_axis=0, tiled=True)
     contract_sum.step(chain)
     expand_sum.step(chain)
-    frame_contract_sum = Reduce(contract_stages, chain.enter(*frame_contract_blocks))
+    frame_contract_sum = Reduce(frame_contract_stages, chain.enter(*frame_contract_blocks))
     frame_expand_sum = Reduce(frame_expand_stages, chain.enter(*frame_expand_blocks))
     table_pair = Pair(chain.enter(table_in))
-    project_stages = tuple("yxnf")
+    project_stages = tuple("ynxf")
     arrays = chain.enter(*codec_kept.both())
     blocks = grad_rows(
         (arrays, 0, width), (projected_pair.both(), 0, 3 * width), order, project_stages, 4, 0
     )
     project_blocks = grad_rows(
-        (arrays, width, width), (arrays, 2 * width, width), order, project_stages, 4, 3, blocks
+        (arrays, width, width), (output_pair.both(), 0, width), order, project_stages, 4, 3, blocks
     )
     chain.leave(*project_blocks)
     table_stages = tuple("xynf")
@@ -2124,6 +2140,8 @@
         0,
     )
     chain.leave(*table_blocks)
+    project_sum = Reduce(project_stages, chain.enter(*project_blocks))
+    table_sum = Reduce(table_stages, chain.enter(*table_blocks))
     output = codec_result(codec_mixed, chain.enter(codec_activated), live, codec_contract_all)
     chain.leave(output)
     output = jnp.transpose(output, (1, 0, 2)).reshape(row_count, frames_dev, positions, width)
@@ -2160,26 +2178,24 @@
     chain.leave(*blocks)
     riders = gain_pair.own + gain_pair.other
     frame_project_sum = Reduce(table_stages, blocks, chain.enter(riders))
-    project_sum = Reduce(project_stages, chain.enter(*project_blocks))
-    contract_sum.step(chain)
-    expand_sum.step(chain)
-    frame_contract_sum.step(chain)
-    frame_expand_sum.step(chain)
-    table_sum = Reduce(table_stages, chain.enter(*table_blocks))
-    take_first = finish([contract_sum, expand_sum], chain)
-    frame_project_sum.step(chain)
-    take_second = finish([frame_contract_sum, frame_expand_sum], chain)
     project_sum.step(chain)
     table_sum.step(chain)
+    frame_expand_sum.step(chain)
+    expand_sum.step(chain)
     frame_project_sum.step(chain)
+    frame_contract_sum.step(chain)
     project_sum.step(chain)
+    contract_sum.step(chain)
+    take_second = finish([frame_contract_sum, frame_expand_sum], chain)
     table_sum.step(chain)
+    frame_project_sum.step(chain)
+    take_first = finish([contract_sum, expand_sum], chain)
+    take_fourth = finish([project_sum, table_sum], chain)
     take_third = finish([frame_project_sum], chain)
-    take_fourth = finish([project_sum, table_sum], chain)
+    take_second()
     take_first()
-    take_second()
+    take_fourth()
     take_third()
-    take_fourth()
 
     height = frame_project.shape[0]
     project_units = project_sum.result()

time: 738 us -> 719 us (0.974)
  local copies, waits for them, and re-layouts: 83.1 us -> 65.8 us
  other arithmetic: 66.4 us -> 55.9 us
    pallas_call x4 -> x8, Pallas kernels: 41.2 us -> 45.8 us  [join_weights(): pl.pallas_call(functools.partial(join_kernel, shapes, flips), in_specs=[p...]
    ppermute x60 -> x61, starting transfers between devices: 54.8 us -> 56 us  [swap(): lax.ppermute(values, axis, [(i, i ^ bit) for i in range(lax.axis_size(axi...]
    ppermute x60 -> x61, waiting for transfers between devices: 182 us -> 181 us  [swap(): lax.ppermute(values, axis, [(i, i ^ bit) for i in range(lax.axis_size(axi...]
    unnamed x149 -> x147, local copies, waits for them, and re-layouts: 45.6 us -> 45.2 us
  transfers between devices with their start and end apart: 65 -> 66, of which waited for: 28 -> 28; matrix products, arithmetic and copies ran while one was open for 14% -> 11% of each run, Pallas kernels for 32% -> 35%
where the time goes in v6:
time: 719 us; the launch traced here: 709 us
  Pallas kernels  306 us (43%)
  waiting for transfers between devices  196 us (27%)
  starting transfers between devices  83.5 us (12%)
  local copies, waits for them, and re-layouts  65.8 us (9%)
  other arithmetic  55.9 us (8%)
    ppermute x61, waiting for transfers between devices, swap(): lax.ppermute(values, axis, [(i, i ^ bit) for i in range(lax.axis_size(axi...  181 us
    pallas_call x9, Pallas kernels, grad_call(): pl.pallas_call(kernel, grid_spec=pltpu.PrefetchScalarGridSpec(num_scalar_...  75.4 us
    ppermute x61, starting transfers between devices, swap(): lax.ppermute(values, axis, [(i, i ^ bit) for i in range(lax.axis_size(axi...  56 us
    pallas_call x8, Pallas kernels, join_weights(): pl.pallas_call(functools.partial(join_kernel, shapes, flips), in_specs=[p...  45.8 us
    unnamed x147, local copies, waits for them, and re-layouts  45.2 us
    pallas_call x1, Pallas kernels, codec_rear(): dense_call(codec_rear_kernel, inner // tile, [held(base.shape), held(entr...  40.4 us
    convert_element_type x20, other arithmetic, give(): given = self.total(False).astype(BF)  36.7 us
    pallas_call x1, Pallas kernels, frame_rear(): dense_call(frame_rear_kernel, inner // tile, [held(hidden.shape), held(fr...  15.5 us
  transfers between devices with their start and end apart: 66, of which 28 were waited for; matrix products, arithmetic and copies ran while one was open for 11% of the time, Pallas kernels for 35%

profile of v6, /device:TPU:0, one launch (start us, length us, event | category | flops | bytes accessed | tf_op | source)
XLA Modules:
  0.0 709.0 jit_solution(15050982671287153092)
XLA Ops:
  5.0 3.3 pack_weights.5
  8.9 3.5 pack_weights.7
  14.7 2.6 collective-permute-start
  17.9 5.8 all-to-all-start
  23.7 6.5 all-to-all-done
  39.3 4.0 join_weights.8
  43.3 4.5 collective-permute-done.1.refs_1_
  48.7 8.5 %collective-permute-done.7.refs_0_ = bf16[576,1024]{1,0:T(8,128)(2,1)} collective-permute-done((bf16[576,1024]{1,0:T(8,128)(2,1)}, bf16[576,1024]{1,0:T(8,128)(2,1)}, u32[]{:S(2)}, u32[]{:S(2)}) %collective-permute-start.7) | collective-permute-done | bytes 1179680 | tf_op jit(solution)/shard_map/ppermute | solution.py:46
  59.9 5.4 collective-permute-done.5.refs_3_
  72.1 2.6 join_weights.9
  76.1 6.4 frame_front.1
  82.5 14.4 %collective-permute-done.12.refs_1_ = bf16[576,1024]{1,0:T(8,128)(2,1)S(1)} collective-permute-done((bf16[576,1024]{1,0:T(8,128)(2,1)}, bf16[576,1024]{1,0:T(8,128)(2,1)S(1)}, u32[]{:S(2)}, u32[]{:S(2)}) %collective-permute-start.12) | collective-permute-done | bytes 1179680 | tf_op jit(solution)/shard_map/ppermute | solution.py:46
  98.5 4.8 all-to-all-start.1
  103.3 7.4 %join_weights.10 = (bf16[1024,4096]{1,0:T(8,128)(2,1)}, bf16[4096,1024]{1,0:T(8,128)(2,1)}, bf16[1024,1024]{1,0:T(8,128)(2,1)S(1)}) custom-call(s32[2]{0:T(128)S(1)} %pad_add_fusion.1.place_ref, bf16[2304,1024]{1,0:T(8,128)(2,1)} %get-tuple-element.321.refs_0_, bf16[2304,1024]{1,0:T(8,128)(2,1)} %collective-permute-done.8.refs_1_), custom_call_target="tpu_custom_call" | custom-call | flops 1 | bytes 1 | tf_op jit(solution)/shard_map/join_weights/pallas_call | solution.py:1057
  110.8 4.8 join_weights.11
  115.6 7.4 %join_weights.12 = (bf16[1024,4096]{1,0:T(8,128)(2,1)}, bf16[4096,1024]{1,0:T(8,128)(2,1)}, bf16[1024,1024]{1,0:T(8,128)(2,1)S(1)}) custom-call(s32[2]{0:T(128)S(1)} %pad_add_fusion.1.place_ref, bf16[2304,1024]{1,0:T(8,128)(2,1)} %get-tuple-element.330.refs_0_, bf16[2304,1024]{1,0:T(8,128)(2,1)} %collective-permute-done.9.refs_1_), custom_call_target="tpu_custom_call" | custom-call | flops 1 | bytes 1 | tf_op jit(solution)/shard_map/join_weights/pallas_call | solution.py:1057
  129.1 12.5 %collective-permute-done.15.refs_3_ = bf16[288,1024]{1,0:T(8,128)(2,1)S(1)} collective-permute-done((bf16[288,1024]{1,0:T(8,128)(2,1)S(1)}, bf16[288,1024]{1,0:T(8,128)(2,1)S(1)}, u32[]{:S(2)}, u32[]{:S(2)}) %collective-permute-start.15) | collective-permute-done | bytes 589856 | tf_op jit(solution)/shard_map/ppermute | solution.py:46
  142.5 5.7 collective-permute-done.16.refs_4_
  151.2 4.4 far_pack.4.refs_0_
  157.7 10.0 %frame_attend.1 = bf16[8,2,128,128]{3,2,1,0:T(8,128)(2,1)S(1)} custom-call(bf16[8,2,128,384]{3,2,1,0:T(8,128)(2,1)} %all-to-all-done.1.packed_ref, s32[2,1024,1]{2,1,0:T(8,128)S(1)} %copy.71.seg_col_ref, s32[2,1,1024]{2,1,0:T(1,128)S(1)} %broadcast_in_dim.16.seg_row_ref), custom_call_target="tpu_custom_call" | custom-call | flops 1 | bytes 1 | tf_op jit(solution)/shard_map/frame_attend/pallas_call | solution.py:462
  168.5 8.3 %all-to-all-start.2 = ((bf16[8,2,128,128]{3,2,1,0:T(8,128)(2,1)}), bf16[8,2,128,128]{3,2,1,0:T(8,128)(2,1)}, u32[]{:S(2)}, u32[]{:S(2)}) async-start(bf16[8,2,128,128]{3,2,1,0:T(8,128)(2,1)} %copy-done.22), calls=%async_computation.2 | async-start | bytes 1048576 | tf_op jit(solution)/shard_map/all_to_all | solution.py:1988
  176.8 7.5 %join_weights.13 = (bf16[1024,4096]{1,0:T(8,128)(2,1)}, bf16[4096,1024]{1,0:T(8,128)(2,1)}, bf16[1024,1024]{1,0:T(8,128)(2,1)S(1)}) custom-call(s32[2]{0:T(128)S(1)} %pad_add_fusion.1.place_ref, bf16[2304,1024]{1,0:T(8,128)(2,1)} %far_pack.4.refs_0_, ...), custom_call_target="tpu_custom_call", output_to_operand_aliasing={{0}: (3, {}), {1}: (4, {}), {2}: (5, {})} | custom-call | flops 1 | bytes 1 | tf_op jit(solution)/shard_map/join_weights/pallas_call | solution.py:1057
  184.3 3.5 collective-permute-done.18.refs_1_
  189.2 8.3 %all-to-all-done.2.packed_ref = bf16[8,2,128,128]{3,2,1,0:T(8,128)(2,1)} async-done(((bf16[8,2,128,128]{3,2,1,0:T(8,128)(2,1)}), bf16[8,2,128,128]{3,2,1,0:T(8,128)(2,1)}, u32[]{:S(2)}, u32[]{:S(2)}) %all-to-all-start.2) | async-done | bytes 524320 | tf_op jit(solution)/shard_map/all_to_all | solution.py:1988
  202.3 15.5 %frame_rear.1 = (bf16[256,7168]{1,0:T(8,128)(2,1)}, f32[256,1024]{1,0:T(8,128)}, bf16[256,4096]{1,0:T(8,128)(2,1)}, bf16[256,1024]{1,0:T(8,128)(2,1)}) custom-call(bf16[256,1024]{1,0:T(8,128)(2,1)} %bitcast.270, bf16[256,1024]{1,0:T(8,128)(2,1)} %get-tuple-element.312.front_ref, bf16[8,2,128,128]{3,2,1,0:T(8,128)(2,1)} %all-to-all-done.2.packed_ref, ...), custom_call_target="tpu_custom_call" | custom-call | flops 1 | bytes 1 | tf_op jit(solution)/shard_map/frame_rear/pallas_call | solution.py:1196
  218.0 4.8 far_pack.5.refs_0_
  223.1 4.8 join_weights.14
  230.2 6.2 gather_fusion
  236.4 10.5 %codec_front.1 = (bf16[768,1024]{1,0:T(8,128)(2,1)}, bf16[3,256,3072]{2,1,0:T(8,128)(2,1)}) custom-call(bf16[256,1024]{1,0:T(8,128)(2,1)} %get-tuple-element.372.base_ref, bf16[2,256,1024]{2,1,0:T(8,128)(2,1)} %bitcast.265, f32[1,1024]{1,0:T(1,128)} %bitcast.290, bf16[1024,3072]{1,0:T(8,128)(2,1)} %get-tuple-element.371.weight_ref), custom_call_target="tpu_custom_call" | custom-call | flops 1 | bytes 1 | tf_op jit(solution)/shard_map/codec_front/pallas_call | solution.py:1363
  248.4 6.3 codec_attend.1
  256.4 7.4 %join_weights.15 = (bf16[1024,4096]{1,0:T(8,128)(2,1)}, bf16[4096,1024]{1,0:T(8,128)(2,1)}, bf16[1024,1024]{1,0:T(8,128)(2,1)S(1)}) custom-call(s32[2]{0:T(128)S(1)} %pad_add_fusion.1.place_ref, bf16[2304,1024]{1,0:T(8,128)(2,1)} %far_pack.5.refs_0_, ...), custom_call_target="tpu_custom_call", output_to_operand_aliasing={{0}: (3, {}), {1}: (4, {}), {2}: (5, {})} | custom-call | flops 1 | bytes 1 | tf_op jit(solution)/shard_map/join_weights/pallas_call | solution.py:1057
  265.2 40.4 %codec_rear.1 = (f32[768,1024]{1,0:T(8,128)}, bf16[768,4096]{1,0:T(8,128)(2,1)}, bf16[768,5120]{1,0:T(8,128)(2,1)}, bf16[768,1024]{1,0:T(8,128)(2,1)}, f32[768,1...) custom-call(bf16[256,1024]{1,0:T(8,128)(2,1)} %get-tuple-element.372.base_ref, ...), custom_call_target="tpu_custom_call" | custom-call | flops 1 | bytes 1 | tf_op jit(solution)/shard_map/codec_rear/pallas_call | solution.py:1440
  307.6 8.5 %codec_attend_grads.1 = bf16[3,256,3072]{2,1,0:T(8,128)(2,1)} custom-call(bf16[3,256,3072]{2,1,0:T(8,128)(2,1)} %get-tuple-element.374.packed_ref, bf16[3,256,1024]{2,1,0:T(8,128)(2,1)S(1)} %copy-done.33, bf16[1024,128]{1,0:T(8,128)(2,1)S(1)} %fusion.25.marks_ref), custom_call_target="tpu_custom_call" | custom-call | flops 1 | bytes 1 | tf_op jit(solution)/shard_map/codec_attend_grads/pallas_call | solution.py:627
  316.1 13.3 %codec_front_grads.1 = (bf16[256,1024]{1,0:T(8,128)(2,1)}, bf16[512,1024]{1,0:T(8,128)(2,1)}, f32[1,1024]{1,0:T(1,128)}) custom-call(bf16[768,3072]{1,0:T(8,128)(2,1)} %bitcast.262, bf16[256,1024]{1,0:T(8,128)(2,1)} %get-tuple-element.372.base_ref, bf16[2,256,1024]{2,1,0:T(8,128)(2,1)} %bitcast.267, f32[1,1024]{1,0:T(1,128)} %bitcast.291, ...), custom_call_target="tpu_custom_call" | custom-call | flops 1 | bytes 1 | tf_op jit(solution)/shard_map/codec_front_grads/pallas_call | solution.py:1548
  329.5 14.9 %frame_rear_grads.1 = (bf16[256,6144]{1,0:T(8,128)(2,1)}, f32[256,1024]{1,0:T(8,128)}, bf16[8,2,128,128]{3,2,1,0:T(8,128)(2,1)}, f32[1,1024]{1,0:T(1,128)}) custom-call(bf16[256,1024]{1,0:T(8,128)(2,1)} %get-tuple-element.395.grad_ref, bf16[256,4096]{1,0:T(8,128)(2,1)} %get-tuple-element.396.slope_ref, f32[256,1024]{1,0:T(8,128)} %get-tuple-element.397.mixed_ref, ...), custom_call_target="tpu_custom_call" | custom-call | flops 1 | bytes 1 | tf_op jit(solution)/shard_map/frame_rear_grads/pallas_call | solution.py:1265
  344.8 4.1 all-to-all-start.3
  349.1 11.7 %grad_columns.2 = (bf16[2,2,2,4,256,128]{5,4,3,2,1,0:T(8,128)(2,1)S(1)}, bf16[2,2,2,4,256,128]{5,4,3,2,1,0:T(8,128)(2,1)}) custom-call(s32[27]{0:T(128)S(1)} %stack.69.order_ref, bf16[768,1024]{1,0:T(8,128)(2,1)S(1)} %bitcast.259, bf16[768,1024]{1,0:T(8,128)(2,1)S(1)} %collective-permute-done.24.latter_rec, ...), custom_call_target="tpu_custom_call" | custom-call | flops 1 | bytes 1 | tf_op jit(solution)/shard_map/grad_columns/pallas_call | solution.py:731
  362.1 13.2 %grad_rows.6 = (bf16[2,2,2,4,256,128]{5,4,3,2,1,0:T(8,128)(2,1)S(1)}, bf16[2,2,2,4,256,128]{5,4,3,2,1,0:T(8,128)(2,1)S(1)}) custom-call(s32[27]{0:T(128)S(1)} %stack.69.order_ref, bf16[768,5120]{1,0:T(8,128)(2,1)} %get-tuple-element.408.far_own.own_own.latter_own, bf16[768,5120]{1,0:T(8,128)(2,1)} %collective-permute-done.28.far_rec.own_rec.latter_rec, ...), custom_call_target="tpu_custom_call" | custom-call | flops 1 | bytes 1 | tf_op jit(solution)/shard_map/grad_rows/pallas_call | solution.py:731
  382.6 14.9 %frame_attend_grads.1 = bf16[8,2,128,384]{3,2,1,0:T(8,128)(2,1)S(1)} custom-call(bf16[8,2,128,384]{3,2,1,0:T(8,128)(2,1)} %all-to-all-done.1.packed_ref, bf16[8,2,128,128]{3,2,1,0:T(8,128)(2,1)} %all-to-all-done.3.grad_ref, s32[2,1024,1]{2,1,0:T(8,128)S(1)} %copy-done.8, s32[2,1,1024]{2,1,0:T(1,128)S(1)} %broadcast_in_dim.16.seg_row_ref), custom_call_target="tpu_custom_call" | custom-call | flops 1 | bytes 1 | tf_op jit(solution)/shard_map/frame_attend_grads/pallas_call | solution.py:477
  398.6 7.3 %grad_columns.3 = (bf16[2,2,2,4,256,128]{5,4,3,2,1,0:T(8,128)(2,1)}, bf16[2,2,2,4,256,128]{5,4,3,2,1,0:T(8,128)(2,1)S(1)}) custom-call(s32[27]{0:T(128)S(1)} %stack.69.order_ref, bf16[256,6144]{1,0:T(8,128)(2,1)} %get-tuple-element.428.latter_own, bf16[256,6144]{1,0:T(8,128)(2,1)} %collective-permute-done.29.latter_rec, ...), custom_call_target="tpu_custom_call" | custom-call | flops 1 | bytes 1 | tf_op jit(solution)/shard_map/grad_columns/pallas_call | solution.py:731
  407.3 9.3 %grad_rows.7 = (bf16[2,2,2,5,256,128]{5,4,3,2,1,0:T(8,128)(2,1)}, bf16[2,2,2,5,256,128]{5,4,3,2,1,0:T(8,128)(2,1)S(1)}) custom-call(s32[27]{0:T(128)S(1)} %stack.69.order_ref, bf16[256,7168]{1,0:T(8,128)(2,1)} %get-tuple-element.377.former_own.far_own.own_own, bf16[256,7168]{1,0:T(8,128)(2,1)} %collective-permute-done.25.former_rec.far_rec.own_rec, ...), custom_call_target="tpu_custom_call" | custom-call | flops 1 | bytes 1 | tf_op jit(solution)/shard_map/grad_rows/pallas_call | solution.py:731
  416.6 3.9 grad_rows.8
  424.8 4.5 all-to-all-start.4
  429.4 2.9 fusion.3
  432.4 2.6 fusion.4
  441.0 12.7 %grad_rows.9 = (bf16[2,2,2,4,256,128]{5,4,3,2,1,0:T(8,128)(2,1)}, bf16[2,2,2,4,256,128]{5,4,3,2,1,0:T(8,128)(2,1)S(1)}) custom-call(s32[27]{0:T(128)S(1)} %stack.69.order_ref, bf16[768,2048]{1,0:T(8,128)(2,1)} %bitcast.252, bf16[768,2048]{1,0:T(8,128)(2,1)} %copy-done.47, bf16[768,2048]{1,0:T(8,128)(2,1)} %bitcast.253, bf16[768,2048]{1,0:T(8,128)(2,1)} %copy-done.47, ...), custom_call_target="tpu_custom_call" | custom-call | flops 1 | bytes 1 | tf_op jit(solution)/shard_map/grad_rows/pallas_call | solution.py:731
  455.0 4.7 grad_rows.10
  459.7 4.4 grad_table.1
  465.1 13.7 %codec_result.1 = bf16[3,256,1024]{2,1,0:T(8,128)(2,1)} custom-call(f32[768,1024]{1,0:T(8,128)} %get-tuple-element.386.mixed_ref, bf16[768,4096]{1,0:T(8,128)(2,1)} %get-tuple-element.456.former_own.active_ref, f32[256,1]{1,0:T(8,128)} %copy.73.live_ref, bf16[4096,1024]{1,0:T(8,128)(2,1)} %get-tuple-element.382.contract_ref), custom_call_target="tpu_custom_call" | custom-call | flops 1 | bytes 1 | tf_op jit(solution)/shard_map/codec_result/pallas_call | solution.py:1497
  481.0 21.8 %collective-permute-done.37 = bf16[2,2,4,256,128]{4,3,2,1,0:T(8,128)(2,1)} collective-permute-done((bf16[2,2,4,256,128]{4,3,2,1,0:T(8,128)(2,1)}, bf16[2,2,4,256,128]{4,3,2,1,0:T(8,128)(2,1)}, u32[]{:S(2)}, u32[]{:S(2)}) %collective-permute-start.37) | collective-permute-done | bytes 1048608 | tf_op jit(solution)/shard_map/ppermute | solution.py:46
  502.8 3.0 collective-permute-done.39
  505.8 2.8 fusion.5
  508.6 2.7 fusion.1
  511.4 7.9 %frame_front_grads.1 = (bf16[256,3072]{1,0:T(8,128)(2,1)}, f32[256,1024]{1,0:T(8,128)}, f32[1,1024]{1,0:T(1,128)}) custom-call(bf16[8,2,128,384]{3,2,1,0:T(8,128)(2,1)} %all-to-all-done.4.packed_ref, bf16[256,1024]{1,0:T(8,128)(2,1)} %bitcast.271, f32[1,1024]{1,0:T(1,128)} %bitcast.293, f32[256,1024]{1,0:T(8,128)} %get-tuple-element.470.mixed_grad_ref, ...), custom_call_target="tpu_custom_call" | custom-call | flops 1 | bytes 1 | tf_op jit(solution)/shard_map/frame_front_grads/pallas_call | solution.py:1319
  525.7 8.1 %grad_rows.11 = (bf16[2,2,2,3,256,128]{5,4,3,2,1,0:T(8,128)(2,1)S(1)}, bf16[2,2,2,3,256,128]{5,4,3,2,1,0:T(8,128)(2,1)S(1)}) custom-call(s32[27]{0:T(128)S(1)} %stack.69.order_ref, bf16[256,7168]{1,0:T(8,128)(2,1)} %get-tuple-element.377.former_own.far_own.own_own, bf16[256,7168]{1,0:T(8,128)(2,1)} %collective-permute-done.25.former_rec.far_rec.own_rec, ...), custom_call_target="tpu_custom_call" | custom-call | flops 1 | bytes 1 | tf_op jit(solution)/shard_map/grad_rows/pallas_call | solution.py:731
  541.3 26.3 %collective-permute-done.41 = bf16[2,2,2,4,256,128]{5,4,3,2,1,0:T(8,128)(2,1)} collective-permute-done((bf16[2,2,2,4,256,128]{5,4,3,2,1,0:T(8,128)(2,1)}, bf16[2,2,2,4,256,128]{5,4,3,2,1,0:T(8,128)(2,1)}, u32[]{:S(2)}, u32[]{:S(2)}) %collective-permute-start.41) | collective-permute-done | bytes 2097184 | tf_op jit(solution)/shard_map/ppermute | solution.py:46
  583.0 20.7 %collective-permute-done.45 = bf16[2,2,4,256,128]{4,3,2,1,0:T(8,128)(2,1)} collective-permute-done((bf16[2,2,4,256,128]{4,3,2,1,0:T(8,128)(2,1)}, bf16[2,2,4,256,128]{4,3,2,1,0:T(8,128)(2,1)}, u32[]{:S(2)}, u32[]{:S(2)}) %collective-permute-start.45) | collective-permute-done | bytes 1048608 | tf_op jit(solution)/shard_map/ppermute | solution.py:46
  615.2 5.3 collective-permute-done.48
  623.2 2.9 collective-permute-start.58
  635.3 3.5 collective-permute-start.57
  638.8 7.0 collective-permute-done.51
  652.2 7.1 collective-permute-done.59
  671.2 16.6 %collective-permute-done.57 = bf16[8,256,128]{2,1,0:T(8,128)(2,1)} collective-permute-done((bf16[8,256,128]{2,1,0:T(8,128)(2,1)}, bf16[8,256,128]{2,1,0:T(8,128)(2,1)}, u32[]{:S(2)}, u32[]{:S(2)}) %collective-permute-start.57) | collective-permute-done | bytes 524320 | tf_op jit(solution)/shard_map/ppermute | solution.py:46
  687.8 8.4 %collective-permute-done.56 = bf16[6,256,128]{2,1,0:T(8,128)(2,1)} collective-permute-done((bf16[6,256,128]{2,1,0:T(8,128)(2,1)}, bf16[6,256,128]{2,1,0:T(8,128)(2,1)}, u32[]{:S(2)}, u32[]{:S(2)}) %collective-permute-start.56) | collective-permute-done | bytes 393248 | tf_op jit(solution)/shard_map/ppermute | solution.py:46
  (357 shorter events, 167.8 us)
Async XLA Ops:
  8.4 40.3 %collective-permute-start.8 = (bf16[2304,1024]{1,0:T(8,128)(2,1)}, bf16[2304,1024]{1,0:T(8,128)(2,1)}, u32[]{:S(2)}, u32[]{:S(2)}) collective-permute-start(bf16[2304,1024]{1,0:T(8,128)(2,1)} %get-tuple-element.321.refs_0_), channel_id=1, source_target_pairs={{0,1},{1,0},{2,3},{3,2},{4,5},{5,4},{6,7},{7,6},{8,9},{9,8},{10,11... | collective-permute-start | bytes 14155784 | tf_op jit(solution)/shard_map/ppermute | solution.py:46
  12.5 55.7 %collective-permute-start.9 = (bf16[2304,1024]{1,0:T(8,128)(2,1)}, bf16[2304,1024]{1,0:T(8,128)(2,1)}, u32[]{:S(2)}, u32[]{:S(2)}) collective-permute-start(bf16[2304,1024]{1,0:T(8,128)(2,1)} %get-tuple-element.330.refs_0_), channel_id=1, source_target_pairs={{0,1},{1,0},{2,3},{3,2},{4,5},{5,4},{6,7},{7,6},{8,9},{9,8},{10,11... | collective-permute-start | bytes 14155784 | tf_op jit(solution)/shard_map/ppermute | solution.py:46
  14.2 16.0 %collective-permute-start.3 = (bf16[896,1024]{1,0:T(8,128)(2,1)S(1)}, bf16[896,1024]{1,0:T(8,128)(2,1)}, u32[]{:S(2)}, u32[]{:S(2)}) collective-permute-start(bf16[896,1024]{1,0:T(8,128)(2,1)S(1)} %get-tuple-element.290.refs_0_), channel_id=1, source_target_pairs={{0,1},{1,0},{2,3},{3,2},{4,5},{5,4},{6,7},{7,6},{8,9},{9,8},{10,11... | collective-permute-start | bytes 5505032 | tf_op jit(solution)/shard_map/ppermute | solution.py:46
  14.7 15.5 %collective-permute-start = (bf16[224,1024]{1,0:T(8,128)(2,1)}, bf16[224,1024]{1,0:T(8,128)(2,1)S(1)}, u32[]{:S(2)}, u32[]{:S(2)}) collective-permute-start(bf16[224,1024]{1,0:T(8,128)(2,1)} %get-tuple-element.282), channel_id=1, source_target_pairs={{0,2},{1,3},{2,0},{3,1},{4,6},{5,7},{6,4},{7,5},{8,10},{9,11},{10,... | collective-permute-start | bytes 1376264 | tf_op jit(solution)/shard_map/ppermute | solution.py:46
  17.9 12.3 %all-to-all-start = ((s32[8,2,128]{2,1,0:T(2,128)}), s32[8,2,128]{2,1,0:T(2,128)S(1)}, u32[]{:S(2)}, u32[]{:S(2)}) async-start(s32[8,2,128]{2,1,0:T(2,128)} %broadcast_in_dim.13), calls=%async_computation | async-start | bytes 16384 | tf_op jit(solution)/shard_map/all_to_all | solution.py:1926
  30.2 26.9 %collective-permute-start.7 = (bf16[576,1024]{1,0:T(8,128)(2,1)}, bf16[576,1024]{1,0:T(8,128)(2,1)}, u32[]{:S(2)}, u32[]{:S(2)}) collective-permute-start(bf16[576,1024]{1,0:T(8,128)(2,1)} %copy-done.46), channel_id=1, source_target_pairs={{0,2},{1,3},{2,0},{3,1},{4,6},{5,7},{6,4},{7,5},{8,10},{9,11},{10,... | collective-permute-start | bytes 3538952 | tf_op jit(solution)/shard_map/ppermute | solution.py:46
  30.8 5.2 collective-permute-start.4
  34.9 13.0 %collective-permute-start.1 = (bf16[224,1024]{1,0:T(8,128)(2,1)S(1)}, bf16[224,1024]{1,0:T(8,128)(2,1)S(1)}, u32[]{:S(2)}, u32[]{:S(2)}) collective-permute-start(bf16[224,1024]{1,0:T(8,128)(2,1)S(1)} %collective-permute-done.refs_0_), channel_id=1, source_target_pairs={{0,4},{4,0},{8,12},{12,8},{16,20},{20,16},{24,28},{28,24},{1,5},{5... | collective-permute-start | bytes 1376264 | tf_op jit(solution)/shard_map/ppermute | solution.py:46
  36.1 12.6 %collective-permute-start.2 = (bf16[224,1024]{1,0:T(8,128)(2,1)S(1)}, bf16[224,1024]{1,0:T(8,128)(2,1)S(1)}, u32[]{:S(2)}, u32[]{:S(2)}) collective-permute-start(bf16[224,1024]{1,0:T(8,128)(2,1)S(1)} %collective-permute-done.refs_0_), channel_id=1, source_target_pairs={{0,8},{4,12},{8,0},{12,4},{16,24},{20,28},{24,16},{28,20},{1,9},{5... | collective-permute-start | bytes 1376264 | tf_op jit(solution)/shard_map/ppermute | solution.py:46
  57.2 18.9 %collective-permute-start.11 = (bf16[1280,1024]{1,0:T(8,128)(2,1)}, bf16[1280,1024]{1,0:T(8,128)(2,1)}, u32[]{:S(2)}, u32[]{:S(2)}) collective-permute-start(bf16[1280,1024]{1,0:T(8,128)(2,1)} %get-tuple-element.360.refs_0_), channel_id=1, source_target_pairs={{0,1},{1,0},{2,3},{3,2},{4,5},{5,4},{6,7},{7,6},{8,9},{9,8},{10,11... | collective-permute-start | bytes 7864328 | tf_op jit(solution)/shard_map/ppermute | solution.py:46
  57.2 8.1 %collective-permute-start.5 = (bf16[112,1024]{1,0:T(8,128)(2,1)S(1)}, bf16[112,1024]{1,0:T(8,128)(2,1)S(1)}, u32[]{:S(2)}, u32[]{:S(2)}) collective-permute-start(bf16[112,1024]{1,0:T(8,128)(2,1)S(1)} %slice.385), channel_id=1, source_target_pairs={{0,4},{4,0},{8,12},{12,8},{16,20},{20,16},{24,28},{28,24},{1,5},{5... | collective-permute-start | bytes 688136 | tf_op jit(solution)/shard_map/ppermute | solution.py:46
  58.3 7.7 %collective-permute-start.6 = (bf16[112,1024]{1,0:T(8,128)(2,1)S(1)}, bf16[112,1024]{1,0:T(8,128)(2,1)S(1)}, u32[]{:S(2)}, u32[]{:S(2)}) collective-permute-start(bf16[112,1024]{1,0:T(8,128)(2,1)S(1)} %slice.386), channel_id=1, source_target_pairs={{0,8},{4,12},{8,0},{12,4},{16,24},{20,28},{24,16},{28,20},{1,9},{5... | collective-permute-start | bytes 688136 | tf_op jit(solution)/shard_map/ppermute | solution.py:46
  68.3 28.6 %collective-permute-start.12 = (bf16[576,1024]{1,0:T(8,128)(2,1)}, bf16[576,1024]{1,0:T(8,128)(2,1)S(1)}, u32[]{:S(2)}, u32[]{:S(2)}) collective-permute-start(bf16[576,1024]{1,0:T(8,128)(2,1)} %collective-permute-done.7.refs_0_), channel_id=1, source_target_pairs={{0,4},{4,0},{8,12},{12,8},{16,20},{20,16},{24,28},{28,24},{1,5},{5... | collective-permute-start | bytes 3538952 | tf_op jit(solution)/shard_map/ppermute | solution.py:46
  69.3 28.4 %collective-permute-start.13 = (bf16[576,1024]{1,0:T(8,128)(2,1)}, bf16[576,1024]{1,0:T(8,128)(2,1)}, u32[]{:S(2)}, u32[]{:S(2)}) collective-permute-start(bf16[576,1024]{1,0:T(8,128)(2,1)} %collective-permute-done.7.refs_0_), channel_id=1, source_target_pairs={{0,8},{4,12},{8,0},{12,4},{16,24},{20,28},{24,16},{28,20},{1,9},{5... | collective-permute-start | bytes 3538952 | tf_op jit(solution)/shard_map/ppermute | solution.py:46
  70.5 28.1 %collective-permute-start.14 = (bf16[576,1024]{1,0:T(8,128)(2,1)}, bf16[576,1024]{1,0:T(8,128)(2,1)}, u32[]{:S(2)}, u32[]{:S(2)}) collective-permute-start(bf16[576,1024]{1,0:T(8,128)(2,1)} %get-tuple-element.314), channel_id=1, source_target_pairs={{0,2},{1,3},{2,0},{3,1},{4,6},{5,7},{6,4},{7,5},{8,10},{9,11},{10,... | collective-permute-start | bytes 3538952 | tf_op jit(solution)/shard_map/ppermute | solution.py:46
  98.5 50.5 %all-to-all-start.1 = ((bf16[8,2,128,384]{3,2,1,0:T(8,128)(2,1)}), bf16[8,2,128,384]{3,2,1,0:T(8,128)(2,1)}, u32[]{:S(2)}, u32[]{:S(2)}) async-start(bf16[8,2,128,384]{3,2,1,0:T(8,128)(2,1)} %get-tuple-element.315), calls=%async_computation.1 | async-start | bytes 3145728 | tf_op jit(solution)/shard_map/all_to_all | solution.py:1972
  125.5 16.2 %collective-permute-start.15 = (bf16[288,1024]{1,0:T(8,128)(2,1)S(1)}, bf16[288,1024]{1,0:T(8,128)(2,1)S(1)}, u32[]{:S(2)}, u32[]{:S(2)}) collective-permute-start(bf16[288,1024]{1,0:T(8,128)(2,1)S(1)} %slice.389), channel_id=1, source_target_pairs={{0,4},{4,0},{8,12},{12,8},{16,20},{20,16},{24,28},{28,24},{1,5},{5... | collective-permute-start | bytes 1769480 | tf_op jit(solution)/shard_map/ppermute | solution.py:46
  127.6 20.6 %collective-permute-start.16 = (bf16[288,1024]{1,0:T(8,128)(2,1)S(1)}, bf16[288,1024]{1,0:T(8,128)(2,1)S(1)}, u32[]{:S(2)}, u32[]{:S(2)}) collective-permute-start(bf16[288,1024]{1,0:T(8,128)(2,1)S(1)} %slice.390), channel_id=1, source_target_pairs={{0,8},{4,12},{8,0},{12,4},{16,24},{20,28},{24,16},{28,20},{1,9},{5... | collective-permute-start | bytes 1769480 | tf_op jit(solution)/shard_map/ppermute | solution.py:46
  155.6 12.9 %collective-permute-start.17 = (bf16[2304,1024]{1,0:T(8,128)(2,1)}, bf16[2304,1024]{1,0:T(8,128)(2,1)}, u32[]{:S(2)}, u32[]{:S(2)}) collective-permute-start(bf16[2304,1024]{1,0:T(8,128)(2,1)} %far_pack.4.refs_0_), channel_id=1, source_target_pairs={{0,1},{1,0},{2,3},{3,2},{4,5},{5,4},{6,7},{7,6},{8,9},{9,8},{10,11... | collective-permute-start | bytes 14155784 | tf_op jit(solution)/shard_map/ppermute | solution.py:46
  155.7 62.2 %collective-permute-start.20 = (bf16[1280,1024]{1,0:T(8,128)(2,1)}, bf16[1280,1024]{1,0:T(8,128)(2,1)}, u32[]{:S(2)}, u32[]{:S(2)}) collective-permute-start(bf16[1280,1024]{1,0:T(8,128)(2,1)} %get-tuple-element.360.refs_0_), channel_id=1, source_target_pairs={{0,2},{1,3},{2,0},{3,1},{4,6},{5,7},{6,4},{7,5},{8,10},{9,11},{10,... | collective-permute-start | bytes 7864328 | tf_op jit(solution)/shard_map/ppermute | solution.py:46
  157.3 30.5 %collective-permute-start.18 = (bf16[576,1024]{1,0:T(8,128)(2,1)}, bf16[576,1024]{1,0:T(8,128)(2,1)}, u32[]{:S(2)}, u32[]{:S(2)}) collective-permute-start(bf16[576,1024]{1,0:T(8,128)(2,1)} %collective-permute-done.14.refs_0_), channel_id=1, source_target_pairs={{0,4},{4,0},{8,12},{12,8},{16,20},{20,16},{24,28},{28,24},{1,5},{5... | collective-permute-start | bytes 3538952 | tf_op jit(solution)/shard_map/ppermute | solution.py:46
  157.3 31.9 %collective-permute-start.19 = (bf16[576,1024]{1,0:T(8,128)(2,1)}, bf16[576,1024]{1,0:T(8,128)(2,1)}, u32[]{:S(2)}, u32[]{:S(2)}) collective-permute-start(bf16[576,1024]{1,0:T(8,128)(2,1)} %collective-permute-done.14.refs_0_), channel_id=1, source_target_pairs={{0,8},{4,12},{8,0},{12,4},{16,24},{20,28},{24,16},{28,20},{1,9},{5... | collective-permute-start | bytes 3538952 | tf_op jit(solution)/shard_map/ppermute | solution.py:46
  168.5 29.0 %all-to-all-start.2 = ((bf16[8,2,128,128]{3,2,1,0:T(8,128)(2,1)}), bf16[8,2,128,128]{3,2,1,0:T(8,128)(2,1)}, u32[]{:S(2)}, u32[]{:S(2)}) async-start(bf16[8,2,128,128]{3,2,1,0:T(8,128)(2,1)} %copy-done.22), calls=%async_computation.2 | async-start | bytes 1048576 | tf_op jit(solution)/shard_map/all_to_all | solution.py:1988
  198.7 19.2 %collective-permute-start.21 = (bf16[288,1024]{1,0:T(8,128)(2,1)S(1)}, bf16[288,1024]{1,0:T(8,128)(2,1)S(1)}, u32[]{:S(2)}, u32[]{:S(2)}) collective-permute-start(bf16[288,1024]{1,0:T(8,128)(2,1)S(1)} %slice.392), channel_id=1, source_target_pairs={{0,4},{4,0},{8,12},{12,8},{16,20},{20,16},{24,28},{28,24},{1,5},{5... | collective-permute-start | bytes 1769480 | tf_op jit(solution)/shard_map/ppermute | solution.py:46
  199.8 18.1 %collective-permute-start.22 = (bf16[288,1024]{1,0:T(8,128)(2,1)S(1)}, bf16[288,1024]{1,0:T(8,128)(2,1)S(1)}, u32[]{:S(2)}, u32[]{:S(2)}) collective-permute-start(bf16[288,1024]{1,0:T(8,128)(2,1)S(1)} %slice.393), channel_id=1, source_target_pairs={{0,8},{4,12},{8,0},{12,4},{16,24},{20,28},{24,16},{28,20},{1,9},{5... | collective-permute-start | bytes 1769480 | tf_op jit(solution)/shard_map/ppermute | solution.py:46
  217.9 5.2 collective-permute-start.23
  227.8 28.5 %collective-permute-start.26 = (bf16[2304,1024]{1,0:T(8,128)(2,1)}, bf16[2304,1024]{1,0:T(8,128)(2,1)}, u32[]{:S(2)}, u32[]{:S(2)}) collective-permute-start(bf16[2304,1024]{1,0:T(8,128)(2,1)} %far_pack.5.refs_0_), channel_id=1, source_target_pairs={{0,1},{1,0},{2,3},{3,2},{4,5},{5,4},{6,7},{7,6},{8,9},{9,8},{10,11... | collective-permute-start | bytes 14155784 | tf_op jit(solution)/shard_map/ppermute | solution.py:46
  228.2 37.0 %collective-permute-start.25 = (bf16[256,7168]{1,0:T(8,128)(2,1)}, bf16[256,7168]{1,0:T(8,128)(2,1)}, u32[]{:S(2)}, u32[]{:S(2)}) collective-permute-start(bf16[256,7168]{1,0:T(8,128)(2,1)} %get-tuple-element.377.former_own.far_own.own_own), channel_id=1, source_target_pairs={{0,1},{1,0},{2,3},{3,2},{4,5},{5,4},{6,7},{7,6},{8,9},{9,8},{10,11... | collective-permute-start | bytes 11010056 | tf_op jit(solution)/shard_map/ppermute | solution.py:46
  228.4 18.5 %collective-permute-start.24 = (bf16[768,1024]{1,0:T(8,128)(2,1)S(1)}, bf16[768,1024]{1,0:T(8,128)(2,1)S(1)}, u32[]{:S(2)}, u32[]{:S(2)}) collective-permute-start(bf16[768,1024]{1,0:T(8,128)(2,1)S(1)} %bitcast.258), channel_id=1, source_target_pairs={{0,1},{1,0},{2,3},{3,2},{4,5},{5,4},{6,7},{7,6},{8,9},{9,8},{10,11... | collective-permute-start | bytes 4718600 | tf_op jit(solution)/shard_map/ppermute | solution.py:46
  305.6 38.8 %collective-permute-start.28 = (bf16[768,5120]{1,0:T(8,128)(2,1)}, bf16[768,5120]{1,0:T(8,128)(2,1)}, u32[]{:S(2)}, u32[]{:S(2)}) collective-permute-start(bf16[768,5120]{1,0:T(8,128)(2,1)} %get-tuple-element.408.far_own.own_own.latter_own), channel_id=1, source_target_pairs={{0,1},{1,0},{2,3},{3,2},{4,5},{5,4},{6,7},{7,6},{8,9},{9,8},{10,11... | collective-permute-start | bytes 23592968 | tf_op jit(solution)/shard_map/ppermute | solution.py:46
  306.0 38.4 %collective-permute-start.27 = (bf16[768,4096]{1,0:T(8,128)(2,1)}, bf16[768,4096]{1,0:T(8,128)(2,1)}, u32[]{:S(2)}, u32[]{:S(2)}) collective-permute-start(bf16[768,4096]{1,0:T(8,128)(2,1)} %get-tuple-element.456.former_own.active_ref), channel_id=1, source_target_pairs={{0,1},{1,0},{2,3},{3,2},{4,5},{5,4},{6,7},{7,6},{8,9},{9,8},{10,11... | collective-permute-start | bytes 18874376 | tf_op jit(solution)/shard_map/ppermute | solution.py:46
  344.4 33.7 %collective-permute-start.29 = (bf16[256,6144]{1,0:T(8,128)(2,1)}, bf16[256,6144]{1,0:T(8,128)(2,1)}, u32[]{:S(2)}, u32[]{:S(2)}) collective-permute-start(bf16[256,6144]{1,0:T(8,128)(2,1)} %get-tuple-element.428.latter_own), channel_id=1, source_target_pairs={{0,1},{1,0},{2,3},{3,2},{4,5},{5,4},{6,7},{7,6},{8,9},{9,8},{10,11... | collective-permute-start | bytes 9437192 | tf_op jit(solution)/shard_map/ppermute | solution.py:46
  344.8 33.3 %all-to-all-start.3 = ((bf16[8,2,128,128]{3,2,1,0:T(8,128)(2,1)}), bf16[8,2,128,128]{3,2,1,0:T(8,128)(2,1)}, u32[]{:S(2)}, u32[]{:S(2)}) async-start(bf16[8,2,128,128]{3,2,1,0:T(8,128)(2,1)} %get-tuple-element.403), calls=%async_computation.3 | async-start | bytes 1048576 | tf_op jit(solution)/shard_map/all_to_all | solution.py:2069
  378.1 46.8 %collective-permute-start.33 = (bf16[768,3072]{1,0:T(8,128)(2,1)}, bf16[768,3072]{1,0:T(8,128)(2,1)}, u32[]{:S(2)}, u32[]{:S(2)}) collective-permute-start(bf16[768,3072]{1,0:T(8,128)(2,1)} %bitcast.263), channel_id=1, source_target_pairs={{0,1},{1,0},{2,3},{3,2},{4,5},{5,4},{6,7},{7,6},{8,9},{9,8},{10,11... | collective-permute-start | bytes 14155784 | tf_op jit(solution)/shard_map/ppermute | solution.py:46
  378.3 44.8 %collective-permute-start.32 = (bf16[768,2048]{1,0:T(8,128)(2,1)S(1)}, bf16[768,2048]{1,0:T(8,128)(2,1)S(1)}, u32[]{:S(2)}, u32[]{:S(2)}) collective-permute-start(bf16[768,2048]{1,0:T(8,128)(2,1)S(1)} %bitcast.256), channel_id=1, source_target_pairs={{0,1},{1,0},{2,3},{3,2},{4,5},{5,4},{6,7},{7,6},{8,9},{9,8},{10,11... | collective-permute-start | bytes 9437192 | tf_op jit(solution)/shard_map/ppermute | solution.py:46
  378.6 50.8 %collective-permute-start.31 = (bf16[2,2,2,4,256,128]{5,4,3,2,1,0:T(8,128)(2,1)}, bf16[2,2,2,4,256,128]{5,4,3,2,1,0:T(8,128)(2,1)}, u32[]{:S(2)}, u32[]{:S(2)}) collective-permute-start(bf16[2,2,2,4,256,128]{5,4,3,2,1,0:T(8,128)(2,1)} %copy-done.44), channel_id=1, source_target_pairs={{0,2},{1,3},{2,0},{3,1},{4,6},{5,7},{6,4},{7,5},{8,10},{9,11},{10,... | collective-permute-start | bytes 6291464 | tf_op jit(solution)/shard_map/ppermute | solution.py:46
  379.4 50.1 %collective-permute-start.30 = (bf16[2,2,2,4,256,128]{5,4,3,2,1,0:T(8,128)(2,1)}, bf16[2,2,2,4,256,128]{5,4,3,2,1,0:T(8,128)(2,1)}, u32[]{:S(2)}, u32[]{:S(2)}) collective-permute-start(bf16[2,2,2,4,256,128]{5,4,3,2,1,0:T(8,128)(2,1)} %copy-done.45), channel_id=1, source_target_pairs={{0,4},{4,0},{8,12},{12,8},{16,20},{20,16},{24,28},{28,24},{1,5},{5... | collective-permute-start | bytes 6291464 | tf_op jit(solution)/shard_map/ppermute | solution.py:46
  381.4 40.6 %collective-permute-start.34 = (bf16[768,1024]{1,0:T(8,128)(2,1)}, bf16[768,1024]{1,0:T(8,128)(2,1)S(1)}, u32[]{:S(2)}, u32[]{:S(2)}) collective-permute-start(bf16[768,1024]{1,0:T(8,128)(2,1)} %get-tuple-element.421.latter_own), channel_id=1, source_target_pairs={{0,1},{1,0},{2,3},{3,2},{4,5},{5,4},{6,7},{7,6},{8,9},{9,8},{10,11... | collective-permute-start | bytes 4718600 | tf_op jit(solution)/shard_map/ppermute | solution.py:46
  424.8 77.9 %all-to-all-start.4 = ((bf16[8,2,128,384]{3,2,1,0:T(8,128)(2,1)}), bf16[8,2,128,384]{3,2,1,0:T(8,128)(2,1)}, u32[]{:S(2)}, u32[]{:S(2)}) async-start(bf16[8,2,128,384]{3,2,1,0:T(8,128)(2,1)} %copy-done.14), calls=%async_computation.4 | async-start | bytes 3145728 | tf_op jit(solution)/shard_map/all_to_all | solution.py:2117
  434.9 70.9 %collective-permute-start.39 = (bf16[2,2,2,5,256,128]{5,4,3,2,1,0:T(8,128)(2,1)}, bf16[2,2,2,5,256,128]{5,4,3,2,1,0:T(8,128)(2,1)}, u32[]{:S(2)}, u32[]{:S(2)}) collective-permute-start(bf16[2,2,2,5,256,128]{5,4,3,2,1,0:T(8,128)(2,1)} %get-tuple-element.459), channel_id=1, source_target_pairs={{0,4},{4,0},{8,12},{12,8},{16,20},{20,16},{24,28},{28,24},{1,5},{5... | collective-permute-start | bytes 7864328 | tf_op jit(solution)/shard_map/ppermute | solution.py:46
  436.9 65.8 %collective-permute-start.38 = (bf16[2,2,2,4,256,128]{5,4,3,2,1,0:T(8,128)(2,1)}, bf16[2,2,2,4,256,128]{5,4,3,2,1,0:T(8,128)(2,1)}, u32[]{:S(2)}, u32[]{:S(2)}) collective-permute-start(bf16[2,2,2,4,256,128]{5,4,3,2,1,0:T(8,128)(2,1)} %get-tuple-element.457), channel_id=1, source_target_pairs={{0,2},{1,3},{2,0},{3,1},{4,6},{5,7},{6,4},{7,5},{8,10},{9,11},{10,... | collective-permute-start | bytes 6291464 | tf_op jit(solution)/shard_map/ppermute | solution.py:46
  438.1 21.6 %collective-permute-start.35 = (bf16[512,1024]{1,0:T(8,128)(2,1)S(1)}, bf16[512,1024]{1,0:T(8,128)(2,1)S(1)}, u32[]{:S(2)}, u32[]{:S(2)}) collective-permute-start(bf16[512,1024]{1,0:T(8,128)(2,1)S(1)} %copy-done.36), channel_id=1, source_target_pairs={{0,1},{1,0},{2,3},{3,2},{4,5},{5,4},{6,7},{7,6},{8,9},{9,8},{10,11... | collective-permute-start | bytes 3145736 | tf_op jit(solution)/shard_map/ppermute | solution.py:46
  438.1 42.9 %collective-permute-start.36 = (bf16[2,2,4,256,128]{4,3,2,1,0:T(8,128)(2,1)}, bf16[2,2,4,256,128]{4,3,2,1,0:T(8,128)(2,1)}, u32[]{:S(2)}, u32[]{:S(2)}) collective-permute-start(bf16[2,2,4,256,128]{4,3,2,1,0:T(8,128)(2,1)} %fusion.3), channel_id=1, source_target_pairs={{0,8},{4,12},{8,0},{12,4},{16,24},{20,28},{24,16},{28,20},{1,9},{5... | collective-permute-start | bytes 3145736 | tf_op jit(solution)/shard_map/ppermute | solution.py:46
  439.6 63.2 %collective-permute-start.37 = (bf16[2,2,4,256,128]{4,3,2,1,0:T(8,128)(2,1)}, bf16[2,2,4,256,128]{4,3,2,1,0:T(8,128)(2,1)}, u32[]{:S(2)}, u32[]{:S(2)}) collective-permute-start(bf16[2,2,4,256,128]{4,3,2,1,0:T(8,128)(2,1)} %fusion.4), channel_id=1, source_target_pairs={{0,8},{4,12},{8,0},{12,4},{16,24},{20,28},{24,16},{28,20},{1,9},{5... | collective-permute-start | bytes 3145736 | tf_op jit(solution)/shard_map/ppermute | solution.py:46
  519.2 3.9 collective-permute-start.42
  519.3 48.4 %collective-permute-start.41 = (bf16[2,2,2,4,256,128]{5,4,3,2,1,0:T(8,128)(2,1)}, bf16[2,2,2,4,256,128]{5,4,3,2,1,0:T(8,128)(2,1)}, u32[]{:S(2)}, u32[]{:S(2)}) collective-permute-start(bf16[2,2,2,4,256,128]{5,4,3,2,1,0:T(8,128)(2,1)} %get-tuple-element.475), channel_id=1, source_target_pairs={{0,2},{1,3},{2,0},{3,1},{4,6},{5,7},{6,4},{7,5},{8,10},{9,11},{10,... | collective-permute-start | bytes 6291464 | tf_op jit(solution)/shard_map/ppermute | solution.py:46
  521.4 49.8 %collective-permute-start.40 = (bf16[2,2,2,2,256,128]{5,4,3,2,1,0:T(8,128)(2,1)}, bf16[2,2,2,2,256,128]{5,4,3,2,1,0:T(8,128)(2,1)}, u32[]{:S(2)}, u32[]{:S(2)}) collective-permute-start(bf16[2,2,2,2,256,128]{5,4,3,2,1,0:T(8,128)(2,1)} %get-tuple-element.473), channel_id=1, source_target_pairs={{0,4},{4,0},{8,12},{12,8},{16,20},{20,16},{24,28},{28,24},{1,5},{5... | collective-permute-start | bytes 3145736 | tf_op jit(solution)/shard_map/ppermute | solution.py:46
  521.4 53.0 %collective-permute-start.47 = (bf16[2,2,5,256,128]{4,3,2,1,0:T(8,128)(2,1)}, bf16[2,2,5,256,128]{4,3,2,1,0:T(8,128)(2,1)}, u32[]{:S(2)}, u32[]{:S(2)}) collective-permute-start(bf16[2,2,5,256,128]{4,3,2,1,0:T(8,128)(2,1)} %fusion.1), channel_id=1, source_target_pairs={{0,8},{4,12},{8,0},{12,4},{16,24},{20,28},{24,16},{28,20},{1,9},{5... | collective-permute-start | bytes 3932168 | tf_op jit(solution)/shard_map/ppermute | solution.py:46
  537.9 43.7 %collective-permute-start.46 = (bf16[6208,128]{1,0:T(8,128)(2,1)S(1)}, bf16[6208,128]{1,0:T(8,128)(2,1)S(1)}, u32[]{:S(2)}, u32[]{:S(2)}) collective-permute-start(bf16[6208,128]{1,0:T(8,128)(2,1)S(1)} %pad_maximum_fusion), channel_id=1, source_target_pairs={{0,4},{4,0},{8,12},{12,8},{16,20},{20,16},{24,28},{28,24},{1,5},{5... | collective-permute-start | bytes 4767752 | tf_op jit(solution)/shard_map/ppermute | solution.py:46
  540.7 63.0 %collective-permute-start.45 = (bf16[2,2,4,256,128]{4,3,2,1,0:T(8,128)(2,1)}, bf16[2,2,4,256,128]{4,3,2,1,0:T(8,128)(2,1)}, u32[]{:S(2)}, u32[]{:S(2)}) collective-permute-start(bf16[2,2,4,256,128]{4,3,2,1,0:T(8,128)(2,1)} %fusion.5), channel_id=1, source_target_pairs={{0,4},{4,0},{8,12},{12,8},{16,20},{20,16},{24,28},{28,24},{1,5},{5... | collective-permute-start | bytes 3145736 | tf_op jit(solution)/shard_map/ppermute | solution.py:46
  570.1 37.3 %collective-permute-start.49 = (bf16[2,2,4,256,128]{4,3,2,1,0:T(8,128)(2,1)}, bf16[2,2,4,256,128]{4,3,2,1,0:T(8,128)(2,1)}, u32[]{:S(2)}, u32[]{:S(2)}) collective-permute-start(bf16[2,2,4,256,128]{4,3,2,1,0:T(8,128)(2,1)} %fusion.6), channel_id=1, source_target_pairs={{0,8},{4,12},{8,0},{12,4},{16,24},{20,28},{24,16},{28,20},{1,9},{5... | collective-permute-start | bytes 3145736 | tf_op jit(solution)/shard_map/ppermute | solution.py:46
  573.2 50.0 %collective-permute-start.44 = (bf16[2,2,2,256,128]{4,3,2,1,0:T(8,128)(2,1)}, bf16[2,2,2,256,128]{4,3,2,1,0:T(8,128)(2,1)}, u32[]{:S(2)}, u32[]{:S(2)}) collective-permute-start(bf16[2,2,2,256,128]{4,3,2,1,0:T(8,128)(2,1)} %fusion.14), channel_id=1, source_target_pairs={{0,2},{1,3},{2,0},{3,1},{4,6},{5,7},{6,4},{7,5},{8,10},{9,11},{10,... | collective-permute-start | bytes 1572872 | tf_op jit(solution)/shard_map/ppermute | solution.py:46
  576.8 36.4 %collective-permute-start.50 = (bf16[2,5,256,128]{3,2,1,0:T(8,128)(2,1)}, bf16[2,5,256,128]{3,2,1,0:T(8,128)(2,1)}, u32[]{:S(2)}, u32[]{:S(2)}) collective-permute-start(bf16[2,5,256,128]{3,2,1,0:T(8,128)(2,1)} %fusion.2), channel_id=1, source_target_pairs={{0,2},{1,3},{2,0},{3,1},{4,6},{5,7},{6,4},{7,5},{8,10},{9,11},{10,... | collective-permute-start | bytes 1966088 | tf_op jit(solution)/shard_map/ppermute | solution.py:46
  581.7 49.7 %collective-permute-start.54 = (bf16[2,4,256,128]{3,2,1,0:T(8,128)(2,1)}, bf16[2,4,256,128]{3,2,1,0:T(8,128)(2,1)}, u32[]{:S(2)}, u32[]{:S(2)}) collective-permute-start(bf16[2,4,256,128]{3,2,1,0:T(8,128)(2,1)} %fusion.10), channel_id=1, source_target_pairs={{0,2},{1,3},{2,0},{3,1},{4,6},{5,7},{6,4},{7,5},{8,10},{9,11},{10,... | collective-permute-start | bytes 1572872 | tf_op jit(solution)/shard_map/ppermute | solution.py:46
  603.7 25.4 %collective-permute-start.53 = (bf16[3136,128]{1,0:T(8,128)(2,1)S(1)}, bf16[3136,128]{1,0:T(8,128)(2,1)S(1)}, u32[]{:S(2)}, u32[]{:S(2)}) collective-permute-start(bf16[3136,128]{1,0:T(8,128)(2,1)S(1)} %pad_maximum_fusion.1), channel_id=1, source_target_pairs={{0,2},{1,3},{2,0},{3,1},{4,6},{5,7},{6,4},{7,5},{8,10},{9,11},{10,... | collective-permute-start | bytes 2408456 | tf_op jit(solution)/shard_map/ppermute | solution.py:46
  607.4 13.1 %collective-permute-start.48 = (bf16[2,4,256,128]{3,2,1,0:T(8,128)(2,1)S(1)}, bf16[2,4,256,128]{3,2,1,0:T(8,128)(2,1)S(1)}, u32[]{:S(2)}, u32[]{:S(2)}) collective-permute-start(bf16[2,4,256,128]{3,2,1,0:T(8,128)(2,1)S(1)} %fusion.9), channel_id=1, source_target_pairs={{0,8},{4,12},{8,0},{12,4},{16,24},{20,28},{24,16},{28,20},{1,9},{5... | collective-permute-start | bytes 1572872 | tf_op jit(solution)/shard_map/ppermute | solution.py:46
  613.3 19.4 %collective-permute-start.52 = (bf16[2,4,256,128]{3,2,1,0:T(8,128)(2,1)}, bf16[2,4,256,128]{3,2,1,0:T(8,128)(2,1)}, u32[]{:S(2)}, u32[]{:S(2)}) collective-permute-start(bf16[2,4,256,128]{3,2,1,0:T(8,128)(2,1)} %fusion.7), channel_id=1, source_target_pairs={{0,4},{4,0},{8,12},{12,8},{16,20},{20,16},{24,28},{28,24},{1,5},{5... | collective-permute-start | bytes 1572872 | tf_op jit(solution)/shard_map/ppermute | solution.py:46
  620.5 27.4 %collective-permute-start.55 = (bf16[2,4,256,128]{3,2,1,0:T(8,128)(2,1)}, bf16[2,4,256,128]{3,2,1,0:T(8,128)(2,1)}, u32[]{:S(2)}, u32[]{:S(2)}) collective-permute-start(bf16[2,4,256,128]{3,2,1,0:T(8,128)(2,1)} %fusion.8), channel_id=1, source_target_pairs={{0,4},{4,0},{8,12},{12,8},{16,20},{20,16},{24,28},{28,24},{1,5},{5... | collective-permute-start | bytes 1572872 | tf_op jit(solution)/shard_map/ppermute | solution.py:46
  623.2 42.3 %collective-permute-start.58 = (bf16[9,256,128]{2,1,0:T(8,128)(2,1)}, bf16[9,256,128]{2,1,0:T(8,128)(2,1)}, u32[]{:S(2)}, u32[]{:S(2)}) collective-permute-start(bf16[9,256,128]{2,1,0:T(8,128)(2,1)} %pad_maximum_fusion.2), channel_id=1, source_target_pairs={{0,16},{4,20},{8,24},{12,28},{16,0},{20,4},{24,8},{28,12},{1,17},{... | collective-permute-start | bytes 1769480 | tf_op jit(solution)/shard_map/ppermute | solution.py:46
  629.1 16.6 %collective-permute-start.51 = (bf16[2,2,256,128]{3,2,1,0:T(8,128)(2,1)}, bf16[2,2,256,128]{3,2,1,0:T(8,128)(2,1)}, u32[]{:S(2)}, u32[]{:S(2)}) collective-permute-start(bf16[2,2,256,128]{3,2,1,0:T(8,128)(2,1)} %fusion.23), channel_id=1, source_target_pairs={{0,8},{4,12},{8,0},{12,4},{16,24},{20,28},{24,16},{28,20},{1,9},{5... | collective-permute-start | bytes 786440 | tf_op jit(solution)/shard_map/ppermute | solution.py:46
  631.4 27.9 %collective-permute-start.59 = (bf16[1600,128]{1,0:T(8,128)(2,1)S(1)}, bf16[1600,128]{1,0:T(8,128)(2,1)S(1)}, u32[]{:S(2)}, u32[]{:S(2)}) collective-permute-start(bf16[1600,128]{1,0:T(8,128)(2,1)S(1)} %pad_maximum_fusion.4), channel_id=1, source_target_pairs={{0,8},{4,12},{8,0},{12,4},{16,24},{20,28},{24,16},{28,20},{1,9},{5... | collective-permute-start | bytes 1228808 | tf_op jit(solution)/shard_map/ppermute | solution.py:46
  635.3 52.5 %collective-permute-start.57 = (bf16[8,256,128]{2,1,0:T(8,128)(2,1)}, bf16[8,256,128]{2,1,0:T(8,128)(2,1)}, u32[]{:S(2)}, u32[]{:S(2)}) collective-permute-start(bf16[8,256,128]{2,1,0:T(8,128)(2,1)} %pad_maximum_fusion.3), channel_id=1, source_target_pairs={{0,16},{4,20},{8,24},{12,28},{16,0},{20,4},{24,8},{28,12},{1,17},{... | collective-permute-start | bytes 1572872 | tf_op jit(solution)/shard_map/ppermute | solution.py:46
  650.0 46.2 %collective-permute-start.56 = (bf16[6,256,128]{2,1,0:T(8,128)(2,1)}, bf16[6,256,128]{2,1,0:T(8,128)(2,1)}, u32[]{:S(2)}, u32[]{:S(2)}) collective-permute-start(bf16[6,256,128]{2,1,0:T(8,128)(2,1)} %pad_maximum_fusion.5), channel_id=1, source_target_pairs={{0,16},{4,20},{8,24},{12,28},{16,0},{20,4},{24,8},{28,12},{1,17},{... | collective-permute-start | bytes 1179656 | tf_op jit(solution)/shard_map/ppermute | solution.py:46
  663.9 41.7 %collective-permute-start.60 = (bf16[832,128]{1,0:T(8,128)(2,1)}, bf16[832,128]{1,0:T(8,128)(2,1)S(1)}, u32[]{:S(2)}, u32[]{:S(2)}) collective-permute-start(bf16[832,128]{1,0:T(8,128)(2,1)} %pad_maximum_fusion.6), channel_id=1, source_target_pairs={{0,16},{4,20},{8,24},{12,28},{16,0},{20,4},{24,8},{28,12},{1,17},{... | collective-permute-start | bytes 638984 | tf_op jit(solution)/shard_map/ppermute | solution.py:46
  (70 other events, 445.8 us)

commit v7 on v6

--- a/solution.py
+++ b/solution.py
@@ -1863,6 +1863,24 @@
         return self.total(True)
 
 
+def together(sums, chain, stage):
+    given = [one.give(chain) for one in sums]
+    message = jnp.concatenate(given, axis=-3)
+    chain.leave(message)
+    message = swap(message, *BITS[stage])
+
+    def take():
+        held = chain.enter(message)
+        chain.leave(held)
+        start = 0
+        for one, part in zip(sums, given):
+            size = part.shape[-3]
+            one.coming = held[..., start : start + size, :, :]
+            start += size
+
+    return take
+
+
 def finish(sums, chain):
     given = jnp.concatenate([one.give(chain) for one in sums], axis=0)
     riders = sums[-1].riders
@@ -1918,28 +1936,29 @@
         ((0, 127), (0, 0)),
     )
     first = Gather([frame_project, gain_rows], spots)
+    chain.leave(first.quarter)
     first.start(chain)
-    chain.leave(first.quarter)
-    second = Gather([frame_expand, frame_contract, frame_output], spots)
-    second.quarter = chain.enter(second.quarter)
+    members = chain.enter(frame_expand, frame_contract, frame_output)
+    second = Gather(members, spots)
     chain.leave(second.quarter)
+    codes = codec_tokens.reshape(1, (positions - 1) * frame_total) + jnp.repeat(
+        jnp.arange(positions - 1, dtype=jnp.int32) * CODES, frame_total
+    )
+    live = padding.reshape(frame_total).astype(F32)[:, None]
+    first.spread(chain)
+    second.start(chain)
     every_segment = lax.all_to_all(
-        jnp.broadcast_to(segments[None], (count, row_count, frames_dev)),
+        jnp.broadcast_to(chain.enter(segments)[None], (count, row_count, frames_dev)),
         "seq",
         split_axis=0,
         concat_axis=0,
         tiled=True,
     )
     every_segment = jnp.transpose(every_segment, (1, 0, 2)).reshape(row_count, count * frames_dev)
-    codes = codec_tokens.reshape(1, (positions - 1) * frame_total) + jnp.repeat(
-        jnp.arange(positions - 1, dtype=jnp.int32) * CODES, frame_total
-    )
-    codes_pair = chain.pair(codes)
     every_segment = chain.enter(every_segment)
     chain.leave(every_segment)
-    live = padding.reshape(frame_total).astype(F32)[:, None]
-    first.spread(chain)
-    second.start(chain)
+    fourth = Gather(chain.enter(codec_expand, codec_contract, codec_output), spots)
+    chain.leave(fourth.quarter)
     contract_in = (
         jnp.transpose(chain.enter(cotangent).reshape(frame_total, positions, width), (1, 0, 2))
         * live.astype(BF)[None]
@@ -1947,17 +1966,13 @@
     chain.leave(contract_in)
     first.join_near(chain)
     first.cross(chain)
-    fourth = Gather([codec_expand, codec_contract, codec_output], spots)
-    fourth.quarter = chain.enter(fourth.quarter)
-    chain.leave(fourth.quarter)
+    third = Gather(chain.enter(codec_project, codebooks), spots, True)
+    chain.leave(third.pack)
+    first.close(chain)
     second.spread(chain)
+    first.send(chain)
     fourth.start(chain)
-    third = Gather([codec_project, codebooks], spots, True)
-    third.pack = chain.enter(third.pack)
-    chain.leave(third.pack)
     third.start(chain)
-    first.close(chain)
-    first.send(chain)
 
     frame_project_all, gains = first.join(chain)
     gains = jnp.transpose(
@@ -1980,6 +1995,7 @@
     second.send(chain)
     fourth.spread(chain)
     contract_pair = Pair(contract_in)
+    codes_pair = Pair(chain.enter(codes))
     packed = chain.enter(packed)
     attended = frame_attend_call(packed, every_segment)
     chain.leave(attended)
@@ -2115,8 +2131,7 @@
     contract_sum.arrive(chain)
     expand_sum.arrive(chain)
     packed_grad = lax.all_to_all(packed_grad, "seq", split_axis=0, concat_axis=0, tiled=True)
-    contract_sum.step(chain)
-    expand_sum.step(chain)
+    take_both = together([contract_sum, expand_sum], chain, "n")
     frame_contract_sum = Reduce(frame_contract_stages, chain.enter(*frame_contract_blocks))
     frame_expand_sum = Reduce(frame_expand_stages, chain.enter(*frame_expand_blocks))
     table_pair = Pair(chain.enter(table_in))
@@ -2142,17 +2157,8 @@
     chain.leave(*table_blocks)
     project_sum = Reduce(project_stages, chain.enter(*project_blocks))
     table_sum = Reduce(table_stages, chain.enter(*table_blocks))
-    output = codec_result(codec_mixed, chain.enter(codec_activated), live, codec_contract_all)
-    chain.leave(output)
-    output = jnp.transpose(output, (1, 0, 2)).reshape(row_count, frames_dev, positions, width)
-
-    packed_grad, contract_sum.coming, expand_sum.coming, frame_contract_sum.coming = chain.enter(
-        packed_grad, contract_sum.coming, expand_sum.coming, frame_contract_sum.coming
-    )
-    packed_grad, frame_expand_sum.coming = chain.enter(packed_grad, frame_expand_sum.coming)
+    packed_grad = chain.enter(packed_grad)
     chain.leave(packed_grad)
-    frame_contract_sum.step(chain)
-    frame_expand_sum.step(chain)
     frame_projected_grad, frames_grad, frame_prenorm_grad = frame_front_grads(
         chain.enter(packed_grad), hidden, gains[0], frame_mixed_grad, frame_project_all
     )
@@ -2178,14 +2184,22 @@
     chain.leave(*blocks)
     riders = gain_pair.own + gain_pair.other
     frame_project_sum = Reduce(table_stages, blocks, chain.enter(riders))
+    frame_expand_sum.arrive(chain)
+    frame_contract_sum.step(chain)
+    frame_expand_sum.step(chain)
+    output = codec_result(codec_mixed, chain.enter(codec_activated), live, codec_contract_all)
+    chain.leave(output)
+    output = jnp.transpose(output, (1, 0, 2)).reshape(row_count, frames_dev, positions, width)
+
     project_sum.step(chain)
+    take_both()
     table_sum.step(chain)
-    frame_expand_sum.step(chain)
-    expand_sum.step(chain)
+    take_expand = together([expand_sum, frame_expand_sum], chain, "y")
     frame_project_sum.step(chain)
     frame_contract_sum.step(chain)
     project_sum.step(chain)
     contract_sum.step(chain)
+    take_expand()
     take_second = finish([frame_contract_sum, frame_expand_sum], chain)
     table_sum.step(chain)
     frame_project_sum.step(chain)

time: 719 us -> 696 us (0.968)
  waiting for transfers between devices: 196 us -> 149 us
  local copies, waits for them, and re-layouts: 65.8 us -> 79.9 us
  blocking collectives: 0 us -> 12.3 us
  starting transfers between devices: 83.5 us -> 73.9 us
  other arithmetic: 55.9 us -> 64 us
    ppermute x61 -> x59, waiting for transfers between devices: 181 us -> 139 us  [swap(): lax.ppermute(values, axis, [(i, i ^ bit) for i in range(lax.axis_size(axi...]
    all_to_all x0 -> x1, blocking collectives: none -> 12.3 us  [shards(): lax.all_to_all(jnp.broadcast_to(chain.enter(segments)[None], (count, row_...]
    ppermute x61 -> x59, starting transfers between devices: 56 us -> 51 us  [swap(): lax.ppermute(values, axis, [(i, i ^ bit) for i in range(lax.axis_size(axi...]
    unnamed x147 -> x149, local copies, waits for them, and re-layouts: 45.2 us -> 45.3 us
  transfers between devices with their start and end apart: 66 -> 63, of which waited for: 28 -> 26; matrix products, arithmetic and copies ran while one was open for 11% -> 14% of each run, Pallas kernels for 35% -> 36%
where the time goes in v7:
time: 696 us; the launch traced here: 686 us
  Pallas kernels  304 us (44%)
  waiting for transfers between devices  149 us (21%)
  local copies, waits for them, and re-layouts  79.9 us (11%)
  starting transfers between devices  73.9 us (11%)
  other arithmetic  64 us (9%)
  blocking collectives  12.3 us (2%)
    ppermute x59, waiting for transfers between devices, swap(): lax.ppermute(values, axis, [(i, i ^ bit) for i in range(lax.axis_size(axi...  139 us
    pallas_call x9, Pallas kernels, grad_call(): pl.pallas_call(kernel, grid_spec=pltpu.PrefetchScalarGridSpec(num_scalar_...  75.2 us
    ppermute x59, starting transfers between devices, swap(): lax.ppermute(values, axis, [(i, i ^ bit) for i in range(lax.axis_size(axi...  51 us
    unnamed x149, local copies, waits for them, and re-layouts  45.3 us
    pallas_call x8, Pallas kernels, join_weights(): pl.pallas_call(functools.partial(join_kernel, shapes, flips), in_specs=[p...  44.2 us
    pallas_call x1, Pallas kernels, codec_rear(): dense_call(codec_rear_kernel, inner // tile, [held(base.shape), held(entr...  40.4 us
    convert_element_type x20, other arithmetic, give(): given = self.total(False).astype(BF)  35.7 us
    pallas_call x1, Pallas kernels, frame_rear(): dense_call(frame_rear_kernel, inner // tile, [held(hidden.shape), held(fr...  15.5 us
  transfers between devices with their start and end apart: 63, of which 26 were waited for; matrix products, arithmetic and copies ran while one was open for 14% of the time, Pallas kernels for 36%

profile of v7, /device:TPU:0, one launch (start us, length us, event | category | flops | bytes accessed | tf_op | source)
XLA Modules:
  0.0 685.5 jit_solution(15040427463097678692)
XLA Ops:
  6.9 3.4 pack_weights.5
  10.8 2.9 collective-permute-start
  13.8 10.8 %collective-permute-done.refs_0_ = bf16[224,1024]{1,0:T(8,128)(2,1)S(1)} collective-permute-done((bf16[224,1024]{1,0:T(8,128)(2,1)S(1)}, bf16[224,1024]{1,0:T(8,128)(2,1)S(1)}, u32[]{:S(2)}, u32[]{:S(2)}) %collective-permute-start) | collective-permute-done | bytes 458784 | tf_op jit(solution)/shard_map/ppermute | solution.py:46
  24.5 12.3 %all_to_all.25 = s32[8,2,128]{2,1,0:T(2,128)S(1)} all-to-all(s32[8,2,128]{2,1,0:T(2,128)S(1)} %broadcast_in_dim.13), channel_id=1, replica_groups=mesh['seq'=8,'mp'=4] {'seq'}, dimensions={0} | all-to-all | bytes 16384 | tf_op jit(solution)/shard_map/all_to_all | solution.py:1950
  36.9 3.5 pack_weights.6
  44.9 2.5 join_weights.8
  47.5 7.2 %collective-permute-done.2.refs_2_ = bf16[224,1024]{1,0:T(8,128)(2,1)S(1)} collective-permute-done((bf16[224,1024]{1,0:T(8,128)(2,1)S(1)}, bf16[224,1024]{1,0:T(8,128)(2,1)S(1)}, u32[]{:S(2)}, u32[]{:S(2)}) %collective-permute-start.2) | collective-permute-done | bytes 458784 | tf_op jit(solution)/shard_map/ppermute | solution.py:46
  64.2 4.8 collective-permute-done.7.refs_0_
  72.9 2.6 join_weights.9
  76.9 6.4 frame_front.1
  83.3 14.4 %collective-permute-done.11.refs_0_ = bf16[576,1024]{1,0:T(8,128)(2,1)} collective-permute-done((bf16[576,1024]{1,0:T(8,128)(2,1)}, bf16[576,1024]{1,0:T(8,128)(2,1)}, u32[]{:S(2)}, u32[]{:S(2)}) %collective-permute-start.11) | collective-permute-done | bytes 1179680 | tf_op jit(solution)/shard_map/ppermute | solution.py:46
  99.2 4.3 all-to-all-start.1
  103.5 7.4 %join_weights.10 = (bf16[1024,4096]{1,0:T(8,128)(2,1)}, bf16[4096,1024]{1,0:T(8,128)(2,1)}, bf16[1024,1024]{1,0:T(8,128)(2,1)S(1)}) custom-call(s32[2]{0:T(128)S(1)} %pad_add_fusion.1.place_ref, bf16[2304,1024]{1,0:T(8,128)(2,1)} %get-tuple-element.332.refs_0_, bf16[2304,1024]{1,0:T(8,128)(2,1)} %collective-permute-done.4.refs_1_), custom_call_target="tpu_custom_call" | custom-call | flops 1 | bytes 1 | tf_op jit(solution)/shard_map/join_weights/pallas_call | solution.py:1057
  110.9 4.7 join_weights.11
  115.6 7.4 %join_weights.12 = (bf16[1024,4096]{1,0:T(8,128)(2,1)}, bf16[4096,1024]{1,0:T(8,128)(2,1)}, bf16[1024,1024]{1,0:T(8,128)(2,1)S(1)}) custom-call(s32[2]{0:T(128)S(1)} %pad_add_fusion.1.place_ref, bf16[2304,1024]{1,0:T(8,128)(2,1)} %get-tuple-element.341.refs_0_, bf16[2304,1024]{1,0:T(8,128)(2,1)} %collective-permute-done.12.refs_1_), custom_call_target="tpu_custom_call" | custom-call | flops 1 | bytes 1 | tf_op jit(solution)/shard_map/join_weights/pallas_call | solution.py:1057
  129.0 18.3 %collective-permute-done.15.refs_4_ = bf16[288,1024]{1,0:T(8,128)(2,1)S(1)} collective-permute-done((bf16[288,1024]{1,0:T(8,128)(2,1)S(1)}, bf16[288,1024]{1,0:T(8,128)(2,1)S(1)}, u32[]{:S(2)}, u32[]{:S(2)}) %collective-permute-start.15) | collective-permute-done | bytes 589856 | tf_op jit(solution)/shard_map/ppermute | solution.py:46
  151.0 4.4 far_pack.4.refs_0_
  156.5 10.0 %frame_attend.1 = bf16[8,2,128,128]{3,2,1,0:T(8,128)(2,1)S(1)} custom-call(bf16[8,2,128,384]{3,2,1,0:T(8,128)(2,1)} %all-to-all-done.1.packed_ref, s32[2,1024,1]{2,1,0:T(8,128)S(1)} %copy.71.seg_col_ref, s32[2,1,1024]{2,1,0:T(1,128)S(1)} %broadcast_in_dim.15.seg_row_ref), custom_call_target="tpu_custom_call" | custom-call | flops 1 | bytes 1 | tf_op jit(solution)/shard_map/frame_attend/pallas_call | solution.py:462
  167.4 8.3 %all-to-all-start.2 = ((bf16[8,2,128,128]{3,2,1,0:T(8,128)(2,1)}), bf16[8,2,128,128]{3,2,1,0:T(8,128)(2,1)}, u32[]{:S(2)}, u32[]{:S(2)}) async-start(bf16[8,2,128,128]{3,2,1,0:T(8,128)(2,1)} %copy-done.21), calls=%async_computation.2 | async-start | bytes 1048576 | tf_op jit(solution)/shard_map/all_to_all | solution.py:2004
  175.7 7.5 %join_weights.13 = (bf16[1024,4096]{1,0:T(8,128)(2,1)}, bf16[4096,1024]{1,0:T(8,128)(2,1)}, bf16[1024,1024]{1,0:T(8,128)(2,1)S(1)}) custom-call(s32[2]{0:T(128)S(1)} %pad_add_fusion.1.place_ref, bf16[2304,1024]{1,0:T(8,128)(2,1)} %far_pack.4.refs_0_, ...), custom_call_target="tpu_custom_call", output_to_operand_aliasing={{0}: (3, {}), {1}: (4, {}), {2}: (5, {})} | custom-call | flops 1 | bytes 1 | tf_op jit(solution)/shard_map/join_weights/pallas_call | solution.py:1057
  183.2 4.9 collective-permute-done.18.refs_2_
  188.1 5.5 all-to-all-done.2.packed_ref
  195.9 3.4 collective-permute-start.21
  199.9 15.5 %frame_rear.1 = (bf16[256,7168]{1,0:T(8,128)(2,1)}, f32[256,1024]{1,0:T(8,128)}, bf16[256,4096]{1,0:T(8,128)(2,1)}, bf16[256,1024]{1,0:T(8,128)(2,1)}) custom-call(bf16[256,1024]{1,0:T(8,128)(2,1)} %bitcast.270, bf16[256,1024]{1,0:T(8,128)(2,1)} %get-tuple-element.322.front_ref, bf16[8,2,128,128]{3,2,1,0:T(8,128)(2,1)} %all-to-all-done.2.packed_ref, ...), custom_call_target="tpu_custom_call" | custom-call | flops 1 | bytes 1 | tf_op jit(solution)/shard_map/frame_rear/pallas_call | solution.py:1196
  215.5 4.8 far_pack.5.refs_0_
  220.6 4.7 join_weights.14
  227.7 6.2 gather_fusion
  233.9 10.5 %codec_front.1 = (bf16[768,1024]{1,0:T(8,128)(2,1)}, bf16[3,256,3072]{2,1,0:T(8,128)(2,1)}) custom-call(bf16[256,1024]{1,0:T(8,128)(2,1)} %get-tuple-element.383.base_ref, bf16[2,256,1024]{2,1,0:T(8,128)(2,1)} %bitcast.265, f32[1,1024]{1,0:T(1,128)} %bitcast.290, bf16[1024,3072]{1,0:T(8,128)(2,1)} %get-tuple-element.382.weight_ref), custom_call_target="tpu_custom_call" | custom-call | flops 1 | bytes 1 | tf_op jit(solution)/shard_map/codec_front/pallas_call | solution.py:1363
  245.8 6.3 codec_attend.1
  253.8 7.4 %join_weights.15 = (bf16[1024,4096]{1,0:T(8,128)(2,1)}, bf16[4096,1024]{1,0:T(8,128)(2,1)}, bf16[1024,1024]{1,0:T(8,128)(2,1)S(1)}) custom-call(s32[2]{0:T(128)S(1)} %pad_add_fusion.1.place_ref, bf16[2304,1024]{1,0:T(8,128)(2,1)} %far_pack.5.refs_0_, ...), custom_call_target="tpu_custom_call", output_to_operand_aliasing={{0}: (3, {}), {1}: (4, {}), {2}: (5, {})} | custom-call | flops 1 | bytes 1 | tf_op jit(solution)/shard_map/join_weights/pallas_call | solution.py:1057
  262.6 40.4 %codec_rear.1 = (f32[768,1024]{1,0:T(8,128)}, bf16[768,4096]{1,0:T(8,128)(2,1)}, bf16[768,5120]{1,0:T(8,128)(2,1)}, bf16[768,1024]{1,0:T(8,128)(2,1)}, f32[768,1...) custom-call(bf16[256,1024]{1,0:T(8,128)(2,1)} %get-tuple-element.383.base_ref, ...), custom_call_target="tpu_custom_call" | custom-call | flops 1 | bytes 1 | tf_op jit(solution)/shard_map/codec_rear/pallas_call | solution.py:1440
  305.0 8.5 %codec_attend_grads.1 = bf16[3,256,3072]{2,1,0:T(8,128)(2,1)} custom-call(bf16[3,256,3072]{2,1,0:T(8,128)(2,1)} %get-tuple-element.385.packed_ref, bf16[3,256,1024]{2,1,0:T(8,128)(2,1)S(1)} %copy-done.33, bf16[1024,128]{1,0:T(8,128)(2,1)S(1)} %fusion.25.marks_ref), custom_call_target="tpu_custom_call" | custom-call | flops 1 | bytes 1 | tf_op jit(solution)/shard_map/codec_attend_grads/pallas_call | solution.py:627
  313.5 13.3 %codec_front_grads.1 = (bf16[256,1024]{1,0:T(8,128)(2,1)}, bf16[512,1024]{1,0:T(8,128)(2,1)}, f32[1,1024]{1,0:T(1,128)}) custom-call(bf16[768,3072]{1,0:T(8,128)(2,1)} %bitcast.262, bf16[256,1024]{1,0:T(8,128)(2,1)} %get-tuple-element.383.base_ref, bf16[2,256,1024]{2,1,0:T(8,128)(2,1)} %bitcast.267, f32[1,1024]{1,0:T(1,128)} %bitcast.291, ...), custom_call_target="tpu_custom_call" | custom-call | flops 1 | bytes 1 | tf_op jit(solution)/shard_map/codec_front_grads/pallas_call | solution.py:1548
  326.9 14.9 %frame_rear_grads.1 = (bf16[256,6144]{1,0:T(8,128)(2,1)}, f32[256,1024]{1,0:T(8,128)}, bf16[8,2,128,128]{3,2,1,0:T(8,128)(2,1)}, f32[1,1024]{1,0:T(1,128)}) custom-call(bf16[256,1024]{1,0:T(8,128)(2,1)} %get-tuple-element.405.grad_ref, bf16[256,4096]{1,0:T(8,128)(2,1)} %get-tuple-element.406.slope_ref, f32[256,1024]{1,0:T(8,128)} %get-tuple-element.407.mixed_ref, ...), custom_call_target="tpu_custom_call" | custom-call | flops 1 | bytes 1 | tf_op jit(solution)/shard_map/frame_rear_grads/pallas_call | solution.py:1265
  342.2 5.7 all-to-all-start.3
  347.9 11.7 %grad_columns.2 = (bf16[2,2,2,4,256,128]{5,4,3,2,1,0:T(8,128)(2,1)S(1)}, bf16[2,2,2,4,256,128]{5,4,3,2,1,0:T(8,128)(2,1)}) custom-call(s32[27]{0:T(128)S(1)} %stack.69.order_ref, bf16[768,1024]{1,0:T(8,128)(2,1)S(1)} %bitcast.259, bf16[768,1024]{1,0:T(8,128)(2,1)S(1)} %collective-permute-done.23.latter_rec, ...), custom_call_target="tpu_custom_call" | custom-call | flops 1 | bytes 1 | tf_op jit(solution)/shard_map/grad_columns/pallas_call | solution.py:731
  361.1 13.2 %grad_rows.6 = (bf16[2,2,2,4,256,128]{5,4,3,2,1,0:T(8,128)(2,1)S(1)}, bf16[2,2,2,4,256,128]{5,4,3,2,1,0:T(8,128)(2,1)S(1)}) custom-call(s32[27]{0:T(128)S(1)} %stack.69.order_ref, bf16[768,5120]{1,0:T(8,128)(2,1)} %get-tuple-element.419.far_own.own_own.latter_own, bf16[768,5120]{1,0:T(8,128)(2,1)} %collective-permute-done.27.far_rec.own_rec.latter_rec, ...), custom_call_target="tpu_custom_call" | custom-call | flops 1 | bytes 1 | tf_op jit(solution)/shard_map/grad_rows/pallas_call | solution.py:731
  381.3 14.9 %frame_attend_grads.1 = bf16[8,2,128,384]{3,2,1,0:T(8,128)(2,1)S(1)} custom-call(bf16[8,2,128,384]{3,2,1,0:T(8,128)(2,1)} %all-to-all-done.1.packed_ref, bf16[8,2,128,128]{3,2,1,0:T(8,128)(2,1)} %all-to-all-done.3.grad_ref, s32[2,1024,1]{2,1,0:T(8,128)S(1)} %copy-done.8, s32[2,1,1024]{2,1,0:T(1,128)S(1)} %broadcast_in_dim.15.seg_row_ref), custom_call_target="tpu_custom_call" | custom-call | flops 1 | bytes 1 | tf_op jit(solution)/shard_map/frame_attend_grads/pallas_call | solution.py:477
  397.3 7.4 %grad_columns.3 = (bf16[2,2,2,4,256,128]{5,4,3,2,1,0:T(8,128)(2,1)}, bf16[2,2,2,4,256,128]{5,4,3,2,1,0:T(8,128)(2,1)S(1)}) custom-call(s32[27]{0:T(128)S(1)} %stack.69.order_ref, bf16[256,6144]{1,0:T(8,128)(2,1)} %get-tuple-element.430.latter_own, bf16[256,6144]{1,0:T(8,128)(2,1)} %collective-permute-done.28.latter_rec, ...), custom_call_target="tpu_custom_call" | custom-call | flops 1 | bytes 1 | tf_op jit(solution)/shard_map/grad_columns/pallas_call | solution.py:731
  406.1 9.3 %grad_rows.7 = (bf16[2,2,2,5,256,128]{5,4,3,2,1,0:T(8,128)(2,1)}, bf16[2,2,2,5,256,128]{5,4,3,2,1,0:T(8,128)(2,1)S(1)}) custom-call(s32[27]{0:T(128)S(1)} %stack.69.order_ref, bf16[256,7168]{1,0:T(8,128)(2,1)} %get-tuple-element.388.former_own.far_own.own_own, bf16[256,7168]{1,0:T(8,128)(2,1)} %collective-permute-done.24.former_rec.far_rec.own_rec, ...), custom_call_target="tpu_custom_call" | custom-call | flops 1 | bytes 1 | tf_op jit(solution)/shard_map/grad_rows/pallas_call | solution.py:731
  415.4 3.9 grad_rows.8
  423.6 4.5 all-to-all-start.4
  428.2 2.9 fusion.3
  436.5 12.7 %grad_rows.9 = (bf16[2,2,2,4,256,128]{5,4,3,2,1,0:T(8,128)(2,1)}, bf16[2,2,2,4,256,128]{5,4,3,2,1,0:T(8,128)(2,1)S(1)}) custom-call(s32[27]{0:T(128)S(1)} %stack.69.order_ref, bf16[768,2048]{1,0:T(8,128)(2,1)} %bitcast.252, bf16[768,2048]{1,0:T(8,128)(2,1)} %copy-done.46, bf16[768,2048]{1,0:T(8,128)(2,1)} %bitcast.253, bf16[768,2048]{1,0:T(8,128)(2,1)} %copy-done.46, ...), custom_call_target="tpu_custom_call" | custom-call | flops 1 | bytes 1 | tf_op jit(solution)/shard_map/grad_rows/pallas_call | solution.py:731
  450.5 4.8 grad_rows.10
  455.3 4.4 grad_table.1
  460.7 4.5 all-to-all-done.4.packed_ref
  466.4 7.9 %frame_front_grads.1 = (bf16[256,3072]{1,0:T(8,128)(2,1)}, f32[256,1024]{1,0:T(8,128)}, f32[1,1024]{1,0:T(1,128)}) custom-call(bf16[8,2,128,384]{3,2,1,0:T(8,128)(2,1)} %copy-done.48, bf16[256,1024]{1,0:T(8,128)(2,1)} %bitcast.271, f32[1,1024]{1,0:T(1,128)} %bitcast.293, f32[256,1024]{1,0:T(8,128)} %get-tuple-element.470.mixed_grad_ref, ...), custom_call_target="tpu_custom_call" | custom-call | flops 1 | bytes 1 | tf_op jit(solution)/shard_map/frame_front_grads/pallas_call | solution.py:1319
  481.4 7.9 %grad_rows.11 = (bf16[2,2,2,3,256,128]{5,4,3,2,1,0:T(8,128)(2,1)S(1)}, bf16[2,2,2,3,256,128]{5,4,3,2,1,0:T(8,128)(2,1)S(1)}) custom-call(s32[27]{0:T(128)S(1)} %stack.69.order_ref, bf16[256,7168]{1,0:T(8,128)(2,1)} %get-tuple-element.388.former_own.far_own.own_own, bf16[256,7168]{1,0:T(8,128)(2,1)} %collective-permute-done.24.former_rec.far_rec.own_rec, ...), custom_call_target="tpu_custom_call" | custom-call | flops 1 | bytes 1 | tf_op jit(solution)/shard_map/grad_rows/pallas_call | solution.py:731
  491.7 12.2 %collective-permute-done.34 = bf16[2,2,2,5,256,128]{5,4,3,2,1,0:T(8,128)(2,1)} collective-permute-done((bf16[2,2,2,5,256,128]{5,4,3,2,1,0:T(8,128)(2,1)}, bf16[2,2,2,5,256,128]{5,4,3,2,1,0:T(8,128)(2,1)}, u32[]{:S(2)}, u32[]{:S(2)}) %collective-permute-start.34) | collective-permute-done | bytes 2621472 | tf_op jit(solution)/shard_map/ppermute | solution.py:46
  503.9 2.8 fusion.5
  506.7 2.8 fusion.1
  509.6 2.7 collective-permute-start.46
  514.5 14.1 %codec_result.1 = bf16[3,256,1024]{2,1,0:T(8,128)(2,1)} custom-call(f32[768,1024]{1,0:T(8,128)} %get-tuple-element.397.mixed_ref, bf16[768,4096]{1,0:T(8,128)(2,1)} %get-tuple-element.490.former_own.active_ref, f32[256,1]{1,0:T(8,128)} %copy.73.live_ref, bf16[4096,1024]{1,0:T(8,128)(2,1)} %get-tuple-element.393.contract_ref), custom_call_target="tpu_custom_call" | custom-call | flops 1 | bytes 1 | tf_op jit(solution)/shard_map/codec_result/pallas_call | solution.py:1497
  537.8 2.7 fusion.36
  542.3 12.3 %collective-permute-done.46 = bf16[2,2,5,256,128]{4,3,2,1,0:T(8,128)(2,1)} collective-permute-done((bf16[2,2,5,256,128]{4,3,2,1,0:T(8,128)(2,1)}, bf16[2,2,5,256,128]{4,3,2,1,0:T(8,128)(2,1)}, u32[]{:S(2)}, u32[]{:S(2)}) %collective-permute-start.46) | collective-permute-done | bytes 1310752 | tf_op jit(solution)/shard_map/ppermute | solution.py:46
  562.6 2.7 slice.451
  567.6 15.2 %collective-permute-done.44 = bf16[2,2,4,256,128]{4,3,2,1,0:T(8,128)(2,1)} collective-permute-done((bf16[2,2,4,256,128]{4,3,2,1,0:T(8,128)(2,1)}, bf16[2,2,4,256,128]{4,3,2,1,0:T(8,128)(2,1)}, u32[]{:S(2)}, u32[]{:S(2)}) %collective-permute-start.44) | collective-permute-done | bytes 1048608 | tf_op jit(solution)/shard_map/ppermute | solution.py:46
  595.4 2.9 collective-permute-done.47
  601.8 2.6 collective-permute-start.56
  621.0 3.2 collective-permute-done.50
  628.1 11.2 %collective-permute-done.57 = bf16[1600,128]{1,0:T(8,128)(2,1)S(1)} collective-permute-done((bf16[1600,128]{1,0:T(8,128)(2,1)S(1)}, bf16[1600,128]{1,0:T(8,128)(2,1)S(1)}, u32[]{:S(2)}, u32[]{:S(2)}) %collective-permute-start.57) | collective-permute-done | bytes 409632 | tf_op jit(solution)/shard_map/ppermute | solution.py:46
  656.1 10.5 %collective-permute-done.55 = bf16[8,256,128]{2,1,0:T(8,128)(2,1)} collective-permute-done((bf16[8,256,128]{2,1,0:T(8,128)(2,1)}, bf16[8,256,128]{2,1,0:T(8,128)(2,1)}, u32[]{:S(2)}, u32[]{:S(2)}) %collective-permute-start.55) | collective-permute-done | bytes 524320 | tf_op jit(solution)/shard_map/ppermute | solution.py:46
  672.3 2.8 collective-permute-done.54
  (359 shorter events, 177.6 us)
Async XLA Ops:
  6.8 30.0 %copy-start.43 = (bf16[256,1024]{1,0:T(8,128)(2,1)S(1)}, bf16[256,1024]{1,0:T(8,128)(2,1)}, u32[]{:S(2)}) copy-start(bf16[256,1024]{1,0:T(8,128)(2,1)} %refs_2_.1) | copy-start | bytes 1572868
  10.2 33.0 %collective-permute-start.4 = (bf16[2304,1024]{1,0:T(8,128)(2,1)}, bf16[2304,1024]{1,0:T(8,128)(2,1)}, u32[]{:S(2)}, u32[]{:S(2)}) collective-permute-start(bf16[2304,1024]{1,0:T(8,128)(2,1)} %get-tuple-element.332.refs_0_), channel_id=1, source_target_pairs={{0,1},{1,0},{2,3},{3,2},{4,5},{5,4},{6,7},{7,6},{8,9},{9,8},{10,11... | collective-permute-start | bytes 14155784 | tf_op jit(solution)/shard_map/ppermute | solution.py:46
  10.7 13.8 %collective-permute-start.3 = (bf16[896,1024]{1,0:T(8,128)(2,1)S(1)}, bf16[896,1024]{1,0:T(8,128)(2,1)S(1)}, u32[]{:S(2)}, u32[]{:S(2)}) collective-permute-start(bf16[896,1024]{1,0:T(8,128)(2,1)S(1)} %get-tuple-element.303.refs_0_), channel_id=1, source_target_pairs={{0,1},{1,0},{2,3},{3,2},{4,5},{5,4},{6,7},{7,6},{8,9},{9,8},{10,11... | collective-permute-start | bytes 5505032 | tf_op jit(solution)/shard_map/ppermute | solution.py:46
  10.8 13.7 %collective-permute-start = (bf16[224,1024]{1,0:T(8,128)(2,1)S(1)}, bf16[224,1024]{1,0:T(8,128)(2,1)S(1)}, u32[]{:S(2)}, u32[]{:S(2)}) collective-permute-start(bf16[224,1024]{1,0:T(8,128)(2,1)S(1)} %get-tuple-element.287), channel_id=1, source_target_pairs={{0,2},{1,3},{2,0},{3,1},{4,6},{5,7},{6,4},{7,5},{8,10},{9,11},{10,... | collective-permute-start | bytes 1376264 | tf_op jit(solution)/shard_map/ppermute | solution.py:46
  40.4 58.8 %collective-permute-start.12 = (bf16[2304,1024]{1,0:T(8,128)(2,1)}, bf16[2304,1024]{1,0:T(8,128)(2,1)}, u32[]{:S(2)}, u32[]{:S(2)}) collective-permute-start(bf16[2304,1024]{1,0:T(8,128)(2,1)} %get-tuple-element.341.refs_0_), channel_id=1, source_target_pairs={{0,1},{1,0},{2,3},{3,2},{4,5},{5,4},{6,7},{7,6},{8,9},{9,8},{10,11... | collective-permute-start | bytes 14155784 | tf_op jit(solution)/shard_map/ppermute | solution.py:46
  40.5 28.5 %collective-permute-start.7 = (bf16[576,1024]{1,0:T(8,128)(2,1)S(1)}, bf16[576,1024]{1,0:T(8,128)(2,1)}, u32[]{:S(2)}, u32[]{:S(2)}) collective-permute-start(bf16[576,1024]{1,0:T(8,128)(2,1)S(1)} %get-tuple-element.314), channel_id=1, source_target_pairs={{0,2},{1,3},{2,0},{3,1},{4,6},{5,7},{6,4},{7,5},{8,10},{9,11},{10,... | collective-permute-start | bytes 3538952 | tf_op jit(solution)/shard_map/ppermute | solution.py:46
  42.1 12.6 %collective-permute-start.2 = (bf16[224,1024]{1,0:T(8,128)(2,1)S(1)}, bf16[224,1024]{1,0:T(8,128)(2,1)S(1)}, u32[]{:S(2)}, u32[]{:S(2)}) collective-permute-start(bf16[224,1024]{1,0:T(8,128)(2,1)S(1)} %collective-permute-done.refs_0_), channel_id=1, source_target_pairs={{0,8},{4,12},{8,0},{12,4},{16,24},{20,28},{24,16},{28,20},{1,9},{5... | collective-permute-start | bytes 1376264 | tf_op jit(solution)/shard_map/ppermute | solution.py:46
  42.6 12.3 %collective-permute-start.1 = (bf16[224,1024]{1,0:T(8,128)(2,1)S(1)}, bf16[224,1024]{1,0:T(8,128)(2,1)S(1)}, u32[]{:S(2)}, u32[]{:S(2)}) collective-permute-start(bf16[224,1024]{1,0:T(8,128)(2,1)S(1)} %collective-permute-done.refs_0_), channel_id=1, source_target_pairs={{0,4},{4,0},{8,12},{12,8},{16,20},{20,16},{24,28},{28,24},{1,5},{5... | collective-permute-start | bytes 1376264 | tf_op jit(solution)/shard_map/ppermute | solution.py:46
  55.0 6.8 collective-permute-start.5
  55.6 6.4 collective-permute-start.6
  69.0 3.8 collective-permute-start.8
  69.0 28.7 %collective-permute-start.11 = (bf16[576,1024]{1,0:T(8,128)(2,1)}, bf16[576,1024]{1,0:T(8,128)(2,1)}, u32[]{:S(2)}, u32[]{:S(2)}) collective-permute-start(bf16[576,1024]{1,0:T(8,128)(2,1)} %get-tuple-element.324), channel_id=1, source_target_pairs={{0,2},{1,3},{2,0},{3,1},{4,6},{5,7},{6,4},{7,5},{8,10},{9,11},{10,... | collective-permute-start | bytes 3538952 | tf_op jit(solution)/shard_map/ppermute | solution.py:46
  70.5 28.3 %collective-permute-start.10 = (bf16[576,1024]{1,0:T(8,128)(2,1)}, bf16[576,1024]{1,0:T(8,128)(2,1)S(1)}, u32[]{:S(2)}, u32[]{:S(2)}) collective-permute-start(bf16[576,1024]{1,0:T(8,128)(2,1)} %collective-permute-done.7.refs_0_), channel_id=1, source_target_pairs={{0,8},{4,12},{8,0},{12,4},{16,24},{20,28},{24,16},{28,20},{1,9},{5... | collective-permute-start | bytes 3538952 | tf_op jit(solution)/shard_map/ppermute | solution.py:46
  71.0 28.1 %collective-permute-start.9 = (bf16[576,1024]{1,0:T(8,128)(2,1)}, bf16[576,1024]{1,0:T(8,128)(2,1)}, u32[]{:S(2)}, u32[]{:S(2)}) collective-permute-start(bf16[576,1024]{1,0:T(8,128)(2,1)} %collective-permute-done.7.refs_0_), channel_id=1, source_target_pairs={{0,4},{4,0},{8,12},{12,8},{16,20},{20,16},{24,28},{28,24},{1,5},{5... | collective-permute-start | bytes 3538952 | tf_op jit(solution)/shard_map/ppermute | solution.py:46
  72.8 30.7 %collective-permute-start.13 = (bf16[1280,1024]{1,0:T(8,128)(2,1)}, bf16[1280,1024]{1,0:T(8,128)(2,1)}, u32[]{:S(2)}, u32[]{:S(2)}) collective-permute-start(bf16[1280,1024]{1,0:T(8,128)(2,1)} %get-tuple-element.371.refs_0_), channel_id=1, source_target_pairs={{0,1},{1,0},{2,3},{3,2},{4,5},{5,4},{6,7},{7,6},{8,9},{9,8},{10,11... | collective-permute-start | bytes 7864328 | tf_op jit(solution)/shard_map/ppermute | solution.py:46
  99.2 49.7 %all-to-all-start.1 = ((bf16[8,2,128,384]{3,2,1,0:T(8,128)(2,1)}), bf16[8,2,128,384]{3,2,1,0:T(8,128)(2,1)}, u32[]{:S(2)}, u32[]{:S(2)}) async-start(bf16[8,2,128,384]{3,2,1,0:T(8,128)(2,1)} %get-tuple-element.326), calls=%async_computation.1 | async-start | bytes 3145728 | tf_op jit(solution)/shard_map/all_to_all | solution.py:1987
  125.5 21.7 %collective-permute-start.15 = (bf16[288,1024]{1,0:T(8,128)(2,1)S(1)}, bf16[288,1024]{1,0:T(8,128)(2,1)S(1)}, u32[]{:S(2)}, u32[]{:S(2)}) collective-permute-start(bf16[288,1024]{1,0:T(8,128)(2,1)S(1)} %slice.402), channel_id=1, source_target_pairs={{0,8},{4,12},{8,0},{12,4},{16,24},{20,28},{24,16},{28,20},{1,9},{5... | collective-permute-start | bytes 1769480 | tf_op jit(solution)/shard_map/ppermute | solution.py:46
  127.5 20.6 %collective-permute-start.14 = (bf16[288,1024]{1,0:T(8,128)(2,1)S(1)}, bf16[288,1024]{1,0:T(8,128)(2,1)S(1)}, u32[]{:S(2)}, u32[]{:S(2)}) collective-permute-start(bf16[288,1024]{1,0:T(8,128)(2,1)S(1)} %slice.401), channel_id=1, source_target_pairs={{0,4},{4,0},{8,12},{12,8},{16,20},{20,16},{24,28},{28,24},{1,5},{5... | collective-permute-start | bytes 1769480 | tf_op jit(solution)/shard_map/ppermute | solution.py:46
  155.4 11.9 %collective-permute-start.16 = (bf16[2304,1024]{1,0:T(8,128)(2,1)}, bf16[2304,1024]{1,0:T(8,128)(2,1)}, u32[]{:S(2)}, u32[]{:S(2)}) collective-permute-start(bf16[2304,1024]{1,0:T(8,128)(2,1)} %far_pack.4.refs_0_), channel_id=1, source_target_pairs={{0,1},{1,0},{2,3},{3,2},{4,5},{5,4},{6,7},{7,6},{8,9},{9,8},{10,11... | collective-permute-start | bytes 14155784 | tf_op jit(solution)/shard_map/ppermute | solution.py:46
  155.5 59.9 %collective-permute-start.19 = (bf16[1280,1024]{1,0:T(8,128)(2,1)}, bf16[1280,1024]{1,0:T(8,128)(2,1)}, u32[]{:S(2)}, u32[]{:S(2)}) collective-permute-start(bf16[1280,1024]{1,0:T(8,128)(2,1)} %get-tuple-element.371.refs_0_), channel_id=1, source_target_pairs={{0,2},{1,3},{2,0},{3,1},{4,6},{5,7},{6,4},{7,5},{8,10},{9,11},{10,... | collective-permute-start | bytes 7864328 | tf_op jit(solution)/shard_map/ppermute | solution.py:46
  156.1 31.9 %collective-permute-start.18 = (bf16[576,1024]{1,0:T(8,128)(2,1)}, bf16[576,1024]{1,0:T(8,128)(2,1)}, u32[]{:S(2)}, u32[]{:S(2)}) collective-permute-start(bf16[576,1024]{1,0:T(8,128)(2,1)} %collective-permute-done.11.refs_0_), channel_id=1, source_target_pairs={{0,8},{4,12},{8,0},{12,4},{16,24},{20,28},{24,16},{28,20},{1,9},{5... | collective-permute-start | bytes 3538952 | tf_op jit(solution)/shard_map/ppermute | solution.py:46
  156.1 31.9 %collective-permute-start.17 = (bf16[576,1024]{1,0:T(8,128)(2,1)}, bf16[576,1024]{1,0:T(8,128)(2,1)}, u32[]{:S(2)}, u32[]{:S(2)}) collective-permute-start(bf16[576,1024]{1,0:T(8,128)(2,1)} %collective-permute-done.11.refs_0_), channel_id=1, source_target_pairs={{0,4},{4,0},{8,12},{12,8},{16,20},{20,16},{24,28},{28,24},{1,5},{5... | collective-permute-start | bytes 3538952 | tf_op jit(solution)/shard_map/ppermute | solution.py:46
  167.4 26.2 %all-to-all-start.2 = ((bf16[8,2,128,128]{3,2,1,0:T(8,128)(2,1)}), bf16[8,2,128,128]{3,2,1,0:T(8,128)(2,1)}, u32[]{:S(2)}, u32[]{:S(2)}) async-start(bf16[8,2,128,128]{3,2,1,0:T(8,128)(2,1)} %copy-done.21), calls=%async_computation.2 | async-start | bytes 1048576 | tf_op jit(solution)/shard_map/all_to_all | solution.py:2004
  195.8 19.7 %collective-permute-start.20 = (bf16[288,1024]{1,0:T(8,128)(2,1)S(1)}, bf16[288,1024]{1,0:T(8,128)(2,1)S(1)}, u32[]{:S(2)}, u32[]{:S(2)}) collective-permute-start(bf16[288,1024]{1,0:T(8,128)(2,1)S(1)} %slice.404), channel_id=1, source_target_pairs={{0,4},{4,0},{8,12},{12,8},{16,20},{20,16},{24,28},{28,24},{1,5},{5... | collective-permute-start | bytes 1769480 | tf_op jit(solution)/shard_map/ppermute | solution.py:46
  195.9 19.6 %collective-permute-start.21 = (bf16[288,1024]{1,0:T(8,128)(2,1)S(1)}, bf16[288,1024]{1,0:T(8,128)(2,1)S(1)}, u32[]{:S(2)}, u32[]{:S(2)}) collective-permute-start(bf16[288,1024]{1,0:T(8,128)(2,1)S(1)} %slice.405), channel_id=1, source_target_pairs={{0,8},{4,12},{8,0},{12,4},{16,24},{20,28},{24,16},{28,20},{1,9},{5... | collective-permute-start | bytes 1769480 | tf_op jit(solution)/shard_map/ppermute | solution.py:46
  215.5 5.2 collective-permute-start.22
  225.4 28.4 %collective-permute-start.25 = (bf16[2304,1024]{1,0:T(8,128)(2,1)}, bf16[2304,1024]{1,0:T(8,128)(2,1)}, u32[]{:S(2)}, u32[]{:S(2)}) collective-permute-start(bf16[2304,1024]{1,0:T(8,128)(2,1)} %far_pack.5.refs_0_), channel_id=1, source_target_pairs={{0,1},{1,0},{2,3},{3,2},{4,5},{5,4},{6,7},{7,6},{8,9},{9,8},{10,11... | collective-permute-start | bytes 14155784 | tf_op jit(solution)/shard_map/ppermute | solution.py:46
  225.7 36.9 %collective-permute-start.24 = (bf16[256,7168]{1,0:T(8,128)(2,1)}, bf16[256,7168]{1,0:T(8,128)(2,1)}, u32[]{:S(2)}, u32[]{:S(2)}) collective-permute-start(bf16[256,7168]{1,0:T(8,128)(2,1)} %get-tuple-element.388.former_own.far_own.own_own), channel_id=1, source_target_pairs={{0,1},{1,0},{2,3},{3,2},{4,5},{5,4},{6,7},{7,6},{8,9},{9,8},{10,11... | collective-permute-start | bytes 11010056 | tf_op jit(solution)/shard_map/ppermute | solution.py:46
  225.9 18.5 %collective-permute-start.23 = (bf16[768,1024]{1,0:T(8,128)(2,1)S(1)}, bf16[768,1024]{1,0:T(8,128)(2,1)S(1)}, u32[]{:S(2)}, u32[]{:S(2)}) collective-permute-start(bf16[768,1024]{1,0:T(8,128)(2,1)S(1)} %bitcast.258), channel_id=1, source_target_pairs={{0,1},{1,0},{2,3},{3,2},{4,5},{5,4},{6,7},{7,6},{8,9},{9,8},{10,11... | collective-permute-start | bytes 4718600 | tf_op jit(solution)/shard_map/ppermute | solution.py:46
  303.0 38.8 %collective-permute-start.27 = (bf16[768,5120]{1,0:T(8,128)(2,1)}, bf16[768,5120]{1,0:T(8,128)(2,1)}, u32[]{:S(2)}, u32[]{:S(2)}) collective-permute-start(bf16[768,5120]{1,0:T(8,128)(2,1)} %get-tuple-element.419.far_own.own_own.latter_own), channel_id=1, source_target_pairs={{0,1},{1,0},{2,3},{3,2},{4,5},{5,4},{6,7},{7,6},{8,9},{9,8},{10,11... | collective-permute-start | bytes 23592968 | tf_op jit(solution)/shard_map/ppermute | solution.py:46
  303.4 38.4 %collective-permute-start.26 = (bf16[768,4096]{1,0:T(8,128)(2,1)}, bf16[768,4096]{1,0:T(8,128)(2,1)}, u32[]{:S(2)}, u32[]{:S(2)}) collective-permute-start(bf16[768,4096]{1,0:T(8,128)(2,1)} %get-tuple-element.490.former_own.active_ref), channel_id=1, source_target_pairs={{0,1},{1,0},{2,3},{3,2},{4,5},{5,4},{6,7},{7,6},{8,9},{9,8},{10,11... | collective-permute-start | bytes 18874376 | tf_op jit(solution)/shard_map/ppermute | solution.py:46
  341.8 35.1 %collective-permute-start.28 = (bf16[256,6144]{1,0:T(8,128)(2,1)}, bf16[256,6144]{1,0:T(8,128)(2,1)}, u32[]{:S(2)}, u32[]{:S(2)}) collective-permute-start(bf16[256,6144]{1,0:T(8,128)(2,1)} %get-tuple-element.430.latter_own), channel_id=1, source_target_pairs={{0,1},{1,0},{2,3},{3,2},{4,5},{5,4},{6,7},{7,6},{8,9},{9,8},{10,11... | collective-permute-start | bytes 9437192 | tf_op jit(solution)/shard_map/ppermute | solution.py:46
  342.2 34.8 %all-to-all-start.3 = ((bf16[8,2,128,128]{3,2,1,0:T(8,128)(2,1)}), bf16[8,2,128,128]{3,2,1,0:T(8,128)(2,1)}, u32[]{:S(2)}, u32[]{:S(2)}) async-start(bf16[8,2,128,128]{3,2,1,0:T(8,128)(2,1)} %get-tuple-element.411), calls=%async_computation.3 | async-start | bytes 1048576 | tf_op jit(solution)/shard_map/all_to_all | solution.py:2085
  376.9 46.7 %collective-permute-start.31 = (bf16[768,3072]{1,0:T(8,128)(2,1)}, bf16[768,3072]{1,0:T(8,128)(2,1)}, u32[]{:S(2)}, u32[]{:S(2)}) collective-permute-start(bf16[768,3072]{1,0:T(8,128)(2,1)} %bitcast.263), channel_id=1, source_target_pairs={{0,1},{1,0},{2,3},{3,2},{4,5},{5,4},{6,7},{7,6},{8,9},{9,8},{10,11... | collective-permute-start | bytes 14155784 | tf_op jit(solution)/shard_map/ppermute | solution.py:46
  376.9 44.9 %collective-permute-start.30 = (bf16[768,2048]{1,0:T(8,128)(2,1)S(1)}, bf16[768,2048]{1,0:T(8,128)(2,1)S(1)}, u32[]{:S(2)}, u32[]{:S(2)}) collective-permute-start(bf16[768,2048]{1,0:T(8,128)(2,1)S(1)} %bitcast.256), channel_id=1, source_target_pairs={{0,1},{1,0},{2,3},{3,2},{4,5},{5,4},{6,7},{7,6},{8,9},{9,8},{10,11... | collective-permute-start | bytes 9437192 | tf_op jit(solution)/shard_map/ppermute | solution.py:46
  377.4 43.3 %collective-permute-start.32 = (bf16[768,1024]{1,0:T(8,128)(2,1)}, bf16[768,1024]{1,0:T(8,128)(2,1)S(1)}, u32[]{:S(2)}, u32[]{:S(2)}) collective-permute-start(bf16[768,1024]{1,0:T(8,128)(2,1)} %get-tuple-element.441.latter_own), channel_id=1, source_target_pairs={{0,1},{1,0},{2,3},{3,2},{4,5},{5,4},{6,7},{7,6},{8,9},{9,8},{10,11... | collective-permute-start | bytes 4718600 | tf_op jit(solution)/shard_map/ppermute | solution.py:46
  377.5 50.6 %collective-permute-start.29 = (bf16[2,2,2,4,256,128]{5,4,3,2,1,0:T(8,128)(2,1)}, bf16[2,2,2,4,256,128]{5,4,3,2,1,0:T(8,128)(2,1)}, u32[]{:S(2)}, u32[]{:S(2)}) collective-permute-start(bf16[2,2,2,4,256,128]{5,4,3,2,1,0:T(8,128)(2,1)} %copy-done.44), channel_id=1, source_target_pairs={{0,2},{1,3},{2,0},{3,1},{4,6},{5,7},{6,4},{7,5},{8,10},{9,11},{10,... | collective-permute-start | bytes 6291464 | tf_op jit(solution)/shard_map/ppermute | solution.py:46
  378.0 50.1 %collective-permute-start.33 = (bf16[2,2,2,4,256,128]{5,4,3,2,1,0:T(8,128)(2,1)}, bf16[2,2,2,4,256,128]{5,4,3,2,1,0:T(8,128)(2,1)}, u32[]{:S(2)}, u32[]{:S(2)}) collective-permute-start(bf16[2,2,2,4,256,128]{5,4,3,2,1,0:T(8,128)(2,1)} %copy-done.45), channel_id=1, source_target_pairs={{0,4},{4,0},{8,12},{12,8},{16,20},{20,16},{24,28},{28,24},{1,5},{5... | collective-permute-start | bytes 6291464 | tf_op jit(solution)/shard_map/ppermute | solution.py:46
  423.6 41.6 %all-to-all-start.4 = ((bf16[8,2,128,384]{3,2,1,0:T(8,128)(2,1)}), bf16[8,2,128,384]{3,2,1,0:T(8,128)(2,1)S(1)}, u32[]{:S(2)}, u32[]{:S(2)}) async-start(bf16[8,2,128,384]{3,2,1,0:T(8,128)(2,1)} %copy-done.14), calls=%async_computation.4 | async-start | bytes 3145728 | tf_op jit(solution)/shard_map/all_to_all | solution.py:2133
  432.6 22.7 %collective-permute-start.36 = (bf16[512,1024]{1,0:T(8,128)(2,1)S(1)}, bf16[512,1024]{1,0:T(8,128)(2,1)S(1)}, u32[]{:S(2)}, u32[]{:S(2)}) collective-permute-start(bf16[512,1024]{1,0:T(8,128)(2,1)S(1)} %copy-done.36), channel_id=1, source_target_pairs={{0,1},{1,0},{2,3},{3,2},{4,5},{5,4},{6,7},{7,6},{8,9},{9,8},{10,11... | collective-permute-start | bytes 3145736 | tf_op jit(solution)/shard_map/ppermute | solution.py:46
  432.6 71.3 %collective-permute-start.34 = (bf16[2,2,2,5,256,128]{5,4,3,2,1,0:T(8,128)(2,1)}, bf16[2,2,2,5,256,128]{5,4,3,2,1,0:T(8,128)(2,1)}, u32[]{:S(2)}, u32[]{:S(2)}) collective-permute-start(bf16[2,2,2,5,256,128]{5,4,3,2,1,0:T(8,128)(2,1)} %get-tuple-element.452), channel_id=1, source_target_pairs={{0,4},{4,0},{8,12},{12,8},{16,20},{20,16},{24,28},{28,24},{1,5},{5... | collective-permute-start | bytes 7864328 | tf_op jit(solution)/shard_map/ppermute | solution.py:46
  434.7 1.8 collective-permute-start.35
  435.0 68.9 %collective-permute-start.39 = (bf16[2,2,2,4,256,128]{5,4,3,2,1,0:T(8,128)(2,1)}, bf16[2,2,2,4,256,128]{5,4,3,2,1,0:T(8,128)(2,1)}, u32[]{:S(2)}, u32[]{:S(2)}) collective-permute-start(bf16[2,2,2,4,256,128]{5,4,3,2,1,0:T(8,128)(2,1)} %get-tuple-element.485), channel_id=1, source_target_pairs={{0,2},{1,3},{2,0},{3,1},{4,6},{5,7},{6,4},{7,5},{8,10},{9,11},{10,... | collective-permute-start | bytes 6291464 | tf_op jit(solution)/shard_map/ppermute | solution.py:46
  474.2 3.6 collective-permute-start.37
  474.2 54.4 %collective-permute-start.42 = (bf16[2,2,2,4,256,128]{5,4,3,2,1,0:T(8,128)(2,1)}, bf16[2,2,2,4,256,128]{5,4,3,2,1,0:T(8,128)(2,1)}, u32[]{:S(2)}, u32[]{:S(2)}) collective-permute-start(bf16[2,2,2,4,256,128]{5,4,3,2,1,0:T(8,128)(2,1)} %get-tuple-element.494), channel_id=1, source_target_pairs={{0,2},{1,3},{2,0},{3,1},{4,6},{5,7},{6,4},{7,5},{8,10},{9,11},{10,... | collective-permute-start | bytes 6291464 | tf_op jit(solution)/shard_map/ppermute | solution.py:46
  476.5 1.2 collective-permute-start.38
  477.8 55.3 %collective-permute-start.41 = (bf16[2,2,8,256,128]{4,3,2,1,0:T(8,128)(2,1)}, bf16[2,2,8,256,128]{4,3,2,1,0:T(8,128)(2,1)}, u32[]{:S(2)}, u32[]{:S(2)}) collective-permute-start(bf16[2,2,8,256,128]{4,3,2,1,0:T(8,128)(2,1)} %pad_maximum_fusion), channel_id=1, source_target_pairs={{0,8},{4,12},{8,0},{12,4},{16,24},{20,28},{24,16},{28,20},{1,9},{5... | collective-permute-start | bytes 6291464 | tf_op jit(solution)/shard_map/ppermute | solution.py:46
  477.9 55.2 %collective-permute-start.40 = (bf16[2,2,2,2,256,128]{5,4,3,2,1,0:T(8,128)(2,1)}, bf16[2,2,2,2,256,128]{5,4,3,2,1,0:T(8,128)(2,1)}, u32[]{:S(2)}, u32[]{:S(2)}) collective-permute-start(bf16[2,2,2,2,256,128]{5,4,3,2,1,0:T(8,128)(2,1)} %get-tuple-element.492), channel_id=1, source_target_pairs={{0,4},{4,0},{8,12},{12,8},{16,20},{20,16},{24,28},{28,24},{1,5},{5... | collective-permute-start | bytes 3145736 | tf_op jit(solution)/shard_map/ppermute | solution.py:46
  509.6 45.1 %collective-permute-start.46 = (bf16[2,2,5,256,128]{4,3,2,1,0:T(8,128)(2,1)}, bf16[2,2,5,256,128]{4,3,2,1,0:T(8,128)(2,1)}, u32[]{:S(2)}, u32[]{:S(2)}) collective-permute-start(bf16[2,2,5,256,128]{4,3,2,1,0:T(8,128)(2,1)} %fusion.1), channel_id=1, source_target_pairs={{0,8},{4,12},{8,0},{12,4},{16,24},{20,28},{24,16},{28,20},{1,9},{5... | collective-permute-start | bytes 3932168 | tf_op jit(solution)/shard_map/ppermute | solution.py:46
  513.5 46.9 %collective-permute-start.45 = (bf16[6208,128]{1,0:T(8,128)(2,1)}, bf16[6208,128]{1,0:T(8,128)(2,1)}, u32[]{:S(2)}, u32[]{:S(2)}) collective-permute-start(bf16[6208,128]{1,0:T(8,128)(2,1)} %pad_maximum_fusion.1), channel_id=1, source_target_pairs={{0,4},{4,0},{8,12},{12,8},{16,20},{20,16},{24,28},{28,24},{1,5},{5... | collective-permute-start | bytes 4767752 | tf_op jit(solution)/shard_map/ppermute | solution.py:46
  528.6 54.2 %collective-permute-start.44 = (bf16[2,2,4,256,128]{4,3,2,1,0:T(8,128)(2,1)}, bf16[2,2,4,256,128]{4,3,2,1,0:T(8,128)(2,1)}, u32[]{:S(2)}, u32[]{:S(2)}) collective-permute-start(bf16[2,2,4,256,128]{4,3,2,1,0:T(8,128)(2,1)} %fusion.5), channel_id=1, source_target_pairs={{0,4},{4,0},{8,12},{12,8},{16,20},{20,16},{24,28},{28,24},{1,5},{5... | collective-permute-start | bytes 3145736 | tf_op jit(solution)/shard_map/ppermute | solution.py:46
  533.1 52.7 %collective-permute-start.49 = (bf16[2,2,4,256,128]{4,3,2,1,0:T(8,128)(2,1)}, bf16[2,2,4,256,128]{4,3,2,1,0:T(8,128)(2,1)}, u32[]{:S(2)}, u32[]{:S(2)}) collective-permute-start(bf16[2,2,4,256,128]{4,3,2,1,0:T(8,128)(2,1)} %fusion.6), channel_id=1, source_target_pairs={{0,8},{4,12},{8,0},{12,4},{16,24},{20,28},{24,16},{28,20},{1,9},{5... | collective-permute-start | bytes 3145736 | tf_op jit(solution)/shard_map/ppermute | solution.py:46
  535.1 69.3 %collective-permute-start.43 = (bf16[2,2,2,256,128]{4,3,2,1,0:T(8,128)(2,1)}, bf16[2,2,2,256,128]{4,3,2,1,0:T(8,128)(2,1)}, u32[]{:S(2)}, u32[]{:S(2)}) collective-permute-start(bf16[2,2,2,256,128]{4,3,2,1,0:T(8,128)(2,1)} %fusion.14), channel_id=1, source_target_pairs={{0,2},{1,3},{2,0},{3,1},{4,6},{5,7},{6,4},{7,5},{8,10},{9,11},{10,... | collective-permute-start | bytes 1572872 | tf_op jit(solution)/shard_map/ppermute | solution.py:46
  557.4 33.5 %collective-permute-start.48 = (bf16[2,9,256,128]{3,2,1,0:T(8,128)(2,1)}, bf16[2,9,256,128]{3,2,1,0:T(8,128)(2,1)}, u32[]{:S(2)}, u32[]{:S(2)}) collective-permute-start(bf16[2,9,256,128]{3,2,1,0:T(8,128)(2,1)} %pad_maximum_fusion.2), channel_id=1, source_target_pairs={{0,2},{1,3},{2,0},{3,1},{4,6},{5,7},{6,4},{7,5},{8,10},{9,11},{10,... | collective-permute-start | bytes 3538952 | tf_op jit(solution)/shard_map/ppermute | solution.py:46
  566.0 42.0 %collective-permute-start.52 = (bf16[3136,128]{1,0:T(8,128)(2,1)S(1)}, bf16[3136,128]{1,0:T(8,128)(2,1)S(1)}, u32[]{:S(2)}, u32[]{:S(2)}) collective-permute-start(bf16[3136,128]{1,0:T(8,128)(2,1)S(1)} %pad_maximum_fusion.3), channel_id=1, source_target_pairs={{0,2},{1,3},{2,0},{3,1},{4,6},{5,7},{6,4},{7,5},{8,10},{9,11},{10,... | collective-permute-start | bytes 2408456 | tf_op jit(solution)/shard_map/ppermute | solution.py:46
  584.4 13.9 %collective-permute-start.47 = (bf16[2,4,256,128]{3,2,1,0:T(8,128)(2,1)S(1)}, bf16[2,4,256,128]{3,2,1,0:T(8,128)(2,1)S(1)}, u32[]{:S(2)}, u32[]{:S(2)}) collective-permute-start(bf16[2,4,256,128]{3,2,1,0:T(8,128)(2,1)S(1)} %fusion.9), channel_id=1, source_target_pairs={{0,8},{4,12},{8,0},{12,4},{16,24},{20,28},{24,16},{28,20},{1,9},{5... | collective-permute-start | bytes 1572872 | tf_op jit(solution)/shard_map/ppermute | solution.py:46
  588.1 31.5 %collective-permute-start.53 = (bf16[2,4,256,128]{3,2,1,0:T(8,128)(2,1)}, bf16[2,4,256,128]{3,2,1,0:T(8,128)(2,1)}, u32[]{:S(2)}, u32[]{:S(2)}) collective-permute-start(bf16[2,4,256,128]{3,2,1,0:T(8,128)(2,1)} %fusion.8), channel_id=1, source_target_pairs={{0,4},{4,0},{8,12},{12,8},{16,20},{20,16},{24,28},{28,24},{1,5},{5... | collective-permute-start | bytes 1572872 | tf_op jit(solution)/shard_map/ppermute | solution.py:46
  590.9 24.5 %collective-permute-start.51 = (bf16[2,4,256,128]{3,2,1,0:T(8,128)(2,1)}, bf16[2,4,256,128]{3,2,1,0:T(8,128)(2,1)}, u32[]{:S(2)}, u32[]{:S(2)}) collective-permute-start(bf16[2,4,256,128]{3,2,1,0:T(8,128)(2,1)} %fusion.7), channel_id=1, source_target_pairs={{0,4},{4,0},{8,12},{12,8},{16,20},{20,16},{24,28},{28,24},{1,5},{5... | collective-permute-start | bytes 1572872 | tf_op jit(solution)/shard_map/ppermute | solution.py:46
  601.8 46.6 %collective-permute-start.56 = (bf16[9,256,128]{2,1,0:T(8,128)(2,1)}, bf16[9,256,128]{2,1,0:T(8,128)(2,1)}, u32[]{:S(2)}, u32[]{:S(2)}) collective-permute-start(bf16[9,256,128]{2,1,0:T(8,128)(2,1)} %pad_maximum_fusion.4), channel_id=1, source_target_pairs={{0,16},{4,20},{8,24},{12,28},{16,0},{20,4},{24,8},{28,12},{1,17},{... | collective-permute-start | bytes 1769480 | tf_op jit(solution)/shard_map/ppermute | solution.py:46
  606.3 17.8 %collective-permute-start.50 = (bf16[2,2,256,128]{3,2,1,0:T(8,128)(2,1)}, bf16[2,2,256,128]{3,2,1,0:T(8,128)(2,1)S(1)}, u32[]{:S(2)}, u32[]{:S(2)}) collective-permute-start(bf16[2,2,256,128]{3,2,1,0:T(8,128)(2,1)} %fusion.23), channel_id=1, source_target_pairs={{0,8},{4,12},{8,0},{12,4},{16,24},{20,28},{24,16},{28,20},{1,9},{5... | collective-permute-start | bytes 786440 | tf_op jit(solution)/shard_map/ppermute | solution.py:46
  615.1 24.2 %collective-permute-start.57 = (bf16[1600,128]{1,0:T(8,128)(2,1)S(1)}, bf16[1600,128]{1,0:T(8,128)(2,1)S(1)}, u32[]{:S(2)}, u32[]{:S(2)}) collective-permute-start(bf16[1600,128]{1,0:T(8,128)(2,1)S(1)} %pad_maximum_fusion.6), channel_id=1, source_target_pairs={{0,8},{4,12},{8,0},{12,4},{16,24},{20,28},{24,16},{28,20},{1,9},{5... | collective-permute-start | bytes 1228808 | tf_op jit(solution)/shard_map/ppermute | solution.py:46
  618.9 47.8 %collective-permute-start.55 = (bf16[8,256,128]{2,1,0:T(8,128)(2,1)}, bf16[8,256,128]{2,1,0:T(8,128)(2,1)}, u32[]{:S(2)}, u32[]{:S(2)}) collective-permute-start(bf16[8,256,128]{2,1,0:T(8,128)(2,1)} %pad_maximum_fusion.5), channel_id=1, source_target_pairs={{0,16},{4,20},{8,24},{12,28},{16,0},{20,4},{24,8},{28,12},{1,17},{... | collective-permute-start | bytes 1572872 | tf_op jit(solution)/shard_map/ppermute | solution.py:46
  626.0 49.1 %collective-permute-start.54 = (bf16[6,256,128]{2,1,0:T(8,128)(2,1)}, bf16[6,256,128]{2,1,0:T(8,128)(2,1)}, u32[]{:S(2)}, u32[]{:S(2)}) collective-permute-start(bf16[6,256,128]{2,1,0:T(8,128)(2,1)} %pad_maximum_fusion.7), channel_id=1, source_target_pairs={{0,16},{4,20},{8,24},{12,28},{16,0},{20,4},{24,8},{28,12},{1,17},{... | collective-permute-start | bytes 1179656 | tf_op jit(solution)/shard_map/ppermute | solution.py:46
  648.5 30.2 %collective-permute-start.58 = (bf16[832,128]{1,0:T(8,128)(2,1)}, bf16[832,128]{1,0:T(8,128)(2,1)}, u32[]{:S(2)}, u32[]{:S(2)}) collective-permute-start(bf16[832,128]{1,0:T(8,128)(2,1)} %pad_maximum_fusion.8), channel_id=1, source_target_pairs={{0,16},{4,20},{8,24},{12,28},{16,0},{20,4},{24,8},{28,12},{1,17},{... | collective-permute-start | bytes 638984 | tf_op jit(solution)/shard_map/ppermute | solution.py:46
  (68 other events, 447.2 us)

commit v8 on v7

--- a/solution.py
+++ b/solution.py
@@ -1762,7 +1762,9 @@
 
     def start(self, chain):
         self.came = swap(chain.enter(self.pack if self.whole else self.quarter), "mp", 2)
-        self.near = chain.pair(self.pack)
+
+    def send_near(self, chain):
+        self.near = Pair(chain.enter(self.pack))
 
     def spread(self, chain):
         self.came = chain.enter(self.came)
@@ -1938,6 +1940,7 @@
     first = Gather([frame_project, gain_rows], spots)
     chain.leave(first.quarter)
     first.start(chain)
+    first.send_near(chain)
     members = chain.enter(frame_expand, frame_contract, frame_output)
     second = Gather(members, spots)
     chain.leave(second.quarter)
@@ -1945,8 +1948,6 @@
         jnp.arange(positions - 1, dtype=jnp.int32) * CODES, frame_total
     )
     live = padding.reshape(frame_total).astype(F32)[:, None]
-    first.spread(chain)
-    second.start(chain)
     every_segment = lax.all_to_all(
         jnp.broadcast_to(chain.enter(segments)[None], (count, row_count, frames_dev)),
         "seq",
@@ -1957,8 +1958,8 @@
     every_segment = jnp.transpose(every_segment, (1, 0, 2)).reshape(row_count, count * frames_dev)
     every_segment = chain.enter(every_segment)
     chain.leave(every_segment)
-    fourth = Gather(chain.enter(codec_expand, codec_contract, codec_output), spots)
-    chain.leave(fourth.quarter)
+    first.spread(chain)
+    second.start(chain)
     contract_in = (
         jnp.transpose(chain.enter(cotangent).reshape(frame_total, positions, width), (1, 0, 2))
         * live.astype(BF)[None]
@@ -1966,6 +1967,8 @@
     chain.leave(contract_in)
     first.join_near(chain)
     first.cross(chain)
+    fourth = Gather(chain.enter(codec_expand, codec_contract, codec_output), spots)
+    chain.leave(fourth.quarter)
     third = Gather(chain.enter(codec_project, codebooks), spots, True)
     chain.leave(third.pack)
     first.close(chain)
@@ -1985,6 +1988,9 @@
     )
     chain.leave(packed)
     packed = lax.all_to_all(packed, "seq", split_axis=0, concat_axis=0, tiled=True)
+    second.send_near(chain)
+    third.send_near(chain)
+    fourth.send_near(chain)
     second.join_near(chain)
     third.join_near(chain)
     fourth.join_near(chain)

time: 696 us -> 681 us (0.978)
  starting transfers between devices: 73.9 us -> 61.5 us
    ppermute x59, starting transfers between devices: 51 us -> 42.8 us  [swap(): lax.ppermute(values, axis, [(i, i ^ bit) for i in range(lax.axis_size(axi...]
    unnamed x149 -> x141, local copies, waits for them, and re-layouts: 45.3 us -> 41.6 us
  transfers between devices with their start and end apart: 63 -> 63, of which waited for: 26 -> 29; matrix products, arithmetic and copies ran while one was open for 14% -> 15% of each run, Pallas kernels for 36% -> 38%
where the time goes in v8:
time: 681 us; the launch traced here: 671 us
  Pallas kernels  304 us (45%)
  waiting for transfers between devices  149 us (22%)
  local copies, waits for them, and re-layouts  77.8 us (11%)
  other arithmetic  64 us (9%)
  starting transfers between devices  61.5 us (9%)
  blocking collectives  12.1 us (2%)
    ppermute x59, waiting for transfers between devices, swap(): lax.ppermute(values, axis, [(i, i ^ bit) for i in range(lax.axis_size(axi...  136 us
    pallas_call x9, Pallas kernels, grad_call(): pl.pallas_call(kernel, grid_spec=pltpu.PrefetchScalarGridSpec(num_scalar_...  75.1 us
    pallas_call x8, Pallas kernels, join_weights(): pl.pallas_call(functools.partial(join_kernel, shapes, flips), in_specs=[p...  44.3 us
    ppermute x59, starting transfers between devices, swap(): lax.ppermute(values, axis, [(i, i ^ bit) for i in range(lax.axis_size(axi...  42.8 us
    unnamed x141, local copies, waits for them, and re-layouts  41.6 us
    pallas_call x1, Pallas kernels, codec_rear(): dense_call(codec_rear_kernel, inner // tile, [held(base.shape), held(entr...  40.4 us
    convert_element_type x20, other arithmetic, give(): given = self.total(False).astype(BF)  35.7 us
    pallas_call x1, Pallas kernels, frame_rear(): dense_call(frame_rear_kernel, inner // tile, [held(hidden.shape), held(fr...  15.5 us
  transfers between devices with their start and end apart: 63, of which 29 were waited for; matrix products, arithmetic and copies ran while one was open for 15% of the time, Pallas kernels for 38%

profile of v8, /device:TPU:0, one launch (start us, length us, event | category | flops | bytes accessed | tf_op | source)
XLA Modules:
  0.0 670.9 jit_solution(9926555969572382528)
XLA Ops:
  4.7 2.6 collective-permute-start
  9.9 3.5 pack_weights.5
  13.5 12.1 %all_to_all.25 = s32[8,2,128]{2,1,0:T(2,128)S(1)} all-to-all(s32[8,2,128]{2,1,0:T(2,128)S(1)} %broadcast_in_dim.13), channel_id=1, replica_groups=mesh['seq'=8,'mp'=4] {'seq'}, dimensions={0} | all-to-all | bytes 16384 | tf_op jit(solution)/shard_map/all_to_all | solution.py:1951
  31.5 5.5 collective-permute-done.2.refs_2_
  39.4 3.5 pack_weights.6
  47.6 4.9 collective-permute-done.6.refs_0_
  56.3 2.6 join_weights.9
  60.4 6.4 frame_front.1
  66.8 14.5 %collective-permute-done.10.refs_0_ = bf16[576,1024]{1,0:T(8,128)(2,1)} collective-permute-done((bf16[576,1024]{1,0:T(8,128)(2,1)}, bf16[576,1024]{1,0:T(8,128)(2,1)}, u32[]{:S(2)}, u32[]{:S(2)}) %collective-permute-start.10) | collective-permute-done | bytes 1179680 | tf_op jit(solution)/shard_map/ppermute | solution.py:46
  82.2 4.3 all-to-all-start.1
  86.5 3.4 collective-permute-done.13.refs_1_
  90.0 7.4 %join_weights.10 = (bf16[1024,4096]{1,0:T(8,128)(2,1)}, bf16[4096,1024]{1,0:T(8,128)(2,1)}, bf16[1024,1024]{1,0:T(8,128)(2,1)S(1)}) custom-call(s32[2]{0:T(128)S(1)} %pad_add_fusion.1.place_ref, bf16[2304,1024]{1,0:T(8,128)(2,1)} %get-tuple-element.331.refs_0_, bf16[2304,1024]{1,0:T(8,128)(2,1)} %collective-permute-done.13.refs_1_), custom_call_target="tpu_custom_call" | custom-call | flops 1 | bytes 1 | tf_op jit(solution)/shard_map/join_weights/pallas_call | solution.py:1057
  97.4 3.1 collective-permute-done.12.refs_1_
  100.5 4.7 join_weights.11
  105.2 7.4 %join_weights.12 = (bf16[1024,4096]{1,0:T(8,128)(2,1)}, bf16[4096,1024]{1,0:T(8,128)(2,1)}, bf16[1024,1024]{1,0:T(8,128)(2,1)S(1)}) custom-call(s32[2]{0:T(128)S(1)} %pad_add_fusion.1.place_ref, bf16[2304,1024]{1,0:T(8,128)(2,1)} %get-tuple-element.340.refs_0_, bf16[2304,1024]{1,0:T(8,128)(2,1)} %collective-permute-done.11.refs_1_), custom_call_target="tpu_custom_call" | custom-call | flops 1 | bytes 1 | tf_op jit(solution)/shard_map/join_weights/pallas_call | solution.py:1057
  118.8 5.8 all-to-all-done.1.packed_ref
  124.6 12.5 %collective-permute-done.15.refs_4_ = bf16[288,1024]{1,0:T(8,128)(2,1)} collective-permute-done((bf16[288,1024]{1,0:T(8,128)(2,1)}, bf16[288,1024]{1,0:T(8,128)(2,1)}, u32[]{:S(2)}, u32[]{:S(2)}) %collective-permute-start.15) | collective-permute-done | bytes 589856 | tf_op jit(solution)/shard_map/ppermute | solution.py:46
  137.1 4.8 far_pack.4.refs_0_
  144.2 10.0 %frame_attend.1 = bf16[8,2,128,128]{3,2,1,0:T(8,128)(2,1)S(1)} custom-call(bf16[8,2,128,384]{3,2,1,0:T(8,128)(2,1)} %all-to-all-done.1.packed_ref, s32[2,1024,1]{2,1,0:T(8,128)S(1)} %copy.71.seg_col_ref, s32[2,1,1024]{2,1,0:T(1,128)S(1)} %broadcast_in_dim.15.seg_row_ref), custom_call_target="tpu_custom_call" | custom-call | flops 1 | bytes 1 | tf_op jit(solution)/shard_map/frame_attend/pallas_call | solution.py:462
  155.1 5.6 all-to-all-start.2
  160.7 7.5 %join_weights.13 = (bf16[1024,4096]{1,0:T(8,128)(2,1)}, bf16[4096,1024]{1,0:T(8,128)(2,1)}, bf16[1024,1024]{1,0:T(8,128)(2,1)S(1)}) custom-call(s32[2]{0:T(128)S(1)} %pad_add_fusion.1.place_ref, bf16[2304,1024]{1,0:T(8,128)(2,1)} %far_pack.4.refs_0_, ...), custom_call_target="tpu_custom_call", output_to_operand_aliasing={{0}: (3, {}), {1}: (4, {}), {2}: (5, {})} | custom-call | flops 1 | bytes 1 | tf_op jit(solution)/shard_map/join_weights/pallas_call | solution.py:1057
  168.1 9.9 %collective-permute-done.18.refs_2_ = bf16[576,1024]{1,0:T(8,128)(2,1)} collective-permute-done((bf16[576,1024]{1,0:T(8,128)(2,1)}, bf16[576,1024]{1,0:T(8,128)(2,1)}, u32[]{:S(2)}, u32[]{:S(2)}) %collective-permute-start.18) | collective-permute-done | bytes 1179680 | tf_op jit(solution)/shard_map/ppermute | solution.py:46
  184.8 15.5 %frame_rear.1 = (bf16[256,7168]{1,0:T(8,128)(2,1)}, f32[256,1024]{1,0:T(8,128)}, bf16[256,4096]{1,0:T(8,128)(2,1)}, bf16[256,1024]{1,0:T(8,128)(2,1)}) custom-call(bf16[256,1024]{1,0:T(8,128)(2,1)} %bitcast.270, bf16[256,1024]{1,0:T(8,128)(2,1)} %get-tuple-element.320.front_ref, bf16[8,2,128,128]{3,2,1,0:T(8,128)(2,1)} %all-to-all-done.2.packed_ref, ...), custom_call_target="tpu_custom_call" | custom-call | flops 1 | bytes 1 | tf_op jit(solution)/shard_map/frame_rear/pallas_call | solution.py:1196
  201.6 4.8 far_pack.5.refs_0_
  206.7 4.7 join_weights.14
  213.8 6.2 gather_fusion
  220.0 10.5 %codec_front.1 = (bf16[768,1024]{1,0:T(8,128)(2,1)}, bf16[3,256,3072]{2,1,0:T(8,128)(2,1)}) custom-call(bf16[256,1024]{1,0:T(8,128)(2,1)} %get-tuple-element.382.base_ref, bf16[2,256,1024]{2,1,0:T(8,128)(2,1)} %bitcast.265, f32[1,1024]{1,0:T(1,128)} %bitcast.290, bf16[1024,3072]{1,0:T(8,128)(2,1)} %get-tuple-element.381.weight_ref), custom_call_target="tpu_custom_call" | custom-call | flops 1 | bytes 1 | tf_op jit(solution)/shard_map/codec_front/pallas_call | solution.py:1363
  231.9 6.3 codec_attend.1
  239.8 7.4 %join_weights.15 = (bf16[1024,4096]{1,0:T(8,128)(2,1)}, bf16[4096,1024]{1,0:T(8,128)(2,1)}, bf16[1024,1024]{1,0:T(8,128)(2,1)S(1)}) custom-call(s32[2]{0:T(128)S(1)} %pad_add_fusion.1.place_ref, bf16[2304,1024]{1,0:T(8,128)(2,1)} %far_pack.5.refs_0_, ...), custom_call_target="tpu_custom_call", output_to_operand_aliasing={{0}: (3, {}), {1}: (4, {}), {2}: (5, {})} | custom-call | flops 1 | bytes 1 | tf_op jit(solution)/shard_map/join_weights/pallas_call | solution.py:1057
  248.7 40.4 %codec_rear.1 = (f32[768,1024]{1,0:T(8,128)}, bf16[768,4096]{1,0:T(8,128)(2,1)}, bf16[768,5120]{1,0:T(8,128)(2,1)}, bf16[768,1024]{1,0:T(8,128)(2,1)}, f32[768,1...) custom-call(bf16[256,1024]{1,0:T(8,128)(2,1)} %get-tuple-element.382.base_ref, ...), custom_call_target="tpu_custom_call" | custom-call | flops 1 | bytes 1 | tf_op jit(solution)/shard_map/codec_rear/pallas_call | solution.py:1440
  291.1 8.5 %codec_attend_grads.1 = bf16[3,256,3072]{2,1,0:T(8,128)(2,1)} custom-call(bf16[3,256,3072]{2,1,0:T(8,128)(2,1)} %get-tuple-element.384.packed_ref, bf16[3,256,1024]{2,1,0:T(8,128)(2,1)S(1)} %copy-done.33, bf16[1024,128]{1,0:T(8,128)(2,1)S(1)} %fusion.25.marks_ref), custom_call_target="tpu_custom_call" | custom-call | flops 1 | bytes 1 | tf_op jit(solution)/shard_map/codec_attend_grads/pallas_call | solution.py:627
  299.6 13.3 %codec_front_grads.1 = (bf16[256,1024]{1,0:T(8,128)(2,1)}, bf16[512,1024]{1,0:T(8,128)(2,1)}, f32[1,1024]{1,0:T(1,128)}) custom-call(bf16[768,3072]{1,0:T(8,128)(2,1)} %bitcast.262, bf16[256,1024]{1,0:T(8,128)(2,1)} %get-tuple-element.382.base_ref, bf16[2,256,1024]{2,1,0:T(8,128)(2,1)} %bitcast.267, f32[1,1024]{1,0:T(1,128)} %bitcast.291, ...), custom_call_target="tpu_custom_call" | custom-call | flops 1 | bytes 1 | tf_op jit(solution)/shard_map/codec_front_grads/pallas_call | solution.py:1548
  312.9 14.9 %frame_rear_grads.1 = (bf16[256,6144]{1,0:T(8,128)(2,1)}, f32[256,1024]{1,0:T(8,128)}, bf16[8,2,128,128]{3,2,1,0:T(8,128)(2,1)}, f32[1,1024]{1,0:T(1,128)}) custom-call(bf16[256,1024]{1,0:T(8,128)(2,1)} %get-tuple-element.404.grad_ref, bf16[256,4096]{1,0:T(8,128)(2,1)} %get-tuple-element.405.slope_ref, f32[256,1024]{1,0:T(8,128)} %get-tuple-element.406.mixed_ref, ...), custom_call_target="tpu_custom_call" | custom-call | flops 1 | bytes 1 | tf_op jit(solution)/shard_map/frame_rear_grads/pallas_call | solution.py:1265
  328.2 4.1 all-to-all-start.3
  332.5 11.7 %grad_columns.2 = (bf16[2,2,2,4,256,128]{5,4,3,2,1,0:T(8,128)(2,1)S(1)}, bf16[2,2,2,4,256,128]{5,4,3,2,1,0:T(8,128)(2,1)}) custom-call(s32[27]{0:T(128)S(1)} %stack.69.order_ref, bf16[768,1024]{1,0:T(8,128)(2,1)S(1)} %bitcast.259, bf16[768,1024]{1,0:T(8,128)(2,1)S(1)} %collective-permute-done.23.latter_rec, ...), custom_call_target="tpu_custom_call" | custom-call | flops 1 | bytes 1 | tf_op jit(solution)/shard_map/grad_columns/pallas_call | solution.py:731
  345.6 13.2 %grad_rows.6 = (bf16[2,2,2,4,256,128]{5,4,3,2,1,0:T(8,128)(2,1)S(1)}, bf16[2,2,2,4,256,128]{5,4,3,2,1,0:T(8,128)(2,1)S(1)}) custom-call(s32[27]{0:T(128)S(1)} %stack.69.order_ref, bf16[768,5120]{1,0:T(8,128)(2,1)} %get-tuple-element.418.far_own.own_own.latter_own, bf16[768,5120]{1,0:T(8,128)(2,1)} %collective-permute-done.27.far_rec.own_rec.latter_rec, ...), custom_call_target="tpu_custom_call" | custom-call | flops 1 | bytes 1 | tf_op jit(solution)/shard_map/grad_rows/pallas_call | solution.py:731
  366.7 14.9 %frame_attend_grads.1 = bf16[8,2,128,384]{3,2,1,0:T(8,128)(2,1)S(1)} custom-call(bf16[8,2,128,384]{3,2,1,0:T(8,128)(2,1)} %all-to-all-done.1.packed_ref, bf16[8,2,128,128]{3,2,1,0:T(8,128)(2,1)} %all-to-all-done.3.grad_ref, s32[2,1024,1]{2,1,0:T(8,128)S(1)} %copy-done.8, s32[2,1,1024]{2,1,0:T(1,128)S(1)} %broadcast_in_dim.15.seg_row_ref), custom_call_target="tpu_custom_call" | custom-call | flops 1 | bytes 1 | tf_op jit(solution)/shard_map/frame_attend_grads/pallas_call | solution.py:477
  382.8 7.3 %grad_columns.3 = (bf16[2,2,2,4,256,128]{5,4,3,2,1,0:T(8,128)(2,1)}, bf16[2,2,2,4,256,128]{5,4,3,2,1,0:T(8,128)(2,1)S(1)}) custom-call(s32[27]{0:T(128)S(1)} %stack.69.order_ref, bf16[256,6144]{1,0:T(8,128)(2,1)} %get-tuple-element.429.latter_own, bf16[256,6144]{1,0:T(8,128)(2,1)} %collective-permute-done.28.latter_rec, ...), custom_call_target="tpu_custom_call" | custom-call | flops 1 | bytes 1 | tf_op jit(solution)/shard_map/grad_columns/pallas_call | solution.py:731
  391.4 9.3 %grad_rows.7 = (bf16[2,2,2,5,256,128]{5,4,3,2,1,0:T(8,128)(2,1)}, bf16[2,2,2,5,256,128]{5,4,3,2,1,0:T(8,128)(2,1)S(1)}) custom-call(s32[27]{0:T(128)S(1)} %stack.69.order_ref, bf16[256,7168]{1,0:T(8,128)(2,1)} %get-tuple-element.387.former_own.far_own.own_own, bf16[256,7168]{1,0:T(8,128)(2,1)} %collective-permute-done.24.former_rec.far_rec.own_rec, ...), custom_call_target="tpu_custom_call" | custom-call | flops 1 | bytes 1 | tf_op jit(solution)/shard_map/grad_rows/pallas_call | solution.py:731
  400.7 3.9 grad_rows.8
  408.9 4.6 all-to-all-start.4
  413.5 2.9 fusion.3
  421.3 12.7 %grad_rows.9 = (bf16[2,2,2,4,256,128]{5,4,3,2,1,0:T(8,128)(2,1)}, bf16[2,2,2,4,256,128]{5,4,3,2,1,0:T(8,128)(2,1)S(1)}) custom-call(s32[27]{0:T(128)S(1)} %stack.69.order_ref, bf16[768,2048]{1,0:T(8,128)(2,1)} %bitcast.252, bf16[768,2048]{1,0:T(8,128)(2,1)} %copy-done.42, bf16[768,2048]{1,0:T(8,128)(2,1)} %bitcast.253, bf16[768,2048]{1,0:T(8,128)(2,1)} %copy-done.42, ...), custom_call_target="tpu_custom_call" | custom-call | flops 1 | bytes 1 | tf_op jit(solution)/shard_map/grad_rows/pallas_call | solution.py:731
  435.3 4.8 grad_rows.10
  440.1 4.4 grad_table.1
  445.5 5.1 all-to-all-done.4.packed_ref
  451.8 7.9 %frame_front_grads.1 = (bf16[256,3072]{1,0:T(8,128)(2,1)}, f32[256,1024]{1,0:T(8,128)}, f32[1,1024]{1,0:T(1,128)}) custom-call(bf16[8,2,128,384]{3,2,1,0:T(8,128)(2,1)} %copy-done.44, bf16[256,1024]{1,0:T(8,128)(2,1)} %bitcast.271, f32[1,1024]{1,0:T(1,128)} %bitcast.293, f32[256,1024]{1,0:T(8,128)} %get-tuple-element.469.mixed_grad_ref, ...), custom_call_target="tpu_custom_call" | custom-call | flops 1 | bytes 1 | tf_op jit(solution)/shard_map/frame_front_grads/pallas_call | solution.py:1319
  466.8 7.9 %grad_rows.11 = (bf16[2,2,2,3,256,128]{5,4,3,2,1,0:T(8,128)(2,1)S(1)}, bf16[2,2,2,3,256,128]{5,4,3,2,1,0:T(8,128)(2,1)S(1)}) custom-call(s32[27]{0:T(128)S(1)} %stack.69.order_ref, bf16[256,7168]{1,0:T(8,128)(2,1)} %get-tuple-element.387.former_own.far_own.own_own, bf16[256,7168]{1,0:T(8,128)(2,1)} %collective-permute-done.24.former_rec.far_rec.own_rec, ...), custom_call_target="tpu_custom_call" | custom-call | flops 1 | bytes 1 | tf_op jit(solution)/shard_map/grad_rows/pallas_call | solution.py:731
  477.0 12.3 %collective-permute-done.34 = bf16[2,2,2,5,256,128]{5,4,3,2,1,0:T(8,128)(2,1)} collective-permute-done((bf16[2,2,2,5,256,128]{5,4,3,2,1,0:T(8,128)(2,1)}, bf16[2,2,2,5,256,128]{5,4,3,2,1,0:T(8,128)(2,1)}, u32[]{:S(2)}, u32[]{:S(2)}) %collective-permute-start.34) | collective-permute-done | bytes 2621472 | tf_op jit(solution)/shard_map/ppermute | solution.py:46
  489.3 2.8 fusion.5
  492.1 2.8 fusion.1
  495.0 2.6 collective-permute-start.46
  499.8 14.1 %codec_result.1 = bf16[3,256,1024]{2,1,0:T(8,128)(2,1)} custom-call(f32[768,1024]{1,0:T(8,128)} %get-tuple-element.396.mixed_ref, bf16[768,4096]{1,0:T(8,128)(2,1)} %get-tuple-element.489.former_own.active_ref, f32[256,1]{1,0:T(8,128)} %copy.73.live_ref, bf16[4096,1024]{1,0:T(8,128)(2,1)} %get-tuple-element.392.contract_ref), custom_call_target="tpu_custom_call" | custom-call | flops 1 | bytes 1 | tf_op jit(solution)/shard_map/codec_result/pallas_call | solution.py:1497
  522.2 2.7 fusion.36
  526.7 13.2 %collective-permute-done.46 = bf16[2,2,5,256,128]{4,3,2,1,0:T(8,128)(2,1)} collective-permute-done((bf16[2,2,5,256,128]{4,3,2,1,0:T(8,128)(2,1)}, bf16[2,2,5,256,128]{4,3,2,1,0:T(8,128)(2,1)}, u32[]{:S(2)}, u32[]{:S(2)}) %collective-permute-start.46) | collective-permute-done | bytes 1310752 | tf_op jit(solution)/shard_map/ppermute | solution.py:46
  543.3 2.6 collective-permute-done.45
  548.0 2.7 slice.451
  552.0 16.2 %collective-permute-done.44 = bf16[2,2,4,256,128]{4,3,2,1,0:T(8,128)(2,1)} collective-permute-done((bf16[2,2,4,256,128]{4,3,2,1,0:T(8,128)(2,1)}, bf16[2,2,4,256,128]{4,3,2,1,0:T(8,128)(2,1)}, u32[]{:S(2)}, u32[]{:S(2)}) %collective-permute-start.44) | collective-permute-done | bytes 1048608 | tf_op jit(solution)/shard_map/ppermute | solution.py:46
  580.7 2.9 collective-permute-done.47
  587.2 2.6 collective-permute-start.56
  606.4 3.1 collective-permute-done.50
  613.5 11.2 %collective-permute-done.57 = bf16[1600,128]{1,0:T(8,128)(2,1)S(1)} collective-permute-done((bf16[1600,128]{1,0:T(8,128)(2,1)S(1)}, bf16[1600,128]{1,0:T(8,128)(2,1)S(1)}, u32[]{:S(2)}, u32[]{:S(2)}) %collective-permute-start.57) | collective-permute-done | bytes 409632 | tf_op jit(solution)/shard_map/ppermute | solution.py:46
  641.5 10.5 %collective-permute-done.55 = bf16[8,256,128]{2,1,0:T(8,128)(2,1)} collective-permute-done((bf16[8,256,128]{2,1,0:T(8,128)(2,1)}, bf16[8,256,128]{2,1,0:T(8,128)(2,1)}, u32[]{:S(2)}, u32[]{:S(2)}) %collective-permute-start.55) | collective-permute-done | bytes 524320 | tf_op jit(solution)/shard_map/ppermute | solution.py:46
  657.7 2.8 collective-permute-done.54
  (351 shorter events, 174.5 us)
Async XLA Ops:
  4.2 24.8 %collective-permute-start.3 = (bf16[896,1024]{1,0:T(8,128)(2,1)S(1)}, bf16[896,1024]{1,0:T(8,128)(2,1)S(1)}, u32[]{:S(2)}, u32[]{:S(2)}) collective-permute-start(bf16[896,1024]{1,0:T(8,128)(2,1)S(1)} %get-tuple-element.297.refs_0_), channel_id=1, source_target_pairs={{0,1},{1,0},{2,3},{3,2},{4,5},{5,4},{6,7},{7,6},{8,9},{9,8},{10,11... | collective-permute-start | bytes 5505032 | tf_op jit(solution)/shard_map/ppermute | solution.py:46
  4.7 20.9 %collective-permute-start = (bf16[224,1024]{1,0:T(8,128)(2,1)S(1)}, bf16[224,1024]{1,0:T(8,128)(2,1)S(1)}, u32[]{:S(2)}, u32[]{:S(2)}) collective-permute-start(bf16[224,1024]{1,0:T(8,128)(2,1)S(1)} %get-tuple-element.287), channel_id=1, source_target_pairs={{0,2},{1,3},{2,0},{3,1},{4,6},{5,7},{6,4},{7,5},{8,10},{9,11},{10,... | collective-permute-start | bytes 1376264 | tf_op jit(solution)/shard_map/ppermute | solution.py:46
  25.6 26.9 %collective-permute-start.6 = (bf16[576,1024]{1,0:T(8,128)(2,1)}, bf16[576,1024]{1,0:T(8,128)(2,1)}, u32[]{:S(2)}, u32[]{:S(2)}) collective-permute-start(bf16[576,1024]{1,0:T(8,128)(2,1)} %get-tuple-element.312), channel_id=1, source_target_pairs={{0,2},{1,3},{2,0},{3,1},{4,6},{5,7},{6,4},{7,5},{8,10},{9,11},{10,... | collective-permute-start | bytes 3538952 | tf_op jit(solution)/shard_map/ppermute | solution.py:46
  26.1 10.9 %collective-permute-start.2 = (bf16[224,1024]{1,0:T(8,128)(2,1)S(1)}, bf16[224,1024]{1,0:T(8,128)(2,1)S(1)}, u32[]{:S(2)}, u32[]{:S(2)}) collective-permute-start(bf16[224,1024]{1,0:T(8,128)(2,1)S(1)} %collective-permute-done.refs_0_), channel_id=1, source_target_pairs={{0,8},{4,12},{8,0},{12,4},{16,24},{20,28},{24,16},{28,20},{1,9},{5... | collective-permute-start | bytes 1376264 | tf_op jit(solution)/shard_map/ppermute | solution.py:46
  26.6 10.6 %collective-permute-start.1 = (bf16[224,1024]{1,0:T(8,128)(2,1)S(1)}, bf16[224,1024]{1,0:T(8,128)(2,1)S(1)}, u32[]{:S(2)}, u32[]{:S(2)}) collective-permute-start(bf16[224,1024]{1,0:T(8,128)(2,1)S(1)} %collective-permute-done.refs_0_), channel_id=1, source_target_pairs={{0,4},{4,0},{8,12},{12,8},{16,20},{20,16},{24,28},{28,24},{1,5},{5... | collective-permute-start | bytes 1376264 | tf_op jit(solution)/shard_map/ppermute | solution.py:46
  37.3 8.2 %collective-permute-start.4 = (bf16[112,1024]{1,0:T(8,128)(2,1)S(1)}, bf16[112,1024]{1,0:T(8,128)(2,1)S(1)}, u32[]{:S(2)}, u32[]{:S(2)}) collective-permute-start(bf16[112,1024]{1,0:T(8,128)(2,1)S(1)} %slice.397), channel_id=1, source_target_pairs={{0,4},{4,0},{8,12},{12,8},{16,20},{20,16},{24,28},{28,24},{1,5},{5... | collective-permute-start | bytes 688136 | tf_op jit(solution)/shard_map/ppermute | solution.py:46
  38.0 7.5 %collective-permute-start.5 = (bf16[112,1024]{1,0:T(8,128)(2,1)S(1)}, bf16[112,1024]{1,0:T(8,128)(2,1)S(1)}, u32[]{:S(2)}, u32[]{:S(2)}) collective-permute-start(bf16[112,1024]{1,0:T(8,128)(2,1)S(1)} %slice.398), channel_id=1, source_target_pairs={{0,8},{4,12},{8,0},{12,4},{16,24},{20,28},{24,16},{28,20},{1,9},{5... | collective-permute-start | bytes 688136 | tf_op jit(solution)/shard_map/ppermute | solution.py:46
  52.5 3.8 collective-permute-start.7
  52.6 28.7 %collective-permute-start.10 = (bf16[576,1024]{1,0:T(8,128)(2,1)}, bf16[576,1024]{1,0:T(8,128)(2,1)}, u32[]{:S(2)}, u32[]{:S(2)}) collective-permute-start(bf16[576,1024]{1,0:T(8,128)(2,1)} %get-tuple-element.322), channel_id=1, source_target_pairs={{0,2},{1,3},{2,0},{3,1},{4,6},{5,7},{6,4},{7,5},{8,10},{9,11},{10,... | collective-permute-start | bytes 3538952 | tf_op jit(solution)/shard_map/ppermute | solution.py:46
  53.1 28.3 %collective-permute-start.9 = (bf16[576,1024]{1,0:T(8,128)(2,1)}, bf16[576,1024]{1,0:T(8,128)(2,1)S(1)}, u32[]{:S(2)}, u32[]{:S(2)}) collective-permute-start(bf16[576,1024]{1,0:T(8,128)(2,1)} %collective-permute-done.6.refs_0_), channel_id=1, source_target_pairs={{0,8},{4,12},{8,0},{12,4},{16,24},{20,28},{24,16},{28,20},{1,9},{5... | collective-permute-start | bytes 3538952 | tf_op jit(solution)/shard_map/ppermute | solution.py:46
  53.6 28.1 %collective-permute-start.8 = (bf16[576,1024]{1,0:T(8,128)(2,1)}, bf16[576,1024]{1,0:T(8,128)(2,1)}, u32[]{:S(2)}, u32[]{:S(2)}) collective-permute-start(bf16[576,1024]{1,0:T(8,128)(2,1)} %collective-permute-done.6.refs_0_), channel_id=1, source_target_pairs={{0,4},{4,0},{8,12},{12,8},{16,20},{20,16},{24,28},{28,24},{1,5},{5... | collective-permute-start | bytes 3538952 | tf_op jit(solution)/shard_map/ppermute | solution.py:46
  81.7 8.3 %collective-permute-start.13 = (bf16[2304,1024]{1,0:T(8,128)(2,1)}, bf16[2304,1024]{1,0:T(8,128)(2,1)}, u32[]{:S(2)}, u32[]{:S(2)}) collective-permute-start(bf16[2304,1024]{1,0:T(8,128)(2,1)} %get-tuple-element.331.refs_0_), channel_id=1, source_target_pairs={{0,1},{1,0},{2,3},{3,2},{4,5},{5,4},{6,7},{7,6},{8,9},{9,8},{10,11... | collective-permute-start | bytes 14155784 | tf_op jit(solution)/shard_map/ppermute | solution.py:46
  81.7 23.4 %collective-permute-start.11 = (bf16[2304,1024]{1,0:T(8,128)(2,1)}, bf16[2304,1024]{1,0:T(8,128)(2,1)}, u32[]{:S(2)}, u32[]{:S(2)}) collective-permute-start(bf16[2304,1024]{1,0:T(8,128)(2,1)} %get-tuple-element.340.refs_0_), channel_id=1, source_target_pairs={{0,1},{1,0},{2,3},{3,2},{4,5},{5,4},{6,7},{7,6},{8,9},{9,8},{10,11... | collective-permute-start | bytes 14155784 | tf_op jit(solution)/shard_map/ppermute | solution.py:46
  82.2 18.2 %collective-permute-start.12 = (bf16[1280,1024]{1,0:T(8,128)(2,1)}, bf16[1280,1024]{1,0:T(8,128)(2,1)}, u32[]{:S(2)}, u32[]{:S(2)}) collective-permute-start(bf16[1280,1024]{1,0:T(8,128)(2,1)} %get-tuple-element.370.refs_0_), channel_id=1, source_target_pairs={{0,1},{1,0},{2,3},{3,2},{4,5},{5,4},{6,7},{7,6},{8,9},{9,8},{10,11... | collective-permute-start | bytes 7864328 | tf_op jit(solution)/shard_map/ppermute | solution.py:46
  82.2 42.4 %all-to-all-start.1 = ((bf16[8,2,128,384]{3,2,1,0:T(8,128)(2,1)}), bf16[8,2,128,384]{3,2,1,0:T(8,128)(2,1)}, u32[]{:S(2)}, u32[]{:S(2)}) async-start(bf16[8,2,128,384]{3,2,1,0:T(8,128)(2,1)} %get-tuple-element.323), calls=%async_computation.1 | async-start | bytes 3145728 | tf_op jit(solution)/shard_map/all_to_all | solution.py:1990
  116.7 20.4 %collective-permute-start.15 = (bf16[288,1024]{1,0:T(8,128)(2,1)}, bf16[288,1024]{1,0:T(8,128)(2,1)}, u32[]{:S(2)}, u32[]{:S(2)}) collective-permute-start(bf16[288,1024]{1,0:T(8,128)(2,1)} %slice.402), channel_id=1, source_target_pairs={{0,8},{4,12},{8,0},{12,4},{16,24},{20,28},{24,16},{28,20},{1,9},{5... | collective-permute-start | bytes 1769480 | tf_op jit(solution)/shard_map/ppermute | solution.py:46
  118.2 18.9 %collective-permute-start.14 = (bf16[288,1024]{1,0:T(8,128)(2,1)}, bf16[288,1024]{1,0:T(8,128)(2,1)}, u32[]{:S(2)}, u32[]{:S(2)}) collective-permute-start(bf16[288,1024]{1,0:T(8,128)(2,1)} %slice.401), channel_id=1, source_target_pairs={{0,4},{4,0},{8,12},{12,8},{16,20},{20,16},{24,28},{28,24},{1,5},{5... | collective-permute-start | bytes 1769480 | tf_op jit(solution)/shard_map/ppermute | solution.py:46
  141.9 13.2 %collective-permute-start.16 = (bf16[2304,1024]{1,0:T(8,128)(2,1)}, bf16[2304,1024]{1,0:T(8,128)(2,1)}, u32[]{:S(2)}, u32[]{:S(2)}) collective-permute-start(bf16[2304,1024]{1,0:T(8,128)(2,1)} %far_pack.4.refs_0_), channel_id=1, source_target_pairs={{0,1},{1,0},{2,3},{3,2},{4,5},{5,4},{6,7},{7,6},{8,9},{9,8},{10,11... | collective-permute-start | bytes 14155784 | tf_op jit(solution)/shard_map/ppermute | solution.py:46
  142.0 59.6 %collective-permute-start.19 = (bf16[1280,1024]{1,0:T(8,128)(2,1)}, bf16[1280,1024]{1,0:T(8,128)(2,1)}, u32[]{:S(2)}, u32[]{:S(2)}) collective-permute-start(bf16[1280,1024]{1,0:T(8,128)(2,1)} %get-tuple-element.370.refs_0_), channel_id=1, source_target_pairs={{0,2},{1,3},{2,0},{3,1},{4,6},{5,7},{6,4},{7,5},{8,10},{9,11},{10,... | collective-permute-start | bytes 7864328 | tf_op jit(solution)/shard_map/ppermute | solution.py:46
  143.6 34.5 %collective-permute-start.18 = (bf16[576,1024]{1,0:T(8,128)(2,1)}, bf16[576,1024]{1,0:T(8,128)(2,1)}, u32[]{:S(2)}, u32[]{:S(2)}) collective-permute-start(bf16[576,1024]{1,0:T(8,128)(2,1)} %collective-permute-done.10.refs_0_), channel_id=1, source_target_pairs={{0,8},{4,12},{8,0},{12,4},{16,24},{20,28},{24,16},{28,20},{1,9},{5... | collective-permute-start | bytes 3538952 | tf_op jit(solution)/shard_map/ppermute | solution.py:46
  143.6 34.5 %collective-permute-start.17 = (bf16[576,1024]{1,0:T(8,128)(2,1)}, bf16[576,1024]{1,0:T(8,128)(2,1)}, u32[]{:S(2)}, u32[]{:S(2)}) collective-permute-start(bf16[576,1024]{1,0:T(8,128)(2,1)} %collective-permute-done.10.refs_0_), channel_id=1, source_target_pairs={{0,4},{4,0},{8,12},{12,8},{16,20},{20,16},{24,28},{28,24},{1,5},{5... | collective-permute-start | bytes 3538952 | tf_op jit(solution)/shard_map/ppermute | solution.py:46
  155.1 25.3 %all-to-all-start.2 = ((bf16[8,2,128,128]{3,2,1,0:T(8,128)(2,1)}), bf16[8,2,128,128]{3,2,1,0:T(8,128)(2,1)}, u32[]{:S(2)}, u32[]{:S(2)}) async-start(bf16[8,2,128,128]{3,2,1,0:T(8,128)(2,1)} %copy-done.21), calls=%async_computation.2 | async-start | bytes 1048576 | tf_op jit(solution)/shard_map/all_to_all | solution.py:2010
  182.6 19.0 %collective-permute-start.20 = (bf16[288,1024]{1,0:T(8,128)(2,1)S(1)}, bf16[288,1024]{1,0:T(8,128)(2,1)S(1)}, u32[]{:S(2)}, u32[]{:S(2)}) collective-permute-start(bf16[288,1024]{1,0:T(8,128)(2,1)S(1)} %slice.404), channel_id=1, source_target_pairs={{0,4},{4,0},{8,12},{12,8},{16,20},{20,16},{24,28},{28,24},{1,5},{5... | collective-permute-start | bytes 1769480 | tf_op jit(solution)/shard_map/ppermute | solution.py:46
  183.4 18.2 %collective-permute-start.21 = (bf16[288,1024]{1,0:T(8,128)(2,1)S(1)}, bf16[288,1024]{1,0:T(8,128)(2,1)S(1)}, u32[]{:S(2)}, u32[]{:S(2)}) collective-permute-start(bf16[288,1024]{1,0:T(8,128)(2,1)S(1)} %slice.405), channel_id=1, source_target_pairs={{0,8},{4,12},{8,0},{12,4},{16,24},{20,28},{24,16},{28,20},{1,9},{5... | collective-permute-start | bytes 1769480 | tf_op jit(solution)/shard_map/ppermute | solution.py:46
  201.6 5.1 collective-permute-start.22
  211.4 28.4 %collective-permute-start.25 = (bf16[2304,1024]{1,0:T(8,128)(2,1)}, bf16[2304,1024]{1,0:T(8,128)(2,1)}, u32[]{:S(2)}, u32[]{:S(2)}) collective-permute-start(bf16[2304,1024]{1,0:T(8,128)(2,1)} %far_pack.5.refs_0_), channel_id=1, source_target_pairs={{0,1},{1,0},{2,3},{3,2},{4,5},{5,4},{6,7},{7,6},{8,9},{9,8},{10,11... | collective-permute-start | bytes 14155784 | tf_op jit(solution)/shard_map/ppermute | solution.py:46
  211.8 36.9 %collective-permute-start.24 = (bf16[256,7168]{1,0:T(8,128)(2,1)}, bf16[256,7168]{1,0:T(8,128)(2,1)}, u32[]{:S(2)}, u32[]{:S(2)}) collective-permute-start(bf16[256,7168]{1,0:T(8,128)(2,1)} %get-tuple-element.387.former_own.far_own.own_own), channel_id=1, source_target_pairs={{0,1},{1,0},{2,3},{3,2},{4,5},{5,4},{6,7},{7,6},{8,9},{9,8},{10,11... | collective-permute-start | bytes 11010056 | tf_op jit(solution)/shard_map/ppermute | solution.py:46
  212.0 18.5 %collective-permute-start.23 = (bf16[768,1024]{1,0:T(8,128)(2,1)S(1)}, bf16[768,1024]{1,0:T(8,128)(2,1)S(1)}, u32[]{:S(2)}, u32[]{:S(2)}) collective-permute-start(bf16[768,1024]{1,0:T(8,128)(2,1)S(1)} %bitcast.258), channel_id=1, source_target_pairs={{0,1},{1,0},{2,3},{3,2},{4,5},{5,4},{6,7},{7,6},{8,9},{9,8},{10,11... | collective-permute-start | bytes 4718600 | tf_op jit(solution)/shard_map/ppermute | solution.py:46
  289.1 38.8 %collective-permute-start.27 = (bf16[768,5120]{1,0:T(8,128)(2,1)}, bf16[768,5120]{1,0:T(8,128)(2,1)}, u32[]{:S(2)}, u32[]{:S(2)}) collective-permute-start(bf16[768,5120]{1,0:T(8,128)(2,1)} %get-tuple-element.418.far_own.own_own.latter_own), channel_id=1, source_target_pairs={{0,1},{1,0},{2,3},{3,2},{4,5},{5,4},{6,7},{7,6},{8,9},{9,8},{10,11... | collective-permute-start | bytes 23592968 | tf_op jit(solution)/shard_map/ppermute | solution.py:46
  289.4 38.4 %collective-permute-start.26 = (bf16[768,4096]{1,0:T(8,128)(2,1)}, bf16[768,4096]{1,0:T(8,128)(2,1)}, u32[]{:S(2)}, u32[]{:S(2)}) collective-permute-start(bf16[768,4096]{1,0:T(8,128)(2,1)} %get-tuple-element.489.former_own.active_ref), channel_id=1, source_target_pairs={{0,1},{1,0},{2,3},{3,2},{4,5},{5,4},{6,7},{7,6},{8,9},{9,8},{10,11... | collective-permute-start | bytes 18874376 | tf_op jit(solution)/shard_map/ppermute | solution.py:46
  327.9 33.6 %collective-permute-start.28 = (bf16[256,6144]{1,0:T(8,128)(2,1)}, bf16[256,6144]{1,0:T(8,128)(2,1)}, u32[]{:S(2)}, u32[]{:S(2)}) collective-permute-start(bf16[256,6144]{1,0:T(8,128)(2,1)} %get-tuple-element.429.latter_own), channel_id=1, source_target_pairs={{0,1},{1,0},{2,3},{3,2},{4,5},{5,4},{6,7},{7,6},{8,9},{9,8},{10,11... | collective-permute-start | bytes 9437192 | tf_op jit(solution)/shard_map/ppermute | solution.py:46
  328.2 33.3 %all-to-all-start.3 = ((bf16[8,2,128,128]{3,2,1,0:T(8,128)(2,1)}), bf16[8,2,128,128]{3,2,1,0:T(8,128)(2,1)}, u32[]{:S(2)}, u32[]{:S(2)}) async-start(bf16[8,2,128,128]{3,2,1,0:T(8,128)(2,1)} %get-tuple-element.410), calls=%async_computation.3 | async-start | bytes 1048576 | tf_op jit(solution)/shard_map/all_to_all | solution.py:2091
  361.5 47.4 %collective-permute-start.31 = (bf16[768,3072]{1,0:T(8,128)(2,1)}, bf16[768,3072]{1,0:T(8,128)(2,1)}, u32[]{:S(2)}, u32[]{:S(2)}) collective-permute-start(bf16[768,3072]{1,0:T(8,128)(2,1)} %bitcast.263), channel_id=1, source_target_pairs={{0,1},{1,0},{2,3},{3,2},{4,5},{5,4},{6,7},{7,6},{8,9},{9,8},{10,11... | collective-permute-start | bytes 14155784 | tf_op jit(solution)/shard_map/ppermute | solution.py:46
  361.8 45.5 %collective-permute-start.30 = (bf16[768,2048]{1,0:T(8,128)(2,1)S(1)}, bf16[768,2048]{1,0:T(8,128)(2,1)S(1)}, u32[]{:S(2)}, u32[]{:S(2)}) collective-permute-start(bf16[768,2048]{1,0:T(8,128)(2,1)S(1)} %bitcast.256), channel_id=1, source_target_pairs={{0,1},{1,0},{2,3},{3,2},{4,5},{5,4},{6,7},{7,6},{8,9},{9,8},{10,11... | collective-permute-start | bytes 9437192 | tf_op jit(solution)/shard_map/ppermute | solution.py:46
  362.0 44.0 %collective-permute-start.32 = (bf16[768,1024]{1,0:T(8,128)(2,1)}, bf16[768,1024]{1,0:T(8,128)(2,1)S(1)}, u32[]{:S(2)}, u32[]{:S(2)}) collective-permute-start(bf16[768,1024]{1,0:T(8,128)(2,1)} %get-tuple-element.440.latter_own), channel_id=1, source_target_pairs={{0,1},{1,0},{2,3},{3,2},{4,5},{5,4},{6,7},{7,6},{8,9},{9,8},{10,11... | collective-permute-start | bytes 4718600 | tf_op jit(solution)/shard_map/ppermute | solution.py:46
  362.3 51.3 %collective-permute-start.29 = (bf16[2,2,2,4,256,128]{5,4,3,2,1,0:T(8,128)(2,1)}, bf16[2,2,2,4,256,128]{5,4,3,2,1,0:T(8,128)(2,1)}, u32[]{:S(2)}, u32[]{:S(2)}) collective-permute-start(bf16[2,2,2,4,256,128]{5,4,3,2,1,0:T(8,128)(2,1)} %copy-done.40), channel_id=1, source_target_pairs={{0,2},{1,3},{2,0},{3,1},{4,6},{5,7},{6,4},{7,5},{8,10},{9,11},{10,... | collective-permute-start | bytes 6291464 | tf_op jit(solution)/shard_map/ppermute | solution.py:46
  363.7 49.8 %collective-permute-start.33 = (bf16[2,2,2,4,256,128]{5,4,3,2,1,0:T(8,128)(2,1)}, bf16[2,2,2,4,256,128]{5,4,3,2,1,0:T(8,128)(2,1)}, u32[]{:S(2)}, u32[]{:S(2)}) collective-permute-start(bf16[2,2,2,4,256,128]{5,4,3,2,1,0:T(8,128)(2,1)} %copy-done.41), channel_id=1, source_target_pairs={{0,4},{4,0},{8,12},{12,8},{16,20},{20,16},{24,28},{28,24},{1,5},{5... | collective-permute-start | bytes 6291464 | tf_op jit(solution)/shard_map/ppermute | solution.py:46
  408.9 41.7 %all-to-all-start.4 = ((bf16[8,2,128,384]{3,2,1,0:T(8,128)(2,1)}), bf16[8,2,128,384]{3,2,1,0:T(8,128)(2,1)S(1)}, u32[]{:S(2)}, u32[]{:S(2)}) async-start(bf16[8,2,128,384]{3,2,1,0:T(8,128)(2,1)} %copy-done.14), calls=%async_computation.4 | async-start | bytes 3145728 | tf_op jit(solution)/shard_map/all_to_all | solution.py:2139
  418.0 22.1 %collective-permute-start.36 = (bf16[512,1024]{1,0:T(8,128)(2,1)S(1)}, bf16[512,1024]{1,0:T(8,128)(2,1)S(1)}, u32[]{:S(2)}, u32[]{:S(2)}) collective-permute-start(bf16[512,1024]{1,0:T(8,128)(2,1)S(1)} %copy-done.36), channel_id=1, source_target_pairs={{0,1},{1,0},{2,3},{3,2},{4,5},{5,4},{6,7},{7,6},{8,9},{9,8},{10,11... | collective-permute-start | bytes 3145736 | tf_op jit(solution)/shard_map/ppermute | solution.py:46
  418.0 71.3 %collective-permute-start.34 = (bf16[2,2,2,5,256,128]{5,4,3,2,1,0:T(8,128)(2,1)}, bf16[2,2,2,5,256,128]{5,4,3,2,1,0:T(8,128)(2,1)}, u32[]{:S(2)}, u32[]{:S(2)}) collective-permute-start(bf16[2,2,2,5,256,128]{5,4,3,2,1,0:T(8,128)(2,1)} %get-tuple-element.451), channel_id=1, source_target_pairs={{0,4},{4,0},{8,12},{12,8},{16,20},{20,16},{24,28},{28,24},{1,5},{5... | collective-permute-start | bytes 7864328 | tf_op jit(solution)/shard_map/ppermute | solution.py:46
  420.1 1.2 collective-permute-start.35
  420.4 68.9 %collective-permute-start.39 = (bf16[2,2,2,4,256,128]{5,4,3,2,1,0:T(8,128)(2,1)}, bf16[2,2,2,4,256,128]{5,4,3,2,1,0:T(8,128)(2,1)}, u32[]{:S(2)}, u32[]{:S(2)}) collective-permute-start(bf16[2,2,2,4,256,128]{5,4,3,2,1,0:T(8,128)(2,1)} %get-tuple-element.484), channel_id=1, source_target_pairs={{0,2},{1,3},{2,0},{3,1},{4,6},{5,7},{6,4},{7,5},{8,10},{9,11},{10,... | collective-permute-start | bytes 6291464 | tf_op jit(solution)/shard_map/ppermute | solution.py:46
  459.6 3.6 collective-permute-start.37
  459.6 54.4 %collective-permute-start.42 = (bf16[2,2,2,4,256,128]{5,4,3,2,1,0:T(8,128)(2,1)}, bf16[2,2,2,4,256,128]{5,4,3,2,1,0:T(8,128)(2,1)}, u32[]{:S(2)}, u32[]{:S(2)}) collective-permute-start(bf16[2,2,2,4,256,128]{5,4,3,2,1,0:T(8,128)(2,1)} %get-tuple-element.493), channel_id=1, source_target_pairs={{0,2},{1,3},{2,0},{3,1},{4,6},{5,7},{6,4},{7,5},{8,10},{9,11},{10,... | collective-permute-start | bytes 6291464 | tf_op jit(solution)/shard_map/ppermute | solution.py:46
  460.9 2.1 collective-permute-start.38
  463.1 55.3 %collective-permute-start.41 = (bf16[2,2,8,256,128]{4,3,2,1,0:T(8,128)(2,1)}, bf16[2,2,8,256,128]{4,3,2,1,0:T(8,128)(2,1)}, u32[]{:S(2)}, u32[]{:S(2)}) collective-permute-start(bf16[2,2,8,256,128]{4,3,2,1,0:T(8,128)(2,1)} %pad_maximum_fusion), channel_id=1, source_target_pairs={{0,8},{4,12},{8,0},{12,4},{16,24},{20,28},{24,16},{28,20},{1,9},{5... | collective-permute-start | bytes 6291464 | tf_op jit(solution)/shard_map/ppermute | solution.py:46
  463.2 55.2 %collective-permute-start.40 = (bf16[2,2,2,2,256,128]{5,4,3,2,1,0:T(8,128)(2,1)}, bf16[2,2,2,2,256,128]{5,4,3,2,1,0:T(8,128)(2,1)}, u32[]{:S(2)}, u32[]{:S(2)}) collective-permute-start(bf16[2,2,2,2,256,128]{5,4,3,2,1,0:T(8,128)(2,1)} %get-tuple-element.491), channel_id=1, source_target_pairs={{0,4},{4,0},{8,12},{12,8},{16,20},{20,16},{24,28},{28,24},{1,5},{5... | collective-permute-start | bytes 3145736 | tf_op jit(solution)/shard_map/ppermute | solution.py:46
  495.0 45.0 %collective-permute-start.46 = (bf16[2,2,5,256,128]{4,3,2,1,0:T(8,128)(2,1)}, bf16[2,2,5,256,128]{4,3,2,1,0:T(8,128)(2,1)}, u32[]{:S(2)}, u32[]{:S(2)}) collective-permute-start(bf16[2,2,5,256,128]{4,3,2,1,0:T(8,128)(2,1)} %fusion.1), channel_id=1, source_target_pairs={{0,8},{4,12},{8,0},{12,4},{16,24},{20,28},{24,16},{28,20},{1,9},{5... | collective-permute-start | bytes 3932168 | tf_op jit(solution)/shard_map/ppermute | solution.py:46
  498.9 47.0 %collective-permute-start.45 = (bf16[6208,128]{1,0:T(8,128)(2,1)}, bf16[6208,128]{1,0:T(8,128)(2,1)}, u32[]{:S(2)}, u32[]{:S(2)}) collective-permute-start(bf16[6208,128]{1,0:T(8,128)(2,1)} %pad_maximum_fusion.1), channel_id=1, source_target_pairs={{0,4},{4,0},{8,12},{12,8},{16,20},{20,16},{24,28},{28,24},{1,5},{5... | collective-permute-start | bytes 4767752 | tf_op jit(solution)/shard_map/ppermute | solution.py:46
  514.0 54.2 %collective-permute-start.44 = (bf16[2,2,4,256,128]{4,3,2,1,0:T(8,128)(2,1)}, bf16[2,2,4,256,128]{4,3,2,1,0:T(8,128)(2,1)}, u32[]{:S(2)}, u32[]{:S(2)}) collective-permute-start(bf16[2,2,4,256,128]{4,3,2,1,0:T(8,128)(2,1)} %fusion.5), channel_id=1, source_target_pairs={{0,4},{4,0},{8,12},{12,8},{16,20},{20,16},{24,28},{28,24},{1,5},{5... | collective-permute-start | bytes 3145736 | tf_op jit(solution)/shard_map/ppermute | solution.py:46
  518.4 52.8 %collective-permute-start.49 = (bf16[2,2,4,256,128]{4,3,2,1,0:T(8,128)(2,1)}, bf16[2,2,4,256,128]{4,3,2,1,0:T(8,128)(2,1)}, u32[]{:S(2)}, u32[]{:S(2)}) collective-permute-start(bf16[2,2,4,256,128]{4,3,2,1,0:T(8,128)(2,1)} %fusion.6), channel_id=1, source_target_pairs={{0,8},{4,12},{8,0},{12,4},{16,24},{20,28},{24,16},{28,20},{1,9},{5... | collective-permute-start | bytes 3145736 | tf_op jit(solution)/shard_map/ppermute | solution.py:46
  520.4 69.4 %collective-permute-start.43 = (bf16[2,2,2,256,128]{4,3,2,1,0:T(8,128)(2,1)}, bf16[2,2,2,256,128]{4,3,2,1,0:T(8,128)(2,1)}, u32[]{:S(2)}, u32[]{:S(2)}) collective-permute-start(bf16[2,2,2,256,128]{4,3,2,1,0:T(8,128)(2,1)} %fusion.14), channel_id=1, source_target_pairs={{0,2},{1,3},{2,0},{3,1},{4,6},{5,7},{6,4},{7,5},{8,10},{9,11},{10,... | collective-permute-start | bytes 1572872 | tf_op jit(solution)/shard_map/ppermute | solution.py:46
  542.6 33.7 %collective-permute-start.48 = (bf16[2,9,256,128]{3,2,1,0:T(8,128)(2,1)}, bf16[2,9,256,128]{3,2,1,0:T(8,128)(2,1)}, u32[]{:S(2)}, u32[]{:S(2)}) collective-permute-start(bf16[2,9,256,128]{3,2,1,0:T(8,128)(2,1)} %pad_maximum_fusion.2), channel_id=1, source_target_pairs={{0,2},{1,3},{2,0},{3,1},{4,6},{5,7},{6,4},{7,5},{8,10},{9,11},{10,... | collective-permute-start | bytes 3538952 | tf_op jit(solution)/shard_map/ppermute | solution.py:46
  551.4 22.7 %copy-start.45 = (bf16[2,2,4,256,128]{4,3,2,1,0:T(8,128)(2,1)S(1)}, bf16[2,2,4,256,128]{4,3,2,1,0:T(8,128)(2,1)}, u32[]{:S(2)}) copy-start(bf16[2,2,4,256,128]{4,3,2,1,0:T(8,128)(2,1)} %get-tuple-element.534) | copy-start | bytes 3145732
  551.4 42.1 %collective-permute-start.52 = (bf16[3136,128]{1,0:T(8,128)(2,1)S(1)}, bf16[3136,128]{1,0:T(8,128)(2,1)S(1)}, u32[]{:S(2)}, u32[]{:S(2)}) collective-permute-start(bf16[3136,128]{1,0:T(8,128)(2,1)S(1)} %pad_maximum_fusion.3), channel_id=1, source_target_pairs={{0,2},{1,3},{2,0},{3,1},{4,6},{5,7},{6,4},{7,5},{8,10},{9,11},{10,... | collective-permute-start | bytes 2408456 | tf_op jit(solution)/shard_map/ppermute | solution.py:46
  569.8 13.9 %collective-permute-start.47 = (bf16[2,4,256,128]{3,2,1,0:T(8,128)(2,1)S(1)}, bf16[2,4,256,128]{3,2,1,0:T(8,128)(2,1)S(1)}, u32[]{:S(2)}, u32[]{:S(2)}) collective-permute-start(bf16[2,4,256,128]{3,2,1,0:T(8,128)(2,1)S(1)} %fusion.9), channel_id=1, source_target_pairs={{0,8},{4,12},{8,0},{12,4},{16,24},{20,28},{24,16},{28,20},{1,9},{5... | collective-permute-start | bytes 1572872 | tf_op jit(solution)/shard_map/ppermute | solution.py:46
  573.5 31.6 %collective-permute-start.53 = (bf16[2,4,256,128]{3,2,1,0:T(8,128)(2,1)}, bf16[2,4,256,128]{3,2,1,0:T(8,128)(2,1)}, u32[]{:S(2)}, u32[]{:S(2)}) collective-permute-start(bf16[2,4,256,128]{3,2,1,0:T(8,128)(2,1)} %fusion.8), channel_id=1, source_target_pairs={{0,4},{4,0},{8,12},{12,8},{16,20},{20,16},{24,28},{28,24},{1,5},{5... | collective-permute-start | bytes 1572872 | tf_op jit(solution)/shard_map/ppermute | solution.py:46
  576.3 24.6 %collective-permute-start.51 = (bf16[2,4,256,128]{3,2,1,0:T(8,128)(2,1)}, bf16[2,4,256,128]{3,2,1,0:T(8,128)(2,1)}, u32[]{:S(2)}, u32[]{:S(2)}) collective-permute-start(bf16[2,4,256,128]{3,2,1,0:T(8,128)(2,1)} %fusion.7), channel_id=1, source_target_pairs={{0,4},{4,0},{8,12},{12,8},{16,20},{20,16},{24,28},{28,24},{1,5},{5... | collective-permute-start | bytes 1572872 | tf_op jit(solution)/shard_map/ppermute | solution.py:46
  587.2 46.7 %collective-permute-start.56 = (bf16[9,256,128]{2,1,0:T(8,128)(2,1)}, bf16[9,256,128]{2,1,0:T(8,128)(2,1)}, u32[]{:S(2)}, u32[]{:S(2)}) collective-permute-start(bf16[9,256,128]{2,1,0:T(8,128)(2,1)} %pad_maximum_fusion.4), channel_id=1, source_target_pairs={{0,16},{4,20},{8,24},{12,28},{16,0},{20,4},{24,8},{28,12},{1,17},{... | collective-permute-start | bytes 1769480 | tf_op jit(solution)/shard_map/ppermute | solution.py:46
  591.7 17.8 %collective-permute-start.50 = (bf16[2,2,256,128]{3,2,1,0:T(8,128)(2,1)}, bf16[2,2,256,128]{3,2,1,0:T(8,128)(2,1)S(1)}, u32[]{:S(2)}, u32[]{:S(2)}) collective-permute-start(bf16[2,2,256,128]{3,2,1,0:T(8,128)(2,1)} %fusion.23), channel_id=1, source_target_pairs={{0,8},{4,12},{8,0},{12,4},{16,24},{20,28},{24,16},{28,20},{1,9},{5... | collective-permute-start | bytes 786440 | tf_op jit(solution)/shard_map/ppermute | solution.py:46
  600.5 24.2 %collective-permute-start.57 = (bf16[1600,128]{1,0:T(8,128)(2,1)S(1)}, bf16[1600,128]{1,0:T(8,128)(2,1)S(1)}, u32[]{:S(2)}, u32[]{:S(2)}) collective-permute-start(bf16[1600,128]{1,0:T(8,128)(2,1)S(1)} %pad_maximum_fusion.6), channel_id=1, source_target_pairs={{0,8},{4,12},{8,0},{12,4},{16,24},{20,28},{24,16},{28,20},{1,9},{5... | collective-permute-start | bytes 1228808 | tf_op jit(solution)/shard_map/ppermute | solution.py:46
  604.3 47.7 %collective-permute-start.55 = (bf16[8,256,128]{2,1,0:T(8,128)(2,1)}, bf16[8,256,128]{2,1,0:T(8,128)(2,1)}, u32[]{:S(2)}, u32[]{:S(2)}) collective-permute-start(bf16[8,256,128]{2,1,0:T(8,128)(2,1)} %pad_maximum_fusion.5), channel_id=1, source_target_pairs={{0,16},{4,20},{8,24},{12,28},{16,0},{20,4},{24,8},{28,12},{1,17},{... | collective-permute-start | bytes 1572872 | tf_op jit(solution)/shard_map/ppermute | solution.py:46
  611.4 49.1 %collective-permute-start.54 = (bf16[6,256,128]{2,1,0:T(8,128)(2,1)}, bf16[6,256,128]{2,1,0:T(8,128)(2,1)}, u32[]{:S(2)}, u32[]{:S(2)}) collective-permute-start(bf16[6,256,128]{2,1,0:T(8,128)(2,1)} %pad_maximum_fusion.7), channel_id=1, source_target_pairs={{0,16},{4,20},{8,24},{12,28},{16,0},{20,4},{24,8},{28,12},{1,17},{... | collective-permute-start | bytes 1179656 | tf_op jit(solution)/shard_map/ppermute | solution.py:46
  633.9 30.2 %collective-permute-start.58 = (bf16[832,128]{1,0:T(8,128)(2,1)}, bf16[832,128]{1,0:T(8,128)(2,1)}, u32[]{:S(2)}, u32[]{:S(2)}) collective-permute-start(bf16[832,128]{1,0:T(8,128)(2,1)} %pad_maximum_fusion.8), channel_id=1, source_target_pairs={{0,16},{4,20},{8,24},{12,28},{16,0},{20,4},{24,8},{28,12},{1,17},{... | collective-permute-start | bytes 638984 | tf_op jit(solution)/shard_map/ppermute | solution.py:46
  (64 other events, 388.1 us)
